TPU v7x, 32 devices: a whole 2x2x4 slice. The times are simulated.
32 devices in a mesh: tp: 4 (over x, core), sp: 8 (over z, y).
Axes of the slice: x: 2, y: 2, z: 4, core: 2. Of those that a mesh axis runs over, the one named last changes fastest.
Arguments:
- hidden: bfloat16 [4096, 2048], P('sp'), may hold values from -6 to 6
- segment_ids: int32 [4096], replicated, may hold values from 0 to 1, as said below
- attn_norm: float32 [2048], replicated, may hold values from 0.5 to 1.5
- query_proj: bfloat16 [2048, 2048], P(None, 'tp'), may hold values from -0.125 to 0.125
- key_proj: bfloat16 [2048, 1024], P(None, 'tp'), may hold values from -0.125 to 0.125
- value_proj: bfloat16 [2048, 1024], P(None, 'tp'), may hold values from -0.125 to 0.125
- gate_proj: bfloat16 [2048, 2048], P(None, 'tp'), may hold values from -0.125 to 0.125
- output_proj: bfloat16 [2048, 2048], P('tp'), may hold values from -1 to 1
- query_norm: float32 [128], replicated, may hold values from 0.5 to 1.5
- key_norm: float32 [128], replicated, may hold values from 0.5 to 1.5
- ffn_norm: float32 [2048], replicated, may hold values from 0.5 to 1.5
- ffn_gate: bfloat16 [2048, 6144], P(None, 'sp'), may hold values from -0.125 to 0.125
- ffn_up: bfloat16 [2048, 6144], P(None, 'sp'), may hold values from -0.125 to 0.125
- ffn_down: bfloat16 [6144, 2048], P('sp'), may hold values from -0.078125 to 0.078125
- upstream: bfloat16 [4096, 2048], P('sp'), may hold values from -6 to 6
Outputs:
- layer_out: bfloat16 [4096, 2048], P('sp')
- hidden_grad: float32 [4096, 2048], P('sp')
- attn_norm_grad: float32 [2048], replicated
- query_grad: float32 [2048, 2048], P(None, 'tp')
- key_grad: float32 [2048, 1024], P(None, 'tp')
- value_grad: float32 [2048, 1024], P(None, 'tp')
- gate_grad: float32 [2048, 2048], P(None, 'tp')
- output_grad: float32 [2048, 2048], P('tp')
- query_norm_grad: float32 [128], replicated
- key_norm_grad: float32 [128], replicated
- ffn_norm_grad: float32 [2048], replicated
- ffn_gate_grad: float32 [2048, 6144], P(None, 'sp')
- ffn_up_grad: float32 [2048, 6144], P(None, 'sp')
- ffn_down_grad: float32 [6144, 2048], P('sp')
Inputs may be any that keep to these rules, and one draw needn't show every extreme that they name: `segment_ids`: ids never fall along the tokens and number 2 sequences; one of them holds five eighths to three quarters of the 4096 tokens, the others have near-equal lengths.
All inputs are finite; a program needn't handle non-finite values.
Results may differ from a plain program's by a relative error of at most 0.028.
Values may be sent and summed in bfloat16 or wider, within the bound.
A program may use at most 256 MiB of HBM per device.

v0:
```python
import math

import jax
import jax.numpy as jnp
from jax import lax
from jax.sharding import PartitionSpec as P

EPSILON = 1e-06
THETA = 1000000.0
NEGATIVE = -1e30


def norm_rows(values, gain):
    scales = lax.rsqrt(jnp.mean(values * values, axis=-1, keepdims=True) + EPSILON)
    return (values * scales * gain, scales)


def norm_back(values, scales, gain, incoming):
    weighted = incoming * gain
    inner_sum = jnp.sum(weighted * values, axis=-1, keepdims=True)
    grad_values = (
        scales * weighted - values * (scales * scales * scales) * inner_sum / values.shape[-1]
    )
    return (grad_values, incoming * values * scales)


def rotary(values, cosine, sine):
    half_width = values.shape[-1] // 2
    front_half = values[..., :half_width]
    back_half = values[..., half_width:]
    return jnp.concatenate(
        [front_half * cosine - back_half * sine, back_half * cosine + front_half * sine], axis=-1
    )


def rotary_back(grads, cosine, sine):
    half_width = grads.shape[-1] // 2
    front_half = grads[..., :half_width]
    back_half = grads[..., half_width:]
    return jnp.concatenate(
        [front_half * cosine + back_half * sine, back_half * cosine - front_half * sine], axis=-1
    )


def outer_sum(left, right):
    return lax.dot_general(
        left, right, (((0,), (0,)), ((), ())), preferred_element_type=jnp.float32
    )


def times_transpose(left, right):
    return lax.dot_general(
        left, right, (((1,), (1,)), ((), ())), preferred_element_type=jnp.float32
    )


def token_positions(segment_ids):
    token_count = segment_ids.shape[0]
    row_index = jnp.arange(token_count, dtype=jnp.int32)
    boundary = jnp.concatenate([jnp.ones((1,), jnp.bool_), segment_ids[1:] != segment_ids[:-1]])
    starts = lax.cummax(jnp.where(boundary, row_index, jnp.zeros_like(row_index)), axis=0)
    return (row_index, starts)


def body(
    hidden,
    segment_ids,
    attn_norm,
    query_proj,
    key_proj,
    value_proj,
    gate_proj,
    output_proj,
    query_norm,
    key_norm,
    ffn_norm,
    ffn_gate,
    ffn_up,
    ffn_down,
    upstream,
):
    rows_dev = hidden.shape[0]
    head_width = query_norm.shape[0]
    local_heads = query_proj.shape[1] // head_width
    local_groups = key_proj.shape[1] // head_width
    per_group = local_heads // local_groups
    quarter = rows_dev // lax.axis_size("tp")
    quarter_first = lax.axis_index("tp") * quarter
    own_first = lax.axis_index("sp") * rows_dev
    score_scale = 1.0 / math.sqrt(head_width)
    row_index, starts = token_positions(segment_ids)
    own_index = own_first + jnp.arange(rows_dev, dtype=jnp.int32)
    own_segments = lax.dynamic_slice_in_dim(segment_ids, own_first, rows_dev)
    own_starts = lax.dynamic_slice_in_dim(starts, own_first, rows_dev)
    steps_half = jnp.arange(head_width // 2, dtype=jnp.float32)
    frequencies = jnp.exp(steps_half * (-2.0 * math.log(THETA) / head_width))
    angles = (own_index - own_starts).astype(jnp.float32)[:, None] * frequencies[None, :]
    cosine = jnp.cos(angles)[:, None, :]
    sine = jnp.sin(angles)[:, None, :]
    hidden_full = hidden.astype(jnp.float32)
    normed_full, attn_scales = norm_rows(hidden_full, attn_norm)
    normed = normed_full.astype(jnp.bfloat16)
    query_raw = jnp.dot(normed, query_proj, preferred_element_type=jnp.float32).reshape(
        rows_dev, local_heads, head_width
    )
    key_raw = jnp.dot(normed, key_proj, preferred_element_type=jnp.float32).reshape(
        rows_dev, local_groups, head_width
    )
    value_rows = jnp.dot(normed, value_proj, preferred_element_type=jnp.float32).astype(
        jnp.bfloat16
    )
    gate_raw = jnp.dot(normed, gate_proj, preferred_element_type=jnp.float32)
    query_normed, query_scales = norm_rows(query_raw, query_norm)
    key_normed, key_scales = norm_rows(key_raw, key_norm)
    query_rot = rotary(query_normed, cosine, sine).astype(jnp.bfloat16)
    key_rot = (
        rotary(key_normed, cosine, sine)
        .astype(jnp.bfloat16)
        .reshape(rows_dev, local_groups * head_width)
    )
    query_grid = query_rot.reshape(rows_dev, local_groups, per_group, head_width).transpose(
        1, 2, 0, 3
    )
    all_keys, all_values = (
        lax.all_gather(key_rot, "sp", axis=0, tiled=True),
        lax.all_gather(value_rows, "sp", axis=0, tiled=True),
    )
    key_total = all_keys.shape[0]
    blocking = math.gcd(key_total, 512)
    first_block = own_starts[0] // blocking
    stop_block = (own_first + rows_dev - 1) // blocking + 1
    grid_shape = (local_groups, per_group, rows_dev)

    def block_inputs(position):
        key_first = position * blocking
        key_block = lax.dynamic_slice_in_dim(all_keys, key_first, blocking).reshape(
            blocking, local_groups, head_width
        )
        value_block = lax.dynamic_slice_in_dim(all_values, key_first, blocking).reshape(
            blocking, local_groups, head_width
        )
        key_index = key_first + jnp.arange(blocking, dtype=jnp.int32)
        key_segments = lax.dynamic_slice_in_dim(segment_ids, key_first, blocking)
        allowed = (own_segments[:, None] == key_segments[None, :]) & (
            key_index[None, :] <= own_index[:, None]
        )
        scores = (
            jnp.einsum("kgqd,nkd->kgqn", query_grid, key_block, preferred_element_type=jnp.float32)
            * score_scale
        )
        return (key_first, key_block, value_block, allowed, scores)

    def stats_step(position, carried):
        maxima, totals = carried
        block_parts = block_inputs(position)
        allowed = block_parts[3]
        masked = jnp.where(allowed, block_parts[4], NEGATIVE)
        new_max = jnp.maximum(maxima, jnp.max(masked, axis=-1))
        exps_kept = jnp.where(allowed, jnp.exp(masked - new_max[..., None]), 0.0)
        return (new_max, totals * jnp.exp(maxima - new_max) + jnp.sum(exps_kept, axis=-1))

    maxima, totals = lax.fori_loop(
        first_block,
        stop_block,
        stats_step,
        (jnp.full(grid_shape, NEGATIVE, jnp.float32), jnp.zeros(grid_shape, jnp.float32)),
    )
    log_totals = maxima + jnp.log(totals)

    def mix_step(position, accum):
        block_parts = block_inputs(position)
        probs_low = jnp.where(
            block_parts[3], jnp.exp(block_parts[4] - log_totals[..., None]), 0.0
        ).astype(jnp.bfloat16)
        return accum + jnp.einsum(
            "kgqn,nkd->kgqd", probs_low, block_parts[2], preferred_element_type=jnp.float32
        )

    mixed_grid = lax.fori_loop(
        first_block, stop_block, mix_step, jnp.zeros(grid_shape + (head_width,), jnp.float32)
    )
    mixed_heads = mixed_grid.transpose(2, 0, 1, 3).reshape(rows_dev, local_heads * head_width)
    gate_sig = jax.nn.sigmoid(gate_raw)
    gated_heads = (mixed_heads * gate_sig).astype(jnp.bfloat16)
    attn_quarter = lax.psum_scatter(
        jnp.dot(gated_heads, output_proj, preferred_element_type=jnp.float32).astype(jnp.bfloat16),
        "tp",
        scatter_dimension=0,
        tiled=True,
    ).astype(jnp.float32)
    middle = lax.dynamic_slice_in_dim(hidden_full, quarter_first, quarter) + attn_quarter
    normed_two_full, ffn_scales = norm_rows(middle, ffn_norm)
    normed_two = normed_two_full.astype(jnp.bfloat16)
    gathered_inputs = lax.all_gather(normed_two, "sp", axis=0, tiled=True)
    gate_vals = jnp.dot(gathered_inputs, ffn_gate, preferred_element_type=jnp.float32)
    up_vals = jnp.dot(gathered_inputs, ffn_up, preferred_element_type=jnp.float32)
    gate_sig_two = jax.nn.sigmoid(gate_vals)
    inner_act = (gate_vals * gate_sig_two * up_vals).astype(jnp.bfloat16)
    mlp_quarter = lax.psum_scatter(
        jnp.dot(inner_act, ffn_down, preferred_element_type=jnp.float32).astype(jnp.bfloat16),
        "sp",
        scatter_dimension=0,
        tiled=True,
    ).astype(jnp.float32)
    out_quarter = (middle + mlp_quarter).astype(jnp.bfloat16)
    layer_out = lax.all_gather(out_quarter, "tp", axis=0, tiled=True)
    grad_quarter = lax.dynamic_slice_in_dim(upstream, quarter_first, quarter)
    grad_piece = lax.all_gather(grad_quarter, "sp", axis=0, tiled=True)
    input_piece = lax.all_gather(normed_two, "sp", axis=0, tiled=True)
    grad_inner = times_transpose(grad_piece, ffn_down)
    grad_gate = (
        grad_inner * up_vals * (gate_sig_two * (1.0 + gate_vals * (1.0 - gate_sig_two)))
    ).astype(jnp.bfloat16)
    grad_up = (grad_inner * (gate_vals * gate_sig_two)).astype(jnp.bfloat16)
    mlp_sums = (
        outer_sum(inner_act, grad_piece),
        outer_sum(input_piece, grad_gate),
        outer_sum(input_piece, grad_up),
        grad_gate,
        grad_up,
    )
    down_acc, gate_acc, up_acc, gate_buffer, up_buffer = mlp_sums
    grad_two = lax.psum_scatter(
        (times_transpose(gate_buffer, ffn_gate) + times_transpose(up_buffer, ffn_up)).astype(
            jnp.bfloat16
        ),
        "sp",
        scatter_dimension=0,
        tiled=True,
    ).astype(jnp.float32)
    norm_grad_two, ffn_gain_terms = norm_back(middle, ffn_scales, ffn_norm, grad_two)
    grad_middle_quarter = grad_quarter.astype(jnp.float32) + norm_grad_two
    grad_middle = lax.all_gather(
        grad_middle_quarter.astype(jnp.bfloat16), "tp", axis=0, tiled=True
    ).astype(grad_middle_quarter.dtype)
    grad_branch = grad_middle.astype(jnp.bfloat16)
    output_w_grad = outer_sum(gated_heads, grad_branch)
    grad_gated = times_transpose(grad_branch, output_proj)
    grad_mixed = (grad_gated * gate_sig).astype(jnp.bfloat16)
    grad_gate_raw = (grad_gated * mixed_heads * (gate_sig * (1.0 - gate_sig))).astype(jnp.bfloat16)
    grad_grid = grad_mixed.reshape(rows_dev, local_groups, per_group, head_width).transpose(
        1, 2, 0, 3
    )
    deltas = jnp.sum(grad_grid.astype(jnp.float32) * mixed_grid, axis=-1)
    group_width = local_groups * head_width

    def back_step(position, carried):
        query_acc, kv_buffer = carried
        key_first, key_block, value_block, allowed, scores = block_inputs(position)
        probs_full = jnp.where(allowed, jnp.exp(scores - log_totals[..., None]), 0.0)
        probs_low = probs_full.astype(jnp.bfloat16)
        grad_probs = jnp.einsum(
            "kgqd,nkd->kgqn", grad_grid, value_block, preferred_element_type=jnp.float32
        )
        grad_scores = (probs_full * (grad_probs - deltas[..., None])).astype(jnp.bfloat16)
        query_acc = query_acc + jnp.einsum(
            "kgqn,nkd->kgqd", grad_scores, key_block, preferred_element_type=jnp.float32
        )
        key_part = (
            jnp.einsum(
                "kgqn,kgqd->nkd", grad_scores, query_grid, preferred_element_type=jnp.float32
            )
            * score_scale
        )
        value_part = jnp.einsum(
            "kgqn,kgqd->nkd", probs_low, grad_grid, preferred_element_type=jnp.float32
        )
        update = jnp.concatenate(
            [key_part.reshape(blocking, group_width), value_part.reshape(blocking, group_width)],
            axis=1,
        )
        return (query_acc, lax.dynamic_update_slice_in_dim(kv_buffer, update, key_first, 0))

    query_acc, kv_buffer = lax.fori_loop(
        first_block,
        stop_block,
        back_step,
        (
            jnp.zeros(grid_shape + (head_width,), jnp.float32),
            jnp.zeros((key_total, 2 * group_width), jnp.float32),
        ),
    )
    kv_grads = lax.psum_scatter(
        kv_buffer.astype(jnp.bfloat16), "sp", scatter_dimension=0, tiled=True
    ).astype(jnp.float32)
    grad_key_rot = kv_grads[:, :group_width].reshape(rows_dev, local_groups, head_width)
    grad_value_low = kv_grads[:, group_width:].astype(jnp.bfloat16)
    grad_query_rot = (
        (query_acc * score_scale).transpose(2, 0, 1, 3).reshape(rows_dev, local_heads, head_width)
    )
    grad_query_raw, query_gain_terms = norm_back(
        query_raw, query_scales, query_norm, rotary_back(grad_query_rot, cosine, sine)
    )
    grad_key_raw, key_gain_terms = norm_back(
        key_raw, key_scales, key_norm, rotary_back(grad_key_rot, cosine, sine)
    )
    grad_query_low = grad_query_raw.reshape(rows_dev, local_heads * head_width).astype(jnp.bfloat16)
    grad_key_low = grad_key_raw.reshape(rows_dev, group_width).astype(jnp.bfloat16)
    query_w_grad = outer_sum(normed, grad_query_low)
    key_w_grad = outer_sum(normed, grad_key_low)
    value_w_grad = outer_sum(normed, grad_value_low)
    gate_w_grad = outer_sum(normed, grad_gate_raw)
    grad_normed_part = (
        times_transpose(grad_query_low, query_proj)
        + times_transpose(grad_key_low, key_proj)
        + times_transpose(grad_value_low, value_proj)
        + times_transpose(grad_gate_raw, gate_proj)
    )
    grad_normed = lax.psum(grad_normed_part.astype(jnp.bfloat16), "tp").astype(jnp.float32)
    norm_grad_one, attn_gain_terms = norm_back(hidden_full, attn_scales, attn_norm, grad_normed)
    hidden_grad = grad_middle + norm_grad_one
    tp_sums = (
        lax.psum(gate_acc.astype(jnp.bfloat16), "tp").astype(jnp.float32),
        lax.psum(up_acc.astype(jnp.bfloat16), "tp").astype(jnp.float32),
        lax.psum(down_acc.astype(jnp.bfloat16), "tp").astype(jnp.float32),
        lax.psum(jnp.sum(ffn_gain_terms, axis=0).astype(jnp.bfloat16), "tp").astype(jnp.float32),
        lax.psum(jnp.sum(query_gain_terms, axis=(0, 1)).astype(jnp.bfloat16), "tp").astype(
            jnp.float32
        ),
        lax.psum(jnp.sum(key_gain_terms, axis=(0, 1)).astype(jnp.bfloat16), "tp").astype(
            jnp.float32
        ),
    )
    sp_sums = (
        lax.psum(query_w_grad.astype(jnp.bfloat16), "sp").astype(jnp.float32),
        lax.psum(key_w_grad.astype(jnp.bfloat16), "sp").astype(jnp.float32),
        lax.psum(value_w_grad.astype(jnp.bfloat16), "sp").astype(jnp.float32),
        lax.psum(gate_w_grad.astype(jnp.bfloat16), "sp").astype(jnp.float32),
        lax.psum(output_w_grad.astype(jnp.bfloat16), "sp").astype(jnp.float32),
        lax.psum(jnp.sum(attn_gain_terms, axis=0).astype(jnp.bfloat16), "sp").astype(jnp.float32),
        lax.psum(tp_sums[3].astype(jnp.bfloat16), "sp").astype(jnp.float32),
        lax.psum(tp_sums[4].astype(jnp.bfloat16), "sp").astype(jnp.float32),
        lax.psum(tp_sums[5].astype(jnp.bfloat16), "sp").astype(jnp.float32),
    )
    return (
        layer_out,
        hidden_grad,
        sp_sums[5],
        sp_sums[0],
        sp_sums[1],
        sp_sums[2],
        sp_sums[3],
        sp_sums[4],
        sp_sums[7],
        sp_sums[8],
        sp_sums[6],
        tp_sums[0],
        tp_sums[1],
        tp_sums[2],
    )


def solution(mesh):
    placed = (
        P("sp", None),
        P(),
        P(),
        P(None, "tp"),
        P(None, "tp"),
        P(None, "tp"),
        P(None, "tp"),
        P("tp", None),
        P(),
        P(),
        P(),
        P(None, "sp"),
        P(None, "sp"),
        P("sp", None),
        P("sp", None),
    )
    return jax.shard_map(
        body,
        mesh=mesh,
        in_specs=placed,
        out_specs=(
            P("sp", None),
            P("sp", None),
            P(),
            P(None, "tp"),
            P(None, "tp"),
            P(None, "tp"),
            P(None, "tp"),
            P("tp", None),
            P(),
            P(),
            P(),
            P(None, "sp"),
            P(None, "sp"),
            P("sp", None),
        ),
        check_vma=False,
    )
```

profile of v0, /device:TPU:0, one launch (start us, length us, event | category | flops | bytes accessed | tf_op | source)
XLA Modules:
  0.0 1271.4 jit_solution(7341668663548912079)
XLA Ops:
  7.3 2.2 fusion.25
  11.7 3.6 multiply_reduce_fusion.5
  18.7 3.3 convolution_convert_fusion.10
  25.3 3.6 multiply_reduce_fusion.3
  31.4 2.0 copy.93
  33.5 38.3 %all-gather.7.cloned.1.call-done = bf16[4096,256]{0,1:T(8,128)(2,1)} async-done(((bf16[512,256]{0,1:T(8,128)(2,1)}), bf16[4096,256]{0,1:T(8,128)(2,1)}) %all-gather.7.cloned.1.call-update) | async-done | bytes 2097168 | tf_op jit(solution)/shard_map/all_gather | solution.py:125
  71.8 4.5 while.37
  73.2 2.0 fusion.157
  76.3 45.5 %all-gather.9.cloned.1.call-done = bf16[4096,256]{1,0:T(8,128)(2,1)} async-done(((bf16[512,256]{1,0:T(8,128)(2,1)}), bf16[4096,256]{1,0:T(8,128)(2,1)}) %all-gather.9.cloned.1.call-update) | async-done | bytes 2097168 | tf_op jit(solution)/shard_map/all_gather | solution.py:126
  121.8 4.1 copy.94
  127.0 6.7 while.38
  127.3 1.9 constant_dynamic-slice_fusion.10
  129.2 4.4 fusion.161
  133.7 2.5 copy.95
  136.2 5.1 fusion.51
  142.2 2.6 convolution_convert_fusion.7
  144.9 4.1 convert_element_type.178
  149.0 58.6 %reduce-scatter.5.cloned.1.call-done = bf16[128,2048]{1,0:T(8,128)(2,1)} async-done(((bf16[512,2048]{1,0:T(8,128)(2,1)}), bf16[128,2048]{1,0:T(8,128)(2,1)}) %reduce-scatter.5.cloned.1.call-update) | async-done | bytes 524304 | tf_op jit(solution)/shard_map/reduce_scatter | solution.py:185
  207.6 1.6 multiply_reduce_fusion.2
  211.2 1.9 constant_dynamic-slice_fusion.5
  213.2 70.9 %all-gather.11.cloned.1.call-done = bf16[1024,2048]{1,0:T(8,128)(2,1)} async-done(((bf16[128,2048]{1,0:T(8,128)(2,1)}), bf16[1024,2048]{1,0:T(8,128)(2,1)}) %all-gather.11.cloned.1.call-update) | async-done | bytes 4194320 | tf_op jit(solution)/shard_map/all_gather | solution.py:194
  284.1 8.4 fusion.78
  292.5 5.1 fusion.77
  297.6 60.4 %all-gather.15.cloned.1.call-done = bf16[1024,2048]{1,0:T(8,128)(2,1)} async-done(((bf16[128,2048]{1,0:T(8,128)(2,1)}), bf16[1024,2048]{1,0:T(8,128)(2,1)}) %all-gather.15.cloned.1.call-update) | async-done | bytes 4194320 | tf_op jit(solution)/shard_map/all_gather | solution.py:208
  358.0 9.8 multiply_convert_fusion
  367.8 3.4 fusion.79
  371.3 5.2 add_convert_fusion
  376.6 6.3 convolution_convert_fusion
  383.0 80.5 %reduce-scatter.9.cloned.1.call-done = bf16[128,2048]{1,0:T(8,128)(2,1)} async-done(((bf16[1024,2048]{1,0:T(8,128)(2,1)}), bf16[128,2048]{1,0:T(8,128)(2,1)}) %reduce-scatter.9.cloned.1.call-update) | async-done | bytes 524304 | tf_op jit(solution)/shard_map/reduce_scatter | solution.py:223
  464.9 90.8 %reduce-scatter.7.cloned.1.call-done = bf16[128,2048]{1,0:T(8,128)(2,1)} async-done(((bf16[1024,2048]{1,0:T(8,128)(2,1)}), bf16[128,2048]{1,0:T(8,128)(2,1)}) %reduce-scatter.7.cloned.1.call-update) | async-done | bytes 524304 | tf_op jit(solution)/shard_map/reduce_scatter | solution.py:199
  555.7 2.9 fusion.41
  559.1 22.0 %all-gather.17.cloned.1.call-done = bf16[512,2048]{1,0:T(8,128)(2,1)} async-done(((bf16[128,2048]{1,0:T(8,128)(2,1)}), bf16[512,2048]{1,0:T(8,128)(2,1)}) %all-gather.17.cloned.1.call-update) | async-done | bytes 2097168 | tf_op jit(solution)/shard_map/all_gather | solution.py:233
  581.0 4.7 multiply_reduce_fusion.1
  586.7 2.5 broadcast_in_dim.45
  589.2 10.6 while.39
  591.4 2.1 fusion.174
  593.6 2.6 fusion.173
  601.3 7.6 convolution_convert_fusion.1
  608.9 4.9 convolution_convert_fusion.2
  613.8 4.9 convolution_convert_fusion.3
  621.7 1.4 multiply_add_fusion.1
  626.3 3.3 fusion.80
  629.6 112.3 %reduce-scatter.11.cloned.1.call-done = bf16[512,512]{0,1:T(8,128)(2,1)} async-done(((bf16[4096,512]{0,1:T(8,128)(2,1)}), bf16[512,512]{0,1:T(8,128)(2,1)}) %reduce-scatter.11.cloned.1.call-update) | async-done | bytes 524304 | tf_op jit(solution)/shard_map/reduce_scatter | solution.py:283
  746.2 1.4 copy-done.7
  748.3 2.8 add_convert_fusion.1
  751.5 4.5 convolution_convert_fusion.4
  756.0 2.8 convolution_convert_fusion.6
  758.8 2.8 convolution_convert_fusion.5
  761.6 2.0 convolution_convert_fusion.9
  763.6 2.0 convolution_convert_fusion.8
  765.7 7.0 all-reduce.2
  772.7 200.6 %all-reduce.9.cloned.1.call-done = (bf16[512,2048]{1,0:T(8,128)(2,1)}, bf16[2048,768]{1,0:T(8,128)(2,1)}, bf16[2048,768]{1,0:T(8,128)(2,1)}, bf16[768,2048]{1,0:T(8,128)(2,1)}) async-done(((bf16[512,2048]{1,0:T(8,128)(2,1)}, bf16[2048,768]{1,0:T(8,128)(2,1)}, bf16[2048,768]{1,0:T(8,128)(2,1)}, bf16[768,2048]{1,0:T(8,128)(2,1)}), (bf16[512,2048]{1,0:T(8,128)(2,1)}, bf16[2048,768]{1,0:T(8,128)(2,1)}, ...) | async-done | bytes 11534352 | tf_op jit(solution)/shard_map/psum | solution.py:309
  973.3 3.2 fusion.32
  976.4 23.1 %all-reduce = (bf16[2048]{0:T(1024)(128)(2,1)S(1)}, bf16[128]{0:T(256)(128)(2,1)S(1)}, bf16[128]{0:T(256)(128)(2,1)S(1)}, bf16[2048]{0:T(1024)(128)(2,1)S(1)}) all-reduce(bf16[2048]{0:T(1024)(128)(2,1)S(1)} %get-tuple-element.381, bf16[128]{0:T(256)(128)(2,1)S(1)} %get-tuple-element.458, ...), channel_id=1, replica_groups=mesh['tp'=4,'sp'=8] {'sp'}, use_global_device_ids=true, to_apply=%region_25.26 | all-reduce | flops 4352 | bytes 17408 | tf_op jit(solution)/shard_map/psum | solution.py:330
  1001.8 5.2 convert_element_type.225
  1007.0 3.2 convert_element_type.227
  1010.2 3.6 convert_element_type.229
  1013.7 3.5 fusion.24
  1017.3 232.3 %all-reduce.7.cloned.1.call-done = (bf16[2048,512]{1,0:T(8,128)(2,1)}, bf16[2048,256]{1,0:T(8,128)(2,1)}, bf16[2048,256]{1,0:T(8,128)(2,1)}, bf16[2048,512]{1,0:T(8,128)(2,1)}, bf16[512,2048]{1,0:T(8,128)(2,1)}) async-done(((bf16[2048,512]{1,0:T(8,128)(2,1)}, bf16[2048,256]{1,0:T(8,128)(2,1)}, bf16[2048,256]{1,0:T(8,128)(2,1)}, bf16[2048,512]{1,0:T(8,128)(2,1)}, bf16[512,2048]{1,0:T(8,128)(2,1)}), ...) | async-done | bytes 8388624 | tf_op jit(solution)/shard_map/psum | solution.py:325
  1249.6 4.3 convert_element_type.209
  1253.8 1.5 convert_element_type.211
  1255.4 1.5 convert_element_type.213
  1256.9 2.6 convert_element_type.215
  1259.5 2.7 convert_element_type.217
  (234 shorter events, 41.3 us)
Async XLA Ops:
  7.2 350.9 %copy-start = (bf16[768,2048]{1,0:T(8,128)(2,1)S(1)}, bf16[768,2048]{1,0:T(8,128)(2,1)}, u32[]{:S(2)}) copy-start(bf16[768,2048]{1,0:T(8,128)(2,1)} %param.34) | copy-start | bytes 9437188
  7.2 64.6 %all-gather.7.cloned.1.call-start = ((), (), s32[]{:S(2)}) async-start(), calls=%async_computation.4 | async-start | bytes 2359296 | tf_op jit(solution)/shard_map/all_gather | solution.py:125
  9.5 7.0 copy-start.55
  10.1 126.1 %copy-start.50 = (f32[512]{0:T(512)}, f32[512]{0:T(512)S(1)}, u32[]{:S(2)}) copy-start(f32[512]{0:T(512)S(1)} %get-tuple-element.509) | copy-start | bytes 6148
  11.7 7.0 copy-start.47
  15.9 6.1 copy-start.45
  16.5 13.9 %copy-start.20 = (f32[512,64]{0,1:T(8,128)}, f32[512,64]{0,1:T(8,128)S(1)}, u32[]{:S(2)}) copy-start(f32[512,64]{0,1:T(8,128)S(1)} %get-tuple-element.506) | copy-start | bytes 393220
  16.5 13.9 %copy-start.22 = (f32[512,64]{0,1:T(8,128)}, f32[512,64]{0,1:T(8,128)S(1)}, u32[]{:S(2)}) copy-start(f32[512,64]{0,1:T(8,128)S(1)} %get-tuple-element.507) | copy-start | bytes 393220
  18.6 3.5 copy-start.41
  18.6 103.2 %all-gather.9.cloned.1.call-start = ((), (), s32[]{:S(2)}) async-start(), calls=%async_computation.5 | async-start | bytes 2359296 | tf_op jit(solution)/shard_map/all_gather | solution.py:126
  22.0 185.6 %reduce-scatter.5.cloned.1.call-start = ((), (), s32[]{:S(2)}) async-start(), calls=%async_computation.6 | async-start | bytes 2621440 | tf_op jit(solution)/shard_map/reduce_scatter | solution.py:185
  25.3 4.9 copy-start.54
  136.2 5.9 copy-start.28
  144.8 139.3 %all-gather.11.cloned.1.call-start = ((), (), s32[]{:S(2)}) async-start(), calls=%async_computation.7 | async-start | bytes 4718592 | tf_op jit(solution)/shard_map/all_gather | solution.py:194
  144.9 65.3 %copy-start.42 = (f32[2048]{0:T(1024)S(1)}, f32[2048]{0:T(1024)}, u32[]{:S(2)}) copy-start(f32[2048]{0:T(1024)} %param.31) | copy-start | bytes 24580
  211.2 146.9 %all-gather.15.cloned.1.call-start = ((), (), s32[]{:S(2)}) async-start(), calls=%async_computation.10 | async-start | bytes 4718592 | tf_op jit(solution)/shard_map/all_gather | solution.py:208
  213.1 250.4 %reduce-scatter.9.cloned.1.call-start = ((), (), s32[]{:S(2)}) async-start(), calls=%async_computation.11 | async-start | bytes 4718592 | tf_op jit(solution)/shard_map/reduce_scatter | solution.py:223
  284.1 8.4 copy-start.57
  284.1 8.4 copy-start.59
  358.0 9.8 copy-start.60
  367.8 3.5 copy-start.64
  367.8 3.5 copy-start.66
  367.8 3.5 copy-start.61
  376.6 179.2 %reduce-scatter.7.cloned.1.call-start = ((), (), s32[]{:S(2)}) async-start(), calls=%async_computation.8 | async-start | bytes 4718592 | tf_op jit(solution)/shard_map/reduce_scatter | solution.py:199
  383.0 80.6 %copy-start.9 = (f32[128,2048]{1,0:T(8,128)S(1)}, f32[128,2048]{1,0:T(8,128)}, u32[]{:S(2)}) copy-start(f32[128,2048]{1,0:T(8,128)} %copy-done.8) | copy-start | bytes 3145732
  383.0 175.7 %copy-start.10 = (f32[2,2,512,128]{3,2,1,0:T(8,128)S(1)}, f32[2,2,512,128]{3,2,1,0:T(8,128)}, u32[]{:S(2)}) copy-start(f32[2,2,512,128]{3,2,1,0:T(8,128)} %get-tuple-element.187) | copy-start | bytes 3145732
  383.0 198.0 %all-gather.17.cloned.1.call-start = ((), (), s32[]{:S(2)}) async-start(), calls=%async_computation.12 | async-start | bytes 2621440 | tf_op jit(solution)/shard_map/all_gather | solution.py:233
  555.7 25.3 %copy-start.16 = (f32[512,512]{0,1:T(8,128)S(1)}, f32[512,512]{0,1:T(8,128)}, u32[]{:S(2)}) copy-start(f32[512,512]{0,1:T(8,128)} %get-tuple-element.517) | copy-start | bytes 3145732
  558.7 183.2 %reduce-scatter.11.cloned.1.call-start = ((), (), s32[]{:S(2)}) async-start(), calls=%async_computation.13 | async-start | bytes 4718592 | tf_op jit(solution)/shard_map/reduce_scatter | solution.py:283
  585.7 3.6 copy-start.2
  599.9 165.8 %all-gather.13.cloned.1.call-start = ((), (), s32[]{:S(2)}) async-start(), calls=%async_computation.9 | async-start | bytes 2621440 | tf_op jit(solution)/shard_map/all_gather | solution.py:206
  601.3 7.6 copy-start.58
  601.3 7.6 copy-start.67
  608.9 4.9 copy-start.65
  613.8 5.1 copy-start.5
  618.7 354.5 %all-reduce.9.cloned.1.call-start = ((), (), s32[]{:S(2)}) async-start(), calls=%async_computation.15 | async-start | bytes 23068672 | tf_op jit(solution)/shard_map/psum | solution.py:309
  619.1 2.6 copy-start.21
  619.1 2.6 copy-start.23
  620.5 2.6 copy-start.12
  623.2 1.8 copy-start.19
  623.8 2.5 copy-start.34
  624.3 5.3 copy-start.24
  629.6 113.5 %copy-start.15 = (f32[512,256]{0,1:T(8,128)S(1)}, f32[512,256]{0,1:T(8,128)}, u32[]{:S(2)}) copy-start(f32[512,256]{0,1:T(8,128)} %get-tuple-element.513) | copy-start | bytes 1572868
  629.6 113.6 %copy-start.46 = (f32[512,2]{0,1:T(2,128)S(1)}, f32[512,2]{0,1:T(2,128)}, u32[]{:S(2)}) copy-start(f32[512,2]{0,1:T(2,128)} %copy-done.45) | copy-start | bytes 12292
  629.6 113.7 %copy-start.52 = (f32[512,2]{0,1:T(2,128)S(1)}, f32[512,2]{0,1:T(2,128)}, u32[]{:S(2)}) copy-start(f32[512,2]{0,1:T(2,128)} %get-tuple-element.504) | copy-start | bytes 12292
  745.4 2.2 copy-start.7
  745.4 2.9 copy-start.29
  745.4 2.9 copy-start.32
  751.2 4.8 copy-start.6
  751.2 4.8 copy-start.25
  751.2 4.8 copy-start.48
  751.2 4.8 copy-start.51
  751.3 498.3 %all-reduce.7.cloned.1.call-start = ((), (), s32[]{:S(2)}) async-start(), calls=%async_computation.14 | async-start | bytes 16777216 | tf_op jit(solution)/shard_map/psum | solution.py:325
  761.6 2.0 copy-start.40
  1001.8 5.2 copy-start.27
  1007.0 3.2 copy-start.26
  1010.2 3.6 copy-start.13
  1010.2 3.6 copy-start.14
  1010.2 3.6 copy-start.53
  1249.6 4.3 copy-start.36
  1253.8 3.0 copy-start.31
  1256.9 2.6 copy-start.30
  1259.5 2.7 copy-start.33
  1259.5 4.8 copy-start.1
  (16 other events, 17.3 us)
Sparse Core Ops, SparseCore 0:
  18.7 53.0 all-gather.6
  74.5 47.2 all-gather.8
  144.9 62.6 reduce-scatter.4
  211.3 72.7 all-gather.10
  286.7 71.3 all-gather.14
  376.7 86.8 reduce-scatter.8
  467.8 87.9 reduce-scatter.6
  558.8 22.1 all-gather.16
  600.0 141.8 reduce-scatter.10
  743.3 22.1 all-gather.12
  769.4 203.7 all-reduce.8
  978.6 270.8 all-reduce.6
where the time goes:
time: 1280 us; the launch traced here: 1270 us
  waiting for transfers between devices  1010 us (79%)
  matrix products  114 us (9%)
  other arithmetic  60.6 us (5%)
  local copies, waits for them, and re-layouts  35.1 us (3%)
  blocking collectives  30.1 us (2%)
  between operations  17.7 us (1%)
    psum x1, waiting for transfers between devices, body(): lax.psum(query_w_grad.astype(jnp.bfloat16), 'sp').astype(jnp.float32)  232 us
    psum x1, waiting for transfers between devices, body(): lax.psum(grad_normed_part.astype(jnp.bfloat16), 'tp').astype(jnp.float32)  201 us
    reduce_scatter x1, waiting for transfers between devices, body(): lax.psum_scatter(kv_buffer.astype(jnp.bfloat16), 'sp', scatter_dimension=...  112 us
    reduce_scatter x1, waiting for transfers between devices, body(): lax.psum_scatter(jnp.dot(inner_act, ffn_down, preferred_element_type=jnp....  90.8 us
    reduce_scatter x1, waiting for transfers between devices, body(): lax.psum_scatter((times_transpose(gate_buffer, ffn_gate) + times_transpos...  80.5 us
    all_gather x1, waiting for transfers between devices, body(): gathered_inputs = lax.all_gather(normed_two, 'sp', axis=0, tiled=True)  70.9 us
    all_gather x1, waiting for transfers between devices, body(): grad_piece = lax.all_gather(grad_quarter, 'sp', axis=0, tiled=True)  60.4 us
    reduce_scatter x1, waiting for transfers between devices, body(): lax.psum_scatter(jnp.dot(gated_heads, output_proj, preferred_element_type...  58.6 us
  transfers between devices with their start and end apart: 12, of which 11 were waited for; matrix products, arithmetic and copies ran while one was open for 9% of the time, Pallas kernels for 0%

commit v1 on v0

v1 whole, which is shorter than its diff:
```python
import functools
import math

import jax
import jax.numpy as jnp
from jax import lax
from jax.experimental import pallas as pl
from jax.experimental.pallas import tpu as pltpu
from jax.sharding import PartitionSpec as P

EPSILON = 1e-06
THETA = 1000000.0
LOG2E = 1.4426950408889634
F32 = jnp.float32
BF16 = jnp.bfloat16


def norm_scales(values):
    return lax.rsqrt(jnp.mean(values * values, axis=-1, keepdims=True) + EPSILON)


def norm_rows(values, gain):
    scales = norm_scales(values)
    return (values * scales * gain, scales)


def norm_back(values, scales, gain, incoming):
    weighted = incoming * gain
    inner_sum = jnp.sum(weighted * values, axis=-1, keepdims=True)
    grad_values = (
        scales * weighted - values * (scales * scales * scales) * inner_sum / values.shape[-1]
    )
    return (grad_values, incoming * values * scales)


def rotary(values, cosine, sine):
    half_width = values.shape[-1] // 2
    front_half = values[..., :half_width]
    back_half = values[..., half_width:]
    return jnp.concatenate(
        [front_half * cosine - back_half * sine, back_half * cosine + front_half * sine], axis=-1
    )


def rotary_back(grads, cosine, sine):
    half_width = grads.shape[-1] // 2
    front_half = grads[..., :half_width]
    back_half = grads[..., half_width:]
    return jnp.concatenate(
        [front_half * cosine + back_half * sine, back_half * cosine - front_half * sine], axis=-1
    )


def matmul(left, right):
    return jnp.dot(left, right, preferred_element_type=F32)


def outer_sum(left, right):
    return lax.dot_general(left, right, (((0,), (0,)), ((), ())), preferred_element_type=F32)


def times_transpose(left, right):
    return lax.dot_general(left, right, (((1,), (1,)), ((), ())), preferred_element_type=F32)


def attn_forward_kernel(first, diagonal, scale, info, starts, queries, kv_a, kv_b, *rest):
    if first:
        acc_out, sum_out = rest
    else:
        acc_in, sum_in, acc_out, sum_out = rest
    rows = queries.shape[0]
    keys_n = kv_a.shape[1]
    per_group = queries.shape[1] // kv_a.shape[2]
    width = kv_a.shape[2]
    if first:
        acc_out[...] = jnp.zeros_like(acc_out)
        sum_out[...] = jnp.zeros_like(sum_out)
    else:
        acc_out[...] = acc_in[...]
        sum_out[...] = sum_in[...]
    own_first = info[0]
    for slot, block in enumerate((kv_a, kv_b)):
        key_first = info[1 + slot]
        live = info[3 + slot] > 0

        def work(masked, causal):
            ones = jnp.ones((keys_n, width), BF16)
            values = jnp.concatenate([block[1], ones], axis=1)
            keys = block[0]
            if masked:
                key_index = key_first + lax.broadcasted_iota(jnp.int32, (rows, keys_n), 1)
                allowed = key_index >= starts[...]
                if causal:
                    row_index = own_first + lax.broadcasted_iota(jnp.int32, (rows, keys_n), 0)
                    allowed = allowed & (key_index <= row_index)
            for head in range(per_group):
                cols = slice(head * width, (head + 1) * width)
                scores = times_transpose(queries[:, cols], keys)
                weights = jnp.exp2(scores * (scale * LOG2E))
                if masked:
                    weights = jnp.where(allowed, weights, 0.0)
                both = matmul(weights.astype(BF16), values)
                acc_out[:, cols] += both[:, :width]
                sum_out[:, cols] += both[:, width:]

        if diagonal and slot == 0:
            work(True, True)
        else:
            full = info[5 + slot] > 0
            pl.when(live & full)(functools.partial(work, False, False))
            pl.when(live & jnp.logical_not(full))(functools.partial(work, True, False))


def attn_forward(info, starts, queries, kv_a, kv_b, carried, scale):
    rows, all_width = queries.shape
    width = 128
    groups = kv_a.shape[2] // width
    group_width = all_width // groups
    keys_n = kv_a.shape[1]
    first = carried is None
    spec_q = pl.BlockSpec((rows, group_width), lambda g, info: (0, g))
    spec_kv = pl.BlockSpec((2, keys_n, width), lambda g, info: (0, 0, g))
    specs = [pl.BlockSpec((rows, 1), lambda g, info: (0, 0)), spec_q, spec_kv, spec_kv]
    operands = [starts, queries, kv_a, kv_b]
    if not first:
        specs += [spec_q, spec_q]
        operands += list(carried)
    return pl.pallas_call(
        functools.partial(attn_forward_kernel, first, first, scale),
        grid_spec=pltpu.PrefetchScalarGridSpec(
            num_scalar_prefetch=1,
            grid=(groups,),
            in_specs=specs,
            out_specs=[spec_q, spec_q],
        ),
        out_shape=[jax.ShapeDtypeStruct((rows, all_width), F32)] * 2,
        compiler_params=pltpu.CompilerParams(dimension_semantics=("arbitrary",)),
        cost_estimate=pl.CostEstimate(
            flops=16 * rows * keys_n * all_width,
            transcendentals=2 * rows * keys_n * all_width // width,
            bytes_accessed=8 * rows * all_width,
        ),
        name="attn_forward",
    )(info, *operands)


def attn_backward_kernel(first, diagonal, scale, info, starts, lse, deltas, queries, grads, kv_a, kv_b, *rest):
    if first:
        grad_q, grad_a, grad_b = rest
    else:
        grad_in, grad_q, grad_a, grad_b = rest
    rows = queries.shape[0]
    keys_n = kv_a.shape[1]
    width = kv_a.shape[2]
    per_group = queries.shape[1] // width
    if first:
        grad_q[...] = jnp.zeros_like(grad_q)
    else:
        grad_q[...] = grad_in[...]
    own_first = info[0]
    for slot, (block, out) in enumerate(((kv_a, grad_a), (kv_b, grad_b))):
        key_first = info[1 + slot]
        live = info[3 + slot] > 0

        def work(masked, causal):
            keys = block[0]
            values = block[1]
            keys_t = keys.T
            if masked:
                key_index = key_first + lax.broadcasted_iota(jnp.int32, (keys_n, rows), 0)
                allowed = key_index >= starts[...]
                if causal:
                    row_index = own_first + lax.broadcasted_iota(jnp.int32, (keys_n, rows), 1)
                    allowed = allowed & (key_index <= row_index)
            total_k = jnp.zeros((keys_n, width), F32)
            total_v = jnp.zeros((keys_n, width), F32)
            for head in range(per_group):
                cols = slice(head * width, (head + 1) * width)
                q_head = queries[:, cols]
                g_head = grads[:, cols]
                scores = times_transpose(keys, q_head)
                probs = jnp.exp2(scores * (scale * LOG2E) - lse[0, head : head + 1, :])
                if masked:
                    probs = jnp.where(allowed, probs, 0.0)
                grad_probs = times_transpose(values, g_head)
                grad_scores = (probs * (grad_probs - deltas[0, head : head + 1, :])).astype(BF16)
                total_v += matmul(probs.astype(BF16), g_head)
                total_k += matmul(grad_scores, q_head)
                grad_q[:, cols] += matmul(keys_t, grad_scores).T
            out[0] = (total_k * scale).astype(BF16)
            out[1] = total_v.astype(BF16)

        if diagonal and slot == 0:
            work(True, True)
        else:
            full = info[5 + slot] > 0
            pl.when(live & full)(functools.partial(work, False, False))
            pl.when(live & jnp.logical_not(full))(functools.partial(work, True, False))

            @pl.when(jnp.logical_not(live))
            def _():
                out[...] = jnp.zeros_like(out)


def attn_backward(info, starts_row, lse, deltas, queries, grads, kv_a, kv_b, carried, diagonal, scale):
    rows, all_width = queries.shape
    width = 128
    groups = kv_a.shape[2] // width
    group_width = all_width // groups
    per_group = group_width // width
    keys_n = kv_a.shape[1]
    first = carried is None
    spec_q = pl.BlockSpec((rows, group_width), lambda g, info: (0, g))
    spec_kv = pl.BlockSpec((2, keys_n, width), lambda g, info: (0, 0, g))
    spec_row = pl.BlockSpec((1, per_group, rows), lambda g, info: (g, 0, 0))
    specs = [
        pl.BlockSpec((1, rows), lambda g, info: (0, 0)),
        spec_row,
        spec_row,
        spec_q,
        spec_q,
        spec_kv,
        spec_kv,
    ]
    operands = [starts_row, lse, deltas, queries, grads, kv_a, kv_b]
    if not first:
        specs.append(spec_q)
        operands.append(carried)
    return pl.pallas_call(
        functools.partial(attn_backward_kernel, first, diagonal, scale),
        grid_spec=pltpu.PrefetchScalarGridSpec(
            num_scalar_prefetch=1,
            grid=(groups,),
            in_specs=specs,
            out_specs=[spec_q, spec_kv, spec_kv],
        ),
        out_shape=[
            jax.ShapeDtypeStruct((rows, all_width), F32),
            jax.ShapeDtypeStruct(kv_a.shape, BF16),
            jax.ShapeDtypeStruct(kv_a.shape, BF16),
        ],
        compiler_params=pltpu.CompilerParams(dimension_semantics=("arbitrary",)),
        cost_estimate=pl.CostEstimate(
            flops=20 * rows * keys_n * all_width,
            transcendentals=2 * rows * keys_n * all_width // width,
            bytes_accessed=8 * rows * all_width,
        ),
        name="attn_backward",
    )(info, *operands)


def body(
    hidden,
    segment_ids,
    attn_norm,
    query_proj,
    key_proj,
    value_proj,
    gate_proj,
    output_proj,
    query_norm,
    key_norm,
    ffn_norm,
    ffn_gate,
    ffn_up,
    ffn_down,
    upstream,
):
    rows_dev, model = hidden.shape
    head_width = query_norm.shape[0]
    heads = query_proj.shape[1] // head_width
    groups = key_proj.shape[1] // head_width
    per_group = heads // groups
    group_width = groups * head_width
    sp_n = lax.axis_size("sp")
    tp_n = lax.axis_size("tp")
    outer = sp_n // 2
    sides = tp_n // 2
    quarter = rows_dev // tp_n
    tp_i = lax.axis_index("tp")
    sp_i = lax.axis_index("sp")
    ring_i = sp_i // 2
    pair_i = sp_i % 2
    side_i = tp_i // 2
    core_i = tp_i % 2
    own_first = sp_i * rows_dev
    quarter_first = tp_i * quarter
    scale = 1.0 / math.sqrt(head_width)

    ring_pairs = [(z * 2 + y, ((z + 1) % outer) * 2 + y) for z in range(outer) for y in range(2)]
    pair_pairs = [(i, i ^ 1) for i in range(sp_n)]
    side_pairs = [(i, i ^ 2) for i in range(tp_n)]
    core_pairs = [(i, i ^ 1) for i in range(tp_n)]

    def ring(value):
        return lax.ppermute(value, "sp", ring_pairs)

    def pair(value):
        return lax.ppermute(value, "sp", pair_pairs)

    def side(value):
        return lax.ppermute(value, "tp", side_pairs)

    def core(value):
        return lax.ppermute(value, "tp", core_pairs)

    def gather_sp(block):
        blocks = []
        for k in range(outer):
            blocks.append((block, pair(block)))
            if k < outer - 1:
                block = ring(block)
        return blocks

    def scatter_sp(parts):
        def paired(k):
            return parts[k][0] + pair(parts[k][1].astype(BF16)).astype(F32)

        total = paired(1 % outer)
        for k in range(2, outer + 1):
            total = ring(total.astype(BF16)).astype(F32) + paired(k % outer)
        return total

    first_id = segment_ids[0]
    second_start = jnp.sum((segment_ids == first_id).astype(jnp.int32))
    own_index = own_first + jnp.arange(rows_dev, dtype=jnp.int32)
    own_starts = jnp.where(own_index < second_start, 0, second_start)
    steps_half = jnp.arange(head_width // 2, dtype=F32)
    frequencies = jnp.exp(steps_half * (-2.0 * math.log(THETA) / head_width))
    angles = (own_index - own_starts).astype(F32)[:, None] * frequencies[None, :]
    cosine = jnp.cos(angles)[:, None, :]
    sine = jnp.sin(angles)[:, None, :]

    hidden_full = hidden.astype(F32)
    normed_full, attn_scales = norm_rows(hidden_full, attn_norm)
    normed = normed_full.astype(BF16)
    key_raw = matmul(normed, key_proj).reshape(rows_dev, groups, head_width)
    value_rows = matmul(normed, value_proj).astype(BF16)
    key_normed, key_scales = norm_rows(key_raw, key_norm)
    key_rot = rotary(key_normed, cosine, sine).astype(BF16).reshape(rows_dev, group_width)
    kv_own = jnp.stack([key_rot, value_rows])

    low, high = (outer // 4, 3 * outer // 4) if outer % 4 == 0 else (0, outer)
    reach = high - 1 if low else outer - 1

    def up_pairs(step):
        return [
            (z * 2 + y, (z + 1) * 2 + y)
            for z in range(outer - 1)
            for y in range(2)
            if z + 1 - step >= 0 and (z + 1 - step >= low or z + 1 < high)
        ]

    kv_blocks = []
    travelling = kv_own
    for k in range(reach + 1):
        kv_blocks.append((travelling, pair(travelling)))
        if k < reach:
            travelling = lax.ppermute(travelling, "sp", up_pairs(k + 1))

    query_raw = matmul(normed, query_proj).reshape(rows_dev, heads, head_width)
    gate_raw = matmul(normed, gate_proj)
    query_normed, query_scales = norm_rows(query_raw, query_norm)
    queries = rotary(query_normed, cosine, sine).astype(BF16).reshape(rows_dev, heads * head_width)

    grad_quarter = lax.dynamic_slice_in_dim(upstream, quarter_first, quarter)
    up_blocks = gather_sp(grad_quarter)

    row_start_low = own_starts[0]
    row_start_high = own_starts[-1]

    def block_info(k):
        shards = [(ring_i - k) * 2 + pair_i, (ring_i - k) * 2 + (1 - pair_i)]
        entries = [own_first] + [shard * rows_dev for shard in shards]
        live = []
        full = []
        for shard in shards:
            token = shard * rows_dev
            live.append((shard >= 0) & (shard <= sp_i) & (token + rows_dev - 1 >= row_start_low))
            full.append((token >= row_start_high) & (shard < sp_i))
        return jnp.stack(entries + [v.astype(jnp.int32) for v in live + full]).astype(jnp.int32)

    infos = [block_info(k) for k in range(reach + 1)]
    starts_column = own_starts[:, None]
    starts_row = own_starts[None, :]
    carried = None
    for k in range(reach + 1):
        carried = attn_forward(
            infos[k], starts_column, queries, kv_blocks[k][0], kv_blocks[k][1], carried, scale
        )
    mix_acc, mix_sum = carried
    mixed = mix_acc / mix_sum
    lse = jnp.log2(mix_sum.reshape(rows_dev, heads, head_width)[:, :, 0])
    lse_rows = lse.T.reshape(groups, per_group, rows_dev)
    gate_sig = jax.nn.sigmoid(gate_raw)
    gated = (mixed * gate_sig).astype(BF16)

    def scatter_tp(part):
        part = part.reshape(sides, 2, quarter, model)
        keep = lax.dynamic_index_in_dim(part, core_i, 1, keepdims=False)
        send = lax.dynamic_index_in_dim(part, 1 - core_i, 1, keepdims=False)
        keep = keep + core(send.astype(BF16)).astype(F32)
        mine = lax.dynamic_index_in_dim(keep, side_i, 0, keepdims=False)
        other = lax.dynamic_index_in_dim(keep, 1 - side_i, 0, keepdims=False)
        return mine + side(other.astype(BF16)).astype(F32)

    def gather_tp(block):
        far = side(block)
        swap_side = side_i == 1
        two = jnp.where(swap_side, jnp.stack([far, block]), jnp.stack([block, far]))
        near = core(two)
        swap_core = core_i == 1
        full = jnp.where(
            swap_core, jnp.stack([near, two], axis=1), jnp.stack([two, near], axis=1)
        )
        return full.reshape((rows_dev,) + block.shape[1:])

    attn_quarter = scatter_tp(matmul(gated, output_proj))
    hidden_quarter = lax.dynamic_slice_in_dim(hidden, quarter_first, quarter).astype(F32)
    middle = hidden_quarter + attn_quarter
    normed_two_full, ffn_scales = norm_rows(middle, ffn_norm)
    normed_two = normed_two_full.astype(BF16)

    two_blocks = gather_sp(normed_two)
    rows_list, up_list, inner_list, gate_list, grad_up_list = [None] * outer, [None] * outer, [None] * outer, [None] * outer, [None] * outer
    grad_parts = [None] * outer
    for k in list(range(1, outer)) + [0]:
        rows_k = jnp.concatenate(two_blocks[k])
        up_k = jnp.concatenate(up_blocks[k])
        gate_vals = matmul(rows_k, ffn_gate)
        up_vals = matmul(rows_k, ffn_up)
        sig = jax.nn.sigmoid(gate_vals)
        grad_inner = times_transpose(up_k, ffn_down)
        grad_gate = (grad_inner * up_vals * (sig * (1.0 + gate_vals * (1.0 - sig)))).astype(BF16)
        grad_up = (grad_inner * (gate_vals * sig)).astype(BF16)
        inner = (gate_vals * sig * up_vals).astype(BF16)
        grad_parts[k] = (
            times_transpose(grad_gate, ffn_gate) + times_transpose(grad_up, ffn_up)
        ).reshape(2, quarter, model)
        rows_list[k], up_list[k], inner_list[k] = rows_k, up_k, inner
        gate_list[k], grad_up_list[k] = grad_gate, grad_up
    grad_two = scatter_sp(grad_parts)

    norm_grad_two, ffn_gain_terms = norm_back(middle, ffn_scales, ffn_norm, grad_two)
    grad_middle_quarter = grad_quarter.astype(F32) + norm_grad_two
    grad_branch = gather_tp(grad_middle_quarter.astype(BF16))

    mlp_parts = [matmul(inner_list[k], ffn_down).reshape(2, quarter, model) for k in range(outer)]
    mlp_quarter = scatter_sp(mlp_parts)
    layer_out = gather_tp((middle + mlp_quarter).astype(BF16))

    rows_all = jnp.concatenate(rows_list)
    up_all = jnp.concatenate(up_list)
    inner_all = jnp.concatenate(inner_list)
    gate_all = jnp.concatenate(gate_list)
    grad_up_all = jnp.concatenate(grad_up_list)

    def reduce_tp(part):
        half = part.shape[0] // 2
        keep = lax.dynamic_slice_in_dim(part, core_i * half, half)
        send = lax.dynamic_slice_in_dim(part, (1 - core_i) * half, half)
        keep = (keep + core(send.astype(BF16)).astype(F32)).astype(BF16)
        keep = (keep.astype(F32) + side(keep).astype(F32)).astype(BF16)
        near = core(keep)
        total = jnp.where(
            core_i == 1, jnp.concatenate([near, keep]), jnp.concatenate([keep, near])
        )
        return total.astype(F32)

    ffn_gate_grad = reduce_tp(outer_sum(rows_all, gate_all))
    ffn_up_grad = reduce_tp(outer_sum(rows_all, grad_up_all))
    ffn_down_grad = reduce_tp(outer_sum(inner_all, up_all))

    output_part = outer_sum(gated, grad_branch)
    grad_gated = times_transpose(grad_branch, output_proj)
    grad_mixed = (grad_gated * gate_sig).astype(BF16)
    grad_gate_raw = (grad_gated * mixed * (gate_sig * (1.0 - gate_sig))).astype(BF16)
    deltas = jnp.sum(
        (grad_mixed.astype(F32) * mixed).reshape(rows_dev, heads, head_width), axis=-1
    )
    delta_rows = deltas.T.reshape(groups, per_group, rows_dev)

    def down_pairs(step):
        return [(b, a) for a, b in up_pairs(step)]

    query_acc = None
    travelling = None
    for k in list(range(reach, -1, -1)):
        query_acc, grad_a, grad_b = attn_backward(
            infos[k], starts_row, lse_rows, delta_rows, queries, grad_mixed,
            kv_blocks[k][0], kv_blocks[k][1], query_acc, k == 0, scale,
        )
        total = grad_a.astype(F32) + pair(grad_b).astype(F32)
        if travelling is not None:
            total = total + travelling.astype(F32)
        if k > 0:
            travelling = lax.ppermute(total.astype(BF16), "sp", down_pairs(k))
    grad_key_rot = total[0].reshape(rows_dev, groups, head_width)
    grad_value_low = total[1].astype(BF16)
    grad_query_rot = (query_acc * scale).reshape(rows_dev, heads, head_width)
    grad_query_raw, query_gain_terms = norm_back(
        query_raw, query_scales, query_norm, rotary_back(grad_query_rot, cosine, sine)
    )
    grad_key_raw, key_gain_terms = norm_back(
        key_raw, key_scales, key_norm, rotary_back(grad_key_rot, cosine, sine)
    )
    grad_query_low = grad_query_raw.reshape(rows_dev, heads * head_width).astype(BF16)
    grad_key_low = grad_key_raw.reshape(rows_dev, group_width).astype(BF16)

    def reduce_sp(part):
        count, width = part.shape
        half = count // 2
        chunk = half // outer
        keep = lax.dynamic_slice_in_dim(part, pair_i * half, half)
        send = lax.dynamic_slice_in_dim(part, (1 - pair_i) * half, half)
        keep = keep + pair(send.astype(BF16)).astype(F32)

        def piece(k):
            return lax.dynamic_slice_in_dim(keep, ((ring_i - k) % outer) * chunk, chunk)

        total = piece(1 % outer)
        for k in range(2, outer + 1):
            total = ring(total.astype(BF16)).astype(F32) + piece(k % outer)
        block = total.astype(BF16)
        out = jnp.zeros((count, width), F32)
        for k in range(outer):
            at = ((ring_i - k) % outer) * chunk
            out = lax.dynamic_update_slice(out, block.astype(F32), (pair_i * half + at, 0))
            out = lax.dynamic_update_slice(
                out, pair(block).astype(F32), ((1 - pair_i) * half + at, 0)
            )
            if k < outer - 1:
                block = ring(block)
        return out

    output_grad = reduce_sp(output_part)
    gate_grad = reduce_sp(outer_sum(normed, grad_gate_raw))
    query_grad = reduce_sp(outer_sum(normed, grad_query_low))
    key_grad = reduce_sp(outer_sum(normed, grad_key_low))
    value_grad = reduce_sp(outer_sum(normed, grad_value_low))

    grad_normed_part = (
        times_transpose(grad_query_low, query_proj)
        + times_transpose(grad_key_low, key_proj)
        + times_transpose(grad_value_low, value_proj)
        + times_transpose(grad_gate_raw, gate_proj)
    )
    grad_normed = scatter_tp(grad_normed_part)
    scales_quarter = lax.dynamic_slice_in_dim(attn_scales, quarter_first, quarter)
    norm_grad_one, attn_gain_terms = norm_back(
        hidden_quarter, scales_quarter, attn_norm, grad_normed
    )
    hidden_grad = gather_tp((grad_middle_quarter + norm_grad_one).astype(BF16)).astype(F32)

    gains = jnp.concatenate(
        [
            jnp.sum(attn_gain_terms, axis=0),
            jnp.sum(ffn_gain_terms, axis=0),
            jnp.sum(query_gain_terms, axis=(0, 1)),
            jnp.sum(key_gain_terms, axis=(0, 1)),
        ]
    )
    for axis, size in (("tp", tp_n), ("sp", sp_n)):
        bit = 1
        while bit < size:
            gains = gains + lax.ppermute(gains, axis, [(i, i ^ bit) for i in range(size)])
            bit *= 2
    return (
        layer_out,
        hidden_grad,
        gains[:model],
        query_grad,
        key_grad,
        value_grad,
        gate_grad,
        output_grad,
        gains[2 * model : 2 * model + head_width],
        gains[2 * model + head_width :],
        gains[model : 2 * model],
        ffn_gate_grad,
        ffn_up_grad,
        ffn_down_grad,
    )


def solution(mesh):
    placed = (
        P("sp", None),
        P(),
        P(),
        P(None, "tp"),
        P(None, "tp"),
        P(None, "tp"),
        P(None, "tp"),
        P("tp", None),
        P(),
        P(),
        P(),
        P(None, "sp"),
        P(None, "sp"),
        P("sp", None),
        P("sp", None),
    )
    return jax.shard_map(
        body,
        mesh=mesh,
        in_specs=placed,
        out_specs=(
            P("sp", None),
            P("sp", None),
            P(),
            P(None, "tp"),
            P(None, "tp"),
            P(None, "tp"),
            P(None, "tp"),
            P("tp", None),
            P(),
            P(),
            P(),
            P(None, "sp"),
            P(None, "sp"),
            P("sp", None),
        ),
        check_vma=False,
    )
```

time: 1280 us -> 772 us (0.60)
  waiting for transfers between devices: 1010 us -> 332 us
  starting transfers between devices: 0.88 us -> 158 us
  matrix products: 114 us -> 80.3 us
  other arithmetic: 60.6 us -> 92.3 us
  blocking collectives: 30.1 us -> 0 us
  local copies, waits for them, and re-layouts: 35.1 us -> 63.5 us
  Pallas kernels: 0 us -> 26.7 us
    psum x2 -> x0, waiting for transfers between devices: 433 us -> none  [the longest x1 232 us: body(): lax.psum(query_w_grad.astype(jnp.bfloat16), 'sp').astype(jnp.float32)]
    reduce_scatter x4 -> x0, waiting for transfers between devices: 342 us -> none  [the longest x1 112 us: body(): lax.psum_scatter(kv_buffer.astype(jnp.bfloat16), 'sp', scatter_dimension=...]
    ppermute x0 -> x117, waiting for transfers between devices: none -> 332 us  [the longest x47 149 us: pair(): return lax.ppermute(value, 'sp', pair_pairs)]
    all_gather x6 -> x0, waiting for transfers between devices: 237 us -> none  [the longest x1 70.9 us: body(): gathered_inputs = lax.all_gather(normed_two, 'sp', axis=0, tiled=True)]
    ppermute x0 -> x117, starting transfers between devices: none -> 158 us  [the longest x42 74.9 us: ring(): return lax.ppermute(value, 'sp', ring_pairs)]
    psum x2 -> x0, blocking collectives: 30.1 us -> none  [the longest x1 23.1 us: body(): lax.psum(jnp.sum(attn_gain_terms, axis=0).astype(jnp.bfloat16), 'sp')]
    pallas_call x0 -> x6, Pallas kernels: none -> 26.7 us  [the longest x3 14 us: attn_backward(): pl.pallas_call(functools.partial(attn_backward_kernel, first, diagonal, s...]
    dot_general x15 -> x17, matrix products: 52.2 us -> 30.9 us  [matmul(): return jnp.dot(left, right, preferred_element_type=F32)]
  transfers between devices with their start and end apart: 12 -> 117, of which waited for: 11 -> 55; matrix products, arithmetic and copies ran while one was open for 9% -> 26% of each run, Pallas kernels for 0% -> 4%
where the time goes in v1:
time: 772 us; the launch traced here: 764 us
  waiting for transfers between devices  332 us (43%)
  starting transfers between devices  158 us (20%)
  other arithmetic  92.3 us (12%)
  matrix products  80.3 us (10%)
  local copies, waits for them, and re-layouts  63.5 us (8%)
  Pallas kernels  26.7 us (3%)
  between operations  10.9 us (1%)
    ppermute x47, waiting for transfers between devices, pair(): return lax.ppermute(value, 'sp', pair_pairs)  149 us
    ppermute x42, waiting for transfers between devices, ring(): return lax.ppermute(value, 'sp', ring_pairs)  98.4 us
    ppermute x42, starting transfers between devices, ring(): return lax.ppermute(value, 'sp', ring_pairs)  74.9 us
    ppermute x47, starting transfers between devices, pair(): return lax.ppermute(value, 'sp', pair_pairs)  64.4 us
    ppermute x8, waiting for transfers between devices, side(): return lax.ppermute(value, 'tp', side_pairs)  52.8 us
    dot_general x17, matrix products, matmul(): return jnp.dot(left, right, preferred_element_type=F32)  30.9 us
    unnamed x133, local copies, waits for them, and re-layouts  28 us
    dot_general x17, matrix products, times_transpose(): lax.dot_general(left, right, (((1,), (1,)), ((), ())), preferred_element_...  27.7 us
  transfers between devices with their start and end apart: 117, of which 55 were waited for; matrix products, arithmetic and copies ran while one was open for 26% of the time, Pallas kernels for 4%

profile of v1, /device:TPU:0, one launch (start us, length us, event | category | flops | bytes accessed | tf_op | source)
XLA Modules:
  0.0 763.8 jit_solution(4769897240052198319)
XLA Ops:
  6.2 3.5 fusion.34
  25.2 4.3 collective-permute-start
  32.9 4.6 multiply_reduce_fusion.4
  42.7 4.7 fusion.33
  69.1 5.1 attn_forward.3
  74.2 3.8 attn_forward.4
  78.0 3.8 attn_forward.5
  81.8 3.3 multiply_convert_fusion.2
  90.8 6.9 collective-permute-start.27
  105.2 6.8 collective-permute-done.27
  112.0 3.6 collective-permute-start.31
  143.1 4.3 collective-permute-done.32
  151.8 4.7 collective-permute-done.19
  173.7 14.8 %collective-permute-done.8 = bf16[128,2048]{1,0:T(8,128)(2,1)S(1)} collective-permute-done((bf16[128,2048]{1,0:T(8,128)(2,1)S(1)}, bf16[128,2048]{1,0:T(8,128)(2,1)S(1)}, u32[]{:S(2)}, u32[]{:S(2)}) %collective-permute-start.8) | collective-permute-done | bytes 524320 | tf_op jit(solution)/shard_map/ppermute | solution.py:299
  201.5 18.6 %collective-permute-done.12 = bf16[128,2048]{1,0:T(8,128)(2,1)S(1)} collective-permute-done((bf16[128,2048]{1,0:T(8,128)(2,1)S(1)}, bf16[128,2048]{1,0:T(8,128)(2,1)S(1)}, u32[]{:S(2)}, u32[]{:S(2)}) %collective-permute-start.12) | collective-permute-done | bytes 524320 | tf_op jit(solution)/shard_map/ppermute | solution.py:299
  237.3 13.6 %collective-permute-done.16 = bf16[128,2048]{1,0:T(8,128)(2,1)S(1)} collective-permute-done((bf16[128,2048]{1,0:T(8,128)(2,1)S(1)}, bf16[128,2048]{1,0:T(8,128)(2,1)S(1)}, u32[]{:S(2)}, u32[]{:S(2)}) %collective-permute-start.16) | collective-permute-done | bytes 524320 | tf_op jit(solution)/shard_map/ppermute | solution.py:299
  261.6 5.3 fusion.23
  272.8 3.7 collective-permute-done.17
  279.6 8.2 %collective-permute-done.33 = bf16[128,2048]{1,0:T(8,128)(2,1)S(1)} collective-permute-done((bf16[128,2048]{1,0:T(8,128)(2,1)S(1)}, bf16[128,2048]{1,0:T(8,128)(2,1)S(1)}, u32[]{:S(2)}, u32[]{:S(2)}) %collective-permute-start.33) | collective-permute-done | bytes 524320 | tf_op jit(solution)/shard_map/ppermute | solution.py:299
  291.0 3.5 fusion.15
  295.2 8.9 %collective-permute-done.34 = bf16[128,2048]{1,0:T(8,128)(2,1)S(1)} collective-permute-done((bf16[128,2048]{1,0:T(8,128)(2,1)S(1)}, bf16[128,2048]{1,0:T(8,128)(2,1)S(1)}, u32[]{:S(2)}, u32[]{:S(2)}) %collective-permute-start.34) | collective-permute-done | bytes 524320 | tf_op jit(solution)/shard_map/ppermute | solution.py:296
  309.3 3.5 fusion.7
  314.0 8.2 %collective-permute-done.37 = bf16[128,2048]{1,0:T(8,128)(2,1)S(1)} collective-permute-done((bf16[128,2048]{1,0:T(8,128)(2,1)S(1)}, bf16[128,2048]{1,0:T(8,128)(2,1)S(1)}, u32[]{:S(2)}, u32[]{:S(2)}) %collective-permute-start.37) | collective-permute-done | bytes 524320 | tf_op jit(solution)/shard_map/ppermute | solution.py:302
  322.4 9.3 %collective-permute-done.21 = bf16[128,2048]{1,0:T(8,128)(2,1)S(1)} collective-permute-done((bf16[128,2048]{1,0:T(8,128)(2,1)S(1)}, bf16[128,2048]{1,0:T(8,128)(2,1)S(1)}, u32[]{:S(2)}, u32[]{:S(2)}) %collective-permute-start.21) | collective-permute-done | bytes 524320 | tf_op jit(solution)/shard_map/ppermute | solution.py:302
  348.5 3.3 attn_backward.3
  351.8 3.7 attn_backward.4
  355.5 7.0 attn_backward.5
  366.5 5.3 collective-permute-start.39
  391.0 4.0 collective-permute-done.41
  397.3 3.7 add_convert_fusion
  401.0 6.1 collective-permute-done.112
  409.4 3.4 add_convert_fusion.2
  412.9 27.4 %collective-permute-done.109 = bf16[1024,768]{1,0:T(8,128)(2,1)} collective-permute-done((bf16[1024,768]{1,0:T(8,128)(2,1)}, bf16[1024,768]{1,0:T(8,128)(2,1)}, u32[]{:S(2)}, u32[]{:S(2)}) %collective-permute-start.109) | collective-permute-done | bytes 1572896 | tf_op jit(solution)/shard_map/ppermute | solution.py:302
  442.7 3.4 add_convert_fusion.4
  447.9 27.5 %collective-permute-done.86 = bf16[1024,512]{1,0:T(8,128)(2,1)S(1)} collective-permute-done((bf16[1024,512]{1,0:T(8,128)(2,1)S(1)}, bf16[1024,512]{1,0:T(8,128)(2,1)S(1)}, u32[]{:S(2)}, u32[]{:S(2)}) %collective-permute-start.86) | collective-permute-done | bytes 1048608 | tf_op jit(solution)/shard_map/ppermute | solution.py:299
  476.0 5.5 collective-permute-start.54
  481.5 8.9 %collective-permute-start.87 = (bf16[256,512]{1,0:T(8,128)(2,1)S(1)}, bf16[256,512]{1,0:T(8,128)(2,1)S(1)}, u32[]{:S(2)}, u32[]{:S(2)}) collective-permute-start(bf16[256,512]{1,0:T(8,128)(2,1)S(1)} %dynamic-slice_convert_fusion.11), channel_id=1, source_target_pairs={{0,2},{1,3},{2,4},{3,5},{4,6},{5,7},{6,0},{7,1},{8,10},{9,11},{10,... | collective-permute-start | bytes 786440 | tf_op jit(solution)/shard_map/ppermute | solution.py:296
  490.6 6.5 collective-permute-start.98
  497.2 5.5 collective-permute-start.55
  504.6 3.7 collective-permute-start.88
  510.3 3.7 collective-permute-start.99
  518.0 3.5 collective-permute-done.99
  525.5 7.3 collective-permute-done.43
  579.0 8.1 %collective-permute-done.58 = bf16[256,512]{1,0:T(8,128)(2,1)S(1)} collective-permute-done((bf16[256,512]{1,0:T(8,128)(2,1)S(1)}, bf16[256,512]{1,0:T(8,128)(2,1)S(1)}, u32[]{:S(2)}, u32[]{:S(2)}) %collective-permute-start.58) | collective-permute-done | bytes 262176 | tf_op jit(solution)/shard_map/ppermute | solution.py:296
  587.3 3.8 collective-permute-done.91
  597.0 5.3 fusion.5
  602.3 5.1 fusion.3
  608.2 4.9 fusion.4
  613.9 7.3 collective-permute-done.65
  621.3 6.7 collective-permute-done.76
  630.3 6.9 collective-permute-done.59
  641.9 3.5 collective-permute-done.66
  648.3 11.8 %collective-permute-done.67 = bf16[256,256]{1,0:T(8,128)(2,1)S(1)} collective-permute-done((bf16[256,256]{1,0:T(8,128)(2,1)S(1)}, bf16[256,256]{1,0:T(8,128)(2,1)S(1)}, u32[]{:S(2)}, u32[]{:S(2)}) %collective-permute-start.67) | collective-permute-done | bytes 131104 | tf_op jit(solution)/shard_map/ppermute | solution.py:296
  660.3 6.6 collective-permute-done.78
  671.2 4.9 collective-permute-done.61
  676.2 5.6 collective-permute-done.94
  690.7 12.1 %collective-permute-done.70 = bf16[256,256]{1,0:T(8,128)(2,1)S(1)} collective-permute-done((bf16[256,256]{1,0:T(8,128)(2,1)S(1)}, bf16[256,256]{1,0:T(8,128)(2,1)S(1)}, u32[]{:S(2)}, u32[]{:S(2)}) %collective-permute-start.70) | collective-permute-done | bytes 131104 | tf_op jit(solution)/shard_map/ppermute | solution.py:299
  702.9 6.7 collective-permute-done.71
  711.1 3.5 collective-permute-done.81
  714.6 7.1 collective-permute-done.82
  724.2 4.3 collective-permute-done.73
  734.7 12.6 %collective-permute-done.49 = f32[4352]{0:T(1024)S(1)} collective-permute-done((f32[4352]{0:T(1024)S(1)}, f32[4352]{0:T(1024)S(1)}, u32[]{:S(2)}, u32[]{:S(2)}) %collective-permute-start.49) | collective-permute-done | bytes 17440 | tf_op jit(solution)/shard_map/ppermute | solution.py:566
  751.5 3.5 collective-permute-done.51
  755.0 4.6 collective-permute-done.52
  (538 shorter events, 321.5 us)
Async XLA Ops:
  22.2 46.9 %collective-permute-start.4 = (bf16[2,512,256]{2,1,0:T(8,128)(2,1)}, bf16[2,512,256]{2,1,0:T(8,128)(2,1)}, u32[]{:S(2)}, u32[]{:S(2)}) collective-permute-start(bf16[2,512,256]{2,1,0:T(8,128)(2,1)} %pad_maximum_fusion.5.kv_a), channel_id=1, source_target_pairs={{0,1},{1,0},{2,3},{3,2},{4,5},{5,4},{6,7},{7,6},{8,9},{9,8},{10,11... | collective-permute-start | bytes 1572872 | tf_op jit(solution)/shard_map/ppermute | solution.py:299
  25.2 22.2 %collective-permute-start = (bf16[2,512,256]{2,1,0:T(8,128)(2,1)}, bf16[2,512,256]{2,1,0:T(8,128)(2,1)}, u32[]{:S(2)}, u32[]{:S(2)}) collective-permute-start(bf16[2,512,256]{2,1,0:T(8,128)(2,1)} %pad_maximum_fusion.5.kv_a), channel_id=1, source_target_pairs={{0,2},{1,3},{2,4},{3,5},{4,6},{5,7},{8,10},{9,11},{10,12},{11,13},... | collective-permute-start | bytes 1572872 | tf_op jit(solution)/shard_map/ppermute | solution.py:359
  31.7 69.7 %collective-permute-start.35 = (bf16[128,2048]{1,0:T(8,128)(2,1)}, bf16[128,2048]{1,0:T(8,128)(2,1)}, u32[]{:S(2)}, u32[]{:S(2)}) collective-permute-start(bf16[128,2048]{1,0:T(8,128)(2,1)} %get-tuple-element.49), channel_id=1, source_target_pairs={{0,1},{1,0},{2,3},{3,2},{4,5},{5,4},{6,7},{7,6},{8,9},{9,8},{10,11... | collective-permute-start | bytes 1572872 | tf_op jit(solution)/shard_map/ppermute | solution.py:299
  32.2 58.7 %collective-permute-start.23 = (bf16[128,2048]{1,0:T(8,128)(2,1)}, bf16[128,2048]{1,0:T(8,128)(2,1)}, u32[]{:S(2)}, u32[]{:S(2)}) collective-permute-start(bf16[128,2048]{1,0:T(8,128)(2,1)} %get-tuple-element.49), channel_id=1, source_target_pairs={{0,2},{1,3},{2,4},{3,5},{4,6},{5,7},{6,0},{7,1},{8,10},{9,11},{10,... | collective-permute-start | bytes 1572872 | tf_op jit(solution)/shard_map/ppermute | solution.py:296
  50.7 23.5 %collective-permute-start.3 = (bf16[2,512,256]{2,1,0:T(8,128)(2,1)}, bf16[2,512,256]{2,1,0:T(8,128)(2,1)}, u32[]{:S(2)}, u32[]{:S(2)}) collective-permute-start(bf16[2,512,256]{2,1,0:T(8,128)(2,1)} %collective-permute-done.kv_a), channel_id=1, source_target_pairs={{0,1},{1,0},{2,3},{3,2},{4,5},{5,4},{6,7},{7,6},{8,9},{9,8},{10,11... | collective-permute-start | bytes 1572872 | tf_op jit(solution)/shard_map/ppermute | solution.py:299
  60.1 17.9 %collective-permute-start.2 = (bf16[2,512,256]{2,1,0:T(8,128)(2,1)}, bf16[2,512,256]{2,1,0:T(8,128)(2,1)}, u32[]{:S(2)}, u32[]{:S(2)}) collective-permute-start(bf16[2,512,256]{2,1,0:T(8,128)(2,1)} %collective-permute-done.1.kv_a), channel_id=1, source_target_pairs={{0,1},{1,0},{2,3},{3,2},{4,5},{5,4},{6,7},{7,6},{8,9},{9,8},{10,11... | collective-permute-start | bytes 1572872 | tf_op jit(solution)/shard_map/ppermute | solution.py:299
  89.6 29.2 %collective-permute-start.5 = (bf16[2,128,2048]{2,1,0:T(8,128)(2,1)}, bf16[2,128,2048]{2,1,0:T(8,128)(2,1)}, u32[]{:S(2)}, u32[]{:S(2)}) collective-permute-start(bf16[2,128,2048]{2,1,0:T(8,128)(2,1)} %fusion.48), channel_id=1, source_target_pairs={{0,8},{8,0},{16,24},{24,16},{1,9},{9,1},{17,25},{25,17},{2,10},{10... | collective-permute-start | bytes 3145736 | tf_op jit(solution)/shard_map/ppermute | solution.py:305
  90.8 21.1 %collective-permute-start.27 = (bf16[128,2048]{1,0:T(8,128)(2,1)}, bf16[128,2048]{1,0:T(8,128)(2,1)}, u32[]{:S(2)}, u32[]{:S(2)}) collective-permute-start(bf16[128,2048]{1,0:T(8,128)(2,1)} %collective-permute-done.23), channel_id=1, source_target_pairs={{0,2},{1,3},{2,4},{3,5},{4,6},{5,7},{6,0},{7,1},{8,10},{9,11},{10,... | collective-permute-start | bytes 1572872 | tf_op jit(solution)/shard_map/ppermute | solution.py:296
  98.3 26.3 %collective-permute-start.24 = (bf16[128,2048]{1,0:T(8,128)(2,1)}, bf16[128,2048]{1,0:T(8,128)(2,1)S(1)}, u32[]{:S(2)}, u32[]{:S(2)}) collective-permute-start(bf16[128,2048]{1,0:T(8,128)(2,1)} %collective-permute-done.23), channel_id=1, source_target_pairs={{0,1},{1,0},{2,3},{3,2},{4,5},{5,4},{6,7},{7,6},{8,9},{9,8},{10,11... | collective-permute-start | bytes 1572872 | tf_op jit(solution)/shard_map/ppermute | solution.py:299
  112.0 20.3 %collective-permute-start.31 = (bf16[128,2048]{1,0:T(8,128)(2,1)}, bf16[128,2048]{1,0:T(8,128)(2,1)}, u32[]{:S(2)}, u32[]{:S(2)}) collective-permute-start(bf16[128,2048]{1,0:T(8,128)(2,1)} %collective-permute-done.27), channel_id=1, source_target_pairs={{0,2},{1,3},{2,4},{3,5},{4,6},{5,7},{6,0},{7,1},{8,10},{9,11},{10,... | collective-permute-start | bytes 1572872 | tf_op jit(solution)/shard_map/ppermute | solution.py:296
  115.6 17.1 %collective-permute-start.28 = (bf16[128,2048]{1,0:T(8,128)(2,1)}, bf16[128,2048]{1,0:T(8,128)(2,1)}, u32[]{:S(2)}, u32[]{:S(2)}) collective-permute-start(bf16[128,2048]{1,0:T(8,128)(2,1)} %collective-permute-done.27), channel_id=1, source_target_pairs={{0,1},{1,0},{2,3},{3,2},{4,5},{5,4},{6,7},{7,6},{8,9},{9,8},{10,11... | collective-permute-start | bytes 1572872 | tf_op jit(solution)/shard_map/ppermute | solution.py:299
  149.3 18.2 %collective-permute-start.7 = (bf16[128,2048]{1,0:T(8,128)(2,1)}, bf16[128,2048]{1,0:T(8,128)(2,1)S(1)}, u32[]{:S(2)}, u32[]{:S(2)}) collective-permute-start(bf16[128,2048]{1,0:T(8,128)(2,1)} %get-tuple-element.51), channel_id=1, source_target_pairs={{0,2},{1,3},{2,4},{3,5},{4,6},{5,7},{6,0},{7,1},{8,10},{9,11},{10,... | collective-permute-start | bytes 1572872 | tf_op jit(solution)/shard_map/ppermute | solution.py:296
  165.4 139.2 %collective-permute-start.20 = (bf16[128,2048]{1,0:T(8,128)(2,1)S(1)}, bf16[128,2048]{1,0:T(8,128)(2,1)S(1)}, u32[]{:S(2)}, u32[]{:S(2)}) collective-permute-start(bf16[128,2048]{1,0:T(8,128)(2,1)S(1)} %slice.263), channel_id=1, source_target_pairs={{0,1},{1,0},{2,3},{3,2},{4,5},{5,4},{6,7},{7,6},{8,9},{9,8},{10,11... | collective-permute-start | bytes 1572872 | tf_op jit(solution)/shard_map/ppermute | solution.py:299
  167.5 21.0 %collective-permute-start.8 = (bf16[128,2048]{1,0:T(8,128)(2,1)S(1)}, bf16[128,2048]{1,0:T(8,128)(2,1)S(1)}, u32[]{:S(2)}, u32[]{:S(2)}) collective-permute-start(bf16[128,2048]{1,0:T(8,128)(2,1)S(1)} %collective-permute-done.7), channel_id=1, source_target_pairs={{0,1},{1,0},{2,3},{3,2},{4,5},{5,4},{6,7},{7,6},{8,9},{9,8},{10,11... | collective-permute-start | bytes 1572872 | tf_op jit(solution)/shard_map/ppermute | solution.py:299
  169.7 26.9 %collective-permute-start.11 = (bf16[128,2048]{1,0:T(8,128)(2,1)S(1)}, bf16[128,2048]{1,0:T(8,128)(2,1)S(1)}, u32[]{:S(2)}, u32[]{:S(2)}) collective-permute-start(bf16[128,2048]{1,0:T(8,128)(2,1)S(1)} %collective-permute-done.7), channel_id=1, source_target_pairs={{0,2},{1,3},{2,4},{3,5},{4,6},{5,7},{6,0},{7,1},{8,10},{9,11},{10,... | collective-permute-start | bytes 1572872 | tf_op jit(solution)/shard_map/ppermute | solution.py:296
  194.0 28.2 %collective-permute-start.9 = (bf16[128,2048]{1,0:T(8,128)(2,1)S(1)}, bf16[128,2048]{1,0:T(8,128)(2,1)S(1)}, u32[]{:S(2)}, u32[]{:S(2)}) collective-permute-start(bf16[128,2048]{1,0:T(8,128)(2,1)S(1)} %slice.266), channel_id=1, source_target_pairs={{0,1},{1,0},{2,3},{3,2},{4,5},{5,4},{6,7},{7,6},{8,9},{9,8},{10,11... | collective-permute-start | bytes 1572872 | tf_op jit(solution)/shard_map/ppermute | solution.py:299
  196.6 23.5 %collective-permute-start.12 = (bf16[128,2048]{1,0:T(8,128)(2,1)S(1)}, bf16[128,2048]{1,0:T(8,128)(2,1)S(1)}, u32[]{:S(2)}, u32[]{:S(2)}) collective-permute-start(bf16[128,2048]{1,0:T(8,128)(2,1)S(1)} %collective-permute-done.11), channel_id=1, source_target_pairs={{0,1},{1,0},{2,3},{3,2},{4,5},{5,4},{6,7},{7,6},{8,9},{9,8},{10,11... | collective-permute-start | bytes 1572872 | tf_op jit(solution)/shard_map/ppermute | solution.py:299
  198.3 33.0 %collective-permute-start.25 = (bf16[128,2048]{1,0:T(8,128)(2,1)S(1)}, bf16[128,2048]{1,0:T(8,128)(2,1)S(1)}, u32[]{:S(2)}, u32[]{:S(2)}) collective-permute-start(bf16[128,2048]{1,0:T(8,128)(2,1)S(1)} %slice.262), channel_id=1, source_target_pairs={{0,1},{1,0},{2,3},{3,2},{4,5},{5,4},{6,7},{7,6},{8,9},{9,8},{10,11... | collective-permute-start | bytes 1572872 | tf_op jit(solution)/shard_map/ppermute | solution.py:299
  199.9 35.5 %collective-permute-start.15 = (bf16[128,2048]{1,0:T(8,128)(2,1)S(1)}, bf16[128,2048]{1,0:T(8,128)(2,1)S(1)}, u32[]{:S(2)}, u32[]{:S(2)}) collective-permute-start(bf16[128,2048]{1,0:T(8,128)(2,1)S(1)} %collective-permute-done.11), channel_id=1, source_target_pairs={{0,2},{1,3},{2,4},{3,5},{4,6},{5,7},{6,0},{7,1},{8,10},{9,11},{10,... | collective-permute-start | bytes 1572872 | tf_op jit(solution)/shard_map/ppermute | solution.py:296
  222.3 32.4 %collective-permute-start.10 = (bf16[128,2048]{1,0:T(8,128)(2,1)S(1)}, bf16[128,2048]{1,0:T(8,128)(2,1)S(1)}, u32[]{:S(2)}, u32[]{:S(2)}) collective-permute-start(bf16[128,2048]{1,0:T(8,128)(2,1)S(1)} %fusion.63), channel_id=1, source_target_pairs={{0,2},{1,3},{2,4},{3,5},{4,6},{5,7},{6,0},{7,1},{8,10},{9,11},{10,... | collective-permute-start | bytes 1572872 | tf_op jit(solution)/shard_map/ppermute | solution.py:296
  228.3 26.4 %collective-permute-start.13 = (bf16[128,2048]{1,0:T(8,128)(2,1)S(1)}, bf16[128,2048]{1,0:T(8,128)(2,1)S(1)}, u32[]{:S(2)}, u32[]{:S(2)}) collective-permute-start(bf16[128,2048]{1,0:T(8,128)(2,1)S(1)} %slice.265), channel_id=1, source_target_pairs={{0,1},{1,0},{2,3},{3,2},{4,5},{5,4},{6,7},{7,6},{8,9},{9,8},{10,11... | collective-permute-start | bytes 1572872 | tf_op jit(solution)/shard_map/ppermute | solution.py:299
  231.4 35.4 %collective-permute-start.26 = (bf16[128,2048]{1,0:T(8,128)(2,1)S(1)}, bf16[128,2048]{1,0:T(8,128)(2,1)S(1)}, u32[]{:S(2)}, u32[]{:S(2)}) collective-permute-start(bf16[128,2048]{1,0:T(8,128)(2,1)S(1)} %fusion.55), channel_id=1, source_target_pairs={{0,2},{1,3},{2,4},{3,5},{4,6},{5,7},{6,0},{7,1},{8,10},{9,11},{10,... | collective-permute-start | bytes 1572872 | tf_op jit(solution)/shard_map/ppermute | solution.py:296
  254.9 16.6 %collective-permute-start.14 = (bf16[128,2048]{1,0:T(8,128)(2,1)S(1)}, bf16[128,2048]{1,0:T(8,128)(2,1)S(1)}, u32[]{:S(2)}, u32[]{:S(2)}) collective-permute-start(bf16[128,2048]{1,0:T(8,128)(2,1)S(1)} %fusion.62), channel_id=1, source_target_pairs={{0,2},{1,3},{2,4},{3,5},{4,6},{5,7},{6,0},{7,1},{8,10},{9,11},{10,... | collective-permute-start | bytes 1572872 | tf_op jit(solution)/shard_map/ppermute | solution.py:296
  260.0 16.5 %collective-permute-start.17 = (bf16[128,2048]{1,0:T(8,128)(2,1)S(1)}, bf16[128,2048]{1,0:T(8,128)(2,1)S(1)}, u32[]{:S(2)}, u32[]{:S(2)}) collective-permute-start(bf16[128,2048]{1,0:T(8,128)(2,1)S(1)} %slice.264), channel_id=1, source_target_pairs={{0,1},{1,0},{2,3},{3,2},{4,5},{5,4},{6,7},{7,6},{8,9},{9,8},{10,11... | collective-permute-start | bytes 1572872 | tf_op jit(solution)/shard_map/ppermute | solution.py:299
  270.4 17.3 %collective-permute-start.33 = (bf16[128,2048]{1,0:T(8,128)(2,1)S(1)}, bf16[128,2048]{1,0:T(8,128)(2,1)S(1)}, u32[]{:S(2)}, u32[]{:S(2)}) collective-permute-start(bf16[128,2048]{1,0:T(8,128)(2,1)S(1)} %slice.260), channel_id=1, source_target_pairs={{0,1},{1,0},{2,3},{3,2},{4,5},{5,4},{6,7},{7,6},{8,9},{9,8},{10,11... | collective-permute-start | bytes 1572872 | tf_op jit(solution)/shard_map/ppermute | solution.py:299
  271.6 23.7 %collective-permute-start.36 = (bf16[128,2048]{1,0:T(8,128)(2,1)S(1)}, bf16[128,2048]{1,0:T(8,128)(2,1)S(1)}, u32[]{:S(2)}, u32[]{:S(2)}) collective-permute-start(bf16[128,2048]{1,0:T(8,128)(2,1)S(1)} %slice.259), channel_id=1, source_target_pairs={{0,1},{1,0},{2,3},{3,2},{4,5},{5,4},{6,7},{7,6},{8,9},{9,8},{10,11... | collective-permute-start | bytes 1572872 | tf_op jit(solution)/shard_map/ppermute | solution.py:299
  276.5 57.7 %collective-permute-start.114 = (bf16[384,2048]{1,0:T(8,128)(2,1)S(1)}, bf16[384,2048]{1,0:T(8,128)(2,1)S(1)}, u32[]{:S(2)}, u32[]{:S(2)}) collective-permute-start(bf16[384,2048]{1,0:T(8,128)(2,1)S(1)} %dynamic-slice_convert_fusion), channel_id=1, source_target_pairs={{0,8},{8,0},{16,24},{24,16},{1,9},{9,1},{17,25},{25,17},{2,10},{10... | collective-permute-start | bytes 4718600 | tf_op jit(solution)/shard_map/ppermute | solution.py:305
  278.1 26.5 %collective-permute-start.18 = (bf16[128,2048]{1,0:T(8,128)(2,1)S(1)}, bf16[128,2048]{1,0:T(8,128)(2,1)S(1)}, u32[]{:S(2)}, u32[]{:S(2)}) collective-permute-start(bf16[128,2048]{1,0:T(8,128)(2,1)S(1)} %fusion.60), channel_id=1, source_target_pairs={{0,2},{1,3},{2,4},{3,5},{4,6},{5,7},{6,0},{7,1},{8,10},{9,11},{10,... | collective-permute-start | bytes 1572872 | tf_op jit(solution)/shard_map/ppermute | solution.py:296
  312.8 18.9 %collective-permute-start.21 = (bf16[128,2048]{1,0:T(8,128)(2,1)S(1)}, bf16[128,2048]{1,0:T(8,128)(2,1)S(1)}, u32[]{:S(2)}, u32[]{:S(2)}) collective-permute-start(bf16[128,2048]{1,0:T(8,128)(2,1)S(1)} %get-tuple-element.99), channel_id=1, source_target_pairs={{0,16},{8,24},{16,0},{24,8},{1,17},{9,25},{17,1},{25,9},{2,18},{10... | collective-permute-start | bytes 1572872 | tf_op jit(solution)/shard_map/ppermute | solution.py:302
  313.2 24.4 %collective-permute-start.111 = (bf16[1024,768]{1,0:T(8,128)(2,1)S(1)}, bf16[1024,768]{1,0:T(8,128)(2,1)S(1)}, u32[]{:S(2)}, u32[]{:S(2)}) collective-permute-start(bf16[1024,768]{1,0:T(8,128)(2,1)S(1)} %dynamic-slice_convert_fusion.1), channel_id=1, source_target_pairs={{0,8},{8,0},{16,24},{24,16},{1,9},{9,1},{17,25},{25,17},{2,10},{10... | collective-permute-start | bytes 4718600 | tf_op jit(solution)/shard_map/ppermute | solution.py:305
  313.4 25.9 %collective-permute-start.108 = (bf16[1024,768]{1,0:T(8,128)(2,1)S(1)}, bf16[1024,768]{1,0:T(8,128)(2,1)S(1)}, u32[]{:S(2)}, u32[]{:S(2)}) collective-permute-start(bf16[1024,768]{1,0:T(8,128)(2,1)S(1)} %dynamic-slice_convert_fusion.2), channel_id=1, source_target_pairs={{0,8},{8,0},{16,24},{24,16},{1,9},{9,1},{17,25},{25,17},{2,10},{10... | collective-permute-start | bytes 4718600 | tf_op jit(solution)/shard_map/ppermute | solution.py:305
  322.3 20.3 %collective-permute-start.38 = (bf16[2,128,2048]{2,1,0:T(8,128)(2,1)S(1)}, bf16[2,128,2048]{2,1,0:T(8,128)(2,1)S(1)}, u32[]{:S(2)}, u32[]{:S(2)}) collective-permute-start(bf16[2,128,2048]{2,1,0:T(8,128)(2,1)S(1)} %maximum_select_fusion.8), channel_id=1, source_target_pairs={{0,8},{8,0},{16,24},{24,16},{1,9},{9,1},{17,25},{25,17},{2,10},{10... | collective-permute-start | bytes 3145736 | tf_op jit(solution)/shard_map/ppermute | solution.py:305
  332.8 48.3 %collective-permute-start.22 = (bf16[2,128,2048]{2,1,0:T(8,128)(2,1)}, bf16[2,128,2048]{2,1,0:T(8,128)(2,1)}, u32[]{:S(2)}, u32[]{:S(2)}) collective-permute-start(bf16[2,128,2048]{2,1,0:T(8,128)(2,1)} %maximum_select_fusion.6), channel_id=1, source_target_pairs={{0,8},{8,0},{16,24},{24,16},{1,9},{9,1},{17,25},{25,17},{2,10},{10... | collective-permute-start | bytes 3145736 | tf_op jit(solution)/shard_map/ppermute | solution.py:305
  335.8 61.1 %collective-permute-start.115 = (bf16[384,2048]{1,0:T(8,128)(2,1)}, bf16[384,2048]{1,0:T(8,128)(2,1)}, u32[]{:S(2)}, u32[]{:S(2)}) collective-permute-start(bf16[384,2048]{1,0:T(8,128)(2,1)} %add_convert_fusion.1), channel_id=1, source_target_pairs={{0,16},{8,24},{16,0},{24,8},{1,17},{9,25},{17,1},{25,9},{2,18},{10... | collective-permute-start | bytes 4718600 | tf_op jit(solution)/shard_map/ppermute | solution.py:302
  339.0 68.1 %collective-permute-start.112 = (bf16[1024,768]{1,0:T(8,128)(2,1)}, bf16[1024,768]{1,0:T(8,128)(2,1)}, u32[]{:S(2)}, u32[]{:S(2)}) collective-permute-start(bf16[1024,768]{1,0:T(8,128)(2,1)} %add_convert_fusion.3), channel_id=1, source_target_pairs={{0,16},{8,24},{16,0},{24,8},{1,17},{9,25},{17,1},{25,9},{2,18},{10... | collective-permute-start | bytes 4718600 | tf_op jit(solution)/shard_map/ppermute | solution.py:302
  340.9 99.4 %collective-permute-start.109 = (bf16[1024,768]{1,0:T(8,128)(2,1)}, bf16[1024,768]{1,0:T(8,128)(2,1)}, u32[]{:S(2)}, u32[]{:S(2)}) collective-permute-start(bf16[1024,768]{1,0:T(8,128)(2,1)} %add_convert_fusion.5), channel_id=1, source_target_pairs={{0,16},{8,24},{16,0},{24,8},{1,17},{9,25},{17,1},{25,9},{2,18},{10... | collective-permute-start | bytes 4718600 | tf_op jit(solution)/shard_map/ppermute | solution.py:302
  366.5 155.8 %collective-permute-start.39 = (bf16[2,512,256]{2,1,0:T(8,128)(2,1)}, bf16[2,512,256]{2,1,0:T(8,128)(2,1)}, u32[]{:S(2)}, u32[]{:S(2)}) collective-permute-start(bf16[2,512,256]{2,1,0:T(8,128)(2,1)} %get-tuple-element.39), channel_id=1, source_target_pairs={{0,1},{1,0},{2,3},{3,2},{4,5},{5,4},{6,7},{7,6},{8,9},{9,8},{10,11... | collective-permute-start | bytes 1572872 | tf_op jit(solution)/shard_map/ppermute | solution.py:299
  395.0 52.5 %collective-permute-start.97 = (bf16[256,2048]{1,0:T(8,128)(2,1)S(1)}, bf16[256,2048]{1,0:T(8,128)(2,1)S(1)}, u32[]{:S(2)}, u32[]{:S(2)}) collective-permute-start(bf16[256,2048]{1,0:T(8,128)(2,1)S(1)} %dynamic-slice_convert_fusion.3), channel_id=1, source_target_pairs={{0,1},{1,0},{2,3},{3,2},{4,5},{5,4},{6,7},{7,6},{8,9},{9,8},{10,11... | collective-permute-start | bytes 3145736 | tf_op jit(solution)/shard_map/ppermute | solution.py:299
  396.9 49.2 %collective-permute-start.53 = (bf16[1024,512]{1,0:T(8,128)(2,1)S(1)}, bf16[1024,512]{1,0:T(8,128)(2,1)S(1)}, u32[]{:S(2)}, u32[]{:S(2)}) collective-permute-start(bf16[1024,512]{1,0:T(8,128)(2,1)S(1)} %dynamic-slice_convert_fusion.5), channel_id=1, source_target_pairs={{0,1},{1,0},{2,3},{3,2},{4,5},{5,4},{6,7},{7,6},{8,9},{9,8},{10,11... | collective-permute-start | bytes 3145736 | tf_op jit(solution)/shard_map/ppermute | solution.py:299
  407.1 68.9 %collective-permute-start.40 = (bf16[2,512,256]{2,1,0:T(8,128)(2,1)S(1)}, bf16[2,512,256]{2,1,0:T(8,128)(2,1)S(1)}, u32[]{:S(2)}, u32[]{:S(2)}) collective-permute-start(bf16[2,512,256]{2,1,0:T(8,128)(2,1)S(1)} %copy-done.57), channel_id=1, source_target_pairs={{0,1},{1,0},{2,3},{3,2},{4,5},{5,4},{6,7},{7,6},{8,9},{9,8},{10,11... | collective-permute-start | bytes 1572872 | tf_op jit(solution)/shard_map/ppermute | solution.py:299
  440.3 35.2 %collective-permute-start.86 = (bf16[1024,512]{1,0:T(8,128)(2,1)S(1)}, bf16[1024,512]{1,0:T(8,128)(2,1)S(1)}, u32[]{:S(2)}, u32[]{:S(2)}) collective-permute-start(bf16[1024,512]{1,0:T(8,128)(2,1)S(1)} %dynamic-slice_convert_fusion.4), channel_id=1, source_target_pairs={{0,1},{1,0},{2,3},{3,2},{4,5},{5,4},{6,7},{7,6},{8,9},{9,8},{10,11... | collective-permute-start | bytes 3145736 | tf_op jit(solution)/shard_map/ppermute | solution.py:299
  446.1 35.3 %collective-permute-start.42 = (bf16[2,512,256]{2,1,0:T(8,128)(2,1)S(1)}, bf16[2,512,256]{2,1,0:T(8,128)(2,1)S(1)}, u32[]{:S(2)}, u32[]{:S(2)}) collective-permute-start(bf16[2,512,256]{2,1,0:T(8,128)(2,1)S(1)} %add_convert_fusion.7), channel_id=1, source_target_pairs={{4,2},{5,3},{6,4},{7,5},{12,10},{13,11},{14,12},{15,13},{20,18},{2... | collective-permute-start | bytes 1572872 | tf_op jit(solution)/shard_map/ppermute | solution.py:497
  447.5 149.3 %collective-permute-start.116 = (bf16[384,2048]{1,0:T(8,128)(2,1)}, bf16[384,2048]{1,0:T(8,128)(2,1)}, u32[]{:S(2)}, u32[]{:S(2)}) collective-permute-start(bf16[384,2048]{1,0:T(8,128)(2,1)} %add_convert_fusion), channel_id=1, source_target_pairs={{0,8},{8,0},{16,24},{24,16},{1,9},{9,1},{17,25},{25,17},{2,10},{10... | collective-permute-start | bytes 4718600 | tf_op jit(solution)/shard_map/ppermute | solution.py:305
  475.5 132.7 %collective-permute-start.113 = (bf16[1024,768]{1,0:T(8,128)(2,1)}, bf16[1024,768]{1,0:T(8,128)(2,1)}, u32[]{:S(2)}, u32[]{:S(2)}) collective-permute-start(bf16[1024,768]{1,0:T(8,128)(2,1)} %add_convert_fusion.2), channel_id=1, source_target_pairs={{0,8},{8,0},{16,24},{24,16},{1,9},{9,1},{17,25},{25,17},{2,10},{10... | collective-permute-start | bytes 4718600 | tf_op jit(solution)/shard_map/ppermute | solution.py:305
  515.9 16.9 %collective-permute-start.43 = (bf16[2,512,256]{2,1,0:T(8,128)(2,1)S(1)}, bf16[2,512,256]{2,1,0:T(8,128)(2,1)S(1)}, u32[]{:S(2)}, u32[]{:S(2)}) collective-permute-start(bf16[2,512,256]{2,1,0:T(8,128)(2,1)S(1)} %add_convert_fusion.6), channel_id=1, source_target_pairs={{2,0},{3,1},{4,2},{5,3},{6,4},{7,5},{10,8},{11,9},{12,10},{13,11},... | collective-permute-start | bytes 1572872 | tf_op jit(solution)/shard_map/ppermute | solution.py:497
  521.5 80.8 %collective-permute-start.110 = (bf16[1024,768]{1,0:T(8,128)(2,1)}, bf16[1024,768]{1,0:T(8,128)(2,1)}, u32[]{:S(2)}, u32[]{:S(2)}) collective-permute-start(bf16[1024,768]{1,0:T(8,128)(2,1)} %add_convert_fusion.4), channel_id=1, source_target_pairs={{0,8},{8,0},{16,24},{24,16},{1,9},{9,1},{17,25},{25,17},{2,10},{10... | collective-permute-start | bytes 4718600 | tf_op jit(solution)/shard_map/ppermute | solution.py:305
  522.3 35.1 %collective-permute-start.100 = (bf16[64,2048]{1,0:T(8,128)(2,1)}, bf16[64,2048]{1,0:T(8,128)(2,1)}, u32[]{:S(2)}, u32[]{:S(2)}) collective-permute-start(bf16[64,2048]{1,0:T(8,128)(2,1)} %add_convert_fusion.10), channel_id=1, source_target_pairs={{0,2},{1,3},{2,4},{3,5},{4,6},{5,7},{6,0},{7,1},{8,10},{9,11},{10,... | collective-permute-start | bytes 786440 | tf_op jit(solution)/shard_map/ppermute | solution.py:296
  532.7 29.3 %collective-permute-start.56 = (bf16[256,512]{1,0:T(8,128)(2,1)}, bf16[256,512]{1,0:T(8,128)(2,1)}, u32[]{:S(2)}, u32[]{:S(2)}) collective-permute-start(bf16[256,512]{1,0:T(8,128)(2,1)} %add_convert_fusion.16), channel_id=1, source_target_pairs={{0,2},{1,3},{2,4},{3,5},{4,6},{5,7},{6,0},{7,1},{8,10},{9,11},{10,... | collective-permute-start | bytes 786440 | tf_op jit(solution)/shard_map/ppermute | solution.py:296
  591.0 16.4 %collective-permute-start.64 = (bf16[1024,256]{1,0:T(8,128)(2,1)S(1)}, bf16[1024,256]{1,0:T(8,128)(2,1)S(1)}, u32[]{:S(2)}, u32[]{:S(2)}) collective-permute-start(bf16[1024,256]{1,0:T(8,128)(2,1)S(1)} %dynamic-slice_convert_fusion.7), channel_id=1, source_target_pairs={{0,1},{1,0},{2,3},{3,2},{4,5},{5,4},{6,7},{7,6},{8,9},{9,8},{10,11... | collective-permute-start | bytes 1572872 | tf_op jit(solution)/shard_map/ppermute | solution.py:299
  595.4 17.8 %collective-permute-start.75 = (bf16[1024,256]{1,0:T(8,128)(2,1)S(1)}, bf16[1024,256]{1,0:T(8,128)(2,1)S(1)}, u32[]{:S(2)}, u32[]{:S(2)}) collective-permute-start(bf16[1024,256]{1,0:T(8,128)(2,1)S(1)} %dynamic-slice_convert_fusion.6), channel_id=1, source_target_pairs={{0,1},{1,0},{2,3},{3,2},{4,5},{5,4},{6,7},{7,6},{8,9},{9,8},{10,11... | collective-permute-start | bytes 1572872 | tf_op jit(solution)/shard_map/ppermute | solution.py:299
  596.9 71.7 %collective-permute-start.44 = (bf16[2,128,2048]{2,1,0:T(8,128)(2,1)S(1)}, bf16[2,128,2048]{2,1,0:T(8,128)(2,1)S(1)}, u32[]{:S(2)}, u32[]{:S(2)}) collective-permute-start(bf16[2,128,2048]{2,1,0:T(8,128)(2,1)S(1)} %fusion.49), channel_id=1, source_target_pairs={{0,8},{8,0},{16,24},{24,16},{1,9},{9,1},{17,25},{25,17},{2,10},{10... | collective-permute-start | bytes 3145736 | tf_op jit(solution)/shard_map/ppermute | solution.py:305
  602.3 27.3 %collective-permute-start.104 = (bf16[64,2048]{1,0:T(8,128)(2,1)S(1)}, bf16[64,2048]{1,0:T(8,128)(2,1)S(1)}, u32[]{:S(2)}, u32[]{:S(2)}) collective-permute-start(bf16[64,2048]{1,0:T(8,128)(2,1)S(1)} %collective-permute-done.102), channel_id=1, source_target_pairs={{0,2},{1,3},{2,4},{3,5},{4,6},{5,7},{6,0},{7,1},{8,10},{9,11},{10,... | collective-permute-start | bytes 786440 | tf_op jit(solution)/shard_map/ppermute | solution.py:296
  607.5 22.1 %collective-permute-start.103 = (bf16[64,2048]{1,0:T(8,128)(2,1)S(1)}, bf16[64,2048]{1,0:T(8,128)(2,1)S(1)}, u32[]{:S(2)}, u32[]{:S(2)}) collective-permute-start(bf16[64,2048]{1,0:T(8,128)(2,1)S(1)} %collective-permute-done.102), channel_id=1, source_target_pairs={{0,1},{1,0},{2,3},{3,2},{4,5},{5,4},{6,7},{7,6},{8,9},{9,8},{10,11... | collective-permute-start | bytes 786440 | tf_op jit(solution)/shard_map/ppermute | solution.py:299
  608.2 32.0 %collective-permute-start.60 = (bf16[256,512]{1,0:T(8,128)(2,1)S(1)}, bf16[256,512]{1,0:T(8,128)(2,1)S(1)}, u32[]{:S(2)}, u32[]{:S(2)}) collective-permute-start(bf16[256,512]{1,0:T(8,128)(2,1)S(1)} %collective-permute-done.58), channel_id=1, source_target_pairs={{0,2},{1,3},{2,4},{3,5},{4,6},{5,7},{6,0},{7,1},{8,10},{9,11},{10,... | collective-permute-start | bytes 786440 | tf_op jit(solution)/shard_map/ppermute | solution.py:296
  640.2 29.4 %collective-permute-start.106 = (bf16[64,2048]{1,0:T(8,128)(2,1)S(1)}, bf16[64,2048]{1,0:T(8,128)(2,1)S(1)}, u32[]{:S(2)}, u32[]{:S(2)}) collective-permute-start(bf16[64,2048]{1,0:T(8,128)(2,1)S(1)} %collective-permute-done.104), channel_id=1, source_target_pairs={{0,2},{1,3},{2,4},{3,5},{4,6},{5,7},{6,0},{7,1},{8,10},{9,11},{10,... | collective-permute-start | bytes 786440 | tf_op jit(solution)/shard_map/ppermute | solution.py:296
  640.3 28.6 %collective-permute-start.105 = (bf16[64,2048]{1,0:T(8,128)(2,1)S(1)}, bf16[64,2048]{1,0:T(8,128)(2,1)S(1)}, u32[]{:S(2)}, u32[]{:S(2)}) collective-permute-start(bf16[64,2048]{1,0:T(8,128)(2,1)S(1)} %collective-permute-done.104), channel_id=1, source_target_pairs={{0,1},{1,0},{2,3},{3,2},{4,5},{5,4},{6,7},{7,6},{8,9},{9,8},{10,11... | collective-permute-start | bytes 786440 | tf_op jit(solution)/shard_map/ppermute | solution.py:299
  645.4 37.9 %collective-permute-start.62 = (bf16[256,512]{1,0:T(8,128)(2,1)S(1)}, bf16[256,512]{1,0:T(8,128)(2,1)S(1)}, u32[]{:S(2)}, u32[]{:S(2)}) collective-permute-start(bf16[256,512]{1,0:T(8,128)(2,1)S(1)} %collective-permute-done.60), channel_id=1, source_target_pairs={{0,2},{1,3},{2,4},{3,5},{4,6},{5,7},{6,0},{7,1},{8,10},{9,11},{10,... | collective-permute-start | bytes 786440 | tf_op jit(solution)/shard_map/ppermute | solution.py:296
  683.5 47.9 %collective-permute-start.45 = (bf16[128,2048]{1,0:T(8,128)(2,1)S(1)}, bf16[128,2048]{1,0:T(8,128)(2,1)S(1)}, u32[]{:S(2)}, u32[]{:S(2)}) collective-permute-start(bf16[128,2048]{1,0:T(8,128)(2,1)S(1)} %fusion.91), channel_id=1, source_target_pairs={{0,16},{8,24},{16,0},{24,8},{1,17},{9,25},{17,1},{25,9},{2,18},{10... | collective-permute-start | bytes 1572872 | tf_op jit(solution)/shard_map/ppermute | solution.py:302
  684.5 37.2 %collective-permute-start.107 = (bf16[64,2048]{1,0:T(8,128)(2,1)S(1)}, bf16[64,2048]{1,0:T(8,128)(2,1)S(1)}, u32[]{:S(2)}, u32[]{:S(2)}) collective-permute-start(bf16[64,2048]{1,0:T(8,128)(2,1)S(1)} %collective-permute-done.106), channel_id=1, source_target_pairs={{0,1},{1,0},{2,3},{3,2},{4,5},{5,4},{6,7},{7,6},{8,9},{9,8},{10,11... | collective-permute-start | bytes 786440 | tf_op jit(solution)/shard_map/ppermute | solution.py:299
  686.0 37.3 %collective-permute-start.63 = (bf16[256,512]{1,0:T(8,128)(2,1)S(1)}, bf16[256,512]{1,0:T(8,128)(2,1)S(1)}, u32[]{:S(2)}, u32[]{:S(2)}) collective-permute-start(bf16[256,512]{1,0:T(8,128)(2,1)S(1)} %collective-permute-done.62), channel_id=1, source_target_pairs={{0,1},{1,0},{2,3},{3,2},{4,5},{5,4},{6,7},{7,6},{8,9},{9,8},{10,11... | collective-permute-start | bytes 786440 | tf_op jit(solution)/shard_map/ppermute | solution.py:299
  688.1 35.4 %collective-permute-start.96 = (bf16[256,512]{1,0:T(8,128)(2,1)S(1)}, bf16[256,512]{1,0:T(8,128)(2,1)S(1)}, u32[]{:S(2)}, u32[]{:S(2)}) collective-permute-start(bf16[256,512]{1,0:T(8,128)(2,1)S(1)} %collective-permute-done.95), channel_id=1, source_target_pairs={{0,1},{1,0},{2,3},{3,2},{4,5},{5,4},{6,7},{7,6},{8,9},{9,8},{10,11... | collective-permute-start | bytes 786440 | tf_op jit(solution)/shard_map/ppermute | solution.py:299
  728.4 23.0 %collective-permute-start.74 = (bf16[256,256]{1,0:T(8,128)(2,1)S(1)}, bf16[256,256]{1,0:T(8,128)(2,1)S(1)}, u32[]{:S(2)}, u32[]{:S(2)}) collective-permute-start(bf16[256,256]{1,0:T(8,128)(2,1)S(1)} %collective-permute-done.73), channel_id=1, source_target_pairs={{0,1},{1,0},{2,3},{3,2},{4,5},{5,4},{6,7},{7,6},{8,9},{9,8},{10,11... | collective-permute-start | bytes 393224 | tf_op jit(solution)/shard_map/ppermute | solution.py:299
  730.1 24.8 %collective-permute-start.85 = (bf16[256,256]{1,0:T(8,128)(2,1)S(1)}, bf16[256,256]{1,0:T(8,128)(2,1)S(1)}, u32[]{:S(2)}, u32[]{:S(2)}) collective-permute-start(bf16[256,256]{1,0:T(8,128)(2,1)S(1)} %collective-permute-done.84), channel_id=1, source_target_pairs={{0,1},{1,0},{2,3},{3,2},{4,5},{5,4},{6,7},{7,6},{8,9},{9,8},{10,11... | collective-permute-start | bytes 393224 | tf_op jit(solution)/shard_map/ppermute | solution.py:299
  732.5 18.6 %collective-permute-start.46 = (bf16[128,2048]{1,0:T(8,128)(2,1)S(1)}, bf16[128,2048]{1,0:T(8,128)(2,1)S(1)}, u32[]{:S(2)}, u32[]{:S(2)}) collective-permute-start(bf16[128,2048]{1,0:T(8,128)(2,1)S(1)} %fusion.44), channel_id=1, source_target_pairs={{0,16},{8,24},{16,0},{24,8},{1,17},{9,25},{17,1},{25,9},{2,18},{10... | collective-permute-start | bytes 1572872 | tf_op jit(solution)/shard_map/ppermute | solution.py:302
  (112 other events, 1346.5 us)

commit v2 on v1

--- a/solution.py
+++ b/solution.py
@@ -249,6 +249,305 @@
     )(info, *operands)
 
 
+def finish_kernel(
+    outer, sides, sp_n, tp_n, streams, width_scale,
+    *refs,
+):
+    MESH = pl.DeviceIdType.MESH
+    parts = refs[:streams]
+    (part_ref, hidden_ref, scale_ref, gain_ref, middle_ref, sums_ref) = refs[streams : streams + 6]
+    outs = refs[streams + 6 : 2 * streams + 6]
+    grad_out, sums_out = refs[2 * streams + 6 : 2 * streams + 8]
+    rest = refs[2 * streams + 8 :]
+    got = rest[:streams]
+    staged = rest[streams : 2 * streams]
+    (near_got, far_got, keep_buf, far_stage, sums_got, sums_stage) = rest[2 * streams : 2 * streams + 6]
+    (reduce_send, reduce_recv, gather_send, gather_recv, pair_send, pair_recv) = rest[
+        2 * streams + 6 : 2 * streams + 12
+    ]
+    tp_send, tp_recv, sums_send, sums_recv = rest[2 * streams + 12 :]
+
+    sp_i = lax.axis_index("sp")
+    tp_i = lax.axis_index("tp")
+    line = sp_i // 2
+    half = sp_i % 2
+    side = tp_i // 2
+    core = tp_i % 2
+    last = outer - 1
+
+    def sp_at(z, y):
+        return (tp_i, z * 2 + y)
+
+    pair_dev = sp_at(line, 1 - half)
+    core_dev = (side * 2 + (1 - core), sp_i)
+    side_dev = ((1 - side) * 2 + core, sp_i)
+
+    tp_bits = []
+    bit = 1
+    while bit < tp_n:
+        tp_bits.append(bit)
+        bit *= 2
+    sp_bits = []
+    bit = 1
+    while bit < sp_n:
+        sp_bits.append(bit)
+        bit *= 2
+
+    def flip(value, bit):
+        return value + bit - 2 * bit * ((value // bit) % 2)
+
+    sum_devs = [(flip(tp_i, b), sp_i) for b in tp_bits] + [(tp_i, flip(sp_i, b)) for b in sp_bits]
+
+    barrier = pltpu.get_barrier_semaphore()
+    greeted = [sp_at((line + 1) % outer, half), sp_at((line + outer - 1) % outer, half)] + sum_devs
+    for device in greeted:
+        pl.semaphore_signal(barrier, inc=1, device_id=device, device_id_type=MESH)
+    pl.semaphore_wait(barrier, len(greeted))
+
+    def remote(src, dst, send, recv, device):
+        return pltpu.make_async_remote_copy(
+            src_ref=src, dst_ref=dst, send_sem=send, recv_sem=recv,
+            device_id=device, device_id_type=MESH,
+        )
+
+    places = (line, last - line)
+    nexts = (sp_at(jnp.minimum(line + 1, last), half), sp_at(jnp.maximum(line - 1, 0), half))
+    signs = (1, -1)
+
+    def rows_of(stream, index):
+        count = parts[stream].shape[0] // outer
+        return pl.ds(pl.multiple_of(index * count, count), count)
+
+    def reduce_copy(stream, way, step, src):
+        return remote(
+            src, got[stream].at[way, step - 1], reduce_send.at[stream, way, step - 1],
+            reduce_recv.at[stream, way, step - 1], nexts[way],
+        )
+
+    def clamp(index):
+        return jnp.clip(index, 0, last)
+
+    def reduce_step(stream, step):
+        for way in range(2):
+            place, sign = places[way], signs[way]
+            target = clamp(line + sign * (outer - step))
+            own = parts[stream].at[rows_of(stream, target), :]
+
+            @pl.when(place == 0)
+            def _():
+                reduce_copy(stream, way, step, own).start()
+
+            if step > 1:
+
+                @pl.when((place > 0) & (place <= step - 1))
+                def _():
+                    reduce_copy(stream, way, step - 1, own).wait_recv()
+                    stage = staged[stream].at[way, step - 2]
+                    stage[...] = (
+                        got[stream][way, step - 2].astype(F32) + own[...].astype(F32)
+                    ).astype(BF16)
+                    reduce_copy(stream, way, step, stage).start()
+
+    def gather_copy(stream, way, step, origin):
+        block = outs[stream].at[half, rows_of(stream, origin), :]
+        return remote(
+            block, block, gather_send.at[stream, way, step - 1],
+            gather_recv.at[stream, way, step - 1], nexts[way],
+        )
+
+    def pair_copy(stream, slot, origin):
+        block = outs[stream].at[half, rows_of(stream, origin), :]
+        return remote(block, block, pair_send.at[stream, slot], pair_recv.at[stream, slot], pair_dev)
+
+    def reduce_final(stream):
+        own = parts[stream].at[rows_of(stream, line), :]
+        block = outs[stream].at[half, rows_of(stream, line), :]
+        for way in range(2):
+
+            @pl.when(places[way] > 0)
+            def _():
+                reduce_copy(stream, way, last, own).wait_recv()
+
+        up = jnp.where(line > 0, got[stream][0, last - 1].astype(F32), 0.0)
+        down = jnp.where(line < last, got[stream][1, last - 1].astype(F32), 0.0)
+        block[...] = (own[...].astype(F32) + up + down).astype(BF16)
+        for way in range(2):
+
+            @pl.when(places[way] < last)
+            def _():
+                gather_copy(stream, way, 1, line).start()
+
+        pair_copy(stream, 0, line).start()
+
+    def gather_step(stream, step):
+        for way in range(2):
+            place, sign = places[way], signs[way]
+            origin = clamp(line - sign * step)
+
+            @pl.when(place >= step)
+            def _():
+                gather_copy(stream, way, step, origin).wait_recv()
+                if step < last:
+
+                    @pl.when(place < last)
+                    def _():
+                        gather_copy(stream, way, step + 1, origin).start()
+
+                pair_copy(stream, 1 + way * last + step - 1, origin).start()
+
+    def drain(stream):
+        pair_copy(stream, 0, line).wait()
+        for way in range(2):
+            place, sign = places[way], signs[way]
+            for step in range(1, outer):
+                origin = clamp(line - sign * step)
+
+                @pl.when(place <= step - 1)
+                def _():
+                    reduce_copy(stream, way, step, parts[stream].at[rows_of(stream, 0), :]).wait_send()
+
+                @pl.when((place >= step - 1) & (place < last))
+                def _():
+                    gather_copy(stream, way, step, origin).wait_send()
+
+                @pl.when(place >= step)
+                def _():
+                    pair_copy(stream, 1 + way * last + step - 1, origin).wait()
+
+    def near_copy(index):
+        return remote(
+            part_ref.at[index, 1 - core], near_got.at[index], tp_send.at[index], tp_recv.at[index],
+            core_dev,
+        )
+
+    def far_copy():
+        return remote(far_stage, far_got, tp_send.at[sides], tp_recv.at[sides], side_dev)
+
+    def spread_copy(slot, s, device):
+        block = grad_out.at[s, core]
+        return remote(block, block, tp_send.at[sides + slot], tp_recv.at[sides + slot], device)
+
+    def input_step(step):
+        if step == 0:
+            for index in range(sides):
+                near_copy(index).start()
+        if step == 1:
+            for index in range(sides):
+                near_copy(index).wait_recv()
+            keep_buf[...] = part_ref[side, core].astype(F32) + near_got[side].astype(F32)
+            far_stage[...] = (
+                part_ref[1 - side, core].astype(F32) + near_got[1 - side].astype(F32)
+            ).astype(BF16)
+            far_copy().start()
+        if step == 2:
+            far_copy().wait_recv()
+            incoming = keep_buf[...] + far_got[...].astype(F32)
+            values = hidden_ref[...].astype(F32)
+            scales = scale_ref[...]
+            weighted = incoming * gain_ref[...]
+            inner_sum = jnp.sum(weighted * values, axis=-1, keepdims=True)
+            grads = scales * weighted - values * (scales * scales * scales) * inner_sum * width_scale
+            grad_out[side, core] = (middle_ref[...] + grads).astype(BF16)
+            spread_copy(1, side, side_dev).start()
+            spread_copy(2, side, core_dev).start()
+        if step == 3:
+            spread_copy(1, side, side_dev).wait_recv()
+            spread_copy(3, 1 - side, core_dev).start()
+        if step == 4:
+            spread_copy(2, side, core_dev).wait_recv()
+            spread_copy(3, 1 - side, core_dev).wait_recv()
+            for index in range(sides):
+                near_copy(index).wait_send()
+            far_copy().wait_send()
+            spread_copy(1, side, side_dev).wait_send()
+            spread_copy(2, side, core_dev).wait_send()
+            spread_copy(3, 1 - side, core_dev).wait_send()
+
+    rounds = len(sum_devs)
+
+    def sums_copy(step):
+        src = sums_ref if step == 0 else sums_stage.at[step - 1]
+        return remote(
+            src, sums_got.at[step], sums_send.at[step], sums_recv.at[step], sum_devs[step]
+        )
+
+    def sums_step(step):
+        if step > 0:
+            sums_copy(step - 1).wait_recv()
+            before = sums_ref[...] if step == 1 else sums_stage[step - 2]
+            total = before + sums_got[step - 1]
+            if step == rounds:
+                sums_out[...] = total
+            else:
+                sums_stage[step - 1] = total
+        if step < rounds:
+            sums_copy(step).start()
+        if step == rounds:
+            for index in range(rounds):
+                sums_copy(index).wait_send()
+
+    extra = []
+    for index in range(5):
+        extra.append(functools.partial(input_step, index))
+    for index in range(rounds + 1):
+        extra.append(functools.partial(sums_step, index))
+    for turn in range(streams + 1):
+        for step in range(1, outer + 1):
+            if turn < streams:
+                if step < outer:
+                    reduce_step(turn, step)
+                else:
+                    reduce_final(turn)
+            if turn > 0 and step < outer:
+                gather_step(turn - 1, step)
+            if extra:
+                extra.pop(0)()
+    for step in extra:
+        step()
+    for stream in range(streams):
+        drain(stream)
+
+
+def finish(parts, part, hidden, scales, gain, middle, sums, outer, sp_n, tp_n):
+    streams = len(parts)
+    sides = tp_n // 2
+    quarter, model = hidden.shape
+    last = outer - 1
+    rounds = (tp_n - 1).bit_length() + (sp_n - 1).bit_length()
+    vmem = pl.BlockSpec(memory_space=pltpu.VMEM)
+    chunk = [(2, last, p.shape[0] // outer, p.shape[1]) for p in parts]
+    dma = pltpu.SemaphoreType.DMA
+    return pl.pallas_call(
+        functools.partial(finish_kernel, outer, sides, sp_n, tp_n, streams, 1.0 / model),
+        out_shape=[jax.ShapeDtypeStruct((2,) + p.shape, BF16) for p in parts]
+        + [
+            jax.ShapeDtypeStruct((sides, 2, quarter, model), BF16),
+            jax.ShapeDtypeStruct(sums.shape, F32),
+        ],
+        in_specs=[vmem] * (streams + 6),
+        out_specs=[vmem] * (streams + 2),
+        scratch_shapes=[pltpu.VMEM(c, BF16) for c in chunk]
+        + [pltpu.VMEM(c, BF16) for c in chunk]
+        + [
+            pltpu.VMEM((sides, quarter, model), BF16),
+            pltpu.VMEM((quarter, model), BF16),
+            pltpu.VMEM((quarter, model), F32),
+            pltpu.VMEM((quarter, model), BF16),
+            pltpu.VMEM((rounds,) + sums.shape, F32),
+            pltpu.VMEM((rounds,) + sums.shape, F32),
+        ]
+        + [dma((streams, 2, last))] * 4
+        + [dma((streams, 1 + 2 * last))] * 2
+        + [dma((sides + 4,))] * 2
+        + [dma((rounds,))] * 2,
+        compiler_params=pltpu.CompilerParams(
+            collective_id=1, has_side_effects=True, vmem_limit_bytes=60 * 1024 * 1024
+        ),
+        cost_estimate=pl.CostEstimate(flops=10**9, bytes_accessed=10**8, transcendentals=0),
+        name="finish",
+    )(*parts, part, hidden, scales, gain, middle, sums)
+
+
 def body(
     hidden,
     segment_ids,
@@ -363,6 +662,17 @@
     query_normed, query_scales = norm_rows(query_raw, query_norm)
     queries = rotary(query_normed, cosine, sine).astype(BF16).reshape(rows_dev, heads * head_width)
 
+    def swap_half(value):
+        piece = model // 4
+        mine = pair(lax.dynamic_slice_in_dim(value, ((1 - pair_i) * 2 + core_i) * piece, piece, 1))
+        near = core(mine)
+        return jnp.where(
+            core_i == 1, jnp.concatenate([near, mine], 1), jnp.concatenate([mine, near], 1)
+        )
+
+    normed_own = lax.dynamic_slice_in_dim(normed, pair_i * (model // 2), model // 2, 1)
+    both_normed = jnp.concatenate([normed_own, swap_half(normed)])
+
     grad_quarter = lax.dynamic_slice_in_dim(upstream, quarter_first, quarter)
     up_blocks = gather_sp(grad_quarter)
 
@@ -394,6 +704,7 @@
     lse_rows = lse.T.reshape(groups, per_group, rows_dev)
     gate_sig = jax.nn.sigmoid(gate_raw)
     gated = (mixed * gate_sig).astype(BF16)
+    gated_other = pair(gated)
 
     def scatter_tp(part):
         part = part.reshape(sides, 2, quarter, model)
@@ -471,10 +782,15 @@
     ffn_up_grad = reduce_tp(outer_sum(rows_all, grad_up_all))
     ffn_down_grad = reduce_tp(outer_sum(inner_all, up_all))
 
-    output_part = outer_sum(gated, grad_branch)
+    branch_other = swap_half(grad_branch)
+    branch_own = lax.dynamic_slice_in_dim(grad_branch, pair_i * (model // 2), model // 2, 1)
+    output_half = outer_sum(
+        jnp.concatenate([gated, gated_other]), jnp.concatenate([branch_own, branch_other])
+    )
     grad_gated = times_transpose(grad_branch, output_proj)
     grad_mixed = (grad_gated * gate_sig).astype(BF16)
     grad_gate_raw = (grad_gated * mixed * (gate_sig * (1.0 - gate_sig))).astype(BF16)
+    gate_half = outer_sum(both_normed, jnp.concatenate([grad_gate_raw, pair(grad_gate_raw)]))
     deltas = jnp.sum(
         (grad_mixed.astype(F32) * mixed).reshape(rows_dev, heads, head_width), axis=-1
     )
@@ -506,38 +822,16 @@
     )
     grad_query_low = grad_query_raw.reshape(rows_dev, heads * head_width).astype(BF16)
     grad_key_low = grad_key_raw.reshape(rows_dev, group_width).astype(BF16)
-
-    def reduce_sp(part):
-        count, width = part.shape
-        half = count // 2
-        chunk = half // outer
-        keep = lax.dynamic_slice_in_dim(part, pair_i * half, half)
-        send = lax.dynamic_slice_in_dim(part, (1 - pair_i) * half, half)
-        keep = keep + pair(send.astype(BF16)).astype(F32)
-
-        def piece(k):
-            return lax.dynamic_slice_in_dim(keep, ((ring_i - k) % outer) * chunk, chunk)
-
-        total = piece(1 % outer)
-        for k in range(2, outer + 1):
-            total = ring(total.astype(BF16)).astype(F32) + piece(k % outer)
-        block = total.astype(BF16)
-        out = jnp.zeros((count, width), F32)
-        for k in range(outer):
-            at = ((ring_i - k) % outer) * chunk
-            out = lax.dynamic_update_slice(out, block.astype(F32), (pair_i * half + at, 0))
-            out = lax.dynamic_update_slice(
-                out, pair(block).astype(F32), ((1 - pair_i) * half + at, 0)
-            )
-            if k < outer - 1:
-                block = ring(block)
-        return out
-
-    output_grad = reduce_sp(output_part)
-    gate_grad = reduce_sp(outer_sum(normed, grad_gate_raw))
-    query_grad = reduce_sp(outer_sum(normed, grad_query_low))
-    key_grad = reduce_sp(outer_sum(normed, grad_key_low))
-    value_grad = reduce_sp(outer_sum(normed, grad_value_low))
+    grad_kv_low = jnp.concatenate([grad_key_low, grad_value_low], axis=1)
+
+    both_queries = jnp.concatenate([grad_query_low, pair(grad_query_low)])
+    both_kv = jnp.concatenate([grad_kv_low, pair(grad_kv_low)])
+    parts = [
+        output_half.astype(BF16),
+        gate_half.astype(BF16),
+        outer_sum(both_normed, both_queries).astype(BF16),
+        outer_sum(both_normed, both_kv).astype(BF16),
+    ]
 
     grad_normed_part = (
         times_transpose(grad_query_low, query_proj)
@@ -545,26 +839,38 @@
         + times_transpose(grad_value_low, value_proj)
         + times_transpose(grad_gate_raw, gate_proj)
     )
-    grad_normed = scatter_tp(grad_normed_part)
-    scales_quarter = lax.dynamic_slice_in_dim(attn_scales, quarter_first, quarter)
-    norm_grad_one, attn_gain_terms = norm_back(
-        hidden_quarter, scales_quarter, attn_norm, grad_normed
-    )
-    hidden_grad = gather_tp((grad_middle_quarter + norm_grad_one).astype(BF16)).astype(F32)
-
     gains = jnp.concatenate(
         [
-            jnp.sum(attn_gain_terms, axis=0),
+            jnp.sum(grad_normed_part * hidden_full * attn_scales, axis=0),
             jnp.sum(ffn_gain_terms, axis=0),
             jnp.sum(query_gain_terms, axis=(0, 1)),
             jnp.sum(key_gain_terms, axis=(0, 1)),
         ]
     )
-    for axis, size in (("tp", tp_n), ("sp", sp_n)):
-        bit = 1
-        while bit < size:
-            gains = gains + lax.ppermute(gains, axis, [(i, i ^ bit) for i in range(size)])
-            bit *= 2
+    gains_at = 2 * model + 2 * head_width
+    gains = jnp.pad(gains, (0, -gains_at % 1024)).reshape(-1, 128)
+    scales_quarter = lax.dynamic_slice_in_dim(attn_scales, quarter_first, quarter)
+    finished = finish(
+        parts,
+        grad_normed_part.astype(BF16).reshape(sides, 2, quarter, model),
+        lax.dynamic_slice_in_dim(hidden, quarter_first, quarter),
+        scales_quarter,
+        attn_norm[None, :],
+        grad_middle_quarter,
+        gains,
+        outer,
+        sp_n,
+        tp_n,
+    )
+    output_all, gate_all_w, query_all, kv_all, input_all, gains = finished
+    output_grad = jnp.concatenate([output_all[0], output_all[1]], axis=1).astype(F32)
+    gate_grad = gate_all_w.reshape(model, heads * head_width).astype(F32)
+    query_grad = query_all.reshape(model, heads * head_width).astype(F32)
+    kv_all = kv_all.reshape(model, 2 * group_width)
+    key_grad = kv_all[:, :group_width].astype(F32)
+    value_grad = kv_all[:, group_width:].astype(F32)
+    hidden_grad = input_all.reshape(rows_dev, model).astype(F32)
+    gains = gains.reshape(-1)
     return (
         layer_out,
         hidden_grad,
@@ -575,7 +881,7 @@
         gate_grad,
         output_grad,
         gains[2 * model : 2 * model + head_width],
-        gains[2 * model + head_width :],
+        gains[2 * model + head_width : gains_at],
         gains[model : 2 * model],
         ffn_gate_grad,
         ffn_up_grad,

time: 772 us -> 669 us (0.87)
  waiting for transfers between devices: 332 us -> 159 us
  Pallas kernels: 26.7 us -> 170 us
  starting transfers between devices: 158 us -> 81.9 us
    pallas_call x0 -> x1, Pallas kernels: none -> 143 us  [finish(): pl.pallas_call(functools.partial(finish_kernel, outer, sides, sp_n, tp_n,...]
    ppermute x42 -> x12, waiting for transfers between devices: 98.4 us -> 14.7 us  [ring(): return lax.ppermute(value, 'sp', ring_pairs)]
    ppermute x42 -> x12, starting transfers between devices: 74.9 us -> 27.8 us  [ring(): return lax.ppermute(value, 'sp', ring_pairs)]
    ppermute x47 -> x28, waiting for transfers between devices: 149 us -> 112 us  [pair(): return lax.ppermute(value, 'sp', pair_pairs)]
    ppermute x8 -> x6, waiting for transfers between devices: 52.8 us -> 18.9 us  [side(): return lax.ppermute(value, 'tp', side_pairs)]
    ppermute x47 -> x28, starting transfers between devices: 64.4 us -> 37.8 us  [pair(): return lax.ppermute(value, 'sp', pair_pairs)]
    ppermute x5 -> x0, waiting for transfers between devices: 24 us -> none  [body(): lax.ppermute(gains, axis, [(i, i ^ bit) for i in range(size)])]
    convert_element_type x12 -> x6, other arithmetic: 3.7 us -> 14.2 us  [the longest x1 2.74 us: body(): query_grad = query_all.reshape(model, heads * head_width).astype(F32)]
  transfers between devices with their start and end apart: 117 -> 61, of which waited for: 55 -> 20; matrix products, arithmetic and copies ran while one was open for 26% -> 32% of each run, Pallas kernels for 4% -> 26%
where the time goes in v2:
time: 669 us; the launch traced here: 660 us
  Pallas kernels  170 us (25%)
  waiting for transfers between devices  159 us (24%)
  other arithmetic  89.8 us (13%)
  starting transfers between devices  81.9 us (12%)
  matrix products  81.3 us (12%)
  local copies, waits for them, and re-layouts  68.8 us (10%)
  between operations  10.1 us (2%)
    pallas_call x1, Pallas kernels, finish(): pl.pallas_call(functools.partial(finish_kernel, outer, sides, sp_n, tp_n,...  143 us
    ppermute x28, waiting for transfers between devices, pair(): return lax.ppermute(value, 'sp', pair_pairs)  112 us
    ppermute x28, starting transfers between devices, pair(): return lax.ppermute(value, 'sp', pair_pairs)  37.8 us
    dot_general x17, matrix products, times_transpose(): lax.dot_general(left, right, (((1,), (1,)), ((), ())), preferred_element_...  32.5 us
    unnamed x131, local copies, waits for them, and re-layouts  28 us
    ppermute x12, starting transfers between devices, ring(): return lax.ppermute(value, 'sp', ring_pairs)  27.8 us
    dot_general x17, matrix products, matmul(): return jnp.dot(left, right, preferred_element_type=F32)  27.4 us
    dot_general x7, matrix products, outer_sum(): lax.dot_general(left, right, (((0,), (0,)), ((), ())), preferred_element_...  21.4 us
  transfers between devices with their start and end apart: 61, of which 20 were waited for; matrix products, arithmetic and copies ran while one was open for 32% of the time, Pallas kernels for 26%

profile of v2, /device:TPU:0, one launch (start us, length us, event | category | flops | bytes accessed | tf_op | source)
XLA Modules:
  0.0 660.4 jit_solution(1851797621401103982)
XLA Ops:
  14.0 2.6 fusion.42
  17.5 3.0 collective-permute-start.4
  20.5 4.3 collective-permute-start
  30.0 4.5 multiply_reduce_fusion.4
  34.5 2.5 copy.117
  68.8 4.6 attn_forward.3
  73.4 3.8 attn_forward.4
  77.2 6.6 collective-permute-done.2.kv_b
  83.8 3.8 attn_forward.5
  87.6 3.3 multiply_convert_fusion.2
  96.9 3.2 collective-permute-start.28
  110.5 3.0 collective-permute-done.28
  114.0 3.4 collective-permute-start.32
  125.1 2.5 maximum_select_fusion.9
  129.5 2.5 reshape.437
  137.1 2.6 multiply_reduce_fusion.3
  145.3 3.5 collective-permute-done.33
  150.7 2.5 collective-permute-start.7
  153.2 4.4 collective-permute-done.19
  157.6 3.2 fusion.99
  163.0 2.5 multiply_convert_fusion.3
  171.6 2.7 collective-permute-start.11
  175.5 15.8 %collective-permute-done.8 = bf16[128,2048]{1,0:T(8,128)(2,1)S(1)} collective-permute-done((bf16[128,2048]{1,0:T(8,128)(2,1)S(1)}, bf16[128,2048]{1,0:T(8,128)(2,1)S(1)}, u32[]{:S(2)}, u32[]{:S(2)}) %collective-permute-start.8) | collective-permute-done | bytes 524320 | tf_op jit(solution)/shard_map/ppermute | solution.py:598
  193.4 2.4 multiply_convert_fusion.9
  202.7 2.5 collective-permute-start.15
  205.3 17.6 %collective-permute-done.12 = bf16[128,2048]{1,0:T(8,128)(2,1)S(1)} collective-permute-done((bf16[128,2048]{1,0:T(8,128)(2,1)S(1)}, bf16[128,2048]{1,0:T(8,128)(2,1)S(1)}, u32[]{:S(2)}, u32[]{:S(2)}) %collective-permute-start.12) | collective-permute-done | bytes 524320 | tf_op jit(solution)/shard_map/ppermute | solution.py:598
  225.2 2.5 collective-permute-start.10
  227.7 2.4 multiply_convert_fusion.7
  234.3 2.7 collective-permute-start.27
  240.9 13.7 %collective-permute-done.16 = bf16[128,2048]{1,0:T(8,128)(2,1)S(1)} collective-permute-done((bf16[128,2048]{1,0:T(8,128)(2,1)S(1)}, bf16[128,2048]{1,0:T(8,128)(2,1)S(1)}, u32[]{:S(2)}, u32[]{:S(2)}) %collective-permute-start.16) | collective-permute-done | bytes 524320 | tf_op jit(solution)/shard_map/ppermute | solution.py:598
  260.3 2.5 multiply_convert_fusion.5
  264.4 5.3 fusion.28
  275.5 3.2 collective-permute-done.17
  282.1 7.8 %collective-permute-done.34 = bf16[128,2048]{1,0:T(8,128)(2,1)S(1)} collective-permute-done((bf16[128,2048]{1,0:T(8,128)(2,1)S(1)}, bf16[128,2048]{1,0:T(8,128)(2,1)S(1)}, u32[]{:S(2)}, u32[]{:S(2)}) %collective-permute-start.34) | collective-permute-done | bytes 524320 | tf_op jit(solution)/shard_map/ppermute | solution.py:598
  290.1 3.6 collective-permute-start.35
  293.7 3.5 fusion.20
  297.3 9.6 %collective-permute-done.35 = bf16[128,2048]{1,0:T(8,128)(2,1)S(1)} collective-permute-done((bf16[128,2048]{1,0:T(8,128)(2,1)S(1)}, bf16[128,2048]{1,0:T(8,128)(2,1)S(1)}, u32[]{:S(2)}, u32[]{:S(2)}) %collective-permute-start.35) | collective-permute-done | bytes 524320 | tf_op jit(solution)/shard_map/ppermute | solution.py:595
  307.3 2.8 fusion.123
  310.6 3.5 fusion.12
  316.7 8.2 %collective-permute-done.38 = bf16[128,2048]{1,0:T(8,128)(2,1)S(1)} collective-permute-done((bf16[128,2048]{1,0:T(8,128)(2,1)S(1)}, bf16[128,2048]{1,0:T(8,128)(2,1)S(1)}, u32[]{:S(2)}, u32[]{:S(2)}) %collective-permute-start.38) | collective-permute-done | bytes 524320 | tf_op jit(solution)/shard_map/ppermute | solution.py:601
  325.1 8.2 %collective-permute-done.21 = bf16[128,2048]{1,0:T(8,128)(2,1)S(1)} collective-permute-done((bf16[128,2048]{1,0:T(8,128)(2,1)S(1)}, bf16[128,2048]{1,0:T(8,128)(2,1)S(1)}, u32[]{:S(2)}, u32[]{:S(2)}) %collective-permute-start.21) | collective-permute-done | bytes 524320 | tf_op jit(solution)/shard_map/ppermute | solution.py:601
  348.4 3.3 attn_backward.3
  353.5 3.7 attn_backward.4
  357.2 7.2 %attn_backward.5 = (f32[512,512]{1,0:T(8,128)}, bf16[2,512,256]{2,1,0:T(8,128)(2,1)}, bf16[2,512,256]{2,1,0:T(8,128)(2,1)}) custom-call(s32[7]{0:T(128)} %stack.213.info, s32[1,512]{1,0:T(1,128)} %compare_select_fusion.starts, f32[2,2,512]{2,1,0:T(2,128)} %reshape.438.lse, f32[2,2,512]{2,1,0:T(2,128)} %reshape.440.deltas, bf16[512,512]{1,0:T(8,128)(2,1)} %bitcast.249, ...), custom_call_target="tpu_custom_call" | custom-call | flops 2684354560 | bytes 2097152 | tf_op jit(solution)/shard_map/attn_backward/pallas_call | solution.py:229
  373.7 3.5 collective-permute-start.45
  378.3 3.3 fusion.144
  386.1 14.2 %collective-permute-done.44 = bf16[512,512]{1,0:T(8,128)(2,1)S(1)} collective-permute-done((bf16[512,512]{1,0:T(8,128)(2,1)S(1)}, bf16[512,512]{1,0:T(8,128)(2,1)S(1)}, u32[]{:S(2)}, u32[]{:S(2)}) %collective-permute-start.44) | collective-permute-done | bytes 524320 | tf_op jit(solution)/shard_map/ppermute | solution.py:598
  410.4 3.4 add_convert_fusion.2
  414.7 3.7 add_convert_fusion
  418.4 7.9 %collective-permute-done.47 = bf16[2,512,256]{2,1,0:T(8,128)(2,1)S(1)} collective-permute-done((bf16[2,512,256]{2,1,0:T(8,128)(2,1)S(1)}, bf16[2,512,256]{2,1,0:T(8,128)(2,1)S(1)}, u32[]{:S(2)}, u32[]{:S(2)}) %collective-permute-start.47) | collective-permute-done | bytes 524320 | tf_op jit(solution)/shard_map/ppermute | solution.py:598
  428.0 9.5 %collective-permute-done.40 = bf16[512,512]{1,0:T(8,128)(2,1)S(1)} collective-permute-done((bf16[512,512]{1,0:T(8,128)(2,1)S(1)}, bf16[512,512]{1,0:T(8,128)(2,1)S(1)}, u32[]{:S(2)}, u32[]{:S(2)}) %collective-permute-start.40) | collective-permute-done | bytes 524320 | tf_op jit(solution)/shard_map/ppermute | solution.py:598
  438.3 2.6 collective-permute-done.53
  447.1 13.5 %collective-permute-done.50 = bf16[2,512,256]{2,1,0:T(8,128)(2,1)S(1)} collective-permute-done((bf16[2,512,256]{2,1,0:T(8,128)(2,1)S(1)}, bf16[2,512,256]{2,1,0:T(8,128)(2,1)S(1)}, u32[]{:S(2)}, u32[]{:S(2)}) %collective-permute-start.50) | collective-permute-done | bytes 524320 | tf_op jit(solution)/shard_map/ppermute | solution.py:813
  460.9 2.8 fusion.126
  470.1 4.8 fusion.4
  475.5 5.9 collective-permute-done.51
  483.7 143.4 %finish.1 = (bf16[2,512,1024]{2,1,0:T(8,128)(2,1)}, bf16[2,1024,512]{2,1,0:T(8,128)(2,1)}, bf16[2,1024,512]{2,1,0:T(8,128)(2,1)}, bf16[2,1024,512]{2,1,0:T(8,128...) custom-call(bf16[512,1024]{1,0:T(8,128)(2,1)} %fusion.36.refs_0_, ...), custom_call_target="tpu_custom_call" | custom-call | flops 1000000000 | bytes 100000000 | tf_op jit(solution)/shard_map/finish/pallas_call | solution.py:520
  630.2 2.5 maximum_convert_fusion
  634.0 5.5 fusion.7
  641.9 2.7 bitcast_convert_fusion.1
  644.6 5.0 fusion.6
  649.6 2.7 bitcast_convert_fusion.2
  652.4 2.7 bitcast_convert_fusion.3
  655.1 5.1 fusion.5
  (363 shorter events, 198.4 us)
Async XLA Ops:
  0.6 162.3 %copy-start = (bf16[768,2048]{1,0:T(8,128)(2,1)S(1)}, bf16[768,2048]{1,0:T(8,128)(2,1)}, u32[]{:S(2)}) copy-start(bf16[768,2048]{1,0:T(8,128)(2,1)} %param.28) | copy-start | bytes 9437188
  17.5 49.8 %collective-permute-start.4 = (bf16[2,512,256]{2,1,0:T(8,128)(2,1)}, bf16[2,512,256]{2,1,0:T(8,128)(2,1)}, u32[]{:S(2)}, u32[]{:S(2)}) collective-permute-start(bf16[2,512,256]{2,1,0:T(8,128)(2,1)} %pad_maximum_fusion.9.kv_a), channel_id=1, source_target_pairs={{0,1},{1,0},{2,3},{3,2},{4,5},{5,4},{6,7},{7,6},{8,9},{9,8},{10,11... | collective-permute-start | bytes 1572872 | tf_op jit(solution)/shard_map/ppermute | solution.py:598
  20.5 25.9 %collective-permute-start = (bf16[2,512,256]{2,1,0:T(8,128)(2,1)}, bf16[2,512,256]{2,1,0:T(8,128)(2,1)}, u32[]{:S(2)}, u32[]{:S(2)}) collective-permute-start(bf16[2,512,256]{2,1,0:T(8,128)(2,1)} %pad_maximum_fusion.9.kv_a), channel_id=1, source_target_pairs={{0,2},{1,3},{2,4},{3,5},{4,6},{5,7},{8,10},{9,11},{10,12},{11,13},... | collective-permute-start | bytes 1572872 | tf_op jit(solution)/shard_map/ppermute | solution.py:658
  26.9 68.5 %collective-permute-start.24 = (bf16[128,2048]{1,0:T(8,128)(2,1)}, bf16[128,2048]{1,0:T(8,128)(2,1)}, u32[]{:S(2)}, u32[]{:S(2)}) collective-permute-start(bf16[128,2048]{1,0:T(8,128)(2,1)} %get-tuple-element.59), channel_id=1, source_target_pairs={{0,2},{1,3},{2,4},{3,5},{4,6},{5,7},{6,0},{7,1},{8,10},{9,11},{10,... | collective-permute-start | bytes 1572872 | tf_op jit(solution)/shard_map/ppermute | solution.py:595
  27.7 79.1 %collective-permute-start.36 = (bf16[128,2048]{1,0:T(8,128)(2,1)}, bf16[128,2048]{1,0:T(8,128)(2,1)}, u32[]{:S(2)}, u32[]{:S(2)}) collective-permute-start(bf16[128,2048]{1,0:T(8,128)(2,1)} %get-tuple-element.59), channel_id=1, source_target_pairs={{0,1},{1,0},{2,3},{3,2},{4,5},{5,4},{6,7},{7,6},{8,9},{9,8},{10,11... | collective-permute-start | bytes 1572872 | tf_op jit(solution)/shard_map/ppermute | solution.py:598
  46.4 12.5 %collective-permute-start.1 = (bf16[2,512,256]{2,1,0:T(8,128)(2,1)}, bf16[2,512,256]{2,1,0:T(8,128)(2,1)}, u32[]{:S(2)}, u32[]{:S(2)}) collective-permute-start(bf16[2,512,256]{2,1,0:T(8,128)(2,1)} %collective-permute-done.kv_a), channel_id=1, source_target_pairs={{2,4},{3,5},{4,6},{5,7},{10,12},{11,13},{12,14},{13,15},{18,20},{1... | collective-permute-start | bytes 1572872 | tf_op jit(solution)/shard_map/ppermute | solution.py:658
  57.4 16.0 %collective-permute-start.3 = (bf16[2,512,256]{2,1,0:T(8,128)(2,1)}, bf16[2,512,256]{2,1,0:T(8,128)(2,1)}, u32[]{:S(2)}, u32[]{:S(2)}) collective-permute-start(bf16[2,512,256]{2,1,0:T(8,128)(2,1)} %collective-permute-done.kv_a), channel_id=1, source_target_pairs={{0,1},{1,0},{2,3},{3,2},{4,5},{5,4},{6,7},{7,6},{8,9},{9,8},{10,11... | collective-permute-start | bytes 1572872 | tf_op jit(solution)/shard_map/ppermute | solution.py:598
  59.0 24.8 %collective-permute-start.2 = (bf16[2,512,256]{2,1,0:T(8,128)(2,1)}, bf16[2,512,256]{2,1,0:T(8,128)(2,1)}, u32[]{:S(2)}, u32[]{:S(2)}) collective-permute-start(bf16[2,512,256]{2,1,0:T(8,128)(2,1)} %collective-permute-done.1.kv_a), channel_id=1, source_target_pairs={{0,1},{1,0},{2,3},{3,2},{4,5},{5,4},{6,7},{7,6},{8,9},{9,8},{10,11... | collective-permute-start | bytes 1572872 | tf_op jit(solution)/shard_map/ppermute | solution.py:598
  67.3 39.5 %collective-permute-start.42 = (bf16[512,512]{1,0:T(8,128)(2,1)}, bf16[512,512]{1,0:T(8,128)(2,1)}, u32[]{:S(2)}, u32[]{:S(2)}) collective-permute-start(bf16[512,512]{1,0:T(8,128)(2,1)} %constant_dynamic-slice_fusion), channel_id=1, source_target_pairs={{0,1},{1,0},{2,3},{3,2},{4,5},{5,4},{6,7},{7,6},{8,9},{9,8},{10,11... | collective-permute-start | bytes 1572872 | tf_op jit(solution)/shard_map/ppermute | solution.py:598
  95.4 23.9 %collective-permute-start.5 = (bf16[2,128,2048]{2,1,0:T(8,128)(2,1)}, bf16[2,128,2048]{2,1,0:T(8,128)(2,1)}, u32[]{:S(2)}, u32[]{:S(2)}) collective-permute-start(bf16[2,128,2048]{2,1,0:T(8,128)(2,1)} %fusion.48), channel_id=1, source_target_pairs={{0,8},{8,0},{16,24},{24,16},{1,9},{9,1},{17,25},{25,17},{2,10},{10... | collective-permute-start | bytes 3145736 | tf_op jit(solution)/shard_map/ppermute | solution.py:604
  95.4 22.0 %collective-permute-start.25 = (bf16[128,2048]{1,0:T(8,128)(2,1)}, bf16[128,2048]{1,0:T(8,128)(2,1)}, u32[]{:S(2)}, u32[]{:S(2)}) collective-permute-start(bf16[128,2048]{1,0:T(8,128)(2,1)} %collective-permute-done.24), channel_id=1, source_target_pairs={{0,1},{1,0},{2,3},{3,2},{4,5},{5,4},{6,7},{7,6},{8,9},{9,8},{10,11... | collective-permute-start | bytes 1572872 | tf_op jit(solution)/shard_map/ppermute | solution.py:598
  96.9 16.5 %collective-permute-start.28 = (bf16[128,2048]{1,0:T(8,128)(2,1)}, bf16[128,2048]{1,0:T(8,128)(2,1)}, u32[]{:S(2)}, u32[]{:S(2)}) collective-permute-start(bf16[128,2048]{1,0:T(8,128)(2,1)} %collective-permute-done.24), channel_id=1, source_target_pairs={{0,2},{1,3},{2,4},{3,5},{4,6},{5,7},{6,0},{7,1},{8,10},{9,11},{10,... | collective-permute-start | bytes 1572872 | tf_op jit(solution)/shard_map/ppermute | solution.py:595
  106.7 18.4 %collective-permute-start.43 = (bf16[512,512]{1,0:T(8,128)(2,1)}, bf16[512,512]{1,0:T(8,128)(2,1)S(1)}, u32[]{:S(2)}, u32[]{:S(2)}) collective-permute-start(bf16[512,512]{1,0:T(8,128)(2,1)} %collective-permute-done.42), channel_id=1, source_target_pairs={{0,8},{8,0},{16,24},{24,16},{1,9},{9,1},{17,25},{25,17},{2,10},{10... | collective-permute-start | bytes 1572872 | tf_op jit(solution)/shard_map/ppermute | solution.py:604
  113.5 21.7 %collective-permute-start.29 = (bf16[128,2048]{1,0:T(8,128)(2,1)}, bf16[128,2048]{1,0:T(8,128)(2,1)}, u32[]{:S(2)}, u32[]{:S(2)}) collective-permute-start(bf16[128,2048]{1,0:T(8,128)(2,1)} %collective-permute-done.28), channel_id=1, source_target_pairs={{0,1},{1,0},{2,3},{3,2},{4,5},{5,4},{6,7},{7,6},{8,9},{9,8},{10,11... | collective-permute-start | bytes 1572872 | tf_op jit(solution)/shard_map/ppermute | solution.py:598
  114.0 19.6 %collective-permute-start.32 = (bf16[128,2048]{1,0:T(8,128)(2,1)}, bf16[128,2048]{1,0:T(8,128)(2,1)}, u32[]{:S(2)}, u32[]{:S(2)}) collective-permute-start(bf16[128,2048]{1,0:T(8,128)(2,1)} %collective-permute-done.28), channel_id=1, source_target_pairs={{0,2},{1,3},{2,4},{3,5},{4,6},{5,7},{6,0},{7,1},{8,10},{9,11},{10,... | collective-permute-start | bytes 1572872 | tf_op jit(solution)/shard_map/ppermute | solution.py:595
  123.6 13.5 %collective-permute-start.6 = (bf16[128,2048]{1,0:T(8,128)(2,1)}, bf16[128,2048]{1,0:T(8,128)(2,1)}, u32[]{:S(2)}, u32[]{:S(2)}) collective-permute-start(bf16[128,2048]{1,0:T(8,128)(2,1)} %fusion.101), channel_id=1, source_target_pairs={{0,16},{8,24},{16,0},{24,8},{1,17},{9,25},{17,1},{25,9},{2,18},{10... | collective-permute-start | bytes 1572872 | tf_op jit(solution)/shard_map/ppermute | solution.py:601
  133.6 15.2 %collective-permute-start.33 = (bf16[128,2048]{1,0:T(8,128)(2,1)}, bf16[128,2048]{1,0:T(8,128)(2,1)}, u32[]{:S(2)}, u32[]{:S(2)}) collective-permute-start(bf16[128,2048]{1,0:T(8,128)(2,1)} %collective-permute-done.32), channel_id=1, source_target_pairs={{0,1},{1,0},{2,3},{3,2},{4,5},{5,4},{6,7},{7,6},{8,9},{9,8},{10,11... | collective-permute-start | bytes 1572872 | tf_op jit(solution)/shard_map/ppermute | solution.py:598
  141.8 15.8 %collective-permute-start.19 = (bf16[128,2048]{1,0:T(8,128)(2,1)}, bf16[128,2048]{1,0:T(8,128)(2,1)}, u32[]{:S(2)}, u32[]{:S(2)}) collective-permute-start(bf16[128,2048]{1,0:T(8,128)(2,1)} %get-tuple-element.61), channel_id=1, source_target_pairs={{0,1},{1,0},{2,3},{3,2},{4,5},{5,4},{6,7},{7,6},{8,9},{9,8},{10,11... | collective-permute-start | bytes 1572872 | tf_op jit(solution)/shard_map/ppermute | solution.py:598
  150.7 19.4 %collective-permute-start.7 = (bf16[128,2048]{1,0:T(8,128)(2,1)}, bf16[128,2048]{1,0:T(8,128)(2,1)S(1)}, u32[]{:S(2)}, u32[]{:S(2)}) collective-permute-start(bf16[128,2048]{1,0:T(8,128)(2,1)} %get-tuple-element.61), channel_id=1, source_target_pairs={{0,2},{1,3},{2,4},{3,5},{4,6},{5,7},{6,0},{7,1},{8,10},{9,11},{10,... | collective-permute-start | bytes 1572872 | tf_op jit(solution)/shard_map/ppermute | solution.py:595
  168.5 128.8 %collective-permute-start.37 = (bf16[128,2048]{1,0:T(8,128)(2,1)S(1)}, bf16[128,2048]{1,0:T(8,128)(2,1)S(1)}, u32[]{:S(2)}, u32[]{:S(2)}) collective-permute-start(bf16[128,2048]{1,0:T(8,128)(2,1)S(1)} %slice.299), channel_id=1, source_target_pairs={{0,1},{1,0},{2,3},{3,2},{4,5},{5,4},{6,7},{7,6},{8,9},{9,8},{10,11... | collective-permute-start | bytes 1572872 | tf_op jit(solution)/shard_map/ppermute | solution.py:598
  170.1 21.2 %collective-permute-start.8 = (bf16[128,2048]{1,0:T(8,128)(2,1)S(1)}, bf16[128,2048]{1,0:T(8,128)(2,1)S(1)}, u32[]{:S(2)}, u32[]{:S(2)}) collective-permute-start(bf16[128,2048]{1,0:T(8,128)(2,1)S(1)} %collective-permute-done.7), channel_id=1, source_target_pairs={{0,1},{1,0},{2,3},{3,2},{4,5},{5,4},{6,7},{7,6},{8,9},{9,8},{10,11... | collective-permute-start | bytes 1572872 | tf_op jit(solution)/shard_map/ppermute | solution.py:598
  171.6 27.8 %collective-permute-start.11 = (bf16[128,2048]{1,0:T(8,128)(2,1)S(1)}, bf16[128,2048]{1,0:T(8,128)(2,1)S(1)}, u32[]{:S(2)}, u32[]{:S(2)}) collective-permute-start(bf16[128,2048]{1,0:T(8,128)(2,1)S(1)} %collective-permute-done.7), channel_id=1, source_target_pairs={{0,2},{1,3},{2,4},{3,5},{4,6},{5,7},{6,0},{7,1},{8,10},{9,11},{10,... | collective-permute-start | bytes 1572872 | tf_op jit(solution)/shard_map/ppermute | solution.py:595
  196.9 28.2 %collective-permute-start.9 = (bf16[128,2048]{1,0:T(8,128)(2,1)S(1)}, bf16[128,2048]{1,0:T(8,128)(2,1)S(1)}, u32[]{:S(2)}, u32[]{:S(2)}) collective-permute-start(bf16[128,2048]{1,0:T(8,128)(2,1)S(1)} %slice.306), channel_id=1, source_target_pairs={{0,1},{1,0},{2,3},{3,2},{4,5},{5,4},{6,7},{7,6},{8,9},{9,8},{10,11... | collective-permute-start | bytes 1572872 | tf_op jit(solution)/shard_map/ppermute | solution.py:598
  199.5 23.5 %collective-permute-start.12 = (bf16[128,2048]{1,0:T(8,128)(2,1)S(1)}, bf16[128,2048]{1,0:T(8,128)(2,1)S(1)}, u32[]{:S(2)}, u32[]{:S(2)}) collective-permute-start(bf16[128,2048]{1,0:T(8,128)(2,1)S(1)} %collective-permute-done.11), channel_id=1, source_target_pairs={{0,1},{1,0},{2,3},{3,2},{4,5},{5,4},{6,7},{7,6},{8,9},{9,8},{10,11... | collective-permute-start | bytes 1572872 | tf_op jit(solution)/shard_map/ppermute | solution.py:598
  201.2 33.0 %collective-permute-start.26 = (bf16[128,2048]{1,0:T(8,128)(2,1)S(1)}, bf16[128,2048]{1,0:T(8,128)(2,1)S(1)}, u32[]{:S(2)}, u32[]{:S(2)}) collective-permute-start(bf16[128,2048]{1,0:T(8,128)(2,1)S(1)} %slice.302), channel_id=1, source_target_pairs={{0,1},{1,0},{2,3},{3,2},{4,5},{5,4},{6,7},{7,6},{8,9},{9,8},{10,11... | collective-permute-start | bytes 1572872 | tf_op jit(solution)/shard_map/ppermute | solution.py:598
  202.7 35.3 %collective-permute-start.15 = (bf16[128,2048]{1,0:T(8,128)(2,1)S(1)}, bf16[128,2048]{1,0:T(8,128)(2,1)S(1)}, u32[]{:S(2)}, u32[]{:S(2)}) collective-permute-start(bf16[128,2048]{1,0:T(8,128)(2,1)S(1)} %collective-permute-done.11), channel_id=1, source_target_pairs={{0,2},{1,3},{2,4},{3,5},{4,6},{5,7},{6,0},{7,1},{8,10},{9,11},{10,... | collective-permute-start | bytes 1572872 | tf_op jit(solution)/shard_map/ppermute | solution.py:595
  225.2 33.0 %collective-permute-start.10 = (bf16[128,2048]{1,0:T(8,128)(2,1)S(1)}, bf16[128,2048]{1,0:T(8,128)(2,1)S(1)}, u32[]{:S(2)}, u32[]{:S(2)}) collective-permute-start(bf16[128,2048]{1,0:T(8,128)(2,1)S(1)} %fusion.62), channel_id=1, source_target_pairs={{0,2},{1,3},{2,4},{3,5},{4,6},{5,7},{6,0},{7,1},{8,10},{9,11},{10,... | collective-permute-start | bytes 1572872 | tf_op jit(solution)/shard_map/ppermute | solution.py:595
  231.2 27.0 %collective-permute-start.13 = (bf16[128,2048]{1,0:T(8,128)(2,1)S(1)}, bf16[128,2048]{1,0:T(8,128)(2,1)S(1)}, u32[]{:S(2)}, u32[]{:S(2)}) collective-permute-start(bf16[128,2048]{1,0:T(8,128)(2,1)S(1)} %slice.305), channel_id=1, source_target_pairs={{0,1},{1,0},{2,3},{3,2},{4,5},{5,4},{6,7},{7,6},{8,9},{9,8},{10,11... | collective-permute-start | bytes 1572872 | tf_op jit(solution)/shard_map/ppermute | solution.py:598
  234.3 35.4 %collective-permute-start.27 = (bf16[128,2048]{1,0:T(8,128)(2,1)S(1)}, bf16[128,2048]{1,0:T(8,128)(2,1)S(1)}, u32[]{:S(2)}, u32[]{:S(2)}) collective-permute-start(bf16[128,2048]{1,0:T(8,128)(2,1)S(1)} %fusion.54), channel_id=1, source_target_pairs={{0,2},{1,3},{2,4},{3,5},{4,6},{5,7},{6,0},{7,1},{8,10},{9,11},{10,... | collective-permute-start | bytes 1572872 | tf_op jit(solution)/shard_map/ppermute | solution.py:595
  238.1 16.5 %collective-permute-start.16 = (bf16[128,2048]{1,0:T(8,128)(2,1)S(1)}, bf16[128,2048]{1,0:T(8,128)(2,1)S(1)}, u32[]{:S(2)}, u32[]{:S(2)}) collective-permute-start(bf16[128,2048]{1,0:T(8,128)(2,1)S(1)} %collective-permute-done.15), channel_id=1, source_target_pairs={{0,1},{1,0},{2,3},{3,2},{4,5},{5,4},{6,7},{7,6},{8,9},{9,8},{10,11... | collective-permute-start | bytes 1572872 | tf_op jit(solution)/shard_map/ppermute | solution.py:598
  254.6 15.1 %collective-permute-start.30 = (bf16[128,2048]{1,0:T(8,128)(2,1)S(1)}, bf16[128,2048]{1,0:T(8,128)(2,1)S(1)}, u32[]{:S(2)}, u32[]{:S(2)}) collective-permute-start(bf16[128,2048]{1,0:T(8,128)(2,1)S(1)} %slice.301), channel_id=1, source_target_pairs={{0,1},{1,0},{2,3},{3,2},{4,5},{5,4},{6,7},{7,6},{8,9},{9,8},{10,11... | collective-permute-start | bytes 1572872 | tf_op jit(solution)/shard_map/ppermute | solution.py:598
  258.4 17.0 %collective-permute-start.14 = (bf16[128,2048]{1,0:T(8,128)(2,1)S(1)}, bf16[128,2048]{1,0:T(8,128)(2,1)S(1)}, u32[]{:S(2)}, u32[]{:S(2)}) collective-permute-start(bf16[128,2048]{1,0:T(8,128)(2,1)S(1)} %fusion.61), channel_id=1, source_target_pairs={{0,2},{1,3},{2,4},{3,5},{4,6},{5,7},{6,0},{7,1},{8,10},{9,11},{10,... | collective-permute-start | bytes 1572872 | tf_op jit(solution)/shard_map/ppermute | solution.py:595
  263.8 14.9 %collective-permute-start.17 = (bf16[128,2048]{1,0:T(8,128)(2,1)S(1)}, bf16[128,2048]{1,0:T(8,128)(2,1)S(1)}, u32[]{:S(2)}, u32[]{:S(2)}) collective-permute-start(bf16[128,2048]{1,0:T(8,128)(2,1)S(1)} %slice.304), channel_id=1, source_target_pairs={{0,1},{1,0},{2,3},{3,2},{4,5},{5,4},{6,7},{7,6},{8,9},{9,8},{10,11... | collective-permute-start | bytes 1572872 | tf_op jit(solution)/shard_map/ppermute | solution.py:598
  269.9 11.0 %collective-permute-start.31 = (bf16[128,2048]{1,0:T(8,128)(2,1)S(1)}, bf16[128,2048]{1,0:T(8,128)(2,1)S(1)}, u32[]{:S(2)}, u32[]{:S(2)}) collective-permute-start(bf16[128,2048]{1,0:T(8,128)(2,1)S(1)} %fusion.53), channel_id=1, source_target_pairs={{0,2},{1,3},{2,4},{3,5},{4,6},{5,7},{6,0},{7,1},{8,10},{9,11},{10,... | collective-permute-start | bytes 1572872 | tf_op jit(solution)/shard_map/ppermute | solution.py:595
  273.0 17.0 %collective-permute-start.34 = (bf16[128,2048]{1,0:T(8,128)(2,1)S(1)}, bf16[128,2048]{1,0:T(8,128)(2,1)S(1)}, u32[]{:S(2)}, u32[]{:S(2)}) collective-permute-start(bf16[128,2048]{1,0:T(8,128)(2,1)S(1)} %slice.300), channel_id=1, source_target_pairs={{0,1},{1,0},{2,3},{3,2},{4,5},{5,4},{6,7},{7,6},{8,9},{9,8},{10,11... | collective-permute-start | bytes 1572872 | tf_op jit(solution)/shard_map/ppermute | solution.py:598
  275.4 31.8 %collective-permute-start.20 = (bf16[128,2048]{1,0:T(8,128)(2,1)S(1)}, bf16[128,2048]{1,0:T(8,128)(2,1)S(1)}, u32[]{:S(2)}, u32[]{:S(2)}) collective-permute-start(bf16[128,2048]{1,0:T(8,128)(2,1)S(1)} %slice.303), channel_id=1, source_target_pairs={{0,1},{1,0},{2,3},{3,2},{4,5},{5,4},{6,7},{7,6},{8,9},{9,8},{10,11... | collective-permute-start | bytes 1572872 | tf_op jit(solution)/shard_map/ppermute | solution.py:598
  278.7 56.1 %collective-permute-start.58 = (bf16[384,2048]{1,0:T(8,128)(2,1)S(1)}, bf16[384,2048]{1,0:T(8,128)(2,1)S(1)}, u32[]{:S(2)}, u32[]{:S(2)}) collective-permute-start(bf16[384,2048]{1,0:T(8,128)(2,1)S(1)} %dynamic-slice_convert_fusion), channel_id=1, source_target_pairs={{0,8},{8,0},{16,24},{24,16},{1,9},{9,1},{17,25},{25,17},{2,10},{10... | collective-permute-start | bytes 4718600 | tf_op jit(solution)/shard_map/ppermute | solution.py:604
  281.0 26.3 %collective-permute-start.18 = (bf16[128,2048]{1,0:T(8,128)(2,1)S(1)}, bf16[128,2048]{1,0:T(8,128)(2,1)S(1)}, u32[]{:S(2)}, u32[]{:S(2)}) collective-permute-start(bf16[128,2048]{1,0:T(8,128)(2,1)S(1)} %fusion.59), channel_id=1, source_target_pairs={{0,2},{1,3},{2,4},{3,5},{4,6},{5,7},{6,0},{7,1},{8,10},{9,11},{10,... | collective-permute-start | bytes 1572872 | tf_op jit(solution)/shard_map/ppermute | solution.py:595
  290.1 16.7 %collective-permute-start.35 = (bf16[128,2048]{1,0:T(8,128)(2,1)S(1)}, bf16[128,2048]{1,0:T(8,128)(2,1)S(1)}, u32[]{:S(2)}, u32[]{:S(2)}) collective-permute-start(bf16[128,2048]{1,0:T(8,128)(2,1)S(1)} %fusion.51), channel_id=1, source_target_pairs={{0,2},{1,3},{2,4},{3,5},{4,6},{5,7},{6,0},{7,1},{8,10},{9,11},{10,... | collective-permute-start | bytes 1572872 | tf_op jit(solution)/shard_map/ppermute | solution.py:595
  310.1 14.8 %collective-permute-start.38 = (bf16[128,2048]{1,0:T(8,128)(2,1)S(1)}, bf16[128,2048]{1,0:T(8,128)(2,1)S(1)}, u32[]{:S(2)}, u32[]{:S(2)}) collective-permute-start(bf16[128,2048]{1,0:T(8,128)(2,1)S(1)} %get-tuple-element.66), channel_id=1, source_target_pairs={{0,16},{8,24},{16,0},{24,8},{1,17},{9,25},{17,1},{25,9},{2,18},{10... | collective-permute-start | bytes 1572872 | tf_op jit(solution)/shard_map/ppermute | solution.py:601
  314.2 19.1 %collective-permute-start.21 = (bf16[128,2048]{1,0:T(8,128)(2,1)S(1)}, bf16[128,2048]{1,0:T(8,128)(2,1)S(1)}, u32[]{:S(2)}, u32[]{:S(2)}) collective-permute-start(bf16[128,2048]{1,0:T(8,128)(2,1)S(1)} %get-tuple-element.100), channel_id=1, source_target_pairs={{0,16},{8,24},{16,0},{24,8},{1,17},{9,25},{17,1},{25,9},{2,18},{10... | collective-permute-start | bytes 1572872 | tf_op jit(solution)/shard_map/ppermute | solution.py:601
  315.9 21.1 %collective-permute-start.55 = (bf16[1024,768]{1,0:T(8,128)(2,1)S(1)}, bf16[1024,768]{1,0:T(8,128)(2,1)S(1)}, u32[]{:S(2)}, u32[]{:S(2)}) collective-permute-start(bf16[1024,768]{1,0:T(8,128)(2,1)S(1)} %dynamic-slice_convert_fusion.1), channel_id=1, source_target_pairs={{0,8},{8,0},{16,24},{24,16},{1,9},{9,1},{17,25},{25,17},{2,10},{10... | collective-permute-start | bytes 4718600 | tf_op jit(solution)/shard_map/ppermute | solution.py:604
  316.1 23.8 %collective-permute-start.52 = (bf16[1024,768]{1,0:T(8,128)(2,1)S(1)}, bf16[1024,768]{1,0:T(8,128)(2,1)S(1)}, u32[]{:S(2)}, u32[]{:S(2)}) collective-permute-start(bf16[1024,768]{1,0:T(8,128)(2,1)S(1)} %dynamic-slice_convert_fusion.2), channel_id=1, source_target_pairs={{0,8},{8,0},{16,24},{24,16},{1,9},{9,1},{17,25},{25,17},{2,10},{10... | collective-permute-start | bytes 4718600 | tf_op jit(solution)/shard_map/ppermute | solution.py:604
  325.0 16.5 %collective-permute-start.39 = (bf16[2,128,2048]{2,1,0:T(8,128)(2,1)S(1)}, bf16[2,128,2048]{2,1,0:T(8,128)(2,1)S(1)}, u32[]{:S(2)}, u32[]{:S(2)}) collective-permute-start(bf16[2,128,2048]{2,1,0:T(8,128)(2,1)S(1)} %maximum_select_fusion.7), channel_id=1, source_target_pairs={{0,8},{8,0},{16,24},{24,16},{1,9},{9,1},{17,25},{25,17},{2,10},{10... | collective-permute-start | bytes 3145736 | tf_op jit(solution)/shard_map/ppermute | solution.py:604
  334.4 47.3 %collective-permute-start.22 = (bf16[2,128,2048]{2,1,0:T(8,128)(2,1)}, bf16[2,128,2048]{2,1,0:T(8,128)(2,1)}, u32[]{:S(2)}, u32[]{:S(2)}) collective-permute-start(bf16[2,128,2048]{2,1,0:T(8,128)(2,1)} %maximum_select_fusion.5), channel_id=1, source_target_pairs={{0,8},{8,0},{16,24},{24,16},{1,9},{9,1},{17,25},{25,17},{2,10},{10... | collective-permute-start | bytes 3145736 | tf_op jit(solution)/shard_map/ppermute | solution.py:604
  336.4 77.4 %collective-permute-start.59 = (bf16[384,2048]{1,0:T(8,128)(2,1)}, bf16[384,2048]{1,0:T(8,128)(2,1)}, u32[]{:S(2)}, u32[]{:S(2)}) collective-permute-start(bf16[384,2048]{1,0:T(8,128)(2,1)} %add_convert_fusion.1), channel_id=1, source_target_pairs={{0,16},{8,24},{16,0},{24,8},{1,17},{9,25},{17,1},{25,9},{2,18},{10... | collective-permute-start | bytes 4718600 | tf_op jit(solution)/shard_map/ppermute | solution.py:601
  338.4 70.2 %collective-permute-start.56 = (bf16[1024,768]{1,0:T(8,128)(2,1)}, bf16[1024,768]{1,0:T(8,128)(2,1)}, u32[]{:S(2)}, u32[]{:S(2)}) collective-permute-start(bf16[1024,768]{1,0:T(8,128)(2,1)} %add_convert_fusion.3), channel_id=1, source_target_pairs={{0,16},{8,24},{16,0},{24,8},{1,17},{9,25},{17,1},{25,9},{2,18},{10... | collective-permute-start | bytes 4718600 | tf_op jit(solution)/shard_map/ppermute | solution.py:601
  351.7 55.4 %collective-permute-start.48 = (bf16[2,512,256]{2,1,0:T(8,128)(2,1)}, bf16[2,512,256]{2,1,0:T(8,128)(2,1)}, u32[]{:S(2)}, u32[]{:S(2)}) collective-permute-start(bf16[2,512,256]{2,1,0:T(8,128)(2,1)} %get-tuple-element.49), channel_id=1, source_target_pairs={{0,1},{1,0},{2,3},{3,2},{4,5},{5,4},{6,7},{7,6},{8,9},{9,8},{10,11... | collective-permute-start | bytes 1572872 | tf_op jit(solution)/shard_map/ppermute | solution.py:598
  373.7 30.5 %collective-permute-start.45 = (bf16[512,512]{0,1:T(8,128)(2,1)S(1)}, bf16[512,512]{0,1:T(8,128)(2,1)S(1)}, u32[]{:S(2)}, u32[]{:S(2)}) collective-permute-start(bf16[512,512]{0,1:T(8,128)(2,1)S(1)} %get-tuple-element.77), channel_id=1, source_target_pairs={{0,1},{1,0},{2,3},{3,2},{4,5},{5,4},{6,7},{7,6},{8,9},{9,8},{10,11... | collective-permute-start | bytes 1572872 | tf_op jit(solution)/shard_map/ppermute | solution.py:598
  381.7 18.6 %collective-permute-start.44 = (bf16[512,512]{1,0:T(8,128)(2,1)S(1)}, bf16[512,512]{1,0:T(8,128)(2,1)S(1)}, u32[]{:S(2)}, u32[]{:S(2)}) collective-permute-start(bf16[512,512]{1,0:T(8,128)(2,1)S(1)} %copy-done.27), channel_id=1, source_target_pairs={{0,1},{1,0},{2,3},{3,2},{4,5},{5,4},{6,7},{7,6},{8,9},{9,8},{10,11... | collective-permute-start | bytes 1572872 | tf_op jit(solution)/shard_map/ppermute | solution.py:598
  383.7 18.3 %copy-start.40 = (bf16[512,1024]{1,0:T(8,128)(2,1)S(1)}, bf16[512,1024]{1,0:T(8,128)(2,1)}, u32[]{:S(2)}) copy-start(bf16[512,1024]{1,0:T(8,128)(2,1)} %constant_dynamic-slice_fusion.1) | copy-start | bytes 3145732
  400.2 44.1 %collective-permute-start.23 = (bf16[512,512]{1,0:T(8,128)(2,1)S(1)}, bf16[512,512]{1,0:T(8,128)(2,1)S(1)}, u32[]{:S(2)}, u32[]{:S(2)}) collective-permute-start(bf16[512,512]{1,0:T(8,128)(2,1)S(1)} %copy-done.39), channel_id=1, source_target_pairs={{0,1},{1,0},{2,3},{3,2},{4,5},{5,4},{6,7},{7,6},{8,9},{9,8},{10,11... | collective-permute-start | bytes 1572872 | tf_op jit(solution)/shard_map/ppermute | solution.py:598
  404.3 36.6 %collective-permute-start.53 = (bf16[1024,768]{1,0:T(8,128)(2,1)S(1)}, bf16[1024,768]{1,0:T(8,128)(2,1)S(1)}, u32[]{:S(2)}, u32[]{:S(2)}) collective-permute-start(bf16[1024,768]{1,0:T(8,128)(2,1)S(1)} %copy-done.17), channel_id=1, source_target_pairs={{0,16},{8,24},{16,0},{24,8},{1,17},{9,25},{17,1},{25,9},{2,18},{10... | collective-permute-start | bytes 4718600 | tf_op jit(solution)/shard_map/ppermute | solution.py:601
  407.1 19.1 %collective-permute-start.47 = (bf16[2,512,256]{2,1,0:T(8,128)(2,1)S(1)}, bf16[2,512,256]{2,1,0:T(8,128)(2,1)S(1)}, u32[]{:S(2)}, u32[]{:S(2)}) collective-permute-start(bf16[2,512,256]{2,1,0:T(8,128)(2,1)S(1)} %copy-done.57), channel_id=1, source_target_pairs={{0,1},{1,0},{2,3},{3,2},{4,5},{5,4},{6,7},{7,6},{8,9},{9,8},{10,11... | collective-permute-start | bytes 1572872 | tf_op jit(solution)/shard_map/ppermute | solution.py:598
  408.6 28.9 %collective-permute-start.40 = (bf16[512,512]{1,0:T(8,128)(2,1)S(1)}, bf16[512,512]{1,0:T(8,128)(2,1)S(1)}, u32[]{:S(2)}, u32[]{:S(2)}) collective-permute-start(bf16[512,512]{1,0:T(8,128)(2,1)S(1)} %constant_dynamic-slice_fusion.2), channel_id=1, source_target_pairs={{0,1},{1,0},{2,3},{3,2},{4,5},{5,4},{6,7},{7,6},{8,9},{9,8},{10,11... | collective-permute-start | bytes 1572872 | tf_op jit(solution)/shard_map/ppermute | solution.py:598
  413.8 24.2 %copy-start.50 = (bf16[2,512,256]{2,1,0:T(8,128)(2,1)S(1)}, bf16[2,512,256]{2,1,0:T(8,128)(2,1)}, u32[]{:S(2)}) copy-start(bf16[2,512,256]{2,1,0:T(8,128)(2,1)} %get-tuple-element.46) | copy-start | bytes 1572868
  413.8 23.7 %collective-permute-start.49 = (bf16[2,512,256]{2,1,0:T(8,128)(2,1)S(1)}, bf16[2,512,256]{2,1,0:T(8,128)(2,1)S(1)}, u32[]{:S(2)}, u32[]{:S(2)}) collective-permute-start(bf16[2,512,256]{2,1,0:T(8,128)(2,1)S(1)} %add_convert_fusion.7), channel_id=1, source_target_pairs={{4,2},{5,3},{6,4},{7,5},{12,10},{13,11},{14,12},{15,13},{20,18},{2... | collective-permute-start | bytes 1572872 | tf_op jit(solution)/shard_map/ppermute | solution.py:813
  426.3 20.9 %collective-permute-start.46 = (bf16[2,512,256]{2,1,0:T(8,128)(2,1)S(1)}, bf16[2,512,256]{2,1,0:T(8,128)(2,1)S(1)}, u32[]{:S(2)}, u32[]{:S(2)}) collective-permute-start(bf16[2,512,256]{2,1,0:T(8,128)(2,1)S(1)} %copy-done.56), channel_id=1, source_target_pairs={{0,1},{1,0},{2,3},{3,2},{4,5},{5,4},{6,7},{7,6},{8,9},{9,8},{10,11... | collective-permute-start | bytes 1572872 | tf_op jit(solution)/shard_map/ppermute | solution.py:598
  437.5 6.5 collective-permute-start.41
  437.5 196.4 %collective-permute-start.60 = (bf16[384,2048]{1,0:T(8,128)(2,1)}, bf16[384,2048]{1,0:T(8,128)(2,1)}, u32[]{:S(2)}, u32[]{:S(2)}) collective-permute-start(bf16[384,2048]{1,0:T(8,128)(2,1)} %add_convert_fusion), channel_id=1, source_target_pairs={{0,8},{8,0},{16,24},{24,16},{1,9},{9,1},{17,25},{25,17},{2,10},{10... | collective-permute-start | bytes 4718600 | tf_op jit(solution)/shard_map/ppermute | solution.py:604
  440.8 19.8 %collective-permute-start.50 = (bf16[2,512,256]{2,1,0:T(8,128)(2,1)S(1)}, bf16[2,512,256]{2,1,0:T(8,128)(2,1)S(1)}, u32[]{:S(2)}, u32[]{:S(2)}) collective-permute-start(bf16[2,512,256]{2,1,0:T(8,128)(2,1)S(1)} %add_convert_fusion.6), channel_id=1, source_target_pairs={{2,0},{3,1},{4,2},{5,3},{6,4},{7,5},{10,8},{11,9},{12,10},{13,11},... | collective-permute-start | bytes 1572872 | tf_op jit(solution)/shard_map/ppermute | solution.py:813
  444.0 200.6 %collective-permute-start.57 = (bf16[1024,768]{1,0:T(8,128)(2,1)}, bf16[1024,768]{1,0:T(8,128)(2,1)}, u32[]{:S(2)}, u32[]{:S(2)}) collective-permute-start(bf16[1024,768]{1,0:T(8,128)(2,1)} %add_convert_fusion.2), channel_id=1, source_target_pairs={{0,8},{8,0},{16,24},{24,16},{1,9},{9,1},{17,25},{25,17},{2,10},{10... | collective-permute-start | bytes 4718600 | tf_op jit(solution)/shard_map/ppermute | solution.py:604
  444.3 210.8 %collective-permute-start.54 = (bf16[1024,768]{1,0:T(8,128)(2,1)}, bf16[1024,768]{1,0:T(8,128)(2,1)}, u32[]{:S(2)}, u32[]{:S(2)}) collective-permute-start(bf16[1024,768]{1,0:T(8,128)(2,1)} %add_convert_fusion.4), channel_id=1, source_target_pairs={{0,8},{8,0},{16,24},{24,16},{1,9},{9,1},{17,25},{25,17},{2,10},{10... | collective-permute-start | bytes 4718600 | tf_op jit(solution)/shard_map/ppermute | solution.py:604
  468.2 13.2 %collective-permute-start.51 = (bf16[512,512]{1,0:T(8,128)(2,1)S(1)}, bf16[512,512]{1,0:T(8,128)(2,1)S(1)}, u32[]{:S(2)}, u32[]{:S(2)}) collective-permute-start(bf16[512,512]{1,0:T(8,128)(2,1)S(1)} %pad_maximum_fusion.11), channel_id=1, source_target_pairs={{0,1},{1,0},{2,3},{3,2},{4,5},{5,4},{6,7},{7,6},{8,9},{9,8},{10,11... | collective-permute-start | bytes 1572872 | tf_op jit(solution)/shard_map/ppermute | solution.py:598
  (55 other events, 310.1 us)

commit v3 on v2

--- a/solution.py
+++ b/solution.py
@@ -249,6 +249,382 @@
     )(info, *operands)
 
 
+def middle_kernel(outer, *refs):
+    MESH = pl.DeviceIdType.MESH
+    blocks = 2 * outer
+    (gated, out_proj, hidden_ref, gain_ref, gate_in, up_in, down_in) = refs[:7]
+    ups_in = refs[7 : 7 + blocks]
+    (middle_out, grad_out, gain_out, branch, inner_out, dw_gate, dw_up, dw_down) = refs[
+        7 + blocks : 15 + blocks
+    ]
+    (
+        w_gate, w_up, w_down, ups, rows, grad_inner, inner, grad_gate, grad_up,
+        near_stage, near_got, far_stage, far_got, far_keep, own_keep,
+        keep, y_stage, y_got, z_stage, z_got,
+        load_sem, store_sem, tp_send, tp_recv, zs, zr, ys, yr, rys, ryr, rzs, rzr,
+    ) = refs[15 + blocks :]
+    stage_gate, stage_up, stage_down = w_gate, w_up, w_down
+    quarter, model = hidden_ref.shape
+    group = 2 * quarter
+    chunk = model // outer
+    last = outer - 1
+
+    sp_i = lax.axis_index("sp")
+    tp_i = lax.axis_index("tp")
+    line = sp_i // 2
+    half = sp_i % 2
+    side = tp_i // 2
+    core = tp_i % 2
+
+    def sp_at(z, y):
+        return (tp_i, z * 2 + y)
+
+    pair_dev = sp_at(line, 1 - half)
+    core_dev = (side * 2 + (1 - core), sp_i)
+    side_dev = ((1 - side) * 2 + core, sp_i)
+    nexts = (sp_at(jnp.minimum(line + 1, last), half), sp_at(jnp.maximum(line - 1, 0), half))
+
+    loads = [
+        pltpu.make_async_copy(src, dst, load_sem.at[index])
+        for index, (src, dst) in enumerate(
+            [(down_in, w_down)]
+            + [(ups_in[b], ups.at[pl.ds(b * quarter, quarter), :]) for b in range(blocks)]
+            + [(gate_in, w_gate), (up_in, w_up)]
+        )
+    ]
+    for load in loads:
+        load.start()
+
+    barrier = pltpu.get_barrier_semaphore()
+    greeted = [
+        sp_at((line + 1) % outer, half), sp_at((line + outer - 1) % outer, half),
+        pair_dev, core_dev, side_dev,
+    ]
+    for device in greeted:
+        pl.semaphore_signal(barrier, inc=1, device_id=device, device_id_type=MESH)
+    pl.semaphore_wait(barrier, len(greeted))
+
+    def remote(src, dst, send, recv, device):
+        return pltpu.make_async_remote_copy(
+            src_ref=src, dst_ref=dst, send_sem=send, recv_sem=recv,
+            device_id=device, device_id_type=MESH,
+        )
+
+    def aligned(index, count):
+        return pl.ds(pl.multiple_of(index * count, count), count)
+
+    def near_copy(j):
+        return remote(near_stage.at[j], near_got.at[j], tp_send.at[j], tp_recv.at[j], core_dev)
+
+    def far_copy():
+        return remote(far_stage, far_got, tp_send.at[2], tp_recv.at[2], side_dev)
+
+    def projected(s, c):
+        return matmul(gated[aligned(s * 2 + c, quarter), :], out_proj[...])
+
+    near_stage[0] = projected(1 - side, 1 - core).astype(BF16)
+    near_copy(0).start()
+    near_stage[1] = projected(side, 1 - core).astype(BF16)
+    near_copy(1).start()
+    far_keep[...] = projected(1 - side, core)
+    near_copy(0).wait_recv()
+    far_stage[...] = (far_keep[...] + near_got[0].astype(F32)).astype(BF16)
+    far_copy().start()
+    own_keep[...] = projected(side, core)
+
+    for load in loads[: 1 + blocks]:
+        load.wait()
+
+    def grad_inner_of(k, carry):
+        at = aligned(k, group)
+        grad_inner[at, :] = times_transpose(ups[at, :], w_down[...])
+        return carry
+
+    lax.fori_loop(0, outer, grad_inner_of, 0)
+    near_copy(1).wait_recv()
+    far_copy().wait_recv()
+    middle = hidden_ref[...].astype(F32) + (
+        own_keep[...] + near_got[1].astype(F32) + far_got[...].astype(F32)
+    )
+    middle_out[...] = middle
+    rows[0:quarter, :] = (middle * norm_scales(middle) * gain_ref[...]).astype(BF16)
+
+    def entry(k, j):
+        return pl.ds(pl.multiple_of((k * 2 + j) * quarter, quarter), quarter)
+
+    def wrap(k):
+        return (k + outer) % outer
+
+    def z_copy(way, k):
+        to = wrap(k + 1 - 2 * way)
+        return remote(
+            rows.at[entry(k, 0), :], rows.at[entry(to, 0), :], zs.at[way, k], zr.at[to], nexts[way]
+        )
+
+    def z_arrived(k):
+        return remote(
+            rows.at[entry(k, 0), :], rows.at[entry(k, 0), :], zs.at[0, k], zr.at[k], nexts[0]
+        )
+
+    def y_copy(k):
+        return remote(
+            rows.at[entry(k, 0), :], rows.at[entry(k, 1), :], ys.at[k], yr.at[k], pair_dev
+        )
+
+    short = jnp.minimum(line, last - line)
+
+    def delta_of(i):
+        near = jnp.where(i % 2 == 1, -((i + 1) // 2), (i + 1) // 2)
+        far = jnp.where(line < last - line, i - short, short - i)
+        return jnp.where(i <= 2 * short, near, far)
+
+    def slot_of(delta):
+        return jnp.where(delta <= 0, -delta, outer - delta)
+
+    for way, exists in ((0, line < last), (1, line > 0)):
+        pl.when(exists)(z_copy(way, 0).start)
+    y_copy(0).start()
+
+    def goes_on(delta):
+        return ((delta < 0) & (line < last), (delta > 0) & (line > 0))
+
+    def forward(i):
+        delta = delta_of(i)
+        k = slot_of(delta)
+        z_arrived(k).wait_recv()
+        for way, exists in enumerate(goes_on(delta)):
+            pl.when(exists)(z_copy(way, k).start)
+        y_copy(k).start()
+
+    for load in loads[1 + blocks :]:
+        load.wait()
+    forward(1)
+
+    def turn_forward(i, carry):
+        @pl.when(i + 2 < outer)
+        def _():
+            forward(i + 2)
+
+        k = slot_of(delta_of(i))
+        y_copy(k).wait_recv()
+        at = aligned(k, group)
+        rows_k = rows[at, :]
+        gate_vals = matmul(rows_k, w_gate[...])
+        up_vals = matmul(rows_k, w_up[...])
+        incoming = grad_inner[at, :]
+        sig = jax.nn.sigmoid(gate_vals)
+        silu = gate_vals * sig
+        grad_gate[at, :] = (incoming * up_vals * (sig * (1.0 + gate_vals * (1.0 - sig)))).astype(BF16)
+        grad_up[at, :] = (incoming * silu).astype(BF16)
+        inner[at, :] = (silu * up_vals).astype(BF16)
+        return carry
+
+    lax.fori_loop(0, outer, turn_forward, 0)
+    inner_store = pltpu.make_async_copy(inner, inner_out, store_sem.at[0])
+    inner_store.start()
+
+    def y_sum(k):
+        at = aligned(k, quarter)
+        return remote(y_stage.at[at, :], y_got.at[at, :], rys.at[k], ryr.at[k], pair_dev)
+
+    def turn_parts(step, carry):
+        k = slot_of(delta_of(last - step))
+        at = aligned(k, group)
+        part = times_transpose(grad_gate[at, :], w_gate[...]) + times_transpose(
+            grad_up[at, :], w_up[...]
+        )
+        y_stage[aligned(k, quarter), :] = part[quarter:].astype(BF16)
+        y_sum(k).start()
+        keep[aligned(k, quarter), :] = part[:quarter]
+        return carry
+
+    lax.fori_loop(0, outer, turn_parts, 0)
+
+    def z_sum(way, k):
+        to = wrap(k + 1 - 2 * way)
+        return remote(
+            z_stage.at[aligned(k, quarter), :],
+            z_got.at[pl.ds(pl.multiple_of((way * outer + to) * quarter, quarter), quarter), :],
+            rzs.at[k], rzr.at[way, to], nexts[way],
+        )
+
+    def z_got_at(way, k):
+        return z_got[pl.ds(pl.multiple_of((way * outer + k) * quarter, quarter), quarter), :]
+
+    def z_sum_arrived(way, k):
+        return remote(
+            z_stage.at[aligned(k, quarter), :], z_stage.at[aligned(k, quarter), :],
+            rzs.at[k], rzr.at[way, k], nexts[way],
+        )
+
+    def gate_up_stores(c):
+        at = aligned(c, chunk)
+        return (
+            pltpu.make_async_copy(stage_gate.at[at, :], dw_gate.at[at, :], store_sem.at[1 + 2 * c]),
+            pltpu.make_async_copy(stage_up.at[at, :], dw_up.at[at, :], store_sem.at[2 + 2 * c]),
+        )
+
+    def weight_chunk(c):
+        at = aligned(c, chunk)
+        some = rows[:, at]
+        stage_gate[at, :] = outer_sum(some, grad_gate[...]).astype(BF16)
+        stage_up[at, :] = outer_sum(some, grad_up[...]).astype(BF16)
+        for store in gate_up_stores(c):
+            store.start()
+
+    def turn_sums(step, carry):
+        weight_chunk(step)
+        delta = delta_of(last - step)
+        k = slot_of(delta)
+        at = aligned(k, quarter)
+        y_sum(k).wait_recv()
+        own = keep[at, :] + y_got[at, :].astype(F32)
+        for way, (here, before) in enumerate(
+            ((delta > 0, line > 0), (delta < 0, line < last))
+        ):
+
+            @pl.when(here & before)
+            def _():
+                z_sum_arrived(way, k).wait_recv()
+                z_stage[at, :] = (own + z_got_at(way, k).astype(F32)).astype(BF16)
+
+            @pl.when(here & jnp.logical_not(before))
+            def _():
+                z_stage[at, :] = own.astype(BF16)
+
+            pl.when(here)(z_sum(way, k).start)
+        return carry
+
+    lax.fori_loop(0, last, turn_sums, 0)
+    weight_chunk(last)
+    y_sum(0).wait_recv()
+    for way, exists in ((0, line > 0), (1, line < last)):
+        pl.when(exists)(z_sum_arrived(way, 0).wait_recv)
+    below = jnp.where(line > 0, z_got_at(0, 0).astype(F32), 0.0)
+    above = jnp.where(line < last, z_got_at(1, 0).astype(F32), 0.0)
+    grad_two = keep[0:quarter, :] + y_got[0:quarter, :].astype(F32) + below + above
+
+    values = middle_out[...]
+    back, gain_terms = norm_back(values, norm_scales(values), gain_ref[...], grad_two)
+    grads = ups[0:quarter, :].astype(F32) + back
+    branch[side, core] = grads.astype(BF16)
+
+    def spread_copy(slot, s, device):
+        block = branch.at[s, core]
+        return remote(block, block, tp_send.at[3 + slot], tp_recv.at[3 + slot], device)
+
+    spread_copy(0, side, side_dev).start()
+    spread_copy(1, side, core_dev).start()
+    grad_out[...] = grads
+    gain_out[...] = jnp.sum(gain_terms, axis=0, keepdims=True)
+
+    def down_store(c):
+        at = aligned(c, chunk)
+        return pltpu.make_async_copy(
+            stage_down.at[:, at], dw_down.at[:, at], store_sem.at[1 + 2 * outer + c]
+        )
+
+    def turn_down(c, carry):
+        at = aligned(c, chunk)
+        stage_down[:, at] = outer_sum(inner[...], ups[:, at]).astype(BF16)
+        down_store(c).start()
+        return carry
+
+    lax.fori_loop(0, outer, turn_down, 0)
+    spread_copy(0, side, side_dev).wait_recv()
+    spread_copy(2, 1 - side, core_dev).start()
+    spread_copy(1, side, core_dev).wait_recv()
+
+    inner_store.wait()
+    near_copy(0).wait_send()
+    near_copy(1).wait_send()
+    far_copy().wait_send()
+    for way, exists in ((0, line < last), (1, line > 0)):
+        pl.when(exists)(z_copy(way, 0).wait_send)
+
+    def turn_drain(i, carry):
+        delta = delta_of(i)
+        k = slot_of(delta)
+        y_copy(k).wait_send()
+        y_sum(k).wait_send()
+        for store in gate_up_stores(i):
+            store.wait()
+        down_store(i).wait()
+        for way, exists in enumerate(goes_on(delta)):
+            pl.when(exists)(z_copy(way, k).wait_send)
+        pl.when(delta != 0)(z_sum(0, k).wait_send)
+        return carry
+
+    lax.fori_loop(0, outer, turn_drain, 0)
+    spread_copy(0, side, side_dev).wait_send()
+    spread_copy(1, side, core_dev).wait_send()
+    spread_copy(2, 1 - side, core_dev).wait()
+
+
+def middle_layer(gated, out_proj, hidden, gain, w_gate, w_up, w_down, ups, outer, sides):
+    quarter, model = hidden.shape
+    units = w_down.shape[0]
+    rows_n = 2 * outer * quarter
+    vmem = pl.BlockSpec(memory_space=pltpu.VMEM)
+    anywhere = pl.BlockSpec(memory_space=pl.ANY)
+    dma = pltpu.SemaphoreType.DMA
+    line_rows = outer * quarter
+    return pl.pallas_call(
+        functools.partial(middle_kernel, outer),
+        out_shape=[
+            jax.ShapeDtypeStruct((quarter, model), F32),
+            jax.ShapeDtypeStruct((quarter, model), F32),
+            jax.ShapeDtypeStruct((1, model), F32),
+            jax.ShapeDtypeStruct((sides, 2, quarter, model), BF16),
+            jax.ShapeDtypeStruct((rows_n, units), BF16),
+            jax.ShapeDtypeStruct((model, units), BF16),
+            jax.ShapeDtypeStruct((model, units), BF16),
+            jax.ShapeDtypeStruct((units, model), BF16),
+        ],
+        in_specs=[vmem] * 4 + [anywhere] * (3 + len(ups)),
+        out_specs=[vmem] * 4 + [anywhere] * 4,
+        scratch_shapes=[
+            pltpu.VMEM((model, units), BF16),
+            pltpu.VMEM((model, units), BF16),
+            pltpu.VMEM((units, model), BF16),
+            pltpu.VMEM((rows_n, model), BF16),
+            pltpu.VMEM((rows_n, model), BF16),
+            pltpu.VMEM((rows_n, units), F32),
+            pltpu.VMEM((rows_n, units), BF16),
+            pltpu.VMEM((rows_n, units), BF16),
+            pltpu.VMEM((rows_n, units), BF16),
+            pltpu.VMEM((2, quarter, model), BF16),
+            pltpu.VMEM((2, quarter, model), BF16),
+            pltpu.VMEM((quarter, model), BF16),
+            pltpu.VMEM((quarter, model), BF16),
+            pltpu.VMEM((quarter, model), F32),
+            pltpu.VMEM((quarter, model), F32),
+            pltpu.VMEM((line_rows, model), F32),
+            pltpu.VMEM((line_rows, model), BF16),
+            pltpu.VMEM((line_rows, model), BF16),
+            pltpu.VMEM((line_rows, model), BF16),
+            pltpu.VMEM((2 * line_rows, model), BF16),
+            dma((3 + len(ups),)),
+            dma((1 + 3 * outer,)),
+            dma((6,)),
+            dma((6,)),
+            dma((2, outer)),
+            dma((outer,)),
+            dma((outer,)),
+            dma((outer,)),
+            dma((outer,)),
+            dma((outer,)),
+            dma((outer,)),
+            dma((2, outer)),
+        ],
+        compiler_params=pltpu.CompilerParams(
+            collective_id=2, has_side_effects=True, vmem_limit_bytes=58 * 1024 * 1024
+        ),
+        cost_estimate=pl.CostEstimate(flops=3 * 10**10, bytes_accessed=4 * 10**7, transcendentals=0),
+        name="middle",
+    )(gated, out_proj, hidden, gain, w_gate, w_up, w_down, *ups)
+
+
 def finish_kernel(
     outer, sides, sp_n, tp_n, streams, width_scale,
     *refs,
@@ -726,51 +1102,66 @@
         )
         return full.reshape((rows_dev,) + block.shape[1:])
 
-    attn_quarter = scatter_tp(matmul(gated, output_proj))
-    hidden_quarter = lax.dynamic_slice_in_dim(hidden, quarter_first, quarter).astype(F32)
-    middle = hidden_quarter + attn_quarter
-    normed_two_full, ffn_scales = norm_rows(middle, ffn_norm)
-    normed_two = normed_two_full.astype(BF16)
-
-    two_blocks = gather_sp(normed_two)
-    rows_list, up_list, inner_list, gate_list, grad_up_list = [None] * outer, [None] * outer, [None] * outer, [None] * outer, [None] * outer
-    grad_parts = [None] * outer
-    for k in list(range(1, outer)) + [0]:
-        rows_k = jnp.concatenate(two_blocks[k])
-        up_k = jnp.concatenate(up_blocks[k])
-        gate_vals = matmul(rows_k, ffn_gate)
-        up_vals = matmul(rows_k, ffn_up)
-        sig = jax.nn.sigmoid(gate_vals)
-        grad_inner = times_transpose(up_k, ffn_down)
-        grad_gate = (grad_inner * up_vals * (sig * (1.0 + gate_vals * (1.0 - sig)))).astype(BF16)
-        grad_up = (grad_inner * (gate_vals * sig)).astype(BF16)
-        inner = (gate_vals * sig * up_vals).astype(BF16)
-        grad_parts[k] = (
-            times_transpose(grad_gate, ffn_gate) + times_transpose(grad_up, ffn_up)
-        ).reshape(2, quarter, model)
-        rows_list[k], up_list[k], inner_list[k] = rows_k, up_k, inner
-        gate_list[k], grad_up_list[k] = grad_gate, grad_up
-    grad_two = scatter_sp(grad_parts)
-
-    norm_grad_two, ffn_gain_terms = norm_back(middle, ffn_scales, ffn_norm, grad_two)
-    grad_middle_quarter = grad_quarter.astype(F32) + norm_grad_two
-    grad_branch = gather_tp(grad_middle_quarter.astype(BF16))
+    fused = outer * quarter <= 512 and outer > 1 and tp_n == 4
+    if fused:
+        middle, grad_middle_quarter, ffn_gain_sum, branch, inner_rows, *ffn_parts = middle_layer(
+            gated,
+            output_proj,
+            lax.dynamic_slice_in_dim(hidden, quarter_first, quarter),
+            ffn_norm[None, :],
+            ffn_gate,
+            ffn_up,
+            ffn_down,
+            [block for both in up_blocks for block in both],
+            outer,
+            sides,
+        )
+        grad_branch = branch.reshape(rows_dev, model)
+        ffn_gain_sum = ffn_gain_sum[0]
+        inner_list = [
+            inner_rows[k * 2 * quarter : (k + 1) * 2 * quarter] for k in range(outer)
+        ]
+    else:
+        attn_quarter = scatter_tp(matmul(gated, output_proj))
+        hidden_quarter = lax.dynamic_slice_in_dim(hidden, quarter_first, quarter).astype(F32)
+        middle = hidden_quarter + attn_quarter
+        normed_two_full, ffn_scales = norm_rows(middle, ffn_norm)
+        normed_two = normed_two_full.astype(BF16)
+
+        two_blocks = gather_sp(normed_two)
+        rows_list, up_list, inner_list, gate_list, grad_up_list = [None] * outer, [None] * outer, [None] * outer, [None] * outer, [None] * outer
+        grad_parts = [None] * outer
+        for k in list(range(1, outer)) + [0]:
+            rows_k = jnp.concatenate(two_blocks[k])
+            up_k = jnp.concatenate(up_blocks[k])
+            gate_vals = matmul(rows_k, ffn_gate)
+            up_vals = matmul(rows_k, ffn_up)
+            sig = jax.nn.sigmoid(gate_vals)
+            grad_inner = times_transpose(up_k, ffn_down)
+            grad_gate = (grad_inner * up_vals * (sig * (1.0 + gate_vals * (1.0 - sig)))).astype(BF16)
+            grad_up = (grad_inner * (gate_vals * sig)).astype(BF16)
+            inner = (gate_vals * sig * up_vals).astype(BF16)
+            grad_parts[k] = (
+                times_transpose(grad_gate, ffn_gate) + times_transpose(grad_up, ffn_up)
+            ).reshape(2, quarter, model)
+            rows_list[k], up_list[k], inner_list[k] = rows_k, up_k, inner
+            gate_list[k], grad_up_list[k] = grad_gate, grad_up
+        grad_two = scatter_sp(grad_parts)
+
+        norm_grad_two, ffn_gain_terms = norm_back(middle, ffn_scales, ffn_norm, grad_two)
+        grad_middle_quarter = grad_quarter.astype(F32) + norm_grad_two
+        grad_branch = gather_tp(grad_middle_quarter.astype(BF16))
+        ffn_gain_sum = jnp.sum(ffn_gain_terms, axis=0)
 
     mlp_parts = [matmul(inner_list[k], ffn_down).reshape(2, quarter, model) for k in range(outer)]
     mlp_quarter = scatter_sp(mlp_parts)
     layer_out = gather_tp((middle + mlp_quarter).astype(BF16))
-
-    rows_all = jnp.concatenate(rows_list)
-    up_all = jnp.concatenate(up_list)
-    inner_all = jnp.concatenate(inner_list)
-    gate_all = jnp.concatenate(gate_list)
-    grad_up_all = jnp.concatenate(grad_up_list)
 
     def reduce_tp(part):
         half = part.shape[0] // 2
         keep = lax.dynamic_slice_in_dim(part, core_i * half, half)
         send = lax.dynamic_slice_in_dim(part, (1 - core_i) * half, half)
-        keep = (keep + core(send.astype(BF16)).astype(F32)).astype(BF16)
+        keep = (keep.astype(F32) + core(send.astype(BF16)).astype(F32)).astype(BF16)
         keep = (keep.astype(F32) + side(keep).astype(F32)).astype(BF16)
         near = core(keep)
         total = jnp.where(
@@ -778,9 +1169,18 @@
         )
         return total.astype(F32)
 
-    ffn_gate_grad = reduce_tp(outer_sum(rows_all, gate_all))
-    ffn_up_grad = reduce_tp(outer_sum(rows_all, grad_up_all))
-    ffn_down_grad = reduce_tp(outer_sum(inner_all, up_all))
+    if not fused:
+        rows_all = jnp.concatenate(rows_list)
+        up_all = jnp.concatenate(up_list)
+        inner_all = jnp.concatenate(inner_list)
+        gate_all = jnp.concatenate(gate_list)
+        grad_up_all = jnp.concatenate(grad_up_list)
+        ffn_parts = [
+            outer_sum(rows_all, gate_all),
+            outer_sum(rows_all, grad_up_all),
+            outer_sum(inner_all, up_all),
+        ]
+    ffn_gate_grad, ffn_up_grad, ffn_down_grad = [reduce_tp(part) for part in ffn_parts]
 
     branch_other = swap_half(grad_branch)
     branch_own = lax.dynamic_slice_in_dim(grad_branch, pair_i * (model // 2), model // 2, 1)
@@ -842,7 +1242,7 @@
     gains = jnp.concatenate(
         [
             jnp.sum(grad_normed_part * hidden_full * attn_scales, axis=0),
-            jnp.sum(ffn_gain_terms, axis=0),
+            ffn_gain_sum,
             jnp.sum(query_gain_terms, axis=(0, 1)),
             jnp.sum(key_gain_terms, axis=(0, 1)),
         ]

time: 669 us -> 731 us (1.093)
  Pallas kernels: 170 us -> 368 us
  waiting for transfers between devices: 159 us -> 103 us
  matrix products: 81.3 us -> 45 us
  starting transfers between devices: 81.9 us -> 60.2 us
  local copies, waits for them, and re-layouts: 68.8 us -> 53.2 us
    pallas_call x0 -> x1, Pallas kernels: none -> 133 us  [middle_layer(): pl.pallas_call(functools.partial(middle_kernel, outer), out_shape=[jax.Sh...]
    pallas_call x1, Pallas kernels: 143 us -> 208 us  [finish(): pl.pallas_call(functools.partial(finish_kernel, outer, sides, sp_n, tp_n,...]
    ppermute x28 -> x20, waiting for transfers between devices: 112 us -> 57.9 us  [pair(): return lax.ppermute(value, 'sp', pair_pairs)]
    ppermute x12 -> x6, waiting for transfers between devices: 14.7 us -> 37.9 us  [ring(): return lax.ppermute(value, 'sp', ring_pairs)]
    unnamed x131 -> x142, local copies, waits for them, and re-layouts: 28 us -> 8.23 us
    ppermute x6 -> x4, waiting for transfers between devices: 18.9 us -> 0.01 us  [side(): return lax.ppermute(value, 'tp', side_pairs)]
    dot_general x17 -> x5, matrix products: 32.5 us -> 15.2 us  [times_transpose(): lax.dot_general(left, right, (((1,), (1,)), ((), ())), preferred_element_...]
    ppermute x28 -> x20, starting transfers between devices: 37.8 us -> 25.4 us  [pair(): return lax.ppermute(value, 'sp', pair_pairs)]
  transfers between devices with their start and end apart: 61 -> 43, of which waited for: 20 -> 11; matrix products, arithmetic and copies ran while one was open for 32% -> 22% of each run, Pallas kernels for 26% -> 51%
where the time goes in v3:
time: 731 us; the launch traced here: 724 us
  Pallas kernels  368 us (50%)
  waiting for transfers between devices  103 us (14%)
  other arithmetic  84.6 us (12%)
  starting transfers between devices  60.2 us (8%)
  local copies, waits for them, and re-layouts  53.2 us (7%)
  matrix products  45 us (6%)
  between operations  9.96 us (1%)
    pallas_call x1, Pallas kernels, finish(): pl.pallas_call(functools.partial(finish_kernel, outer, sides, sp_n, tp_n,...  208 us
    pallas_call x1, Pallas kernels, middle_layer(): pl.pallas_call(functools.partial(middle_kernel, outer), out_shape=[jax.Sh...  133 us
    ppermute x20, waiting for transfers between devices, pair(): return lax.ppermute(value, 'sp', pair_pairs)  57.9 us
    ppermute x6, waiting for transfers between devices, ring(): return lax.ppermute(value, 'sp', ring_pairs)  37.9 us
    ppermute x20, starting transfers between devices, pair(): return lax.ppermute(value, 'sp', pair_pairs)  25.4 us
    ppermute x6, starting transfers between devices, ring(): return lax.ppermute(value, 'sp', ring_pairs)  21.1 us
    dot_general x8, matrix products, matmul(): return jnp.dot(left, right, preferred_element_type=F32)  19.6 us
    dot_general x5, matrix products, times_transpose(): lax.dot_general(left, right, (((1,), (1,)), ((), ())), preferred_element_...  15.2 us
  transfers between devices with their start and end apart: 43, of which 11 were waited for; matrix products, arithmetic and copies ran while one was open for 22% of the time, Pallas kernels for 51%

profile of v3, /device:TPU:0, one launch (start us, length us, event | category | flops | bytes accessed | tf_op | source)
XLA Modules:
  0.0 724.1 jit_solution(14692212727168842992)
XLA Ops:
  2.1 2.0 convert_reduce_fusion
  4.1 2.1 fusion
  14.3 3.0 collective-permute-start.4
  17.3 4.3 collective-permute-start
  21.5 1.9 constant_dynamic-slice_fusion.7.refs_7_
  28.2 4.7 fusion.17
  32.9 2.3 multiply_reduce_fusion.1
  45.8 2.1 copy.107
  57.3 2.3 constant_dynamic-slice_fusion.4
  64.9 3.3 collective-permute-start.8
  73.5 4.6 attn_forward.3
  81.5 8.1 %collective-permute-start.10 = (bf16[128,2048]{1,0:T(8,128)(2,1)}, bf16[128,2048]{1,0:T(8,128)(2,1)}, u32[]{:S(2)}, u32[]{:S(2)}) collective-permute-start(bf16[128,2048]{1,0:T(8,128)(2,1)} %collective-permute-done.8.refs_11_), channel_id=1, source_target_pairs={{0,2},{1,3},{2,4},{3,5},{4,6},{5,7},{6,0},{7,1},{8,10},{9,11},{10,... | collective-permute-start | bytes 1572872 | tf_op jit(solution)/shard_map/ppermute | solution.py:971
  89.7 2.5 maximum_select_fusion.7
  92.7 3.8 attn_forward.4
  96.5 10.4 %collective-permute-done.2.kv_b = bf16[2,512,256]{2,1,0:T(8,128)(2,1)S(1)} collective-permute-done((bf16[2,512,256]{2,1,0:T(8,128)(2,1)}, bf16[2,512,256]{2,1,0:T(8,128)(2,1)S(1)}, u32[]{:S(2)}, u32[]{:S(2)}) %collective-permute-start.2) | collective-permute-done | bytes 524320 | tf_op jit(solution)/shard_map/ppermute | solution.py:974
  107.7 3.8 attn_forward.5
  115.6 3.4 multiply_convert_fusion.1
  119.5 9.9 %collective-permute-done.9.refs_12_ = bf16[128,2048]{1,0:T(8,128)(2,1)} collective-permute-done((bf16[128,2048]{1,0:T(8,128)(2,1)}, bf16[128,2048]{1,0:T(8,128)(2,1)}, u32[]{:S(2)}, u32[]{:S(2)}) %collective-permute-start.9) | collective-permute-done | bytes 524320 | tf_op jit(solution)/shard_map/ppermute | solution.py:974
  129.5 11.1 %collective-permute-done.11.refs_14_ = bf16[128,2048]{1,0:T(8,128)(2,1)S(1)} collective-permute-done((bf16[128,2048]{1,0:T(8,128)(2,1)}, bf16[128,2048]{1,0:T(8,128)(2,1)S(1)}, u32[]{:S(2)}, u32[]{:S(2)}) %collective-permute-start.11) | collective-permute-done | bytes 524320 | tf_op jit(solution)/shard_map/ppermute | solution.py:974
  141.4 133.4 %middle.1 = (f32[128,2048]{1,0:T(8,128)}, f32[128,2048]{1,0:T(8,128)}, f32[1,2048]{1,0:T(1,128)}, bf16[2,2,128,2048]{3,2,1,0:T(8,128)(2,1)}, bf16[1024,768]{1,0:...) custom-call(bf16[512,512]{1,0:T(8,128)(2,1)} %get-tuple-element.76.refs_0_, ...), custom_call_target="tpu_custom_call" | custom-call | flops 30000001024 | bytes 40000000 | tf_op jit(solution)/shard_map/middle/pallas_call | solution.py:572
  274.8 3.4 fusion.50
  278.2 2.3 fusion.52
  280.6 2.3 fusion.54
  282.9 2.3 fusion.56
  286.7 2.7 convert_multiply_fusion.3
  295.5 3.3 attn_backward.3
  298.8 4.1 attn_backward.4
  302.9 7.0 attn_backward.5
  309.8 2.3 broadcast_multiply_fusion
  317.6 3.7 collective-permute-start.30
  322.6 2.2 fusion.23
  324.8 2.8 constant_dynamic-slice_fusion.2
  329.9 2.1 collective-permute-start.12
  333.3 3.3 fusion.70
  336.6 2.3 slice.245
  338.9 2.2 slice.246
  341.2 14.9 %collective-permute-done.12 = bf16[128,2048]{1,0:T(8,128)(2,1)S(1)} collective-permute-done((bf16[128,2048]{1,0:T(8,128)(2,1)S(1)}, bf16[128,2048]{1,0:T(8,128)(2,1)S(1)}, u32[]{:S(2)}, u32[]{:S(2)}) %collective-permute-start.12) | collective-permute-done | bytes 524320 | tf_op jit(solution)/shard_map/ppermute | solution.py:974
  359.5 11.4 %collective-permute-done.26 = bf16[512,512]{1,0:T(8,128)(2,1)S(1)} collective-permute-done((bf16[512,512]{1,0:T(8,128)(2,1)S(1)}, bf16[512,512]{1,0:T(8,128)(2,1)S(1)}, u32[]{:S(2)}, u32[]{:S(2)}) %collective-permute-start.26) | collective-permute-done | bytes 524320 | tf_op jit(solution)/shard_map/ppermute | solution.py:974
  371.6 2.3 convolution_convert_fusion.2.refs_1_
  375.6 2.3 convolution_convert_fusion.1.refs_2_
  377.9 8.2 %collective-permute-start.13 = (bf16[128,2048]{1,0:T(8,128)(2,1)S(1)}, bf16[128,2048]{1,0:T(8,128)(2,1)S(1)}, u32[]{:S(2)}, u32[]{:S(2)}) collective-permute-start(bf16[128,2048]{1,0:T(8,128)(2,1)S(1)} %fusion.31), channel_id=1, source_target_pairs={{0,2},{1,3},{2,4},{3,5},{4,6},{5,7},{6,0},{7,1},{8,10},{9,11},{10,... | collective-permute-start | bytes 1572872 | tf_op jit(solution)/shard_map/ppermute | solution.py:971
  389.8 3.4 fusion.12.refs_0_
  393.7 18.3 %collective-permute-done.13 = bf16[128,2048]{1,0:T(8,128)(2,1)S(1)} collective-permute-done((bf16[128,2048]{1,0:T(8,128)(2,1)S(1)}, bf16[128,2048]{1,0:T(8,128)(2,1)S(1)}, u32[]{:S(2)}, u32[]{:S(2)}) %collective-permute-start.13) | collective-permute-done | bytes 524320 | tf_op jit(solution)/shard_map/ppermute | solution.py:971
  413.7 7.3 %collective-permute-done.32 = bf16[2,512,256]{2,1,0:T(8,128)(2,1)S(1)} collective-permute-done((bf16[2,512,256]{2,1,0:T(8,128)(2,1)S(1)}, bf16[2,512,256]{2,1,0:T(8,128)(2,1)S(1)}, u32[]{:S(2)}, u32[]{:S(2)}) %collective-permute-start.32) | collective-permute-done | bytes 524320 | tf_op jit(solution)/shard_map/ppermute | solution.py:1213
  422.5 2.8 fusion.68
  433.0 5.6 fusion.4
  440.1 2.1 add_convert_fusion.3
  443.1 3.2 add_convert_fusion.5
  447.8 7.2 collective-permute-done.15
  457.8 3.3 add_convert_fusion.1
  461.8 10.5 %collective-permute-done.17 = bf16[128,2048]{1,0:T(8,128)(2,1)S(1)} collective-permute-done((bf16[128,2048]{1,0:T(8,128)(2,1)S(1)}, bf16[128,2048]{1,0:T(8,128)(2,1)S(1)}, u32[]{:S(2)}, u32[]{:S(2)}) %collective-permute-start.17) | collective-permute-done | bytes 524320 | tf_op jit(solution)/shard_map/ppermute | solution.py:971
  472.2 2.2 fusion.26
  474.9 2.2 convolution_convert_fusion.refs_3_
  477.2 208.0 %finish.1 = (bf16[2,512,1024]{2,1,0:T(8,128)(2,1)}, bf16[2,1024,512]{2,1,0:T(8,128)(2,1)}, bf16[2,1024,512]{2,1,0:T(8,128)(2,1)}, bf16[2,1024,512]{2,1,0:T(8,128...) custom-call(bf16[512,1024]{1,0:T(8,128)(2,1)} %fusion.12.refs_0_, ...), custom_call_target="tpu_custom_call" | custom-call | flops 1000000000 | bytes 100000000 | tf_op jit(solution)/shard_map/finish/pallas_call | solution.py:896
  685.2 4.3 bitcast_convert_fusion.2
  689.5 2.7 bitcast_convert_fusion.1
  692.2 2.7 bitcast_convert_fusion
  695.0 2.3 slice_convert_fusion
  698.6 2.5 add_convert_fusion
  703.6 2.3 add_convert_fusion.4
  708.3 2.5 maximum_convert_fusion
  714.2 3.4 fusion.7
  717.6 3.0 fusion.5
  720.6 3.0 fusion.6
  (296 shorter events, 102.8 us)
Async XLA Ops:
  0.6 32.3 %copy-start = (bf16[2048,512]{1,0:T(8,128)(2,1)S(1)}, bf16[2048,512]{1,0:T(8,128)(2,1)}, u32[]{:S(2)}) copy-start(bf16[2048,512]{1,0:T(8,128)(2,1)} %param.18) | copy-start | bytes 6291460
  6.2 35.6 %copy-start.53 = (f32[512]{0:T(512)}, f32[512]{0:T(512)S(1)}, u32[]{:S(2)}) copy-start(f32[512]{0:T(512)S(1)} %add_rsqrt_fusion.2) | copy-start | bytes 6148
  12.1 14.7 %copy-start.27 = (f32[512,64]{0,1:T(8,128)}, f32[512,64]{0,1:T(8,128)S(1)}, u32[]{:S(2)}) copy-start(f32[512,64]{0,1:T(8,128)S(1)} %get-tuple-element.108) | copy-start | bytes 393220
  14.3 57.2 %collective-permute-start.4 = (bf16[2,512,256]{2,1,0:T(8,128)(2,1)}, bf16[2,512,256]{2,1,0:T(8,128)(2,1)}, u32[]{:S(2)}, u32[]{:S(2)}) collective-permute-start(bf16[2,512,256]{2,1,0:T(8,128)(2,1)} %pad_maximum_fusion.6.kv_a), channel_id=1, source_target_pairs={{0,1},{1,0},{2,3},{3,2},{4,5},{5,4},{6,7},{7,6},{8,9},{9,8},{10,11... | collective-permute-start | bytes 1572872 | tf_op jit(solution)/shard_map/ppermute | solution.py:974
  17.3 45.5 %collective-permute-start = (bf16[2,512,256]{2,1,0:T(8,128)(2,1)}, bf16[2,512,256]{2,1,0:T(8,128)(2,1)}, u32[]{:S(2)}, u32[]{:S(2)}) collective-permute-start(bf16[2,512,256]{2,1,0:T(8,128)(2,1)} %pad_maximum_fusion.6.kv_a), channel_id=1, source_target_pairs={{0,2},{1,3},{2,4},{3,5},{4,6},{5,7},{8,10},{9,11},{10,12},{11,13},... | collective-permute-start | bytes 1572872 | tf_op jit(solution)/shard_map/ppermute | solution.py:1034
  23.4 41.5 %collective-permute-start.6 = (bf16[128,2048]{1,0:T(8,128)(2,1)}, bf16[128,2048]{1,0:T(8,128)(2,1)}, u32[]{:S(2)}, u32[]{:S(2)}) collective-permute-start(bf16[128,2048]{1,0:T(8,128)(2,1)} %constant_dynamic-slice_fusion.7.refs_7_), channel_id=1, source_target_pairs={{0,2},{1,3},{2,4},{3,5},{4,6},{5,7},{6,0},{7,1},{8,10},{9,11},{10,... | collective-permute-start | bytes 1572872 | tf_op jit(solution)/shard_map/ppermute | solution.py:971
  26.1 42.1 %collective-permute-start.24 = (bf16[512,512]{1,0:T(8,128)(2,1)}, bf16[512,512]{1,0:T(8,128)(2,1)}, u32[]{:S(2)}, u32[]{:S(2)}) collective-permute-start(bf16[512,512]{1,0:T(8,128)(2,1)} %constant_dynamic-slice_fusion.3), channel_id=1, source_target_pairs={{0,1},{1,0},{2,3},{3,2},{4,5},{5,4},{6,7},{7,6},{8,9},{9,8},{10,11... | collective-permute-start | bytes 1572872 | tf_op jit(solution)/shard_map/ppermute | solution.py:974
  41.0 11.5 %copy-start.55 = (f32[512,2]{0,1:T(2,128)S(1)}, f32[512,2]{0,1:T(2,128)}, u32[]{:S(2)}) copy-start(f32[512,2]{0,1:T(2,128)} %get-tuple-element.105) | copy-start | bytes 12292
  54.5 9.8 %copy-start.59 = (f32[128]{0:T(128)S(1)}, f32[128]{0:T(128)}, u32[]{:S(2)}) copy-start(f32[128]{0:T(128)} %param.23) | copy-start | bytes 1540
  54.5 16.4 %copy-start.62 = (f32[128]{0:T(128)S(1)}, f32[128]{0:T(128)}, u32[]{:S(2)}) copy-start(f32[128]{0:T(128)} %param.24) | copy-start | bytes 1540
  62.8 9.2 %collective-permute-start.1 = (bf16[2,512,256]{2,1,0:T(8,128)(2,1)}, bf16[2,512,256]{2,1,0:T(8,128)(2,1)}, u32[]{:S(2)}, u32[]{:S(2)}) collective-permute-start(bf16[2,512,256]{2,1,0:T(8,128)(2,1)} %collective-permute-done.kv_a), channel_id=1, source_target_pairs={{2,4},{3,5},{4,6},{5,7},{10,12},{11,13},{12,14},{13,15},{18,20},{1... | collective-permute-start | bytes 1572872 | tf_op jit(solution)/shard_map/ppermute | solution.py:1034
  64.9 15.1 %collective-permute-start.8 = (bf16[128,2048]{1,0:T(8,128)(2,1)}, bf16[128,2048]{1,0:T(8,128)(2,1)}, u32[]{:S(2)}, u32[]{:S(2)}) collective-permute-start(bf16[128,2048]{1,0:T(8,128)(2,1)} %collective-permute-done.6.refs_9_), channel_id=1, source_target_pairs={{0,2},{1,3},{2,4},{3,5},{4,6},{5,7},{6,0},{7,1},{8,10},{9,11},{10,... | collective-permute-start | bytes 1572872 | tf_op jit(solution)/shard_map/ppermute | solution.py:971
  68.2 13.4 %collective-permute-start.25 = (bf16[512,512]{1,0:T(8,128)(2,1)}, bf16[512,512]{1,0:T(8,128)(2,1)S(1)}, u32[]{:S(2)}, u32[]{:S(2)}) collective-permute-start(bf16[512,512]{1,0:T(8,128)(2,1)} %collective-permute-done.24), channel_id=1, source_target_pairs={{0,8},{8,0},{16,24},{24,16},{1,9},{9,1},{17,25},{25,17},{2,10},{10... | collective-permute-start | bytes 1572872 | tf_op jit(solution)/shard_map/ppermute | solution.py:980
  69.4 22.8 %collective-permute-start.3 = (bf16[2,512,256]{2,1,0:T(8,128)(2,1)}, bf16[2,512,256]{2,1,0:T(8,128)(2,1)}, u32[]{:S(2)}, u32[]{:S(2)}) collective-permute-start(bf16[2,512,256]{2,1,0:T(8,128)(2,1)} %collective-permute-done.kv_a), channel_id=1, source_target_pairs={{0,1},{1,0},{2,3},{3,2},{4,5},{5,4},{6,7},{7,6},{8,9},{9,8},{10,11... | collective-permute-start | bytes 1572872 | tf_op jit(solution)/shard_map/ppermute | solution.py:974
  71.5 48.0 %collective-permute-start.5 = (bf16[128,2048]{1,0:T(8,128)(2,1)}, bf16[128,2048]{1,0:T(8,128)(2,1)}, u32[]{:S(2)}, u32[]{:S(2)}) collective-permute-start(bf16[128,2048]{1,0:T(8,128)(2,1)} %constant_dynamic-slice_fusion.7.refs_7_), channel_id=1, source_target_pairs={{0,1},{1,0},{2,3},{3,2},{4,5},{5,4},{6,7},{7,6},{8,9},{9,8},{10,11... | collective-permute-start | bytes 1572872 | tf_op jit(solution)/shard_map/ppermute | solution.py:974
  72.0 34.9 %collective-permute-start.2 = (bf16[2,512,256]{2,1,0:T(8,128)(2,1)}, bf16[2,512,256]{2,1,0:T(8,128)(2,1)S(1)}, u32[]{:S(2)}, u32[]{:S(2)}) collective-permute-start(bf16[2,512,256]{2,1,0:T(8,128)(2,1)} %collective-permute-done.1.kv_a), channel_id=1, source_target_pairs={{0,1},{1,0},{2,3},{3,2},{4,5},{5,4},{6,7},{7,6},{8,9},{9,8},{10,11... | collective-permute-start | bytes 1572872 | tf_op jit(solution)/shard_map/ppermute | solution.py:974
  80.0 39.5 %collective-permute-start.7 = (bf16[128,2048]{1,0:T(8,128)(2,1)}, bf16[128,2048]{1,0:T(8,128)(2,1)}, u32[]{:S(2)}, u32[]{:S(2)}) collective-permute-start(bf16[128,2048]{1,0:T(8,128)(2,1)} %collective-permute-done.6.refs_9_), channel_id=1, source_target_pairs={{0,1},{1,0},{2,3},{3,2},{4,5},{5,4},{6,7},{7,6},{8,9},{9,8},{10,11... | collective-permute-start | bytes 1572872 | tf_op jit(solution)/shard_map/ppermute | solution.py:974
  81.5 31.9 %collective-permute-start.10 = (bf16[128,2048]{1,0:T(8,128)(2,1)}, bf16[128,2048]{1,0:T(8,128)(2,1)}, u32[]{:S(2)}, u32[]{:S(2)}) collective-permute-start(bf16[128,2048]{1,0:T(8,128)(2,1)} %collective-permute-done.8.refs_11_), channel_id=1, source_target_pairs={{0,2},{1,3},{2,4},{3,5},{4,6},{5,7},{6,0},{7,1},{8,10},{9,11},{10,... | collective-permute-start | bytes 1572872 | tf_op jit(solution)/shard_map/ppermute | solution.py:971
  92.2 37.3 %collective-permute-start.9 = (bf16[128,2048]{1,0:T(8,128)(2,1)}, bf16[128,2048]{1,0:T(8,128)(2,1)}, u32[]{:S(2)}, u32[]{:S(2)}) collective-permute-start(bf16[128,2048]{1,0:T(8,128)(2,1)} %collective-permute-done.8.refs_11_), channel_id=1, source_target_pairs={{0,1},{1,0},{2,3},{3,2},{4,5},{5,4},{6,7},{7,6},{8,9},{9,8},{10,11... | collective-permute-start | bytes 1572872 | tf_op jit(solution)/shard_map/ppermute | solution.py:974
  113.4 27.2 %collective-permute-start.11 = (bf16[128,2048]{1,0:T(8,128)(2,1)}, bf16[128,2048]{1,0:T(8,128)(2,1)S(1)}, u32[]{:S(2)}, u32[]{:S(2)}) collective-permute-start(bf16[128,2048]{1,0:T(8,128)(2,1)} %collective-permute-done.10.refs_13_), channel_id=1, source_target_pairs={{0,1},{1,0},{2,3},{3,2},{4,5},{5,4},{6,7},{7,6},{8,9},{9,8},{10,11... | collective-permute-start | bytes 1572872 | tf_op jit(solution)/shard_map/ppermute | solution.py:974
  119.0 269.2 %collective-permute-start.21 = (bf16[512,512]{1,0:T(8,128)(2,1)}, bf16[512,512]{1,0:T(8,128)(2,1)}, u32[]{:S(2)}, u32[]{:S(2)}) collective-permute-start(bf16[512,512]{1,0:T(8,128)(2,1)} %get-tuple-element.76.refs_0_), channel_id=1, source_target_pairs={{0,1},{1,0},{2,3},{3,2},{4,5},{5,4},{6,7},{7,6},{8,9},{9,8},{10,11... | collective-permute-start | bytes 1572872 | tf_op jit(solution)/shard_map/ppermute | solution.py:974
  141.4 133.4 %copy-start.2 = (bf16[768,2048]{1,0:T(8,128)(2,1)S(1)}, bf16[768,2048]{1,0:T(8,128)(2,1)}, u32[]{:S(2)}) copy-start(bf16[768,2048]{1,0:T(8,128)(2,1)} %refs_6_.1) | copy-start | bytes 9437188
  293.9 64.0 %collective-permute-start.22 = (bf16[512,512]{1,0:T(8,128)(2,1)}, bf16[512,512]{1,0:T(8,128)(2,1)}, u32[]{:S(2)}, u32[]{:S(2)}) collective-permute-start(bf16[512,512]{1,0:T(8,128)(2,1)} %constant_dynamic-slice_fusion.5), channel_id=1, source_target_pairs={{0,1},{1,0},{2,3},{3,2},{4,5},{5,4},{6,7},{7,6},{8,9},{9,8},{10,11... | collective-permute-start | bytes 1572872 | tf_op jit(solution)/shard_map/ppermute | solution.py:974
  317.6 40.8 %collective-permute-start.30 = (bf16[2,512,256]{2,1,0:T(8,128)(2,1)}, bf16[2,512,256]{2,1,0:T(8,128)(2,1)}, u32[]{:S(2)}, u32[]{:S(2)}) collective-permute-start(bf16[2,512,256]{2,1,0:T(8,128)(2,1)} %get-tuple-element.60), channel_id=1, source_target_pairs={{0,1},{1,0},{2,3},{3,2},{4,5},{5,4},{6,7},{7,6},{8,9},{9,8},{10,11... | collective-permute-start | bytes 1572872 | tf_op jit(solution)/shard_map/ppermute | solution.py:974
  324.7 49.2 %collective-permute-start.27 = (bf16[512,512]{0,1:T(8,128)(2,1)S(1)}, bf16[512,512]{0,1:T(8,128)(2,1)S(1)}, u32[]{:S(2)}, u32[]{:S(2)}) collective-permute-start(bf16[512,512]{0,1:T(8,128)(2,1)S(1)} %get-tuple-element.82), channel_id=1, source_target_pairs={{0,1},{1,0},{2,3},{3,2},{4,5},{5,4},{6,7},{7,6},{8,9},{9,8},{10,11... | collective-permute-start | bytes 1572872 | tf_op jit(solution)/shard_map/ppermute | solution.py:974
  329.9 26.2 %collective-permute-start.12 = (bf16[128,2048]{1,0:T(8,128)(2,1)S(1)}, bf16[128,2048]{1,0:T(8,128)(2,1)S(1)}, u32[]{:S(2)}, u32[]{:S(2)}) collective-permute-start(bf16[128,2048]{1,0:T(8,128)(2,1)S(1)} %slice.248), channel_id=1, source_target_pairs={{0,1},{1,0},{2,3},{3,2},{4,5},{5,4},{6,7},{7,6},{8,9},{9,8},{10,11... | collective-permute-start | bytes 1572872 | tf_op jit(solution)/shard_map/ppermute | solution.py:974
  336.6 19.5 %copy-start.44 = (bf16[512,512]{1,0:T(8,128)(2,1)S(1)}, bf16[512,512]{1,0:T(8,128)(2,1)}, u32[]{:S(2)}) copy-start(bf16[512,512]{1,0:T(8,128)(2,1)} %get-tuple-element.80) | copy-start | bytes 1572868
  338.9 19.0 %copy-start.67 = (bf16[2,512,256]{2,1,0:T(8,128)(2,1)S(1)}, bf16[2,512,256]{2,1,0:T(8,128)(2,1)}, u32[]{:S(2)}) copy-start(bf16[2,512,256]{2,1,0:T(8,128)(2,1)} %get-tuple-element.58) | copy-start | bytes 1572868
  338.9 19.4 %copy-start.47 = (bf16[2,512,256]{2,1,0:T(8,128)(2,1)S(1)}, bf16[2,512,256]{2,1,0:T(8,128)(2,1)}, u32[]{:S(2)}) copy-start(bf16[2,512,256]{2,1,0:T(8,128)(2,1)} %get-tuple-element.59) | copy-start | bytes 1572868
  341.2 30.4 %copy-start.33 = (bf16[512,1024]{1,0:T(8,128)(2,1)S(1)}, bf16[512,1024]{1,0:T(8,128)(2,1)}, u32[]{:S(2)}) copy-start(bf16[512,1024]{1,0:T(8,128)(2,1)} %constant_dynamic-slice_fusion.4) | copy-start | bytes 3145732
  341.2 30.4 %copy-start.35 = (bf16[512,1024]{1,0:T(8,128)(2,1)S(1)}, bf16[512,1024]{1,0:T(8,128)(2,1)}, u32[]{:S(2)}) copy-start(bf16[512,1024]{1,0:T(8,128)(2,1)} %maximum_select_fusion.7) | copy-start | bytes 3145732
  356.1 14.8 %collective-permute-start.26 = (bf16[512,512]{1,0:T(8,128)(2,1)S(1)}, bf16[512,512]{1,0:T(8,128)(2,1)S(1)}, u32[]{:S(2)}, u32[]{:S(2)}) collective-permute-start(bf16[512,512]{1,0:T(8,128)(2,1)S(1)} %copy-done.44), channel_id=1, source_target_pairs={{0,1},{1,0},{2,3},{3,2},{4,5},{5,4},{6,7},{7,6},{8,9},{9,8},{10,11... | collective-permute-start | bytes 1572872 | tf_op jit(solution)/shard_map/ppermute | solution.py:974
  358.0 29.7 %collective-permute-start.29 = (bf16[2,512,256]{2,1,0:T(8,128)(2,1)S(1)}, bf16[2,512,256]{2,1,0:T(8,128)(2,1)S(1)}, u32[]{:S(2)}, u32[]{:S(2)}) collective-permute-start(bf16[2,512,256]{2,1,0:T(8,128)(2,1)S(1)} %copy-done.67), channel_id=1, source_target_pairs={{0,1},{1,0},{2,3},{3,2},{4,5},{5,4},{6,7},{7,6},{8,9},{9,8},{10,11... | collective-permute-start | bytes 1572872 | tf_op jit(solution)/shard_map/ppermute | solution.py:974
  358.3 19.6 %collective-permute-start.23 = (bf16[512,512]{1,0:T(8,128)(2,1)}, bf16[512,512]{1,0:T(8,128)(2,1)S(1)}, u32[]{:S(2)}, u32[]{:S(2)}) collective-permute-start(bf16[512,512]{1,0:T(8,128)(2,1)} %collective-permute-done.22), channel_id=1, source_target_pairs={{0,8},{8,0},{16,24},{24,16},{1,9},{9,1},{17,25},{25,17},{2,10},{10... | collective-permute-start | bytes 1572872 | tf_op jit(solution)/shard_map/ppermute | solution.py:980
  370.9 17.1 %collective-permute-start.31 = (bf16[2,512,256]{2,1,0:T(8,128)(2,1)S(1)}, bf16[2,512,256]{2,1,0:T(8,128)(2,1)S(1)}, u32[]{:S(2)}, u32[]{:S(2)}) collective-permute-start(bf16[2,512,256]{2,1,0:T(8,128)(2,1)S(1)} %add_convert_fusion.7), channel_id=1, source_target_pairs={{4,2},{5,3},{6,4},{7,5},{12,10},{13,11},{14,12},{15,13},{20,18},{2... | collective-permute-start | bytes 1572872 | tf_op jit(solution)/shard_map/ppermute | solution.py:1213
  373.9 19.5 %collective-permute-start.14 = (bf16[128,2048]{1,0:T(8,128)(2,1)S(1)}, bf16[128,2048]{1,0:T(8,128)(2,1)S(1)}, u32[]{:S(2)}, u32[]{:S(2)}) collective-permute-start(bf16[128,2048]{1,0:T(8,128)(2,1)S(1)} %slice.247), channel_id=1, source_target_pairs={{0,1},{1,0},{2,3},{3,2},{4,5},{5,4},{6,7},{7,6},{8,9},{9,8},{10,11... | collective-permute-start | bytes 1572872 | tf_op jit(solution)/shard_map/ppermute | solution.py:974
  377.9 9.7 %copy-start.66 = (bf16[2,512,256]{2,1,0:T(8,128)(2,1)S(1)}, bf16[2,512,256]{2,1,0:T(8,128)(2,1)}, u32[]{:S(2)}) copy-start(bf16[2,512,256]{2,1,0:T(8,128)(2,1)} %get-tuple-element.56) | copy-start | bytes 1572868
  377.9 10.1 %copy-start.49 = (bf16[2,512,256]{2,1,0:T(8,128)(2,1)S(1)}, bf16[2,512,256]{2,1,0:T(8,128)(2,1)}, u32[]{:S(2)}) copy-start(bf16[2,512,256]{2,1,0:T(8,128)(2,1)} %get-tuple-element.57) | copy-start | bytes 1572868
  377.9 34.1 %collective-permute-start.13 = (bf16[128,2048]{1,0:T(8,128)(2,1)S(1)}, bf16[128,2048]{1,0:T(8,128)(2,1)S(1)}, u32[]{:S(2)}, u32[]{:S(2)}) collective-permute-start(bf16[128,2048]{1,0:T(8,128)(2,1)S(1)} %fusion.31), channel_id=1, source_target_pairs={{0,2},{1,3},{2,4},{3,5},{4,6},{5,7},{6,0},{7,1},{8,10},{9,11},{10,... | collective-permute-start | bytes 1572872 | tf_op jit(solution)/shard_map/ppermute | solution.py:971
  387.7 25.4 %collective-permute-start.28 = (bf16[2,512,256]{2,1,0:T(8,128)(2,1)S(1)}, bf16[2,512,256]{2,1,0:T(8,128)(2,1)S(1)}, u32[]{:S(2)}, u32[]{:S(2)}) collective-permute-start(bf16[2,512,256]{2,1,0:T(8,128)(2,1)S(1)} %copy-done.66), channel_id=1, source_target_pairs={{0,1},{1,0},{2,3},{3,2},{4,5},{5,4},{6,7},{7,6},{8,9},{9,8},{10,11... | collective-permute-start | bytes 1572872 | tf_op jit(solution)/shard_map/ppermute | solution.py:974
  388.0 51.4 %collective-permute-start.37 = (bf16[1024,768]{1,0:T(8,128)(2,1)}, bf16[1024,768]{1,0:T(8,128)(2,1)}, u32[]{:S(2)}, u32[]{:S(2)}) collective-permute-start(bf16[1024,768]{1,0:T(8,128)(2,1)} %constant_dynamic-slice_fusion.1), channel_id=1, source_target_pairs={{0,8},{8,0},{16,24},{24,16},{1,9},{9,1},{17,25},{25,17},{2,10},{10... | collective-permute-start | bytes 4718600 | tf_op jit(solution)/shard_map/ppermute | solution.py:980
  388.2 32.8 %collective-permute-start.32 = (bf16[2,512,256]{2,1,0:T(8,128)(2,1)S(1)}, bf16[2,512,256]{2,1,0:T(8,128)(2,1)S(1)}, u32[]{:S(2)}, u32[]{:S(2)}) collective-permute-start(bf16[2,512,256]{2,1,0:T(8,128)(2,1)S(1)} %add_convert_fusion.6), channel_id=1, source_target_pairs={{2,0},{3,1},{4,2},{5,3},{6,4},{7,5},{10,8},{11,9},{12,10},{13,11},... | collective-permute-start | bytes 1572872 | tf_op jit(solution)/shard_map/ppermute | solution.py:1213
  393.2 29.0 %copy-start.46 = (bf16[2,512,256]{2,1,0:T(8,128)(2,1)S(1)}, bf16[2,512,256]{2,1,0:T(8,128)(2,1)}, u32[]{:S(2)}) copy-start(bf16[2,512,256]{2,1,0:T(8,128)(2,1)} %get-tuple-element.55) | copy-start | bytes 1572868
  393.4 48.9 %collective-permute-start.34 = (bf16[1024,768]{1,0:T(8,128)(2,1)}, bf16[1024,768]{1,0:T(8,128)(2,1)}, u32[]{:S(2)}, u32[]{:S(2)}) collective-permute-start(bf16[1024,768]{1,0:T(8,128)(2,1)} %constant_dynamic-slice_fusion.2), channel_id=1, source_target_pairs={{0,8},{8,0},{16,24},{24,16},{1,9},{9,1},{17,25},{25,17},{2,10},{10... | collective-permute-start | bytes 4718600 | tf_op jit(solution)/shard_map/ppermute | solution.py:980
  412.0 45.8 %collective-permute-start.40 = (bf16[384,2048]{1,0:T(8,128)(2,1)}, bf16[384,2048]{1,0:T(8,128)(2,1)}, u32[]{:S(2)}, u32[]{:S(2)}) collective-permute-start(bf16[384,2048]{1,0:T(8,128)(2,1)} %constant_dynamic-slice_fusion), channel_id=1, source_target_pairs={{0,8},{8,0},{16,24},{24,16},{1,9},{9,1},{17,25},{25,17},{2,10},{10... | collective-permute-start | bytes 4718600 | tf_op jit(solution)/shard_map/ppermute | solution.py:980
  413.0 48.1 %collective-permute-start.18 = (bf16[128,2048]{1,0:T(8,128)(2,1)}, bf16[128,2048]{1,0:T(8,128)(2,1)}, u32[]{:S(2)}, u32[]{:S(2)}) collective-permute-start(bf16[128,2048]{1,0:T(8,128)(2,1)} %slice.245), channel_id=1, source_target_pairs={{0,1},{1,0},{2,3},{3,2},{4,5},{5,4},{6,7},{7,6},{8,9},{9,8},{10,11... | collective-permute-start | bytes 1572872 | tf_op jit(solution)/shard_map/ppermute | solution.py:974
  421.0 25.3 %collective-permute-start.16 = (bf16[128,2048]{1,0:T(8,128)(2,1)}, bf16[128,2048]{1,0:T(8,128)(2,1)}, u32[]{:S(2)}, u32[]{:S(2)}) collective-permute-start(bf16[128,2048]{1,0:T(8,128)(2,1)} %slice.246), channel_id=1, source_target_pairs={{0,1},{1,0},{2,3},{3,2},{4,5},{5,4},{6,7},{7,6},{8,9},{9,8},{10,11... | collective-permute-start | bytes 1572872 | tf_op jit(solution)/shard_map/ppermute | solution.py:974
  439.4 15.6 %collective-permute-start.15 = (bf16[128,2048]{1,0:T(8,128)(2,1)S(1)}, bf16[128,2048]{1,0:T(8,128)(2,1)S(1)}, u32[]{:S(2)}, u32[]{:S(2)}) collective-permute-start(bf16[128,2048]{1,0:T(8,128)(2,1)S(1)} %copy-done.48), channel_id=1, source_target_pairs={{0,2},{1,3},{2,4},{3,5},{4,6},{5,7},{6,0},{7,1},{8,10},{9,11},{10,... | collective-permute-start | bytes 1572872 | tf_op jit(solution)/shard_map/ppermute | solution.py:971
  442.2 14.3 %copy-start.11 = (f32[256,2048]{1,0:T(8,128)S(1)}, f32[256,2048]{1,0:T(8,128)}, u32[]{:S(2)}) copy-start(f32[256,2048]{1,0:T(8,128)} %fusion.52) | copy-start | bytes 6291460
  442.2 32.7 %collective-permute-start.33 = (bf16[512,512]{1,0:T(8,128)(2,1)S(1)}, bf16[512,512]{1,0:T(8,128)(2,1)S(1)}, u32[]{:S(2)}, u32[]{:S(2)}) collective-permute-start(bf16[512,512]{1,0:T(8,128)(2,1)S(1)} %pad_maximum_fusion.8), channel_id=1, source_target_pairs={{0,1},{1,0},{2,3},{3,2},{4,5},{5,4},{6,7},{7,6},{8,9},{9,8},{10,11... | collective-permute-start | bytes 1572872 | tf_op jit(solution)/shard_map/ppermute | solution.py:974
  443.1 14.7 %copy-start.17 = (bf16[768,2048]{1,0:T(8,128)(2,1)S(1)}, bf16[768,2048]{1,0:T(8,128)(2,1)}, u32[]{:S(2)}) copy-start(bf16[768,2048]{1,0:T(8,128)(2,1)} %get-tuple-element.71) | copy-start | bytes 9437188
  446.3 259.6 %collective-permute-start.38 = (bf16[1024,768]{1,0:T(8,128)(2,1)S(1)}, bf16[1024,768]{1,0:T(8,128)(2,1)}, u32[]{:S(2)}, u32[]{:S(2)}) collective-permute-start(bf16[1024,768]{1,0:T(8,128)(2,1)S(1)} %add_convert_fusion.3), channel_id=1, source_target_pairs={{0,16},{8,24},{16,0},{24,8},{1,17},{9,25},{17,1},{25,9},{2,18},{10... | collective-permute-start | bytes 4718600 | tf_op jit(solution)/shard_map/ppermute | solution.py:977
  455.0 248.6 %collective-permute-start.35 = (bf16[1024,768]{1,0:T(8,128)(2,1)}, bf16[1024,768]{1,0:T(8,128)(2,1)}, u32[]{:S(2)}, u32[]{:S(2)}) collective-permute-start(bf16[1024,768]{1,0:T(8,128)(2,1)} %add_convert_fusion.5), channel_id=1, source_target_pairs={{0,16},{8,24},{16,0},{24,8},{1,17},{9,25},{17,1},{25,9},{2,18},{10... | collective-permute-start | bytes 4718600 | tf_op jit(solution)/shard_map/ppermute | solution.py:977
  457.7 14.5 %copy-start.8 = (f32[256,2048]{1,0:T(8,128)S(1)}, f32[256,2048]{1,0:T(8,128)}, u32[]{:S(2)}) copy-start(f32[256,2048]{1,0:T(8,128)} %fusion.50) | copy-start | bytes 6291460
  457.8 14.5 %copy-start.32 = (f32[128,2048]{1,0:T(8,128)S(1)}, f32[128,2048]{1,0:T(8,128)}, u32[]{:S(2)}) copy-start(f32[128,2048]{1,0:T(8,128)} %get-tuple-element.49) | copy-start | bytes 3145732
  457.8 14.5 %collective-permute-start.17 = (bf16[128,2048]{1,0:T(8,128)(2,1)S(1)}, bf16[128,2048]{1,0:T(8,128)(2,1)S(1)}, u32[]{:S(2)}, u32[]{:S(2)}) collective-permute-start(bf16[128,2048]{1,0:T(8,128)(2,1)S(1)} %fusion.28), channel_id=1, source_target_pairs={{0,2},{1,3},{2,4},{3,5},{4,6},{5,7},{6,0},{7,1},{8,10},{9,11},{10,... | collective-permute-start | bytes 1572872 | tf_op jit(solution)/shard_map/ppermute | solution.py:971
  461.2 13.8 %copy-start.34 = (bf16[512,1024]{1,0:T(8,128)(2,1)S(1)}, bf16[512,1024]{1,0:T(8,128)(2,1)}, u32[]{:S(2)}) copy-start(bf16[512,1024]{1,0:T(8,128)(2,1)} %constant_dynamic-slice_fusion.4) | copy-start | bytes 3145732
  461.2 13.8 %copy-start.36 = (bf16[512,1024]{1,0:T(8,128)(2,1)S(1)}, bf16[512,1024]{1,0:T(8,128)(2,1)}, u32[]{:S(2)}) copy-start(bf16[512,1024]{1,0:T(8,128)(2,1)} %maximum_select_fusion.7) | copy-start | bytes 3145732
  461.2 237.5 %collective-permute-start.41 = (bf16[384,2048]{1,0:T(8,128)(2,1)}, bf16[384,2048]{1,0:T(8,128)(2,1)}, u32[]{:S(2)}, u32[]{:S(2)}) collective-permute-start(bf16[384,2048]{1,0:T(8,128)(2,1)} %add_convert_fusion.1), channel_id=1, source_target_pairs={{0,16},{8,24},{16,0},{24,8},{1,17},{9,25},{17,1},{25,9},{2,18},{10... | collective-permute-start | bytes 4718600 | tf_op jit(solution)/shard_map/ppermute | solution.py:977
  474.4 226.9 %collective-permute-start.19 = (bf16[128,2048]{1,0:T(8,128)(2,1)}, bf16[128,2048]{1,0:T(8,128)(2,1)}, u32[]{:S(2)}, u32[]{:S(2)}) collective-permute-start(bf16[128,2048]{1,0:T(8,128)(2,1)} %fusion.26), channel_id=1, source_target_pairs={{0,16},{8,24},{16,0},{24,8},{1,17},{9,25},{17,1},{25,9},{2,18},{10... | collective-permute-start | bytes 1572872 | tf_op jit(solution)/shard_map/ppermute | solution.py:977
  701.2 13.0 %collective-permute-start.42 = (bf16[384,2048]{1,0:T(8,128)(2,1)S(1)}, bf16[384,2048]{1,0:T(8,128)(2,1)S(1)}, u32[]{:S(2)}, u32[]{:S(2)}) collective-permute-start(bf16[384,2048]{1,0:T(8,128)(2,1)S(1)} %add_convert_fusion), channel_id=1, source_target_pairs={{0,8},{8,0},{16,24},{24,16},{1,9},{9,1},{17,25},{25,17},{2,10},{10... | collective-permute-start | bytes 4718600 | tf_op jit(solution)/shard_map/ppermute | solution.py:980
  703.0 9.5 %collective-permute-start.20 = (bf16[2,128,2048]{2,1,0:T(8,128)(2,1)S(1)}, bf16[2,128,2048]{2,1,0:T(8,128)(2,1)S(1)}, u32[]{:S(2)}, u32[]{:S(2)}) collective-permute-start(bf16[2,128,2048]{2,1,0:T(8,128)(2,1)S(1)} %maximum_select_fusion.4), channel_id=1, source_target_pairs={{0,8},{8,0},{16,24},{24,16},{1,9},{9,1},{17,25},{25,17},{2,10},{10... | collective-permute-start | bytes 3145736 | tf_op jit(solution)/shard_map/ppermute | solution.py:980
  705.8 11.8 %collective-permute-start.36 = (bf16[1024,768]{1,0:T(8,128)(2,1)S(1)}, bf16[1024,768]{1,0:T(8,128)(2,1)S(1)}, u32[]{:S(2)}, u32[]{:S(2)}) collective-permute-start(bf16[1024,768]{1,0:T(8,128)(2,1)S(1)} %add_convert_fusion.4), channel_id=1, source_target_pairs={{0,8},{8,0},{16,24},{24,16},{1,9},{9,1},{17,25},{25,17},{2,10},{10... | collective-permute-start | bytes 4718600 | tf_op jit(solution)/shard_map/ppermute | solution.py:980
  707.7 12.9 %collective-permute-start.39 = (bf16[1024,768]{1,0:T(8,128)(2,1)S(1)}, bf16[1024,768]{1,0:T(8,128)(2,1)S(1)}, u32[]{:S(2)}, u32[]{:S(2)}) collective-permute-start(bf16[1024,768]{1,0:T(8,128)(2,1)S(1)} %add_convert_fusion.2), channel_id=1, source_target_pairs={{0,8},{8,0},{16,24},{24,16},{1,9},{9,1},{17,25},{25,17},{2,10},{10... | collective-permute-start | bytes 4718600 | tf_op jit(solution)/shard_map/ppermute | solution.py:980
  (49 other events, 169.5 us)

commit v4 on v3

--- a/solution.py
+++ b/solution.py
@@ -254,15 +254,15 @@
     blocks = 2 * outer
     (gated, out_proj, hidden_ref, gain_ref, gate_in, up_in, down_in) = refs[:7]
     ups_in = refs[7 : 7 + blocks]
-    (middle_out, grad_out, gain_out, branch, inner_out, dw_gate, dw_up, dw_down) = refs[
-        7 + blocks : 15 + blocks
+    (middle_out, grad_out, gain_out, branch, inner_out, dw_both, dw_down) = refs[
+        7 + blocks : 14 + blocks
     ]
     (
         w_gate, w_up, w_down, ups, rows, grad_inner, inner, grad_gate, grad_up,
         near_stage, near_got, far_stage, far_got, far_keep, own_keep,
         keep, y_stage, y_got, z_stage, z_got,
         load_sem, store_sem, tp_send, tp_recv, zs, zr, ys, yr, rys, ryr, rzs, rzr,
-    ) = refs[15 + blocks :]
+    ) = refs[14 + blocks :]
     stage_gate, stage_up, stage_down = w_gate, w_up, w_down
     quarter, model = hidden_ref.shape
     group = 2 * quarter
@@ -460,8 +460,8 @@
     def gate_up_stores(c):
         at = aligned(c, chunk)
         return (
-            pltpu.make_async_copy(stage_gate.at[at, :], dw_gate.at[at, :], store_sem.at[1 + 2 * c]),
-            pltpu.make_async_copy(stage_up.at[at, :], dw_up.at[at, :], store_sem.at[2 + 2 * c]),
+            pltpu.make_async_copy(stage_gate.at[at, :], dw_both.at[0, at, :], store_sem.at[1 + 2 * c]),
+            pltpu.make_async_copy(stage_up.at[at, :], dw_both.at[1, at, :], store_sem.at[2 + 2 * c]),
         )
 
     def weight_chunk(c):
@@ -577,12 +577,11 @@
             jax.ShapeDtypeStruct((1, model), F32),
             jax.ShapeDtypeStruct((sides, 2, quarter, model), BF16),
             jax.ShapeDtypeStruct((rows_n, units), BF16),
-            jax.ShapeDtypeStruct((model, units), BF16),
-            jax.ShapeDtypeStruct((model, units), BF16),
+            jax.ShapeDtypeStruct((2, model, units), BF16),
             jax.ShapeDtypeStruct((units, model), BF16),
         ],
         in_specs=[vmem] * 4 + [anywhere] * (3 + len(ups)),
-        out_specs=[vmem] * 4 + [anywhere] * 4,
+        out_specs=[vmem] * 4 + [anywhere] * 3,
         scratch_shapes=[
             pltpu.VMEM((model, units), BF16),
             pltpu.VMEM((model, units), BF16),
@@ -1158,16 +1157,17 @@
     layer_out = gather_tp((middle + mlp_quarter).astype(BF16))
 
     def reduce_tp(part):
-        half = part.shape[0] // 2
-        keep = lax.dynamic_slice_in_dim(part, core_i * half, half)
-        send = lax.dynamic_slice_in_dim(part, (1 - core_i) * half, half)
-        keep = (keep.astype(F32) + core(send.astype(BF16)).astype(F32)).astype(BF16)
-        keep = (keep.astype(F32) + side(keep).astype(F32)).astype(BF16)
+        half = part.shape[1] // 2
+        keep = lax.dynamic_slice_in_dim(part, core_i * half, half, 1)
+        send = lax.dynamic_slice_in_dim(part, (1 - core_i) * half, half, 1)
+        return (keep.astype(F32) + core(send.astype(BF16)).astype(F32)).astype(BF16)
+
+    def whole_tp(keep, far):
+        keep = (keep.astype(F32) + far.astype(F32)).astype(BF16)
         near = core(keep)
-        total = jnp.where(
-            core_i == 1, jnp.concatenate([near, keep]), jnp.concatenate([keep, near])
-        )
-        return total.astype(F32)
+        return jnp.where(
+            core_i == 1, jnp.concatenate([near, keep], 1), jnp.concatenate([keep, near], 1)
+        ).astype(F32)
 
     if not fused:
         rows_all = jnp.concatenate(rows_list)
@@ -1176,11 +1176,10 @@
         gate_all = jnp.concatenate(gate_list)
         grad_up_all = jnp.concatenate(grad_up_list)
         ffn_parts = [
-            outer_sum(rows_all, gate_all),
-            outer_sum(rows_all, grad_up_all),
+            jnp.stack([outer_sum(rows_all, gate_all), outer_sum(rows_all, grad_up_all)]),
             outer_sum(inner_all, up_all),
         ]
-    ffn_gate_grad, ffn_up_grad, ffn_down_grad = [reduce_tp(part) for part in ffn_parts]
+    ffn_halves = [reduce_tp(ffn_parts[0]), reduce_tp(ffn_parts[1][None])]
 
     branch_other = swap_half(grad_branch)
     branch_own = lax.dynamic_slice_in_dim(grad_branch, pair_i * (model // 2), model // 2, 1)
@@ -1199,6 +1198,8 @@
     def down_pairs(step):
         return [(b, a) for a, b in up_pairs(step)]
 
+    grad_mixed, ffn_halves = lax.optimization_barrier((grad_mixed, ffn_halves))
+    ffn_halves = [(keep, side(keep)) for keep in ffn_halves]
     query_acc = None
     travelling = None
     for k in list(range(reach, -1, -1)):
@@ -1223,6 +1224,10 @@
     grad_query_low = grad_query_raw.reshape(rows_dev, heads * head_width).astype(BF16)
     grad_key_low = grad_key_raw.reshape(rows_dev, group_width).astype(BF16)
     grad_kv_low = jnp.concatenate([grad_key_low, grad_value_low], axis=1)
+    grad_query_low, grad_kv_low, ffn_halves = lax.optimization_barrier(
+        (grad_query_low, grad_kv_low, ffn_halves)
+    )
+    ffn_grads = [whole_tp(*halves) for halves in ffn_halves]
 
     both_queries = jnp.concatenate([grad_query_low, pair(grad_query_low)])
     both_kv = jnp.concatenate([grad_kv_low, pair(grad_kv_low)])
@@ -1247,6 +1252,7 @@
             jnp.sum(key_gain_terms, axis=(0, 1)),
         ]
     )
+    parts, ffn_grads = lax.optimization_barrier((parts, ffn_grads))
     gains_at = 2 * model + 2 * head_width
     gains = jnp.pad(gains, (0, -gains_at % 1024)).reshape(-1, 128)
     scales_quarter = lax.dynamic_slice_in_dim(attn_scales, quarter_first, quarter)
@@ -1283,9 +1289,9 @@
         gains[2 * model : 2 * model + head_width],
         gains[2 * model + head_width : gains_at],
         gains[model : 2 * model],
-        ffn_gate_grad,
-        ffn_up_grad,
-        ffn_down_grad,
+        ffn_grads[0][0],
+        ffn_grads[0][1],
+        ffn_grads[1][0],
     )
 
 

time: 731 us -> 754 us (1.031)
  waiting for transfers between devices: 103 us -> 178 us
  Pallas kernels: 368 us -> 310 us
  local copies, waits for them, and re-layouts: 53.2 us -> 67.5 us
    pallas_call x1, Pallas kernels: 208 us -> 149 us  [finish(): pl.pallas_call(functools.partial(finish_kernel, outer, sides, sp_n, tp_n,...]
    ppermute x20, waiting for transfers between devices: 57.9 us -> 107 us  [pair(): return lax.ppermute(value, 'sp', pair_pairs)]
    ppermute x4 -> x3, waiting for transfers between devices: 0.01 us -> 46.3 us  [side(): return lax.ppermute(value, 'tp', side_pairs)]
    ppermute x6, waiting for transfers between devices: 37.9 us -> 6.9 us  [ring(): return lax.ppermute(value, 'sp', ring_pairs)]
    squeeze x0 -> x1, local copies, waits for them, and re-layouts: none -> 10.2 us  [body(): ffn_grads[0][1]]
    ppermute x2, waiting for transfers between devices: 7.35 us -> 17 us  [body(): travelling = lax.ppermute(total.astype(BF16), 'sp', down_pairs(k))]
    convert_element_type x9 -> x6, other arithmetic: 24.7 us -> 19.9 us  [the longest x2 8.72 us: whole_tp(): return jnp.where(core_i == 1, jnp.concatenate([near, keep], 1), jnp.conca...]
  transfers between devices with their start and end apart: 43 -> 40, of which waited for: 11 -> 14; matrix products, arithmetic and copies ran while one was open for 22% -> 18% of each run, Pallas kernels for 51% -> 4%
where the time goes in v4:
time: 754 us; the launch traced here: 746 us
  Pallas kernels  310 us (41%)
  waiting for transfers between devices  178 us (24%)
  other arithmetic  85.6 us (11%)
  local copies, waits for them, and re-layouts  67.5 us (9%)
  starting transfers between devices  55.1 us (7%)
  matrix products  40.3 us (5%)
  between operations  9.7 us (1%)
    pallas_call x1, Pallas kernels, finish(): pl.pallas_call(functools.partial(finish_kernel, outer, sides, sp_n, tp_n,...  149 us
    pallas_call x1, Pallas kernels, middle_layer(): pl.pallas_call(functools.partial(middle_kernel, outer), out_shape=[jax.Sh...  133 us
    ppermute x20, waiting for transfers between devices, pair(): return lax.ppermute(value, 'sp', pair_pairs)  107 us
    ppermute x3, waiting for transfers between devices, side(): return lax.ppermute(value, 'tp', side_pairs)  46.3 us
    ppermute x20, starting transfers between devices, pair(): return lax.ppermute(value, 'sp', pair_pairs)  28.2 us
    ppermute x2, waiting for transfers between devices, body(): travelling = lax.ppermute(total.astype(BF16), 'sp', down_pairs(k))  17 us
    dot_general x8, matrix products, matmul(): return jnp.dot(left, right, preferred_element_type=F32)  15.6 us
  transfers between devices with their start and end apart: 40, of which 14 were waited for; matrix products, arithmetic and copies ran while one was open for 18% of the time, Pallas kernels for 4%

profile of v4, /device:TPU:0, one launch (start us, length us, event | category | flops | bytes accessed | tf_op | source)
XLA Modules:
  0.0 745.8 jit_solution(8395859835777738388)
XLA Ops:
  2.1 2.0 convert_reduce_fusion
  4.1 2.1 fusion.1
  14.2 3.0 collective-permute-start.4
  17.2 4.3 collective-permute-start
  28.1 4.7 fusion.17
  32.9 2.3 multiply_reduce_fusion.1
  45.8 2.0 copy.107
  57.2 2.3 constant_dynamic-slice_fusion.2
  60.9 1.9 constant_dynamic-slice_fusion.6.refs_2_.refs_5_
  64.7 3.3 collective-permute-start.8
  73.4 4.6 attn_forward.3
  81.4 8.3 %collective-permute-start.10 = (bf16[128,2048]{1,0:T(8,128)(2,1)}, bf16[128,2048]{1,0:T(8,128)(2,1)}, u32[]{:S(2)}, u32[]{:S(2)}) collective-permute-start(bf16[128,2048]{1,0:T(8,128)(2,1)} %collective-permute-done.8.refs_11_), channel_id=1, source_target_pairs={{0,2},{1,3},{2,4},{3,5},{4,6},{5,7},{6,0},{7,1},{8,10},{9,11},{10,... | collective-permute-start | bytes 1572872 | tf_op jit(solution)/shard_map/ppermute | solution.py:970
  89.6 2.5 maximum_select_fusion.6
  92.6 3.8 attn_forward.4
  96.5 10.3 %collective-permute-done.2.kv_b = bf16[2,512,256]{2,1,0:T(8,128)(2,1)S(1)} collective-permute-done((bf16[2,512,256]{2,1,0:T(8,128)(2,1)}, bf16[2,512,256]{2,1,0:T(8,128)(2,1)S(1)}, u32[]{:S(2)}, u32[]{:S(2)}) %collective-permute-start.2) | collective-permute-done | bytes 524320 | tf_op jit(solution)/shard_map/ppermute | solution.py:973
  107.5 3.8 attn_forward.5
  115.5 3.4 multiply_convert_fusion.1
  118.9 10.4 %collective-permute-done.9.refs_12_ = bf16[128,2048]{1,0:T(8,128)(2,1)} collective-permute-done((bf16[128,2048]{1,0:T(8,128)(2,1)}, bf16[128,2048]{1,0:T(8,128)(2,1)}, u32[]{:S(2)}, u32[]{:S(2)}) %collective-permute-start.9) | collective-permute-done | bytes 524320 | tf_op jit(solution)/shard_map/ppermute | solution.py:973
  129.3 10.7 %collective-permute-done.11.refs_14_ = bf16[128,2048]{1,0:T(8,128)(2,1)S(1)} collective-permute-done((bf16[128,2048]{1,0:T(8,128)(2,1)}, bf16[128,2048]{1,0:T(8,128)(2,1)S(1)}, u32[]{:S(2)}, u32[]{:S(2)}) %collective-permute-start.11) | collective-permute-done | bytes 524320 | tf_op jit(solution)/shard_map/ppermute | solution.py:973
  140.8 133.5 %middle.1 = (f32[128,2048]{1,0:T(8,128)}, f32[128,2048]{1,0:T(8,128)}, f32[1,2048]{1,0:T(1,128)}, bf16[2,2,128,2048]{3,2,1,0:T(8,128)(2,1)}, bf16[1024,768]{1,0:...) custom-call(bf16[512,512]{1,0:T(8,128)(2,1)} %get-tuple-element.104.refs_0_, ...), custom_call_target="tpu_custom_call" | custom-call | flops 30000001024 | bytes 40000000 | tf_op jit(solution)/shard_map/middle/pallas_call | solution.py:572
  274.3 2.1 fusion.50
  280.0 2.7 convert_multiply_fusion.3
  291.6 39.6 %collective-permute-done.12 = bf16[128,2048]{1,0:T(8,128)(2,1)S(1)} collective-permute-done((bf16[128,2048]{1,0:T(8,128)(2,1)S(1)}, bf16[128,2048]{1,0:T(8,128)(2,1)S(1)}, u32[]{:S(2)}, u32[]{:S(2)}) %collective-permute-start.12) | collective-permute-done | bytes 524320 | tf_op jit(solution)/shard_map/ppermute | solution.py:973
  334.8 2.3 fusion.48
  337.1 4.8 collective-permute-done.14
  341.9 4.1 collective-permute-done.13
  346.9 4.3 fusion.69
  364.2 3.5 convolution_convert_fusion.2.refs_1_
  367.7 2.0 maximum_select_fusion.5
  369.7 3.8 collective-permute-done.21
  373.5 2.2 fusion.12.refs_0_
  375.7 8.5 %collective-permute-done.18 = bf16[128,2048]{1,0:T(8,128)(2,1)S(1)} collective-permute-done((bf16[128,2048]{1,0:T(8,128)(2,1)S(1)}, bf16[128,2048]{1,0:T(8,128)(2,1)S(1)}, u32[]{:S(2)}, u32[]{:S(2)}) %collective-permute-start.18) | collective-permute-done | bytes 524320 | tf_op jit(solution)/shard_map/ppermute | solution.py:973
  387.8 10.2 %collective-permute-done.19 = bf16[128,2048]{1,0:T(8,128)(2,1)S(1)} collective-permute-done((bf16[128,2048]{1,0:T(8,128)(2,1)S(1)}, bf16[128,2048]{1,0:T(8,128)(2,1)S(1)}, u32[]{:S(2)}, u32[]{:S(2)}) %collective-permute-start.19) | collective-permute-done | bytes 524320 | tf_op jit(solution)/shard_map/ppermute | solution.py:976
  399.2 4.4 add_convert_fusion.1
  403.6 3.8 attn_backward.3
  410.1 3.8 attn_backward.4
  416.0 7.3 attn_backward.5
  423.4 2.1 add_convert_fusion.4
  429.5 4.7 collective-permute-start.29
  435.9 2.3 add_convert_fusion.3
  439.5 2.1 multiply_reduce_fusion
  441.7 2.7 copy.99
  445.7 2.7 fusion.23
  448.4 3.3 maximum_select_fusion.2
  451.8 17.0 %collective-permute-done.33 = bf16[2,512,256]{2,1,0:T(8,128)(2,1)} collective-permute-done((bf16[2,512,256]{2,1,0:T(8,128)(2,1)}, bf16[2,512,256]{2,1,0:T(8,128)(2,1)}, u32[]{:S(2)}, u32[]{:S(2)}) %collective-permute-start.33) | collective-permute-done | bytes 524320 | tf_op jit(solution)/shard_map/ppermute | solution.py:1214
  471.0 2.0 copy.116
  474.2 1.9 pad_maximum_fusion.7
  476.1 2.0 copy.115
  482.4 36.1 %collective-permute-done.35 = bf16[1,384,2048]{2,1,0:T(8,128)(2,1)} collective-permute-done((bf16[1,384,2048]{2,1,0:T(8,128)(2,1)}, bf16[1,384,2048]{2,1,0:T(8,128)(2,1)}, u32[]{:S(2)}, u32[]{:S(2)}) %collective-permute-start.35) | collective-permute-done | bytes 1572896 | tf_op jit(solution)/shard_map/ppermute | solution.py:976
  518.5 2.9 add_convert_fusion
  522.8 2.1 add_convert_fusion.2
  528.0 3.6 fusion.5
  532.2 19.3 %collective-permute-done.36 = bf16[512,512]{0,1:T(8,128)(2,1)} collective-permute-done((bf16[512,512]{0,1:T(8,128)(2,1)S(1)}, bf16[512,512]{0,1:T(8,128)(2,1)}, u32[]{:S(2)}, u32[]{:S(2)}) %collective-permute-start.36) | collective-permute-done | bytes 524320 | tf_op jit(solution)/shard_map/ppermute | solution.py:973
  551.6 3.6 convolution_convert_fusion.1.refs_2_
  555.2 3.3 convolution_convert_fusion.refs_3_
  558.5 3.6 fusion.6
  562.2 5.1 fusion
  567.2 149.4 %finish.1 = (bf16[2,512,1024]{2,1,0:T(8,128)(2,1)}, bf16[2,1024,512]{2,1,0:T(8,128)(2,1)}, bf16[2,1024,512]{2,1,0:T(8,128)(2,1)}, bf16[2,1024,512]{2,1,0:T(8,128...) custom-call(bf16[512,1024]{1,0:T(8,128)(2,1)} %fusion.12.refs_0_, ...), custom_call_target="tpu_custom_call" | custom-call | flops 1000000000 | bytes 100000000 | tf_op jit(solution)/shard_map/finish/pallas_call | solution.py:895
  719.2 4.3 bitcast_convert_fusion.2
  725.1 2.7 bitcast_convert_fusion.1
  727.8 2.7 bitcast_convert_fusion
  730.6 2.3 slice_convert_fusion
  732.9 10.2 %slice_bitcast_fusion = (f32[2048,768]{1,0:T(8,128)}, f32[2048,768]{1,0:T(8,128)}) fusion(f32[2,2048,768]{2,1,0:T(8,128)} %fusion), kind=kLoop, calls=%fused_computation.2 | loop fusion | bytes 25165824 | tf_op jit(solution)/shard_map/squeeze | solution.py:1293
  743.0 2.5 maximum_convert_fusion
  (289 shorter events, 110.8 us)
Async XLA Ops:
  0.6 32.2 %copy-start = (bf16[2048,512]{1,0:T(8,128)(2,1)S(1)}, bf16[2048,512]{1,0:T(8,128)(2,1)}, u32[]{:S(2)}) copy-start(bf16[2048,512]{1,0:T(8,128)(2,1)} %param.18) | copy-start | bytes 6291460
  6.2 35.6 %copy-start.52 = (f32[512]{0:T(512)}, f32[512]{0:T(512)S(1)}, u32[]{:S(2)}) copy-start(f32[512]{0:T(512)S(1)} %add_rsqrt_fusion.2) | copy-start | bytes 6148
  12.0 14.6 %copy-start.26 = (f32[512,64]{0,1:T(8,128)}, f32[512,64]{0,1:T(8,128)S(1)}, u32[]{:S(2)}) copy-start(f32[512,64]{0,1:T(8,128)S(1)} %get-tuple-element.138) | copy-start | bytes 393220
  14.2 57.1 %collective-permute-start.4 = (bf16[2,512,256]{2,1,0:T(8,128)(2,1)}, bf16[2,512,256]{2,1,0:T(8,128)(2,1)}, u32[]{:S(2)}, u32[]{:S(2)}) collective-permute-start(bf16[2,512,256]{2,1,0:T(8,128)(2,1)} %pad_maximum_fusion.6.kv_a), channel_id=1, source_target_pairs={{0,1},{1,0},{2,3},{3,2},{4,5},{5,4},{6,7},{7,6},{8,9},{9,8},{10,11... | collective-permute-start | bytes 1572872 | tf_op jit(solution)/shard_map/ppermute | solution.py:973
  17.2 45.5 %collective-permute-start = (bf16[2,512,256]{2,1,0:T(8,128)(2,1)}, bf16[2,512,256]{2,1,0:T(8,128)(2,1)}, u32[]{:S(2)}, u32[]{:S(2)}) collective-permute-start(bf16[2,512,256]{2,1,0:T(8,128)(2,1)} %pad_maximum_fusion.6.kv_a), channel_id=1, source_target_pairs={{0,2},{1,3},{2,4},{3,5},{4,6},{5,7},{8,10},{9,11},{10,12},{11,13},... | collective-permute-start | bytes 1572872 | tf_op jit(solution)/shard_map/ppermute | solution.py:1033
  23.4 41.3 %collective-permute-start.6 = (bf16[128,2048]{1,0:T(8,128)(2,1)}, bf16[128,2048]{1,0:T(8,128)(2,1)}, u32[]{:S(2)}, u32[]{:S(2)}) collective-permute-start(bf16[128,2048]{1,0:T(8,128)(2,1)} %constant_dynamic-slice_fusion.5.refs_7_), channel_id=1, source_target_pairs={{0,2},{1,3},{2,4},{3,5},{4,6},{5,7},{6,0},{7,1},{8,10},{9,11},{10,... | collective-permute-start | bytes 1572872 | tf_op jit(solution)/shard_map/ppermute | solution.py:970
  26.0 42.0 %collective-permute-start.24 = (bf16[512,512]{1,0:T(8,128)(2,1)}, bf16[512,512]{1,0:T(8,128)(2,1)}, u32[]{:S(2)}, u32[]{:S(2)}) collective-permute-start(bf16[512,512]{1,0:T(8,128)(2,1)} %constant_dynamic-slice_fusion.1), channel_id=1, source_target_pairs={{0,1},{1,0},{2,3},{3,2},{4,5},{5,4},{6,7},{7,6},{8,9},{9,8},{10,11... | collective-permute-start | bytes 1572872 | tf_op jit(solution)/shard_map/ppermute | solution.py:973
  41.0 11.5 %copy-start.54 = (f32[512,2]{0,1:T(2,128)S(1)}, f32[512,2]{0,1:T(2,128)}, u32[]{:S(2)}) copy-start(f32[512,2]{0,1:T(2,128)} %get-tuple-element.135) | copy-start | bytes 12292
  54.4 9.8 %copy-start.57 = (f32[128]{0:T(128)S(1)}, f32[128]{0:T(128)}, u32[]{:S(2)}) copy-start(f32[128]{0:T(128)} %param.23) | copy-start | bytes 1540
  54.4 16.4 %copy-start.60 = (f32[128]{0:T(128)S(1)}, f32[128]{0:T(128)}, u32[]{:S(2)}) copy-start(f32[128]{0:T(128)} %param.24) | copy-start | bytes 1540
  62.8 9.1 %collective-permute-start.1 = (bf16[2,512,256]{2,1,0:T(8,128)(2,1)}, bf16[2,512,256]{2,1,0:T(8,128)(2,1)}, u32[]{:S(2)}, u32[]{:S(2)}) collective-permute-start(bf16[2,512,256]{2,1,0:T(8,128)(2,1)} %collective-permute-done.kv_a), channel_id=1, source_target_pairs={{2,4},{3,5},{4,6},{5,7},{10,12},{11,13},{12,14},{13,15},{18,20},{1... | collective-permute-start | bytes 1572872 | tf_op jit(solution)/shard_map/ppermute | solution.py:1033
  64.7 15.1 %collective-permute-start.8 = (bf16[128,2048]{1,0:T(8,128)(2,1)}, bf16[128,2048]{1,0:T(8,128)(2,1)}, u32[]{:S(2)}, u32[]{:S(2)}) collective-permute-start(bf16[128,2048]{1,0:T(8,128)(2,1)} %collective-permute-done.6.refs_9_), channel_id=1, source_target_pairs={{0,2},{1,3},{2,4},{3,5},{4,6},{5,7},{6,0},{7,1},{8,10},{9,11},{10,... | collective-permute-start | bytes 1572872 | tf_op jit(solution)/shard_map/ppermute | solution.py:970
  68.0 13.4 %collective-permute-start.25 = (bf16[512,512]{1,0:T(8,128)(2,1)}, bf16[512,512]{1,0:T(8,128)(2,1)S(1)}, u32[]{:S(2)}, u32[]{:S(2)}) collective-permute-start(bf16[512,512]{1,0:T(8,128)(2,1)} %collective-permute-done.24), channel_id=1, source_target_pairs={{0,8},{8,0},{16,24},{24,16},{1,9},{9,1},{17,25},{25,17},{2,10},{10... | collective-permute-start | bytes 1572872 | tf_op jit(solution)/shard_map/ppermute | solution.py:979
  69.3 22.9 %collective-permute-start.3 = (bf16[2,512,256]{2,1,0:T(8,128)(2,1)}, bf16[2,512,256]{2,1,0:T(8,128)(2,1)}, u32[]{:S(2)}, u32[]{:S(2)}) collective-permute-start(bf16[2,512,256]{2,1,0:T(8,128)(2,1)} %collective-permute-done.kv_a), channel_id=1, source_target_pairs={{0,1},{1,0},{2,3},{3,2},{4,5},{5,4},{6,7},{7,6},{8,9},{9,8},{10,11... | collective-permute-start | bytes 1572872 | tf_op jit(solution)/shard_map/ppermute | solution.py:973
  71.4 47.5 %collective-permute-start.5 = (bf16[128,2048]{1,0:T(8,128)(2,1)}, bf16[128,2048]{1,0:T(8,128)(2,1)}, u32[]{:S(2)}, u32[]{:S(2)}) collective-permute-start(bf16[128,2048]{1,0:T(8,128)(2,1)} %constant_dynamic-slice_fusion.5.refs_7_), channel_id=1, source_target_pairs={{0,1},{1,0},{2,3},{3,2},{4,5},{5,4},{6,7},{7,6},{8,9},{9,8},{10,11... | collective-permute-start | bytes 1572872 | tf_op jit(solution)/shard_map/ppermute | solution.py:973
  71.9 34.8 %collective-permute-start.2 = (bf16[2,512,256]{2,1,0:T(8,128)(2,1)}, bf16[2,512,256]{2,1,0:T(8,128)(2,1)S(1)}, u32[]{:S(2)}, u32[]{:S(2)}) collective-permute-start(bf16[2,512,256]{2,1,0:T(8,128)(2,1)} %collective-permute-done.1.kv_a), channel_id=1, source_target_pairs={{0,1},{1,0},{2,3},{3,2},{4,5},{5,4},{6,7},{7,6},{8,9},{9,8},{10,11... | collective-permute-start | bytes 1572872 | tf_op jit(solution)/shard_map/ppermute | solution.py:973
  79.8 39.0 %collective-permute-start.7 = (bf16[128,2048]{1,0:T(8,128)(2,1)}, bf16[128,2048]{1,0:T(8,128)(2,1)}, u32[]{:S(2)}, u32[]{:S(2)}) collective-permute-start(bf16[128,2048]{1,0:T(8,128)(2,1)} %collective-permute-done.6.refs_9_), channel_id=1, source_target_pairs={{0,1},{1,0},{2,3},{3,2},{4,5},{5,4},{6,7},{7,6},{8,9},{9,8},{10,11... | collective-permute-start | bytes 1572872 | tf_op jit(solution)/shard_map/ppermute | solution.py:973
  81.4 31.9 %collective-permute-start.10 = (bf16[128,2048]{1,0:T(8,128)(2,1)}, bf16[128,2048]{1,0:T(8,128)(2,1)}, u32[]{:S(2)}, u32[]{:S(2)}) collective-permute-start(bf16[128,2048]{1,0:T(8,128)(2,1)} %collective-permute-done.8.refs_11_), channel_id=1, source_target_pairs={{0,2},{1,3},{2,4},{3,5},{4,6},{5,7},{6,0},{7,1},{8,10},{9,11},{10,... | collective-permute-start | bytes 1572872 | tf_op jit(solution)/shard_map/ppermute | solution.py:970
  92.1 37.2 %collective-permute-start.9 = (bf16[128,2048]{1,0:T(8,128)(2,1)}, bf16[128,2048]{1,0:T(8,128)(2,1)}, u32[]{:S(2)}, u32[]{:S(2)}) collective-permute-start(bf16[128,2048]{1,0:T(8,128)(2,1)} %collective-permute-done.8.refs_11_), channel_id=1, source_target_pairs={{0,1},{1,0},{2,3},{3,2},{4,5},{5,4},{6,7},{7,6},{8,9},{9,8},{10,11... | collective-permute-start | bytes 1572872 | tf_op jit(solution)/shard_map/ppermute | solution.py:973
  113.3 26.7 %collective-permute-start.11 = (bf16[128,2048]{1,0:T(8,128)(2,1)}, bf16[128,2048]{1,0:T(8,128)(2,1)S(1)}, u32[]{:S(2)}, u32[]{:S(2)}) collective-permute-start(bf16[128,2048]{1,0:T(8,128)(2,1)} %collective-permute-done.10.refs_13_), channel_id=1, source_target_pairs={{0,1},{1,0},{2,3},{3,2},{4,5},{5,4},{6,7},{7,6},{8,9},{9,8},{10,11... | collective-permute-start | bytes 1572872 | tf_op jit(solution)/shard_map/ppermute | solution.py:973
  140.8 133.5 %copy-start.1 = (bf16[768,2048]{1,0:T(8,128)(2,1)S(1)}, bf16[768,2048]{1,0:T(8,128)(2,1)}, u32[]{:S(2)}) copy-start(bf16[768,2048]{1,0:T(8,128)(2,1)} %refs_6_.1) | copy-start | bytes 9437188
  276.4 8.4 %copy-start.11 = (f32[256,2048]{1,0:T(8,128)}, f32[256,2048]{1,0:T(8,128)S(1)}, u32[]{:S(2)}) copy-start(f32[256,2048]{1,0:T(8,128)S(1)} %fusion.50) | copy-start | bytes 6291460
  282.7 68.5 %collective-permute-start.22 = (bf16[512,512]{1,0:T(8,128)(2,1)S(1)}, bf16[512,512]{1,0:T(8,128)(2,1)}, u32[]{:S(2)}, u32[]{:S(2)}) collective-permute-start(bf16[512,512]{1,0:T(8,128)(2,1)S(1)} %constant_dynamic-slice_fusion.3), channel_id=1, source_target_pairs={{0,1},{1,0},{2,3},{3,2},{4,5},{5,4},{6,7},{7,6},{8,9},{9,8},{10,11... | collective-permute-start | bytes 1572872 | tf_op jit(solution)/shard_map/ppermute | solution.py:973
  284.2 78.4 %collective-permute-start.26 = (bf16[512,512]{1,0:T(8,128)(2,1)}, bf16[512,512]{1,0:T(8,128)(2,1)}, u32[]{:S(2)}, u32[]{:S(2)}) collective-permute-start(bf16[512,512]{1,0:T(8,128)(2,1)} %get-tuple-element.110), channel_id=1, source_target_pairs={{0,1},{1,0},{2,3},{3,2},{4,5},{5,4},{6,7},{7,6},{8,9},{9,8},{10,11... | collective-permute-start | bytes 1572872 | tf_op jit(solution)/shard_map/ppermute | solution.py:973
  285.6 72.8 %collective-permute-start.16 = (bf16[128,2048]{1,0:T(8,128)(2,1)}, bf16[128,2048]{1,0:T(8,128)(2,1)}, u32[]{:S(2)}, u32[]{:S(2)}) collective-permute-start(bf16[128,2048]{1,0:T(8,128)(2,1)} %slice.256), channel_id=1, source_target_pairs={{0,1},{1,0},{2,3},{3,2},{4,5},{5,4},{6,7},{7,6},{8,9},{9,8},{10,11... | collective-permute-start | bytes 1572872 | tf_op jit(solution)/shard_map/ppermute | solution.py:973
  287.1 45.8 %slice-start = ((s8[6291456]{0:T(1024)(128)(4,1)}), s8[4194304]{0:T(1024)(128)(4,1)S(1)}, s32[]{:S(2)}) async-start(s8[6291456]{0:T(1024)(128)(4,1)} %bitcast.165), calls=%async_computation | async-start | bytes 8388608
  287.2 45.8 %slice-start.1 = ((s8[6291456]{0:T(1024)(128)(4,1)}), s8[2097152]{0:T(1024)(128)(4,1)S(1)}, s32[]{:S(2)}) async-start(s8[6291456]{0:T(1024)(128)(4,1)} %bitcast.165), calls=%async_computation.1 | async-start | bytes 4194304
  287.2 44.1 %collective-permute-start.12 = (bf16[128,2048]{1,0:T(8,128)(2,1)S(1)}, bf16[128,2048]{1,0:T(8,128)(2,1)S(1)}, u32[]{:S(2)}, u32[]{:S(2)}) collective-permute-start(bf16[128,2048]{1,0:T(8,128)(2,1)S(1)} %slice.258), channel_id=1, source_target_pairs={{0,1},{1,0},{2,3},{3,2},{4,5},{5,4},{6,7},{7,6},{8,9},{9,8},{10,11... | collective-permute-start | bytes 1572872 | tf_op jit(solution)/shard_map/ppermute | solution.py:973
  288.8 53.0 %collective-permute-start.14 = (bf16[128,2048]{1,0:T(8,128)(2,1)S(1)}, bf16[128,2048]{1,0:T(8,128)(2,1)S(1)}, u32[]{:S(2)}, u32[]{:S(2)}) collective-permute-start(bf16[128,2048]{1,0:T(8,128)(2,1)S(1)} %slice.257), channel_id=1, source_target_pairs={{0,1},{1,0},{2,3},{3,2},{4,5},{5,4},{6,7},{7,6},{8,9},{9,8},{10,11... | collective-permute-start | bytes 1572872 | tf_op jit(solution)/shard_map/ppermute | solution.py:973
  331.3 14.6 %collective-permute-start.13 = (bf16[128,2048]{1,0:T(8,128)(2,1)S(1)}, bf16[128,2048]{1,0:T(8,128)(2,1)S(1)}, u32[]{:S(2)}, u32[]{:S(2)}) collective-permute-start(bf16[128,2048]{1,0:T(8,128)(2,1)S(1)} %fusion.31), channel_id=1, source_target_pairs={{0,2},{1,3},{2,4},{3,5},{4,6},{5,7},{6,0},{7,1},{8,10},{9,11},{10,... | collective-permute-start | bytes 1572872 | tf_op jit(solution)/shard_map/ppermute | solution.py:970
  337.1 9.8 %copy-start.28 = (bf16[2048,512]{1,0:T(8,128)(2,1)S(1)}, bf16[2048,512]{1,0:T(8,128)(2,1)}, u32[]{:S(2)}) copy-start(bf16[2048,512]{1,0:T(8,128)(2,1)} %param.21) | copy-start | bytes 6291460
  341.9 57.3 %collective-permute-start.27 = (bf16[2,1024,768]{2,1,0:T(8,128)(2,1)}, bf16[2,1024,768]{2,1,0:T(8,128)(2,1)}, u32[]{:S(2)}, u32[]{:S(2)}) collective-permute-start(bf16[2,1024,768]{2,1,0:T(8,128)(2,1)} %constant_dynamic-slice_fusion), channel_id=1, source_target_pairs={{0,8},{8,0},{16,24},{24,16},{1,9},{9,1},{17,25},{25,17},{2,10},{10... | collective-permute-start | bytes 9437192 | tf_op jit(solution)/shard_map/ppermute | solution.py:979
  346.9 14.0 %collective-permute-start.15 = (bf16[128,2048]{1,0:T(8,128)(2,1)}, bf16[128,2048]{1,0:T(8,128)(2,1)}, u32[]{:S(2)}, u32[]{:S(2)}) collective-permute-start(bf16[128,2048]{1,0:T(8,128)(2,1)} %fusion.30), channel_id=1, source_target_pairs={{0,2},{1,3},{2,4},{3,5},{4,6},{5,7},{6,0},{7,1},{8,10},{9,11},{10,... | collective-permute-start | bytes 1572872 | tf_op jit(solution)/shard_map/ppermute | solution.py:970
  351.3 12.9 %collective-permute-start.23 = (bf16[512,512]{1,0:T(8,128)(2,1)}, bf16[512,512]{1,0:T(8,128)(2,1)}, u32[]{:S(2)}, u32[]{:S(2)}) collective-permute-start(bf16[512,512]{1,0:T(8,128)(2,1)} %collective-permute-done.22), channel_id=1, source_target_pairs={{0,8},{8,0},{16,24},{24,16},{1,9},{9,1},{17,25},{25,17},{2,10},{10... | collective-permute-start | bytes 1572872 | tf_op jit(solution)/shard_map/ppermute | solution.py:979
  355.2 9.0 %copy-start.32 = (bf16[512,1024]{1,0:T(8,128)(2,1)S(1)}, bf16[512,1024]{1,0:T(8,128)(2,1)}, u32[]{:S(2)}) copy-start(bf16[512,1024]{1,0:T(8,128)(2,1)} %constant_dynamic-slice_fusion.2) | copy-start | bytes 3145732
  357.0 7.2 copy-start.34
  358.4 15.1 %collective-permute-start.21 = (bf16[512,512]{1,0:T(8,128)(2,1)}, bf16[512,512]{1,0:T(8,128)(2,1)S(1)}, u32[]{:S(2)}, u32[]{:S(2)}) collective-permute-start(bf16[512,512]{1,0:T(8,128)(2,1)} %get-tuple-element.104.refs_0_), channel_id=1, source_target_pairs={{0,1},{1,0},{2,3},{3,2},{4,5},{5,4},{6,7},{7,6},{8,9},{9,8},{10,11... | collective-permute-start | bytes 1572872 | tf_op jit(solution)/shard_map/ppermute | solution.py:973
  360.9 25.2 %collective-permute-start.28 = (bf16[1,384,2048]{2,1,0:T(8,128)(2,1)}, bf16[1,384,2048]{2,1,0:T(8,128)(2,1)S(1)}, u32[]{:S(2)}, u32[]{:S(2)}) collective-permute-start(bf16[1,384,2048]{2,1,0:T(8,128)(2,1)} %dynamic-slice_bitcast_fusion), channel_id=1, source_target_pairs={{0,8},{8,0},{16,24},{24,16},{1,9},{9,1},{17,25},{25,17},{2,10},{10... | collective-permute-start | bytes 4718600 | tf_op jit(solution)/shard_map/ppermute | solution.py:979
  362.6 21.6 %collective-permute-start.18 = (bf16[128,2048]{1,0:T(8,128)(2,1)S(1)}, bf16[128,2048]{1,0:T(8,128)(2,1)S(1)}, u32[]{:S(2)}, u32[]{:S(2)}) collective-permute-start(bf16[128,2048]{1,0:T(8,128)(2,1)S(1)} %slice.255), channel_id=1, source_target_pairs={{0,1},{1,0},{2,3},{3,2},{4,5},{5,4},{6,7},{7,6},{8,9},{9,8},{10,11... | collective-permute-start | bytes 1572872 | tf_op jit(solution)/shard_map/ppermute | solution.py:973
  364.2 20.1 %collective-permute-start.17 = (bf16[128,2048]{1,0:T(8,128)(2,1)S(1)}, bf16[128,2048]{1,0:T(8,128)(2,1)S(1)}, u32[]{:S(2)}, u32[]{:S(2)}) collective-permute-start(bf16[128,2048]{1,0:T(8,128)(2,1)S(1)} %fusion.28), channel_id=1, source_target_pairs={{0,2},{1,3},{2,4},{3,5},{4,6},{5,7},{6,0},{7,1},{8,10},{9,11},{10,... | collective-permute-start | bytes 1572872 | tf_op jit(solution)/shard_map/ppermute | solution.py:970
  369.6 14.6 %copy-start.8 = (f32[256,2048]{1,0:T(8,128)S(1)}, f32[256,2048]{1,0:T(8,128)}, u32[]{:S(2)}) copy-start(f32[256,2048]{1,0:T(8,128)} %fusion.48) | copy-start | bytes 6291460
  369.6 14.6 %copy-start.31 = (f32[128,2048]{1,0:T(8,128)S(1)}, f32[128,2048]{1,0:T(8,128)}, u32[]{:S(2)}) copy-start(f32[128,2048]{1,0:T(8,128)} %get-tuple-element.63) | copy-start | bytes 3145732
  373.5 25.7 %slice-start.2 = ((s8[6291456]{0:T(1024)(128)(4,1)}), s8[4194304]{0:T(1024)(128)(4,1)S(1)}, s32[]{:S(2)}) async-start(s8[6291456]{0:T(1024)(128)(4,1)} %bitcast.167), calls=%async_computation.2 | async-start | bytes 8388608
  375.7 10.4 %copy-start.16 = (bf16[768,2048]{1,0:T(8,128)(2,1)S(1)}, bf16[768,2048]{1,0:T(8,128)(2,1)}, u32[]{:S(2)}) copy-start(bf16[768,2048]{1,0:T(8,128)(2,1)} %get-tuple-element.67) | copy-start | bytes 9437188
  384.2 15.0 %slice-start.3 = ((s8[6291456]{0:T(1024)(128)(4,1)}), s8[2097152]{0:T(1024)(128)(4,1)S(1)}, s32[]{:S(2)}) async-start(s8[6291456]{0:T(1024)(128)(4,1)} %bitcast.167), calls=%async_computation.3 | async-start | bytes 4194304
  384.5 13.5 %collective-permute-start.19 = (bf16[128,2048]{1,0:T(8,128)(2,1)S(1)}, bf16[128,2048]{1,0:T(8,128)(2,1)S(1)}, u32[]{:S(2)}, u32[]{:S(2)}) collective-permute-start(bf16[128,2048]{1,0:T(8,128)(2,1)S(1)} %fusion.26), channel_id=1, source_target_pairs={{0,16},{8,24},{16,0},{24,8},{1,17},{9,25},{17,1},{25,9},{2,18},{10... | collective-permute-start | bytes 1572872 | tf_op jit(solution)/shard_map/ppermute | solution.py:976
  399.2 49.2 %collective-permute-start.20 = (bf16[2,128,2048]{2,1,0:T(8,128)(2,1)}, bf16[2,128,2048]{2,1,0:T(8,128)(2,1)}, u32[]{:S(2)}, u32[]{:S(2)}) collective-permute-start(bf16[2,128,2048]{2,1,0:T(8,128)(2,1)} %maximum_select_fusion.3), channel_id=1, source_target_pairs={{0,8},{8,0},{16,24},{24,16},{1,9},{9,1},{17,25},{25,17},{2,10},{10... | collective-permute-start | bytes 3145736 | tf_op jit(solution)/shard_map/ppermute | solution.py:979
  407.4 15.9 %collective-permute-start.31 = (bf16[2,512,256]{2,1,0:T(8,128)(2,1)}, bf16[2,512,256]{2,1,0:T(8,128)(2,1)}, u32[]{:S(2)}, u32[]{:S(2)}) collective-permute-start(bf16[2,512,256]{2,1,0:T(8,128)(2,1)} %get-tuple-element.77), channel_id=1, source_target_pairs={{0,1},{1,0},{2,3},{3,2},{4,5},{5,4},{6,7},{7,6},{8,9},{9,8},{10,11... | collective-permute-start | bytes 1572872 | tf_op jit(solution)/shard_map/ppermute | solution.py:973
  413.9 22.0 %collective-permute-start.30 = (bf16[2,512,256]{2,1,0:T(8,128)(2,1)}, bf16[2,512,256]{2,1,0:T(8,128)(2,1)}, u32[]{:S(2)}, u32[]{:S(2)}) collective-permute-start(bf16[2,512,256]{2,1,0:T(8,128)(2,1)} %get-tuple-element.75), channel_id=1, source_target_pairs={{0,1},{1,0},{2,3},{3,2},{4,5},{5,4},{6,7},{7,6},{8,9},{9,8},{10,11... | collective-permute-start | bytes 1572872 | tf_op jit(solution)/shard_map/ppermute | solution.py:973
  414.5 104.0 %collective-permute-start.34 = (bf16[2,1024,768]{2,1,0:T(8,128)(2,1)}, bf16[2,1024,768]{2,1,0:T(8,128)(2,1)}, u32[]{:S(2)}, u32[]{:S(2)}) collective-permute-start(bf16[2,1024,768]{2,1,0:T(8,128)(2,1)} %add_convert_fusion.1), channel_id=1, source_target_pairs={{0,16},{8,24},{16,0},{24,8},{1,17},{9,25},{17,1},{25,9},{2,18},{10... | collective-permute-start | bytes 9437192 | tf_op jit(solution)/shard_map/ppermute | solution.py:976
  416.0 7.3 copy-start.47
  425.4 10.4 %collective-permute-start.32 = (bf16[2,512,256]{2,1,0:T(8,128)(2,1)}, bf16[2,512,256]{2,1,0:T(8,128)(2,1)}, u32[]{:S(2)}, u32[]{:S(2)}) collective-permute-start(bf16[2,512,256]{2,1,0:T(8,128)(2,1)} %add_convert_fusion.4), channel_id=1, source_target_pairs={{4,2},{5,3},{6,4},{7,5},{12,10},{13,11},{14,12},{15,13},{20,18},{2... | collective-permute-start | bytes 1572872 | tf_op jit(solution)/shard_map/ppermute | solution.py:1214
  429.5 22.3 %collective-permute-start.29 = (bf16[2,512,256]{2,1,0:T(8,128)(2,1)}, bf16[2,512,256]{2,1,0:T(8,128)(2,1)}, u32[]{:S(2)}, u32[]{:S(2)}) collective-permute-start(bf16[2,512,256]{2,1,0:T(8,128)(2,1)} %get-tuple-element.73), channel_id=1, source_target_pairs={{0,1},{1,0},{2,3},{3,2},{4,5},{5,4},{6,7},{7,6},{8,9},{9,8},{10,11... | collective-permute-start | bytes 1572872 | tf_op jit(solution)/shard_map/ppermute | solution.py:973
  438.2 30.6 %collective-permute-start.33 = (bf16[2,512,256]{2,1,0:T(8,128)(2,1)}, bf16[2,512,256]{2,1,0:T(8,128)(2,1)}, u32[]{:S(2)}, u32[]{:S(2)}) collective-permute-start(bf16[2,512,256]{2,1,0:T(8,128)(2,1)} %add_convert_fusion.3), channel_id=1, source_target_pairs={{2,0},{3,1},{4,2},{5,3},{6,4},{7,5},{10,8},{11,9},{12,10},{13,11},... | collective-permute-start | bytes 1572872 | tf_op jit(solution)/shard_map/ppermute | solution.py:1214
  441.7 6.7 copy-start.14
  444.4 74.1 %collective-permute-start.35 = (bf16[1,384,2048]{2,1,0:T(8,128)(2,1)}, bf16[1,384,2048]{2,1,0:T(8,128)(2,1)}, u32[]{:S(2)}, u32[]{:S(2)}) collective-permute-start(bf16[1,384,2048]{2,1,0:T(8,128)(2,1)} %fusion.7), channel_id=1, source_target_pairs={{0,16},{8,24},{16,0},{24,8},{1,17},{9,25},{17,1},{25,9},{2,18},{10... | collective-permute-start | bytes 4718600 | tf_op jit(solution)/shard_map/ppermute | solution.py:976
  448.4 20.4 %copy-start.46 = (bf16[2,512,256]{2,1,0:T(8,128)(2,1)S(1)}, bf16[2,512,256]{2,1,0:T(8,128)(2,1)}, u32[]{:S(2)}) copy-start(bf16[2,512,256]{2,1,0:T(8,128)(2,1)} %get-tuple-element.72) | copy-start | bytes 1572868
  481.2 37.2 %copy-start.5 = (bf16[2,1024,768]{2,1,0:T(8,128)(2,1)S(1)}, bf16[2,1024,768]{2,1,0:T(8,128)(2,1)}, u32[]{:S(2)}) copy-start(bf16[2,1024,768]{2,1,0:T(8,128)(2,1)} %add_convert_fusion.1) | copy-start | bytes 9437188
  521.4 40.8 %collective-permute-start.38 = (bf16[2,1024,768]{2,1,0:T(8,128)(2,1)S(1)}, bf16[2,1024,768]{2,1,0:T(8,128)(2,1)S(1)}, u32[]{:S(2)}, u32[]{:S(2)}) collective-permute-start(bf16[2,1024,768]{2,1,0:T(8,128)(2,1)S(1)} %add_convert_fusion), channel_id=1, source_target_pairs={{0,8},{8,0},{16,24},{24,16},{1,9},{9,1},{17,25},{25,17},{2,10},{10... | collective-permute-start | bytes 9437192 | tf_op jit(solution)/shard_map/ppermute | solution.py:979
  525.0 33.6 %collective-permute-start.39 = (bf16[1,384,2048]{2,1,0:T(8,128)(2,1)S(1)}, bf16[1,384,2048]{2,1,0:T(8,128)(2,1)S(1)}, u32[]{:S(2)}, u32[]{:S(2)}) collective-permute-start(bf16[1,384,2048]{2,1,0:T(8,128)(2,1)S(1)} %add_convert_fusion.2), channel_id=1, source_target_pairs={{0,8},{8,0},{16,24},{24,16},{1,9},{9,1},{17,25},{25,17},{2,10},{10... | collective-permute-start | bytes 4718600 | tf_op jit(solution)/shard_map/ppermute | solution.py:979
  526.0 25.6 %copy-start.33 = (bf16[512,1024]{1,0:T(8,128)(2,1)S(1)}, bf16[512,1024]{1,0:T(8,128)(2,1)}, u32[]{:S(2)}) copy-start(bf16[512,1024]{1,0:T(8,128)(2,1)} %constant_dynamic-slice_fusion.2) | copy-start | bytes 3145732
  526.0 29.2 %collective-permute-start.37 = (bf16[512,512]{1,0:T(8,128)(2,1)S(1)}, bf16[512,512]{1,0:T(8,128)(2,1)}, u32[]{:S(2)}, u32[]{:S(2)}) collective-permute-start(bf16[512,512]{1,0:T(8,128)(2,1)S(1)} %copy-done.48), channel_id=1, source_target_pairs={{0,1},{1,0},{2,3},{3,2},{4,5},{5,4},{6,7},{7,6},{8,9},{9,8},{10,11... | collective-permute-start | bytes 1572872 | tf_op jit(solution)/shard_map/ppermute | solution.py:973
  527.4 24.1 %collective-permute-start.36 = (bf16[512,512]{0,1:T(8,128)(2,1)S(1)}, bf16[512,512]{0,1:T(8,128)(2,1)}, u32[]{:S(2)}, u32[]{:S(2)}) collective-permute-start(bf16[512,512]{0,1:T(8,128)(2,1)S(1)} %copy-done.25), channel_id=1, source_target_pairs={{0,1},{1,0},{2,3},{3,2},{4,5},{5,4},{6,7},{7,6},{8,9},{9,8},{10,11... | collective-permute-start | bytes 1572872 | tf_op jit(solution)/shard_map/ppermute | solution.py:973
  532.2 23.0 %copy-start.35 = (bf16[512,1024]{1,0:T(8,128)(2,1)S(1)}, bf16[512,1024]{1,0:T(8,128)(2,1)}, u32[]{:S(2)}) copy-start(bf16[512,1024]{1,0:T(8,128)(2,1)} %maximum_select_fusion.6) | copy-start | bytes 3145732
  (46 other events, 152.0 us)

commit v5 on v4

--- a/solution.py
+++ b/solution.py
@@ -624,6 +624,9 @@
     )(gated, out_proj, hidden, gain, w_gate, w_up, w_down, *ups)
 
 
+FFN_CHUNKS = 6
+
+
 def finish_kernel(
     outer, sides, sp_n, tp_n, streams, width_scale,
     *refs,
@@ -631,16 +634,18 @@
     MESH = pl.DeviceIdType.MESH
     parts = refs[:streams]
     (part_ref, hidden_ref, scale_ref, gain_ref, middle_ref, sums_ref) = refs[streams : streams + 6]
-    outs = refs[streams + 6 : 2 * streams + 6]
-    grad_out, sums_out = refs[2 * streams + 6 : 2 * streams + 8]
-    rest = refs[2 * streams + 8 :]
+    both_in, last_in = refs[streams + 6 : streams + 8]
+    outs = refs[streams + 8 : 2 * streams + 8]
+    grad_out, sums_out, both_out, last_out = refs[2 * streams + 8 : 2 * streams + 12]
+    rest = refs[2 * streams + 12 :]
     got = rest[:streams]
     staged = rest[streams : 2 * streams]
     (near_got, far_got, keep_buf, far_stage, sums_got, sums_stage) = rest[2 * streams : 2 * streams + 6]
-    (reduce_send, reduce_recv, gather_send, gather_recv, pair_send, pair_recv) = rest[
-        2 * streams + 6 : 2 * streams + 12
-    ]
-    tp_send, tp_recv, sums_send, sums_recv = rest[2 * streams + 12 :]
+    rest = rest[2 * streams + 6 :]
+    (both_keep, both_got, both_far, last_keep, last_got, last_far) = rest[:6]
+    (f_load, f_near_send, f_near_recv, f_far_send, f_far_recv, f_store, f_out_send, f_out_recv) = rest[6:14]
+    (reduce_send, reduce_recv, gather_send, gather_recv, pair_send, pair_recv) = rest[14:20]
+    tp_send, tp_recv, sums_send, sums_recv = rest[20:]
 
     sp_i = lax.axis_index("sp")
     tp_i = lax.axis_index("tp")
@@ -838,6 +843,73 @@
             spread_copy(2, side, core_dev).wait_send()
             spread_copy(3, 1 - side, core_dev).wait_send()
 
+    both_half = both_keep.shape[1]
+    last_half = last_keep.shape[0]
+
+    def ffn_at(j, refs, whole, owner):
+        if j < 4:
+            count = both_half // 2
+            start = (j % 2) * count
+            if whole:
+                start = pl.multiple_of(owner * both_half + start, count)
+            return refs[0].at[j // 2, pl.ds(start, count), :]
+        count = last_half // 2
+        start = (j - 4) * count
+        if whole:
+            start = pl.multiple_of(owner * last_half + start, count)
+        return refs[1].at[pl.ds(start, count), :]
+
+    ffn_in = (both_in, last_in)
+    ffn_out = (both_out, last_out)
+
+    def ffn_keep(j):
+        return ffn_at(j, (both_keep, last_keep), False, 0)
+
+    def ffn_got(j):
+        return ffn_at(j, (both_got, last_got), False, 0)
+
+    def ffn_far(j):
+        return ffn_at(j, (both_far, last_far), False, 0)
+
+    def ffn_load(j):
+        return pltpu.make_async_copy(ffn_at(j, ffn_in, True, core), ffn_keep(j), f_load.at[j])
+
+    def ffn_near_copy(j):
+        return remote(
+            ffn_at(j, ffn_in, True, 1 - core), ffn_got(j), f_near_send.at[j], f_near_recv.at[j], core_dev
+        )
+
+    def ffn_far_copy(j):
+        return remote(ffn_keep(j), ffn_far(j), f_far_send.at[j], f_far_recv.at[j], side_dev)
+
+    def ffn_store(j):
+        return pltpu.make_async_copy(ffn_got(j), ffn_at(j, ffn_out, True, core), f_store.at[j])
+
+    def ffn_out_copy(j):
+        return remote(
+            ffn_got(j), ffn_at(j, ffn_out, True, core), f_out_send.at[j], f_out_recv.at[j], core_dev
+        )
+
+    def ffn_sum(j):
+        ffn_load(j).wait()
+        ffn_near_copy(j).wait_recv()
+        keep = ffn_keep(j)
+        keep[...] = (keep[...].astype(F32) + ffn_got(j)[...].astype(F32)).astype(BF16)
+        ffn_far_copy(j).start()
+
+    def ffn_total(j):
+        ffn_far_copy(j).wait_recv()
+        total = ffn_keep(j)[...].astype(F32) + ffn_far(j)[...].astype(F32)
+        ffn_got(j)[...] = total.astype(BF16)
+        ffn_store(j).start()
+        ffn_out_copy(j).start()
+
+    def ffn_drain(j):
+        ffn_near_copy(j).wait_send()
+        ffn_far_copy(j).wait_send()
+        ffn_store(j).wait()
+        ffn_out_copy(j).wait()
+
     rounds = len(sum_devs)
 
     def sums_copy(step):
@@ -861,11 +933,21 @@
             for index in range(rounds):
                 sums_copy(index).wait_send()
 
-    extra = []
-    for index in range(5):
-        extra.append(functools.partial(input_step, index))
-    for index in range(rounds + 1):
-        extra.append(functools.partial(sums_step, index))
+    def later(do, *args):
+        return functools.partial(do, *args)
+
+    extra = [
+        later(input_step, 0), later(input_step, 1), later(ffn_sum, 0), later(ffn_sum, 1),
+        later(input_step, 2), later(ffn_sum, 2), later(ffn_sum, 3), later(input_step, 3),
+        later(ffn_sum, 4), later(ffn_sum, 5), later(sums_step, 0), later(ffn_total, 0),
+        later(sums_step, 1), later(sums_step, 2), later(ffn_total, 1), later(input_step, 4),
+        later(sums_step, 3), later(ffn_total, 2), later(sums_step, 4),
+    ]
+    extra += [later(sums_step, index) for index in range(5, rounds + 1)]
+    extra += [later(ffn_total, index) for index in range(3, FFN_CHUNKS)]
+    for index in range(FFN_CHUNKS):
+        ffn_near_copy(index).start()
+        ffn_load(index).start()
     for turn in range(streams + 1):
         for step in range(1, outer + 1):
             if turn < streams:
@@ -881,15 +963,18 @@
         step()
     for stream in range(streams):
         drain(stream)
-
-
-def finish(parts, part, hidden, scales, gain, middle, sums, outer, sp_n, tp_n):
+    for index in range(FFN_CHUNKS):
+        ffn_drain(index)
+
+
+def finish(parts, part, hidden, scales, gain, middle, sums, ffn, outer, sp_n, tp_n):
     streams = len(parts)
     sides = tp_n // 2
     quarter, model = hidden.shape
     last = outer - 1
     rounds = (tp_n - 1).bit_length() + (sp_n - 1).bit_length()
     vmem = pl.BlockSpec(memory_space=pltpu.VMEM)
+    anywhere = pl.BlockSpec(memory_space=pl.ANY)
     chunk = [(2, last, p.shape[0] // outer, p.shape[1]) for p in parts]
     dma = pltpu.SemaphoreType.DMA
     return pl.pallas_call(
@@ -898,9 +983,10 @@
         + [
             jax.ShapeDtypeStruct((sides, 2, quarter, model), BF16),
             jax.ShapeDtypeStruct(sums.shape, F32),
-        ],
-        in_specs=[vmem] * (streams + 6),
-        out_specs=[vmem] * (streams + 2),
+        ]
+        + [jax.ShapeDtypeStruct(f.shape, BF16) for f in ffn],
+        in_specs=[vmem] * (streams + 6) + [anywhere] * 2,
+        out_specs=[vmem] * (streams + 2) + [anywhere] * 2,
         scratch_shapes=[pltpu.VMEM(c, BF16) for c in chunk]
         + [pltpu.VMEM(c, BF16) for c in chunk]
         + [
@@ -911,6 +997,9 @@
             pltpu.VMEM((rounds,) + sums.shape, F32),
             pltpu.VMEM((rounds,) + sums.shape, F32),
         ]
+        + [pltpu.VMEM((2, ffn[0].shape[1] // 2, ffn[0].shape[2]), BF16)] * 3
+        + [pltpu.VMEM((ffn[1].shape[0] // 2, ffn[1].shape[1]), BF16)] * 3
+        + [dma((FFN_CHUNKS,))] * 8
         + [dma((streams, 2, last))] * 4
         + [dma((streams, 1 + 2 * last))] * 2
         + [dma((sides + 4,))] * 2
@@ -920,7 +1009,7 @@
         ),
         cost_estimate=pl.CostEstimate(flops=10**9, bytes_accessed=10**8, transcendentals=0),
         name="finish",
-    )(*parts, part, hidden, scales, gain, middle, sums)
+    )(*parts, part, hidden, scales, gain, middle, sums, *ffn)
 
 
 def body(
@@ -1156,19 +1245,6 @@
     mlp_quarter = scatter_sp(mlp_parts)
     layer_out = gather_tp((middle + mlp_quarter).astype(BF16))
 
-    def reduce_tp(part):
-        half = part.shape[1] // 2
-        keep = lax.dynamic_slice_in_dim(part, core_i * half, half, 1)
-        send = lax.dynamic_slice_in_dim(part, (1 - core_i) * half, half, 1)
-        return (keep.astype(F32) + core(send.astype(BF16)).astype(F32)).astype(BF16)
-
-    def whole_tp(keep, far):
-        keep = (keep.astype(F32) + far.astype(F32)).astype(BF16)
-        near = core(keep)
-        return jnp.where(
-            core_i == 1, jnp.concatenate([near, keep], 1), jnp.concatenate([keep, near], 1)
-        ).astype(F32)
-
     if not fused:
         rows_all = jnp.concatenate(rows_list)
         up_all = jnp.concatenate(up_list)
@@ -1179,7 +1255,7 @@
             jnp.stack([outer_sum(rows_all, gate_all), outer_sum(rows_all, grad_up_all)]),
             outer_sum(inner_all, up_all),
         ]
-    ffn_halves = [reduce_tp(ffn_parts[0]), reduce_tp(ffn_parts[1][None])]
+    ffn_parts = [part.astype(BF16) for part in ffn_parts]
 
     branch_other = swap_half(grad_branch)
     branch_own = lax.dynamic_slice_in_dim(grad_branch, pair_i * (model // 2), model // 2, 1)
@@ -1198,8 +1274,6 @@
     def down_pairs(step):
         return [(b, a) for a, b in up_pairs(step)]
 
-    grad_mixed, ffn_halves = lax.optimization_barrier((grad_mixed, ffn_halves))
-    ffn_halves = [(keep, side(keep)) for keep in ffn_halves]
     query_acc = None
     travelling = None
     for k in list(range(reach, -1, -1)):
@@ -1224,10 +1298,6 @@
     grad_query_low = grad_query_raw.reshape(rows_dev, heads * head_width).astype(BF16)
     grad_key_low = grad_key_raw.reshape(rows_dev, group_width).astype(BF16)
     grad_kv_low = jnp.concatenate([grad_key_low, grad_value_low], axis=1)
-    grad_query_low, grad_kv_low, ffn_halves = lax.optimization_barrier(
-        (grad_query_low, grad_kv_low, ffn_halves)
-    )
-    ffn_grads = [whole_tp(*halves) for halves in ffn_halves]
 
     both_queries = jnp.concatenate([grad_query_low, pair(grad_query_low)])
     both_kv = jnp.concatenate([grad_kv_low, pair(grad_kv_low)])
@@ -1252,7 +1322,6 @@
             jnp.sum(key_gain_terms, axis=(0, 1)),
         ]
     )
-    parts, ffn_grads = lax.optimization_barrier((parts, ffn_grads))
     gains_at = 2 * model + 2 * head_width
     gains = jnp.pad(gains, (0, -gains_at % 1024)).reshape(-1, 128)
     scales_quarter = lax.dynamic_slice_in_dim(attn_scales, quarter_first, quarter)
@@ -1264,11 +1333,12 @@
         attn_norm[None, :],
         grad_middle_quarter,
         gains,
+        ffn_parts,
         outer,
         sp_n,
         tp_n,
     )
-    output_all, gate_all_w, query_all, kv_all, input_all, gains = finished
+    output_all, gate_all_w, query_all, kv_all, input_all, gains, ffn_both, ffn_last = finished
     output_grad = jnp.concatenate([output_all[0], output_all[1]], axis=1).astype(F32)
     gate_grad = gate_all_w.reshape(model, heads * head_width).astype(F32)
     query_grad = query_all.reshape(model, heads * head_width).astype(F32)
@@ -1289,9 +1359,9 @@
         gains[2 * model : 2 * model + head_width],
         gains[2 * model + head_width : gains_at],
         gains[model : 2 * model],
-        ffn_grads[0][0],
-        ffn_grads[0][1],
-        ffn_grads[1][0],
+        ffn_both[0].astype(F32),
+        ffn_both[1].astype(F32),
+        ffn_last.astype(F32),
     )
 
 

time: 754 us -> 694 us (0.920)
  waiting for transfers between devices: 178 us -> 109 us
  Pallas kernels: 310 us -> 349 us
  other arithmetic: 85.6 us -> 61.6 us
  local copies, waits for them, and re-layouts: 67.5 us -> 47.2 us
  starting transfers between devices: 55.1 us -> 65.1 us
    ppermute x3 -> x1, waiting for transfers between devices: 46.3 us -> 0.01 us  [side(): return lax.ppermute(value, 'tp', side_pairs)]
    pallas_call x1, Pallas kernels: 149 us -> 189 us  [finish(): pl.pallas_call(functools.partial(finish_kernel, outer, sides, sp_n, tp_n,...]
    ppermute x2, waiting for transfers between devices: 17 us -> 0.01 us  [body(): travelling = lax.ppermute(total.astype(BF16), 'sp', down_pairs(k))]
    ppermute x6, starting transfers between devices: 13.9 us -> 28.2 us  [ring(): return lax.ppermute(value, 'sp', ring_pairs)]
    convert_element_type x6 -> x2, other arithmetic: 19.9 us -> 9.32 us  [the longest x1 5.77 us: body(): ffn_both[1].astype(F32)]
    squeeze x1 -> x0, local copies, waits for them, and re-layouts: 10.2 us -> none  [body(): ffn_grads[0][1]]
  transfers between devices with their start and end apart: 40 -> 34, of which waited for: 14 -> 12; matrix products, arithmetic and copies ran while one was open for 18% -> 17% of each run, Pallas kernels for 4% -> 31%
where the time goes in v5:
time: 694 us; the launch traced here: 685 us
  Pallas kernels  349 us (50%)
  waiting for transfers between devices  109 us (16%)
  starting transfers between devices  65.1 us (9%)
  other arithmetic  61.6 us (9%)
  local copies, waits for them, and re-layouts  47.2 us (7%)
  matrix products  43.6 us (6%)
  between operations  9.96 us (1%)
    pallas_call x1, Pallas kernels, finish(): pl.pallas_call(functools.partial(finish_kernel, outer, sides, sp_n, tp_n,...  189 us
    pallas_call x1, Pallas kernels, middle_layer(): pl.pallas_call(functools.partial(middle_kernel, outer), out_shape=[jax.Sh...  133 us
    ppermute x20, waiting for transfers between devices, pair(): return lax.ppermute(value, 'sp', pair_pairs)  104 us
    ppermute x6, starting transfers between devices, ring(): return lax.ppermute(value, 'sp', ring_pairs)  28.2 us
    ppermute x20, starting transfers between devices, pair(): return lax.ppermute(value, 'sp', pair_pairs)  26.3 us
    dot_general x8, matrix products, matmul(): return jnp.dot(left, right, preferred_element_type=F32)  18.9 us
    dot_general x5, matrix products, times_transpose(): lax.dot_general(left, right, (((1,), (1,)), ((), ())), preferred_element_...  15.7 us
    pallas_call x3, Pallas kernels, attn_backward(): pl.pallas_call(functools.partial(attn_backward_kernel, first, diagonal, s...  14.3 us
  transfers between devices with their start and end apart: 34, of which 12 were waited for; matrix products, arithmetic and copies ran while one was open for 17% of the time, Pallas kernels for 31%

profile of v5, /device:TPU:0, one launch (start us, length us, event | category | flops | bytes accessed | tf_op | source)
XLA Modules:
  0.0 685.3 jit_solution(9886882065590699108)
XLA Ops:
  0.7 2.2 fusion
  4.7 2.2 fusion.2
  13.9 5.7 collective-permute-start
  21.1 1.9 constant_dynamic-slice_fusion.4.refs_7_
  27.2 4.7 fusion.14
  32.5 2.9 multiply_reduce_fusion.1
  46.5 2.0 copy.107
  57.9 2.3 constant_dynamic-slice_fusion.1
  61.6 1.9 constant_dynamic-slice_fusion.5.refs_2_.refs_5_
  65.5 3.3 collective-permute-start.8
  74.1 4.6 attn_forward.3
  78.7 1.9 collective-permute-done.8.refs_11_
  82.1 8.3 %collective-permute-start.10 = (bf16[128,2048]{1,0:T(8,128)(2,1)}, bf16[128,2048]{1,0:T(8,128)(2,1)}, u32[]{:S(2)}, u32[]{:S(2)}) collective-permute-start(bf16[128,2048]{1,0:T(8,128)(2,1)} %collective-permute-done.8.refs_11_), channel_id=1, source_target_pairs={{0,2},{1,3},{2,4},{3,5},{4,6},{5,7},{6,0},{7,1},{8,10},{9,11},{10,... | collective-permute-start | bytes 1572872 | tf_op jit(solution)/shard_map/ppermute | solution.py:1059
  90.4 2.5 maximum_select_fusion.4
  93.4 3.8 attn_forward.4
  97.2 10.2 %collective-permute-done.2.kv_b = bf16[2,512,256]{2,1,0:T(8,128)(2,1)S(1)} collective-permute-done((bf16[2,512,256]{2,1,0:T(8,128)(2,1)}, bf16[2,512,256]{2,1,0:T(8,128)(2,1)S(1)}, u32[]{:S(2)}, u32[]{:S(2)}) %collective-permute-start.2) | collective-permute-done | bytes 524320 | tf_op jit(solution)/shard_map/ppermute | solution.py:1062
  108.2 3.8 attn_forward.5
  116.1 3.4 multiply_convert_fusion.1
  119.5 10.4 %collective-permute-done.9.refs_12_ = bf16[128,2048]{1,0:T(8,128)(2,1)} collective-permute-done((bf16[128,2048]{1,0:T(8,128)(2,1)}, bf16[128,2048]{1,0:T(8,128)(2,1)}, u32[]{:S(2)}, u32[]{:S(2)}) %collective-permute-start.9) | collective-permute-done | bytes 524320 | tf_op jit(solution)/shard_map/ppermute | solution.py:1062
  130.0 10.7 %collective-permute-done.11.refs_14_ = bf16[128,2048]{1,0:T(8,128)(2,1)S(1)} collective-permute-done((bf16[128,2048]{1,0:T(8,128)(2,1)}, bf16[128,2048]{1,0:T(8,128)(2,1)S(1)}, u32[]{:S(2)}, u32[]{:S(2)}) %collective-permute-start.11) | collective-permute-done | bytes 524320 | tf_op jit(solution)/shard_map/ppermute | solution.py:1062
  141.4 133.4 %middle.1 = (f32[128,2048]{1,0:T(8,128)}, f32[128,2048]{1,0:T(8,128)}, f32[1,2048]{1,0:T(1,128)}, bf16[2,2,128,2048]{3,2,1,0:T(8,128)(2,1)}, bf16[1024,768]{1,0:...) custom-call(bf16[512,512]{1,0:T(8,128)(2,1)} %get-tuple-element.78.refs_0_, ...), custom_call_target="tpu_custom_call" | custom-call | flops 30000001024 | bytes 40000000 | tf_op jit(solution)/shard_map/middle/pallas_call | solution.py:572
  274.9 3.4 fusion.47
  278.3 2.3 fusion.49
  280.6 2.3 fusion.51
  287.7 2.7 convert_multiply_fusion.3
  294.9 3.3 attn_backward.3
  298.3 4.1 attn_backward.4
  302.3 6.9 %attn_backward.5 = (f32[512,512]{1,0:T(8,128)}, bf16[2,512,256]{2,1,0:T(8,128)(2,1)}, bf16[2,512,256]{2,1,0:T(8,128)(2,1)}) custom-call(s32[7]{0:T(128)} %stack.179.info, s32[1,512]{1,0:T(1,128)} %compare_select_fusion.starts, f32[2,2,512]{2,1,0:T(2,128)} %reshape.340.lse, f32[2,2,512]{2,1,0:T(2,128)} %reshape.342.deltas, bf16[512,512]{1,0:T(8,128)(2,1)} %bitcast.187, ...), custom_call_target="tpu_custom_call" | custom-call | flops 2684354560 | bytes 2097152 | tf_op jit(solution)/shard_map/attn_backward/pallas_call | solution.py:229
  309.2 2.3 broadcast_multiply_fusion
  317.7 3.8 collective-permute-start.30
  321.5 2.0 fusion.20
  323.5 3.3 fusion.67
  327.0 2.2 slice.255
  329.4 1.9 collective-permute-start.22
  331.6 2.9 collective-permute-done.30
  334.5 2.0 collective-permute-start.29
  338.5 29.7 %collective-permute-done.26 = bf16[512,512]{1,0:T(8,128)(2,1)S(1)} collective-permute-done((bf16[512,512]{1,0:T(8,128)(2,1)S(1)}, bf16[512,512]{1,0:T(8,128)(2,1)S(1)}, u32[]{:S(2)}, u32[]{:S(2)}) %collective-permute-start.26) | collective-permute-done | bytes 524320 | tf_op jit(solution)/shard_map/ppermute | solution.py:1062
  368.2 2.0 collective-permute-start.14
  370.2 4.1 collective-permute-start.13
  374.3 2.3 convolution_convert_fusion.1.refs_2_
  376.5 2.2 convolution_convert_fusion.2.refs_1_
  378.8 2.1 collective-permute-start.21
  381.7 9.0 %collective-permute-done.14 = bf16[128,2048]{1,0:T(8,128)(2,1)S(1)} collective-permute-done((bf16[128,2048]{1,0:T(8,128)(2,1)S(1)}, bf16[128,2048]{1,0:T(8,128)(2,1)S(1)}, u32[]{:S(2)}, u32[]{:S(2)}) %collective-permute-start.14) | collective-permute-done | bytes 524320 | tf_op jit(solution)/shard_map/ppermute | solution.py:1062
  390.6 2.0 collective-permute-start.28
  392.7 2.5 collective-permute-done.13
  397.6 4.2 collective-permute-done.21
  401.9 6.1 collective-permute-start.15
  407.9 2.2 fusion.9.refs_0_
  410.2 14.2 %collective-permute-done.28 = bf16[2,512,256]{2,1,0:T(8,128)(2,1)S(1)} collective-permute-done((bf16[2,512,256]{2,1,0:T(8,128)(2,1)S(1)}, bf16[2,512,256]{2,1,0:T(8,128)(2,1)S(1)}, u32[]{:S(2)}, u32[]{:S(2)}) %collective-permute-start.28) | collective-permute-done | bytes 524320 | tf_op jit(solution)/shard_map/ppermute | solution.py:1062
  425.9 2.8 fusion.65
  428.6 6.6 collective-permute-done.16
  436.3 5.7 collective-permute-start.17
  444.3 2.1 fusion.68
  447.6 4.8 fusion.4
  453.1 6.3 collective-permute-done.33
  459.4 2.3 convolution_convert_fusion.refs_3_
  461.7 189.3 %finish.1 = (bf16[2,512,1024]{2,1,0:T(8,128)(2,1)}, bf16[2,1024,512]{2,1,0:T(8,128)(2,1)}, bf16[2,1024,512]{2,1,0:T(8,128)(2,1)}, bf16[2,1024,512]{2,1,0:T(8,128...) custom-call(bf16[512,1024]{1,0:T(8,128)(2,1)} %fusion.9.refs_0_, ...), custom_call_target="tpu_custom_call" | custom-call | flops 1000000000 | bytes 100000000 | tf_op jit(solution)/shard_map/finish/pallas_call | solution.py:980
  656.4 2.7 bitcast_convert_fusion.4
  659.1 2.7 bitcast_convert_fusion.3
  661.9 2.7 bitcast_convert_fusion.2
  666.5 3.6 convert_element_type.248
  670.1 2.7 maximum_convert_fusion
  672.7 2.4 slice_convert_fusion
  676.6 5.8 bitcast_convert_fusion
  (270 shorter events, 82.7 us)
Async XLA Ops:
  0.6 31.9 %copy-start = (bf16[2048,512]{1,0:T(8,128)(2,1)S(1)}, bf16[2048,512]{1,0:T(8,128)(2,1)}, u32[]{:S(2)}) copy-start(bf16[2048,512]{1,0:T(8,128)(2,1)} %param.18) | copy-start | bytes 6291460
  2.9 39.6 %copy-start.52 = (f32[512]{0:T(512)}, f32[512]{0:T(512)S(1)}, u32[]{:S(2)}) copy-start(f32[512]{0:T(512)S(1)} %add_rsqrt_fusion.2) | copy-start | bytes 6148
  11.7 14.6 %copy-start.27 = (f32[512,64]{0,1:T(8,128)}, f32[512,64]{0,1:T(8,128)S(1)}, u32[]{:S(2)}) copy-start(f32[512,64]{0,1:T(8,128)S(1)} %get-tuple-element.112) | copy-start | bytes 393220
  13.9 49.6 %collective-permute-start = (bf16[2,512,256]{2,1,0:T(8,128)(2,1)}, bf16[2,512,256]{2,1,0:T(8,128)(2,1)}, u32[]{:S(2)}, u32[]{:S(2)}) collective-permute-start(bf16[2,512,256]{2,1,0:T(8,128)(2,1)} %pad_maximum_fusion.6.kv_a), channel_id=1, source_target_pairs={{0,2},{1,3},{2,4},{3,5},{4,6},{5,7},{8,10},{9,11},{10,12},{11,13},... | collective-permute-start | bytes 1572872 | tf_op jit(solution)/shard_map/ppermute | solution.py:1122
  19.6 52.4 %collective-permute-start.4 = (bf16[2,512,256]{2,1,0:T(8,128)(2,1)}, bf16[2,512,256]{2,1,0:T(8,128)(2,1)}, u32[]{:S(2)}, u32[]{:S(2)}) collective-permute-start(bf16[2,512,256]{2,1,0:T(8,128)(2,1)} %pad_maximum_fusion.6.kv_a), channel_id=1, source_target_pairs={{0,1},{1,0},{2,3},{3,2},{4,5},{5,4},{6,7},{7,6},{8,9},{9,8},{10,11... | collective-permute-start | bytes 1572872 | tf_op jit(solution)/shard_map/ppermute | solution.py:1062
  23.0 42.4 %collective-permute-start.6 = (bf16[128,2048]{1,0:T(8,128)(2,1)}, bf16[128,2048]{1,0:T(8,128)(2,1)}, u32[]{:S(2)}, u32[]{:S(2)}) collective-permute-start(bf16[128,2048]{1,0:T(8,128)(2,1)} %constant_dynamic-slice_fusion.4.refs_7_), channel_id=1, source_target_pairs={{0,2},{1,3},{2,4},{3,5},{4,6},{5,7},{6,0},{7,1},{8,10},{9,11},{10,... | collective-permute-start | bytes 1572872 | tf_op jit(solution)/shard_map/ppermute | solution.py:1059
  25.7 43.0 %collective-permute-start.24 = (bf16[512,512]{1,0:T(8,128)(2,1)}, bf16[512,512]{1,0:T(8,128)(2,1)}, u32[]{:S(2)}, u32[]{:S(2)}) collective-permute-start(bf16[512,512]{1,0:T(8,128)(2,1)} %constant_dynamic-slice_fusion), channel_id=1, source_target_pairs={{0,1},{1,0},{2,3},{3,2},{4,5},{5,4},{6,7},{7,6},{8,9},{9,8},{10,11... | collective-permute-start | bytes 1572872 | tf_op jit(solution)/shard_map/ppermute | solution.py:1062
  27.2 5.3 copy-start.10
  37.0 4.7 copy-start.6
  42.5 12.1 %copy-start.54 = (f32[512,2]{0,1:T(2,128)S(1)}, f32[512,2]{0,1:T(2,128)}, u32[]{:S(2)}) copy-start(f32[512,2]{0,1:T(2,128)} %get-tuple-element.109) | copy-start | bytes 12292
  54.6 10.4 %copy-start.57 = (f32[128]{0:T(128)S(1)}, f32[128]{0:T(128)}, u32[]{:S(2)}) copy-start(f32[128]{0:T(128)} %param.23) | copy-start | bytes 1540
  54.6 16.9 %copy-start.60 = (f32[128]{0:T(128)S(1)}, f32[128]{0:T(128)}, u32[]{:S(2)}) copy-start(f32[128]{0:T(128)} %param.24) | copy-start | bytes 1540
  63.5 9.1 %collective-permute-start.1 = (bf16[2,512,256]{2,1,0:T(8,128)(2,1)}, bf16[2,512,256]{2,1,0:T(8,128)(2,1)}, u32[]{:S(2)}, u32[]{:S(2)}) collective-permute-start(bf16[2,512,256]{2,1,0:T(8,128)(2,1)} %collective-permute-done.kv_a), channel_id=1, source_target_pairs={{2,4},{3,5},{4,6},{5,7},{10,12},{11,13},{12,14},{13,15},{18,20},{1... | collective-permute-start | bytes 1572872 | tf_op jit(solution)/shard_map/ppermute | solution.py:1122
  65.5 15.1 %collective-permute-start.8 = (bf16[128,2048]{1,0:T(8,128)(2,1)}, bf16[128,2048]{1,0:T(8,128)(2,1)}, u32[]{:S(2)}, u32[]{:S(2)}) collective-permute-start(bf16[128,2048]{1,0:T(8,128)(2,1)} %collective-permute-done.6.refs_9_), channel_id=1, source_target_pairs={{0,2},{1,3},{2,4},{3,5},{4,6},{5,7},{6,0},{7,1},{8,10},{9,11},{10,... | collective-permute-start | bytes 1572872 | tf_op jit(solution)/shard_map/ppermute | solution.py:1059
  68.7 13.4 %collective-permute-start.25 = (bf16[512,512]{1,0:T(8,128)(2,1)}, bf16[512,512]{1,0:T(8,128)(2,1)S(1)}, u32[]{:S(2)}, u32[]{:S(2)}) collective-permute-start(bf16[512,512]{1,0:T(8,128)(2,1)} %collective-permute-done.24), channel_id=1, source_target_pairs={{0,8},{8,0},{16,24},{24,16},{1,9},{9,1},{17,25},{25,17},{2,10},{10... | collective-permute-start | bytes 1572872 | tf_op jit(solution)/shard_map/ppermute | solution.py:1068
  69.9 22.9 %collective-permute-start.3 = (bf16[2,512,256]{2,1,0:T(8,128)(2,1)}, bf16[2,512,256]{2,1,0:T(8,128)(2,1)}, u32[]{:S(2)}, u32[]{:S(2)}) collective-permute-start(bf16[2,512,256]{2,1,0:T(8,128)(2,1)} %collective-permute-done.kv_a), channel_id=1, source_target_pairs={{0,1},{1,0},{2,3},{3,2},{4,5},{5,4},{6,7},{7,6},{8,9},{9,8},{10,11... | collective-permute-start | bytes 1572872 | tf_op jit(solution)/shard_map/ppermute | solution.py:1062
  72.0 47.5 %collective-permute-start.5 = (bf16[128,2048]{1,0:T(8,128)(2,1)}, bf16[128,2048]{1,0:T(8,128)(2,1)}, u32[]{:S(2)}, u32[]{:S(2)}) collective-permute-start(bf16[128,2048]{1,0:T(8,128)(2,1)} %constant_dynamic-slice_fusion.4.refs_7_), channel_id=1, source_target_pairs={{0,1},{1,0},{2,3},{3,2},{4,5},{5,4},{6,7},{7,6},{8,9},{9,8},{10,11... | collective-permute-start | bytes 1572872 | tf_op jit(solution)/shard_map/ppermute | solution.py:1062
  72.5 34.9 %collective-permute-start.2 = (bf16[2,512,256]{2,1,0:T(8,128)(2,1)}, bf16[2,512,256]{2,1,0:T(8,128)(2,1)S(1)}, u32[]{:S(2)}, u32[]{:S(2)}) collective-permute-start(bf16[2,512,256]{2,1,0:T(8,128)(2,1)} %collective-permute-done.1.kv_a), channel_id=1, source_target_pairs={{0,1},{1,0},{2,3},{3,2},{4,5},{5,4},{6,7},{7,6},{8,9},{9,8},{10,11... | collective-permute-start | bytes 1572872 | tf_op jit(solution)/shard_map/ppermute | solution.py:1062
  80.6 39.0 %collective-permute-start.7 = (bf16[128,2048]{1,0:T(8,128)(2,1)}, bf16[128,2048]{1,0:T(8,128)(2,1)}, u32[]{:S(2)}, u32[]{:S(2)}) collective-permute-start(bf16[128,2048]{1,0:T(8,128)(2,1)} %collective-permute-done.6.refs_9_), channel_id=1, source_target_pairs={{0,1},{1,0},{2,3},{3,2},{4,5},{5,4},{6,7},{7,6},{8,9},{9,8},{10,11... | collective-permute-start | bytes 1572872 | tf_op jit(solution)/shard_map/ppermute | solution.py:1062
  82.1 31.9 %collective-permute-start.10 = (bf16[128,2048]{1,0:T(8,128)(2,1)}, bf16[128,2048]{1,0:T(8,128)(2,1)}, u32[]{:S(2)}, u32[]{:S(2)}) collective-permute-start(bf16[128,2048]{1,0:T(8,128)(2,1)} %collective-permute-done.8.refs_11_), channel_id=1, source_target_pairs={{0,2},{1,3},{2,4},{3,5},{4,6},{5,7},{6,0},{7,1},{8,10},{9,11},{10,... | collective-permute-start | bytes 1572872 | tf_op jit(solution)/shard_map/ppermute | solution.py:1059
  92.9 37.1 %collective-permute-start.9 = (bf16[128,2048]{1,0:T(8,128)(2,1)}, bf16[128,2048]{1,0:T(8,128)(2,1)}, u32[]{:S(2)}, u32[]{:S(2)}) collective-permute-start(bf16[128,2048]{1,0:T(8,128)(2,1)} %collective-permute-done.8.refs_11_), channel_id=1, source_target_pairs={{0,1},{1,0},{2,3},{3,2},{4,5},{5,4},{6,7},{7,6},{8,9},{9,8},{10,11... | collective-permute-start | bytes 1572872 | tf_op jit(solution)/shard_map/ppermute | solution.py:1062
  114.0 26.7 %collective-permute-start.11 = (bf16[128,2048]{1,0:T(8,128)(2,1)}, bf16[128,2048]{1,0:T(8,128)(2,1)S(1)}, u32[]{:S(2)}, u32[]{:S(2)}) collective-permute-start(bf16[128,2048]{1,0:T(8,128)(2,1)} %collective-permute-done.10.refs_13_), channel_id=1, source_target_pairs={{0,1},{1,0},{2,3},{3,2},{4,5},{5,4},{6,7},{7,6},{8,9},{9,8},{10,11... | collective-permute-start | bytes 1572872 | tf_op jit(solution)/shard_map/ppermute | solution.py:1062
  141.4 133.4 %copy-start.2 = (bf16[768,2048]{1,0:T(8,128)(2,1)S(1)}, bf16[768,2048]{1,0:T(8,128)(2,1)}, u32[]{:S(2)}) copy-start(bf16[768,2048]{1,0:T(8,128)(2,1)} %refs_6_.1) | copy-start | bytes 9437188
  286.2 50.5 %collective-permute-start.12 = (bf16[128,2048]{1,0:T(8,128)(2,1)}, bf16[128,2048]{1,0:T(8,128)(2,1)}, u32[]{:S(2)}, u32[]{:S(2)}) collective-permute-start(bf16[128,2048]{1,0:T(8,128)(2,1)} %slice.258), channel_id=1, source_target_pairs={{0,1},{1,0},{2,3},{3,2},{4,5},{5,4},{6,7},{7,6},{8,9},{9,8},{10,11... | collective-permute-start | bytes 1572872 | tf_op jit(solution)/shard_map/ppermute | solution.py:1062
  316.2 5.3 copy-start.51
  317.7 16.8 %collective-permute-start.30 = (bf16[2,512,256]{2,1,0:T(8,128)(2,1)}, bf16[2,512,256]{2,1,0:T(8,128)(2,1)S(1)}, u32[]{:S(2)}, u32[]{:S(2)}) collective-permute-start(bf16[2,512,256]{2,1,0:T(8,128)(2,1)} %get-tuple-element.61), channel_id=1, source_target_pairs={{0,1},{1,0},{2,3},{3,2},{4,5},{5,4},{6,7},{7,6},{8,9},{9,8},{10,11... | collective-permute-start | bytes 1572872 | tf_op jit(solution)/shard_map/ppermute | solution.py:1062
  323.5 5.8 copy-start.12
  326.9 43.3 %collective-permute-start.27 = (bf16[512,512]{0,1:T(8,128)(2,1)S(1)}, bf16[512,512]{0,1:T(8,128)(2,1)S(1)}, u32[]{:S(2)}, u32[]{:S(2)}) collective-permute-start(bf16[512,512]{0,1:T(8,128)(2,1)S(1)} %get-tuple-element.86), channel_id=1, source_target_pairs={{0,1},{1,0},{2,3},{3,2},{4,5},{5,4},{6,7},{7,6},{8,9},{9,8},{10,11... | collective-permute-start | bytes 1572872 | tf_op jit(solution)/shard_map/ppermute | solution.py:1062
  329.2 5.3 copy-start.65
  329.2 7.3 %copy-start.48 = (bf16[2,512,256]{2,1,0:T(8,128)(2,1)S(1)}, bf16[2,512,256]{2,1,0:T(8,128)(2,1)}, u32[]{:S(2)}) copy-start(bf16[2,512,256]{2,1,0:T(8,128)(2,1)} %get-tuple-element.60) | copy-start | bytes 1572868
  329.4 8.0 %copy-start.14 = (f32[256,2048]{1,0:T(8,128)S(1)}, f32[256,2048]{1,0:T(8,128)}, u32[]{:S(2)}) copy-start(f32[256,2048]{1,0:T(8,128)} %copy-done.13) | copy-start | bytes 6291460
  329.4 49.4 %collective-permute-start.22 = (bf16[512,512]{1,0:T(8,128)(2,1)S(1)}, bf16[512,512]{1,0:T(8,128)(2,1)S(1)}, u32[]{:S(2)}, u32[]{:S(2)}) collective-permute-start(bf16[512,512]{1,0:T(8,128)(2,1)S(1)} %constant_dynamic-slice_fusion.2), channel_id=1, source_target_pairs={{0,1},{1,0},{2,3},{3,2},{4,5},{5,4},{6,7},{7,6},{8,9},{9,8},{10,11... | collective-permute-start | bytes 1572872 | tf_op jit(solution)/shard_map/ppermute | solution.py:1062
  331.3 36.9 %collective-permute-start.26 = (bf16[512,512]{1,0:T(8,128)(2,1)S(1)}, bf16[512,512]{1,0:T(8,128)(2,1)S(1)}, u32[]{:S(2)}, u32[]{:S(2)}) collective-permute-start(bf16[512,512]{1,0:T(8,128)(2,1)S(1)} %copy-done.44), channel_id=1, source_target_pairs={{0,1},{1,0},{2,3},{3,2},{4,5},{5,4},{6,7},{7,6},{8,9},{9,8},{10,11... | collective-permute-start | bytes 1572872 | tf_op jit(solution)/shard_map/ppermute | solution.py:1062
  331.6 42.7 %copy-start.33 = (bf16[512,1024]{1,0:T(8,128)(2,1)S(1)}, bf16[512,1024]{1,0:T(8,128)(2,1)}, u32[]{:S(2)}) copy-start(bf16[512,1024]{1,0:T(8,128)(2,1)} %constant_dynamic-slice_fusion.1) | copy-start | bytes 3145732
  331.6 42.7 %copy-start.35 = (bf16[512,1024]{1,0:T(8,128)(2,1)S(1)}, bf16[512,1024]{1,0:T(8,128)(2,1)}, u32[]{:S(2)}) copy-start(bf16[512,1024]{1,0:T(8,128)(2,1)} %maximum_select_fusion.4) | copy-start | bytes 3145732
  334.5 46.4 %collective-permute-start.29 = (bf16[2,512,256]{2,1,0:T(8,128)(2,1)S(1)}, bf16[2,512,256]{2,1,0:T(8,128)(2,1)S(1)}, u32[]{:S(2)}, u32[]{:S(2)}) collective-permute-start(bf16[2,512,256]{2,1,0:T(8,128)(2,1)S(1)} %copy-done.65), channel_id=1, source_target_pairs={{0,1},{1,0},{2,3},{3,2},{4,5},{5,4},{6,7},{7,6},{8,9},{9,8},{10,11... | collective-permute-start | bytes 1572872 | tf_op jit(solution)/shard_map/ppermute | solution.py:1062
  336.6 44.8 %collective-permute-start.31 = (bf16[2,512,256]{2,1,0:T(8,128)(2,1)S(1)}, bf16[2,512,256]{2,1,0:T(8,128)(2,1)S(1)}, u32[]{:S(2)}, u32[]{:S(2)}) collective-permute-start(bf16[2,512,256]{2,1,0:T(8,128)(2,1)S(1)} %add_convert_fusion.1), channel_id=1, source_target_pairs={{4,2},{5,3},{6,4},{7,5},{12,10},{13,11},{14,12},{15,13},{20,18},{2... | collective-permute-start | bytes 1572872 | tf_op jit(solution)/shard_map/ppermute | solution.py:1288
  368.2 22.5 %collective-permute-start.14 = (bf16[128,2048]{1,0:T(8,128)(2,1)S(1)}, bf16[128,2048]{1,0:T(8,128)(2,1)S(1)}, u32[]{:S(2)}, u32[]{:S(2)}) collective-permute-start(bf16[128,2048]{1,0:T(8,128)(2,1)S(1)} %slice.257), channel_id=1, source_target_pairs={{0,1},{1,0},{2,3},{3,2},{4,5},{5,4},{6,7},{7,6},{8,9},{9,8},{10,11... | collective-permute-start | bytes 1572872 | tf_op jit(solution)/shard_map/ppermute | solution.py:1062
  370.2 25.0 %collective-permute-start.13 = (bf16[128,2048]{1,0:T(8,128)(2,1)S(1)}, bf16[128,2048]{1,0:T(8,128)(2,1)S(1)}, u32[]{:S(2)}, u32[]{:S(2)}) collective-permute-start(bf16[128,2048]{1,0:T(8,128)(2,1)S(1)} %fusion.28), channel_id=1, source_target_pairs={{0,2},{1,3},{2,4},{3,5},{4,6},{5,7},{6,0},{7,1},{8,10},{9,11},{10,... | collective-permute-start | bytes 1572872 | tf_op jit(solution)/shard_map/ppermute | solution.py:1059
  376.5 4.9 copy-start.49
  378.8 11.9 %copy-start.64 = (bf16[2,512,256]{2,1,0:T(8,128)(2,1)S(1)}, bf16[2,512,256]{2,1,0:T(8,128)(2,1)}, u32[]{:S(2)}) copy-start(bf16[2,512,256]{2,1,0:T(8,128)(2,1)} %get-tuple-element.57) | copy-start | bytes 1572868
  378.8 23.1 %collective-permute-start.21 = (bf16[512,512]{1,0:T(8,128)(2,1)S(1)}, bf16[512,512]{1,0:T(8,128)(2,1)S(1)}, u32[]{:S(2)}, u32[]{:S(2)}) collective-permute-start(bf16[512,512]{1,0:T(8,128)(2,1)S(1)} %copy-done.46), channel_id=1, source_target_pairs={{0,1},{1,0},{2,3},{3,2},{4,5},{5,4},{6,7},{7,6},{8,9},{9,8},{10,11... | collective-permute-start | bytes 1572872 | tf_op jit(solution)/shard_map/ppermute | solution.py:1062
  380.9 272.7 %collective-permute-start.18 = (bf16[128,2048]{1,0:T(8,128)(2,1)}, bf16[128,2048]{1,0:T(8,128)(2,1)}, u32[]{:S(2)}, u32[]{:S(2)}) collective-permute-start(bf16[128,2048]{1,0:T(8,128)(2,1)} %slice.255), channel_id=1, source_target_pairs={{0,1},{1,0},{2,3},{3,2},{4,5},{5,4},{6,7},{7,6},{8,9},{9,8},{10,11... | collective-permute-start | bytes 1572872 | tf_op jit(solution)/shard_map/ppermute | solution.py:1062
  381.4 15.3 %collective-permute-start.23 = (bf16[512,512]{1,0:T(8,128)(2,1)S(1)}, bf16[512,512]{1,0:T(8,128)(2,1)S(1)}, u32[]{:S(2)}, u32[]{:S(2)}) collective-permute-start(bf16[512,512]{1,0:T(8,128)(2,1)S(1)} %collective-permute-done.22), channel_id=1, source_target_pairs={{0,8},{8,0},{16,24},{24,16},{1,9},{9,1},{17,25},{25,17},{2,10},{10... | collective-permute-start | bytes 1572872 | tf_op jit(solution)/shard_map/ppermute | solution.py:1068
  390.6 33.7 %collective-permute-start.28 = (bf16[2,512,256]{2,1,0:T(8,128)(2,1)S(1)}, bf16[2,512,256]{2,1,0:T(8,128)(2,1)S(1)}, u32[]{:S(2)}, u32[]{:S(2)}) collective-permute-start(bf16[2,512,256]{2,1,0:T(8,128)(2,1)S(1)} %copy-done.64), channel_id=1, source_target_pairs={{0,1},{1,0},{2,3},{3,2},{4,5},{5,4},{6,7},{7,6},{8,9},{9,8},{10,11... | collective-permute-start | bytes 1572872 | tf_op jit(solution)/shard_map/ppermute | solution.py:1062
  395.2 29.2 %collective-permute-start.32 = (bf16[2,512,256]{2,1,0:T(8,128)(2,1)S(1)}, bf16[2,512,256]{2,1,0:T(8,128)(2,1)S(1)}, u32[]{:S(2)}, u32[]{:S(2)}) collective-permute-start(bf16[2,512,256]{2,1,0:T(8,128)(2,1)S(1)} %add_convert_fusion), channel_id=1, source_target_pairs={{2,0},{3,1},{4,2},{5,3},{6,4},{7,5},{10,8},{11,9},{12,10},{13,11},... | collective-permute-start | bytes 1572872 | tf_op jit(solution)/shard_map/ppermute | solution.py:1288
  396.7 38.6 %collective-permute-start.16 = (bf16[128,2048]{1,0:T(8,128)(2,1)S(1)}, bf16[128,2048]{1,0:T(8,128)(2,1)S(1)}, u32[]{:S(2)}, u32[]{:S(2)}) collective-permute-start(bf16[128,2048]{1,0:T(8,128)(2,1)S(1)} %slice.256), channel_id=1, source_target_pairs={{0,1},{1,0},{2,3},{3,2},{4,5},{5,4},{6,7},{7,6},{8,9},{9,8},{10,11... | collective-permute-start | bytes 1572872 | tf_op jit(solution)/shard_map/ppermute | solution.py:1062
  397.6 26.7 %copy-start.47 = (bf16[2,512,256]{2,1,0:T(8,128)(2,1)S(1)}, bf16[2,512,256]{2,1,0:T(8,128)(2,1)}, u32[]{:S(2)}) copy-start(bf16[2,512,256]{2,1,0:T(8,128)(2,1)} %get-tuple-element.56) | copy-start | bytes 1572868
  401.9 33.4 %collective-permute-start.15 = (bf16[128,2048]{1,0:T(8,128)(2,1)S(1)}, bf16[128,2048]{1,0:T(8,128)(2,1)S(1)}, u32[]{:S(2)}, u32[]{:S(2)}) collective-permute-start(bf16[128,2048]{1,0:T(8,128)(2,1)S(1)} %fusion.27), channel_id=1, source_target_pairs={{0,2},{1,3},{2,4},{3,5},{4,6},{5,7},{6,0},{7,1},{8,10},{9,11},{10,... | collective-permute-start | bytes 1572872 | tf_op jit(solution)/shard_map/ppermute | solution.py:1059
  428.6 13.6 %copy-start.28 = (f32[512,64]{0,1:T(8,128)S(1)}, f32[512,64]{0,1:T(8,128)}, u32[]{:S(2)}) copy-start(f32[512,64]{0,1:T(8,128)} %copy-done.27) | copy-start | bytes 393220
  428.6 13.7 %copy-start.61 = (f32[128]{0:T(128)S(1)}, f32[128]{0:T(128)}, u32[]{:S(2)}) copy-start(f32[128]{0:T(128)} %param.24) | copy-start | bytes 1540
  435.3 6.7 slice-start.2
  435.3 7.0 %copy-start.17 = (f32[512,256]{0,1:T(8,128)S(1)}, f32[512,256]{0,1:T(8,128)}, u32[]{:S(2)}) copy-start(f32[512,256]{0,1:T(8,128)} %copy-done.16) | copy-start | bytes 1572868
  436.3 217.3 %collective-permute-start.17 = (bf16[128,2048]{1,0:T(8,128)(2,1)}, bf16[128,2048]{1,0:T(8,128)(2,1)}, u32[]{:S(2)}, u32[]{:S(2)}) collective-permute-start(bf16[128,2048]{1,0:T(8,128)(2,1)} %fusion.25), channel_id=1, source_target_pairs={{0,2},{1,3},{2,4},{3,5},{4,6},{5,7},{6,0},{7,1},{8,10},{9,11},{10,... | collective-permute-start | bytes 1572872 | tf_op jit(solution)/shard_map/ppermute | solution.py:1059
  446.5 6.0 copy-start.56
  446.5 12.9 %copy-start.34 = (bf16[512,1024]{1,0:T(8,128)(2,1)S(1)}, bf16[512,1024]{1,0:T(8,128)(2,1)}, u32[]{:S(2)}) copy-start(bf16[512,1024]{1,0:T(8,128)(2,1)} %constant_dynamic-slice_fusion.1) | copy-start | bytes 3145732
  446.5 12.9 %copy-start.36 = (bf16[512,1024]{1,0:T(8,128)(2,1)S(1)}, bf16[512,1024]{1,0:T(8,128)(2,1)}, u32[]{:S(2)}) copy-start(bf16[512,1024]{1,0:T(8,128)(2,1)} %maximum_select_fusion.4) | copy-start | bytes 3145732
  446.6 12.8 %collective-permute-start.33 = (bf16[512,512]{1,0:T(8,128)(2,1)S(1)}, bf16[512,512]{1,0:T(8,128)(2,1)S(1)}, u32[]{:S(2)}, u32[]{:S(2)}) collective-permute-start(bf16[512,512]{1,0:T(8,128)(2,1)S(1)} %pad_maximum_fusion.8), channel_id=1, source_target_pairs={{0,1},{1,0},{2,3},{3,2},{4,5},{5,4},{6,7},{7,6},{8,9},{9,8},{10,11... | collective-permute-start | bytes 1572872 | tf_op jit(solution)/shard_map/ppermute | solution.py:1062
  461.7 191.9 %copy-start.8 = (f32[256,2048]{1,0:T(8,128)S(1)}, f32[256,2048]{1,0:T(8,128)}, u32[]{:S(2)}) copy-start(f32[256,2048]{1,0:T(8,128)} %fusion.47) | copy-start | bytes 6291460
  461.7 192.0 %copy-start.32 = (f32[128,2048]{1,0:T(8,128)S(1)}, f32[128,2048]{1,0:T(8,128)}, u32[]{:S(2)}) copy-start(f32[128,2048]{1,0:T(8,128)} %get-tuple-element.50) | copy-start | bytes 3145732
  650.9 5.5 copy-start.23
  655.1 20.1 %collective-permute-start.19 = (bf16[128,2048]{1,0:T(8,128)(2,1)S(1)}, bf16[128,2048]{1,0:T(8,128)(2,1)S(1)}, u32[]{:S(2)}, u32[]{:S(2)}) collective-permute-start(bf16[128,2048]{1,0:T(8,128)(2,1)S(1)} %fusion.23), channel_id=1, source_target_pairs={{0,16},{8,24},{16,0},{24,8},{1,17},{9,25},{17,1},{25,9},{2,18},{10... | collective-permute-start | bytes 1572872 | tf_op jit(solution)/shard_map/ppermute | solution.py:1065
  670.1 5.3 slice-start
  675.3 7.3 %collective-permute-start.20 = (bf16[2,128,2048]{2,1,0:T(8,128)(2,1)S(1)}, bf16[2,128,2048]{2,1,0:T(8,128)(2,1)S(1)}, u32[]{:S(2)}, u32[]{:S(2)}) collective-permute-start(bf16[2,128,2048]{2,1,0:T(8,128)(2,1)S(1)} %maximum_select_fusion.1), channel_id=1, source_target_pairs={{0,8},{8,0},{16,24},{24,16},{1,9},{9,1},{17,25},{25,17},{2,10},{10... | collective-permute-start | bytes 3145736 | tf_op jit(solution)/shard_map/ppermute | solution.py:1068
  (41 other events, 114.0 us)

commit v6 on v5

--- a/solution.py
+++ b/solution.py
@@ -254,16 +254,17 @@
     blocks = 2 * outer
     (gated, out_proj, hidden_ref, gain_ref, gate_in, up_in, down_in) = refs[:7]
     ups_in = refs[7 : 7 + blocks]
-    (middle_out, grad_out, gain_out, branch, inner_out, dw_both, dw_down) = refs[
-        7 + blocks : 14 + blocks
-    ]
+    (layer_out, grad_out, gain_out, branch, dw_both, dw_down) = refs[7 + blocks : 13 + blocks]
     (
-        w_gate, w_up, w_down, ups, rows, grad_inner, inner, grad_gate, grad_up,
-        near_stage, near_got, far_stage, far_got, far_keep, own_keep,
-        keep, y_stage, y_got, z_stage, z_got,
+        w_gate, w_up, w_down, ups, rows, inner, grad_gate, grad_up,
+        near_buf, far_stage, far_got, middle_buf,
+        keep, y_stage, y_got, z_stage, z_got, part_got, part_far,
         load_sem, store_sem, tp_send, tp_recv, zs, zr, ys, yr, rys, ryr, rzs, rzr,
-    ) = refs[14 + blocks :]
-    stage_gate, stage_up, stage_down = w_gate, w_up, w_down
+        p_near_send, p_near_recv, p_far_send, p_far_recv, p_out_send, p_out_recv,
+    ) = refs[13 + blocks :]
+    stage_gate, stage_up, stage_down = w_gate, w_up, rows
+    far_keep, own_keep = grad_out, middle_buf
+    units = w_down.shape[0]
     quarter, model = hidden_ref.shape
     group = 2 * quarter
     chunk = model // outer
@@ -314,7 +315,7 @@
         return pl.ds(pl.multiple_of(index * count, count), count)
 
     def near_copy(j):
-        return remote(near_stage.at[j], near_got.at[j], tp_send.at[j], tp_recv.at[j], core_dev)
+        return remote(near_buf.at[j], near_buf.at[2 + j], tp_send.at[j], tp_recv.at[j], core_dev)
 
     def far_copy():
         return remote(far_stage, far_got, tp_send.at[2], tp_recv.at[2], side_dev)
@@ -322,31 +323,22 @@
     def projected(s, c):
         return matmul(gated[aligned(s * 2 + c, quarter), :], out_proj[...])
 
-    near_stage[0] = projected(1 - side, 1 - core).astype(BF16)
+    near_buf[0] = projected(1 - side, 1 - core).astype(BF16)
     near_copy(0).start()
-    near_stage[1] = projected(side, 1 - core).astype(BF16)
+    near_buf[1] = projected(side, 1 - core).astype(BF16)
     near_copy(1).start()
     far_keep[...] = projected(1 - side, core)
     near_copy(0).wait_recv()
-    far_stage[...] = (far_keep[...] + near_got[0].astype(F32)).astype(BF16)
+    far_stage[...] = (far_keep[...] + near_buf[2].astype(F32)).astype(BF16)
     far_copy().start()
     own_keep[...] = projected(side, core)
 
-    for load in loads[: 1 + blocks]:
-        load.wait()
-
-    def grad_inner_of(k, carry):
-        at = aligned(k, group)
-        grad_inner[at, :] = times_transpose(ups[at, :], w_down[...])
-        return carry
-
-    lax.fori_loop(0, outer, grad_inner_of, 0)
     near_copy(1).wait_recv()
     far_copy().wait_recv()
     middle = hidden_ref[...].astype(F32) + (
-        own_keep[...] + near_got[1].astype(F32) + far_got[...].astype(F32)
+        own_keep[...] + near_buf[3].astype(F32) + far_got[...].astype(F32)
     )
-    middle_out[...] = middle
+    middle_buf[...] = middle
     rows[0:quarter, :] = (middle * norm_scales(middle) * gain_ref[...]).astype(BF16)
 
     def entry(k, j):
@@ -396,7 +388,7 @@
             pl.when(exists)(z_copy(way, k).start)
         y_copy(k).start()
 
-    for load in loads[1 + blocks :]:
+    for load in loads:
         load.wait()
     forward(1)
 
@@ -411,7 +403,7 @@
         rows_k = rows[at, :]
         gate_vals = matmul(rows_k, w_gate[...])
         up_vals = matmul(rows_k, w_up[...])
-        incoming = grad_inner[at, :]
+        incoming = times_transpose(ups[at, :], w_down[...])
         sig = jax.nn.sigmoid(gate_vals)
         silu = gate_vals * sig
         grad_gate[at, :] = (incoming * up_vals * (sig * (1.0 + gate_vals * (1.0 - sig)))).astype(BF16)
@@ -420,91 +412,173 @@
         return carry
 
     lax.fori_loop(0, outer, turn_forward, 0)
-    inner_store = pltpu.make_async_copy(inner, inner_out, store_sem.at[0])
-    inner_store.start()
-
-    def y_sum(k):
+
+    near_copy(0).wait_send()
+    near_copy(1).wait_send()
+
+    def y_sum(which, k):
         at = aligned(k, quarter)
-        return remote(y_stage.at[at, :], y_got.at[at, :], rys.at[k], ryr.at[k], pair_dev)
+        src = y_stage.at[at, :] if which == 0 else near_buf.at[k]
+        got = y_got.at[aligned(which * outer + k, quarter), :]
+        return remote(src, got, rys.at[which, k], ryr.at[which, k], pair_dev)
+
+    def half_rows(k, j):
+        return pl.ds(pl.multiple_of((k * 2 + j) * quarter, quarter), quarter)
 
     def turn_parts(step, carry):
         k = slot_of(delta_of(last - step))
-        at = aligned(k, group)
-        part = times_transpose(grad_gate[at, :], w_gate[...]) + times_transpose(
-            grad_up[at, :], w_up[...]
-        )
-        y_stage[aligned(k, quarter), :] = part[quarter:].astype(BF16)
-        y_sum(k).start()
-        keep[aligned(k, quarter), :] = part[:quarter]
+        part = times_transpose(grad_gate[half_rows(k, 1), :], w_gate[...]) + times_transpose(
+            grad_up[half_rows(k, 1), :], w_up[...]
+        )
+        y_stage[aligned(k, quarter), :] = part.astype(BF16)
+        y_sum(0, k).start()
         return carry
 
+    def turn_outputs(step, carry):
+        k = slot_of(delta_of(last - step))
+        near_buf[k] = matmul(inner[half_rows(k, 1), :], w_down[...]).astype(BF16)
+        y_sum(1, k).start()
+        part = times_transpose(grad_gate[half_rows(k, 0), :], w_gate[...]) + times_transpose(
+            grad_up[half_rows(k, 0), :], w_up[...]
+        )
+        keep[aligned(k, quarter), :] = part.astype(BF16)
+        return carry
+
     lax.fori_loop(0, outer, turn_parts, 0)
-
-    def z_sum(way, k):
+    lax.fori_loop(0, outer, turn_outputs, 0)
+
+    def z_got_rows(which, way, k):
+        return aligned((which * 2 + way) * outer + k, quarter)
+
+    def z_sum(which, way, k):
         to = wrap(k + 1 - 2 * way)
         return remote(
-            z_stage.at[aligned(k, quarter), :],
-            z_got.at[pl.ds(pl.multiple_of((way * outer + to) * quarter, quarter), quarter), :],
-            rzs.at[k], rzr.at[way, to], nexts[way],
-        )
-
-    def z_got_at(way, k):
-        return z_got[pl.ds(pl.multiple_of((way * outer + k) * quarter, quarter), quarter), :]
-
-    def z_sum_arrived(way, k):
+            z_stage.at[aligned(k, quarter), :], z_got.at[z_got_rows(which, way, to), :],
+            rzs.at[which, k], rzr.at[which, way, to], nexts[way],
+        )
+
+    def z_got_at(which, way, k):
+        return z_got[z_got_rows(which, way, k), :].astype(F32)
+
+    def z_sum_arrived(which, way, k):
         return remote(
-            z_stage.at[aligned(k, quarter), :], z_stage.at[aligned(k, quarter), :],
-            rzs.at[k], rzr.at[way, k], nexts[way],
-        )
-
-    def gate_up_stores(c):
-        at = aligned(c, chunk)
-        return (
-            pltpu.make_async_copy(stage_gate.at[at, :], dw_both.at[0, at, :], store_sem.at[1 + 2 * c]),
-            pltpu.make_async_copy(stage_up.at[at, :], dw_both.at[1, at, :], store_sem.at[2 + 2 * c]),
-        )
-
-    def weight_chunk(c):
-        at = aligned(c, chunk)
-        some = rows[:, at]
-        stage_gate[at, :] = outer_sum(some, grad_gate[...]).astype(BF16)
-        stage_up[at, :] = outer_sum(some, grad_up[...]).astype(BF16)
-        for store in gate_up_stores(c):
-            store.start()
-
-    def turn_sums(step, carry):
-        weight_chunk(step)
+            z_stage.at[aligned(k, quarter), :], z_got.at[z_got_rows(which, way, k), :],
+            rzs.at[which, k], rzr.at[which, way, k], nexts[way],
+        )
+
+    def own_share(which, k):
+        if which == 0:
+            share = keep[aligned(k, quarter), :].astype(F32)
+        else:
+            share = matmul(inner[half_rows(k, 0), :], w_down[...])
+        return share + y_got[aligned(which * outer + k, quarter), :].astype(F32)
+
+    def chain(which, step):
         delta = delta_of(last - step)
         k = slot_of(delta)
         at = aligned(k, quarter)
-        y_sum(k).wait_recv()
-        own = keep[at, :] + y_got[at, :].astype(F32)
-        for way, (here, before) in enumerate(
-            ((delta > 0, line > 0), (delta < 0, line < last))
-        ):
+        y_sum(which, k).wait_recv()
+        own = own_share(which, k)
+        if which == 1:
+            z_sum(0, 0, k).wait_send()
+        for way, (here, before) in enumerate(((delta > 0, line > 0), (delta < 0, line < last))):
 
             @pl.when(here & before)
             def _():
-                z_sum_arrived(way, k).wait_recv()
-                z_stage[at, :] = (own + z_got_at(way, k).astype(F32)).astype(BF16)
+                z_sum_arrived(which, way, k).wait_recv()
+                z_stage[at, :] = (own + z_got_at(which, way, k)).astype(BF16)
 
             @pl.when(here & jnp.logical_not(before))
             def _():
                 z_stage[at, :] = own.astype(BF16)
 
-            pl.when(here)(z_sum(way, k).start)
-        return carry
-
-    lax.fori_loop(0, last, turn_sums, 0)
-    weight_chunk(last)
-    y_sum(0).wait_recv()
-    for way, exists in ((0, line > 0), (1, line < last)):
-        pl.when(exists)(z_sum_arrived(way, 0).wait_recv)
-    below = jnp.where(line > 0, z_got_at(0, 0).astype(F32), 0.0)
-    above = jnp.where(line < last, z_got_at(1, 0).astype(F32), 0.0)
-    grad_two = keep[0:quarter, :] + y_got[0:quarter, :].astype(F32) + below + above
-
-    values = middle_out[...]
+            pl.when(here)(z_sum(which, way, k).start)
+
+    def chain_end(which):
+        y_sum(which, 0).wait_recv()
+        own = own_share(which, 0)
+        for way, exists in ((0, line > 0), (1, line < last)):
+            pl.when(exists)(z_sum_arrived(which, way, 0).wait_recv)
+        below = jnp.where(line > 0, z_got_at(which, 0, 0), 0.0)
+        above = jnp.where(line < last, z_got_at(which, 1, 0), 0.0)
+        return own + below + above
+
+    half_model = model // 2
+    piece = half_model // 2
+
+    def stage_rows(owner, r):
+        return pl.ds(pl.multiple_of(owner * half_model + r * piece, piece), piece)
+
+    stages = (stage_gate, stage_up)
+
+    def piece_at(ref, a, r):
+        return ref.at[a, pl.ds(r * piece, piece), :]
+
+    def piece_near(a, r):
+        return remote(
+            stages[a].at[stage_rows(1 - core, r), :], piece_at(part_got, a, r),
+            p_near_send.at[a, r], p_near_recv.at[a, r], core_dev,
+        )
+
+    def piece_far(a, r):
+        return remote(
+            stages[a].at[stage_rows(core, r), :], piece_at(part_far, a, r),
+            p_far_send.at[a, r], p_far_recv.at[a, r], side_dev,
+        )
+
+    def piece_store(a, r):
+        return pltpu.make_async_copy(
+            piece_at(part_got, a, r), dw_both.at[a, stage_rows(core, r), :], store_sem.at[1 + 2 * a + r]
+        )
+
+    def piece_out(a, r):
+        return remote(
+            piece_at(part_got, a, r), dw_both.at[a, stage_rows(core, r), :],
+            p_out_send.at[a, r], p_out_recv.at[a, r], core_dev,
+        )
+
+    def pieces(mine, r):
+        at = stage_rows(core if mine else 1 - core, r)
+        some = rows[:, at]
+        for a, grads in enumerate((grad_gate, grad_up)):
+            stages[a][at, :] = outer_sum(some, grads[...]).astype(BF16)
+            if not mine:
+                piece_near(a, r).start()
+
+    def pieces_sum(r):
+        at = stage_rows(core, r)
+        for a in range(2):
+            piece_near(a, r).wait_recv()
+            stages[a][at, :] = (
+                stages[a][at, :].astype(F32) + piece_at(part_got, a, r)[...].astype(F32)
+            ).astype(BF16)
+            piece_far(a, r).start()
+
+    def pieces_total(r):
+        for a in range(2):
+            piece_far(a, r).wait_recv()
+            total = stages[a][stage_rows(core, r), :].astype(F32) + piece_at(part_far, a, r)[
+                ...
+            ].astype(F32)
+            piece_at(part_got, a, r)[...] = total.astype(BF16)
+            piece_store(a, r).start()
+            piece_out(a, r).start()
+
+    work = [
+        functools.partial(pieces, False, 0), functools.partial(pieces, True, 0),
+        functools.partial(pieces_sum, 0), functools.partial(pieces, False, 1),
+        functools.partial(pieces, True, 1), functools.partial(pieces_sum, 1),
+    ]
+    for step in range(last):
+        for _ in range(2):
+            if work:
+                work.pop(0)()
+        chain(0, step)
+    for some_work in work:
+        some_work()
+    grad_two = chain_end(0)
+
+    values = middle_buf[...]
     back, gain_terms = norm_back(values, norm_scales(values), gain_ref[...], grad_two)
     grads = ups[0:quarter, :].astype(F32) + back
     branch[side, core] = grads.astype(BF16)
@@ -518,44 +592,54 @@
     grad_out[...] = grads
     gain_out[...] = jnp.sum(gain_terms, axis=0, keepdims=True)
 
-    def down_store(c):
-        at = aligned(c, chunk)
-        return pltpu.make_async_copy(
-            stage_down.at[:, at], dw_down.at[:, at], store_sem.at[1 + 2 * outer + c]
-        )
-
-    def turn_down(c, carry):
-        at = aligned(c, chunk)
-        stage_down[:, at] = outer_sum(inner[...], ups[:, at]).astype(BF16)
-        down_store(c).start()
-        return carry
-
-    lax.fori_loop(0, outer, turn_down, 0)
-    spread_copy(0, side, side_dev).wait_recv()
-    spread_copy(2, 1 - side, core_dev).start()
-    spread_copy(1, side, core_dev).wait_recv()
-
-    inner_store.wait()
-    near_copy(0).wait_send()
-    near_copy(1).wait_send()
-    far_copy().wait_send()
     for way, exists in ((0, line < last), (1, line > 0)):
         pl.when(exists)(z_copy(way, 0).wait_send)
 
-    def turn_drain(i, carry):
+    def turn_sent(i, carry):
         delta = delta_of(i)
         k = slot_of(delta)
         y_copy(k).wait_send()
-        y_sum(k).wait_send()
-        for store in gate_up_stores(i):
-            store.wait()
-        down_store(i).wait()
         for way, exists in enumerate(goes_on(delta)):
             pl.when(exists)(z_copy(way, k).wait_send)
-        pl.when(delta != 0)(z_sum(0, k).wait_send)
         return carry
 
+    lax.fori_loop(0, outer, turn_sent, 0)
+
+    def turn_down(c, carry):
+        at = aligned(c, chunk)
+        stage_down[0:units, at] = outer_sum(inner[...], ups[:, at]).astype(BF16)
+        return carry
+
+    chain(1, 0)
+    lax.fori_loop(0, outer, turn_down, 0)
+    down_store = pltpu.make_async_copy(stage_down.at[pl.ds(0, units), :], dw_down, store_sem.at[0])
+    down_store.start()
+    for step in range(1, last):
+        chain(1, step)
+    spread_copy(0, side, side_dev).wait_recv()
+    spread_copy(2, 1 - side, core_dev).start()
+    pieces_total(0)
+    layer_out[...] = (middle_buf[...] + chain_end(1)).astype(BF16)
+    pieces_total(1)
+    spread_copy(1, side, core_dev).wait_recv()
+
+    down_store.wait()
+    far_copy().wait_send()
+
+    def turn_drain(i, carry):
+        k = slot_of(delta_of(i))
+        for which in range(2):
+            y_sum(which, k).wait_send()
+        pl.when(i > 0)(z_sum(1, 0, k).wait_send)
+        return carry
+
     lax.fori_loop(0, outer, turn_drain, 0)
+    for a in range(2):
+        for r in range(2):
+            piece_near(a, r).wait_send()
+            piece_far(a, r).wait_send()
+            piece_store(a, r).wait()
+            piece_out(a, r).wait()
     spread_copy(0, side, side_dev).wait_send()
     spread_copy(1, side, core_dev).wait_send()
     spread_copy(2, 1 - side, core_dev).wait()
@@ -569,62 +653,62 @@
     anywhere = pl.BlockSpec(memory_space=pl.ANY)
     dma = pltpu.SemaphoreType.DMA
     line_rows = outer * quarter
+    half = (2, model // 2, units)
     return pl.pallas_call(
         functools.partial(middle_kernel, outer),
         out_shape=[
-            jax.ShapeDtypeStruct((quarter, model), F32),
+            jax.ShapeDtypeStruct((quarter, model), BF16),
             jax.ShapeDtypeStruct((quarter, model), F32),
             jax.ShapeDtypeStruct((1, model), F32),
             jax.ShapeDtypeStruct((sides, 2, quarter, model), BF16),
-            jax.ShapeDtypeStruct((rows_n, units), BF16),
             jax.ShapeDtypeStruct((2, model, units), BF16),
             jax.ShapeDtypeStruct((units, model), BF16),
         ],
         in_specs=[vmem] * 4 + [anywhere] * (3 + len(ups)),
-        out_specs=[vmem] * 4 + [anywhere] * 3,
+        out_specs=[vmem] * 4 + [anywhere] * 2,
         scratch_shapes=[
             pltpu.VMEM((model, units), BF16),
             pltpu.VMEM((model, units), BF16),
             pltpu.VMEM((units, model), BF16),
             pltpu.VMEM((rows_n, model), BF16),
             pltpu.VMEM((rows_n, model), BF16),
-            pltpu.VMEM((rows_n, units), F32),
             pltpu.VMEM((rows_n, units), BF16),
             pltpu.VMEM((rows_n, units), BF16),
             pltpu.VMEM((rows_n, units), BF16),
-            pltpu.VMEM((2, quarter, model), BF16),
-            pltpu.VMEM((2, quarter, model), BF16),
+            pltpu.VMEM((4, quarter, model), BF16),
             pltpu.VMEM((quarter, model), BF16),
             pltpu.VMEM((quarter, model), BF16),
             pltpu.VMEM((quarter, model), F32),
-            pltpu.VMEM((quarter, model), F32),
-            pltpu.VMEM((line_rows, model), F32),
-            pltpu.VMEM((line_rows, model), BF16),
             pltpu.VMEM((line_rows, model), BF16),
             pltpu.VMEM((line_rows, model), BF16),
             pltpu.VMEM((2 * line_rows, model), BF16),
+            pltpu.VMEM((line_rows, model), BF16),
+            pltpu.VMEM((4 * line_rows, model), BF16),
+            pltpu.VMEM(half, BF16),
+            pltpu.VMEM(half, BF16),
             dma((3 + len(ups),)),
-            dma((1 + 3 * outer,)),
+            dma((5,)),
             dma((6,)),
             dma((6,)),
             dma((2, outer)),
             dma((outer,)),
             dma((outer,)),
             dma((outer,)),
-            dma((outer,)),
-            dma((outer,)),
-            dma((outer,)),
             dma((2, outer)),
-        ],
+            dma((2, outer)),
+            dma((2, outer)),
+            dma((2, 2, outer)),
+        ]
+        + [dma((2, 2))] * 6,
         compiler_params=pltpu.CompilerParams(
-            collective_id=2, has_side_effects=True, vmem_limit_bytes=58 * 1024 * 1024
+            collective_id=2, has_side_effects=True, vmem_limit_bytes=63 * 1024 * 1024
         ),
         cost_estimate=pl.CostEstimate(flops=3 * 10**10, bytes_accessed=4 * 10**7, transcendentals=0),
         name="middle",
     )(gated, out_proj, hidden, gain, w_gate, w_up, w_down, *ups)
 
 
-FFN_CHUNKS = 6
+FFN_CHUNKS = 2
 
 
 def finish_kernel(
@@ -634,18 +718,18 @@
     MESH = pl.DeviceIdType.MESH
     parts = refs[:streams]
     (part_ref, hidden_ref, scale_ref, gain_ref, middle_ref, sums_ref) = refs[streams : streams + 6]
-    both_in, last_in = refs[streams + 6 : streams + 8]
+    last_in, layer_ref = refs[streams + 6 : streams + 8]
     outs = refs[streams + 8 : 2 * streams + 8]
-    grad_out, sums_out, both_out, last_out = refs[2 * streams + 8 : 2 * streams + 12]
+    grad_out, sums_out, last_out, layer_out = refs[2 * streams + 8 : 2 * streams + 12]
     rest = refs[2 * streams + 12 :]
     got = rest[:streams]
     staged = rest[streams : 2 * streams]
     (near_got, far_got, keep_buf, far_stage, sums_got, sums_stage) = rest[2 * streams : 2 * streams + 6]
     rest = rest[2 * streams + 6 :]
-    (both_keep, both_got, both_far, last_keep, last_got, last_far) = rest[:6]
-    (f_load, f_near_send, f_near_recv, f_far_send, f_far_recv, f_store, f_out_send, f_out_recv) = rest[6:14]
-    (reduce_send, reduce_recv, gather_send, gather_recv, pair_send, pair_recv) = rest[14:20]
-    tp_send, tp_recv, sums_send, sums_recv = rest[20:]
+    (last_keep, last_got, last_far, layer_send, layer_recv) = rest[:5]
+    (f_load, f_near_send, f_near_recv, f_far_send, f_far_recv, f_store, f_out_send, f_out_recv) = rest[5:13]
+    (reduce_send, reduce_recv, gather_send, gather_recv, pair_send, pair_recv) = rest[13:19]
+    tp_send, tp_recv, sums_send, sums_recv = rest[19:]
 
     sp_i = lax.axis_index("sp")
     tp_i = lax.axis_index("tp")
@@ -843,51 +927,41 @@
             spread_copy(2, side, core_dev).wait_send()
             spread_copy(3, 1 - side, core_dev).wait_send()
 
-    both_half = both_keep.shape[1]
     last_half = last_keep.shape[0]
 
-    def ffn_at(j, refs, whole, owner):
-        if j < 4:
-            count = both_half // 2
-            start = (j % 2) * count
-            if whole:
-                start = pl.multiple_of(owner * both_half + start, count)
-            return refs[0].at[j // 2, pl.ds(start, count), :]
-        count = last_half // 2
-        start = (j - 4) * count
+    def ffn_at(j, ref, whole, owner):
+        count = last_half // FFN_CHUNKS
+        start = j * count
         if whole:
             start = pl.multiple_of(owner * last_half + start, count)
-        return refs[1].at[pl.ds(start, count), :]
-
-    ffn_in = (both_in, last_in)
-    ffn_out = (both_out, last_out)
+        return ref.at[pl.ds(start, count), :]
 
     def ffn_keep(j):
-        return ffn_at(j, (both_keep, last_keep), False, 0)
+        return ffn_at(j, last_keep, False, 0)
 
     def ffn_got(j):
-        return ffn_at(j, (both_got, last_got), False, 0)
+        return ffn_at(j, last_got, False, 0)
 
     def ffn_far(j):
-        return ffn_at(j, (both_far, last_far), False, 0)
+        return ffn_at(j, last_far, False, 0)
 
     def ffn_load(j):
-        return pltpu.make_async_copy(ffn_at(j, ffn_in, True, core), ffn_keep(j), f_load.at[j])
+        return pltpu.make_async_copy(ffn_at(j, last_in, True, core), ffn_keep(j), f_load.at[j])
 
     def ffn_near_copy(j):
         return remote(
-            ffn_at(j, ffn_in, True, 1 - core), ffn_got(j), f_near_send.at[j], f_near_recv.at[j], core_dev
+            ffn_at(j, last_in, True, 1 - core), ffn_got(j), f_near_send.at[j], f_near_recv.at[j], core_dev
         )
 
     def ffn_far_copy(j):
         return remote(ffn_keep(j), ffn_far(j), f_far_send.at[j], f_far_recv.at[j], side_dev)
 
     def ffn_store(j):
-        return pltpu.make_async_copy(ffn_got(j), ffn_at(j, ffn_out, True, core), f_store.at[j])
+        return pltpu.make_async_copy(ffn_got(j), ffn_at(j, last_out, True, core), f_store.at[j])
 
     def ffn_out_copy(j):
         return remote(
-            ffn_got(j), ffn_at(j, ffn_out, True, core), f_out_send.at[j], f_out_recv.at[j], core_dev
+            ffn_got(j), ffn_at(j, last_out, True, core), f_out_send.at[j], f_out_recv.at[j], core_dev
         )
 
     def ffn_sum(j):
@@ -936,15 +1010,37 @@
     def later(do, *args):
         return functools.partial(do, *args)
 
+    def layer_copy(slot, s, device):
+        block = layer_out.at[s, core]
+        src = block if slot == 2 else layer_ref
+        return remote(src, block, layer_send.at[slot], layer_recv.at[slot], device)
+
+    def layer_own():
+        return pltpu.make_async_copy(layer_ref, layer_out.at[side, core], layer_send.at[3])
+
+    def layer_step(step):
+        if step == 0:
+            layer_copy(0, side, side_dev).start()
+            layer_copy(1, side, core_dev).start()
+            layer_own().start()
+        if step == 1:
+            layer_copy(0, 1 - side, side_dev).wait_recv()
+            layer_copy(2, 1 - side, core_dev).start()
+        if step == 2:
+            layer_copy(1, side, core_dev).wait_recv()
+            layer_own().wait()
+            layer_copy(0, side, side_dev).wait_send()
+            layer_copy(1, side, core_dev).wait_send()
+            layer_copy(2, 1 - side, core_dev).wait()
+
     extra = [
-        later(input_step, 0), later(input_step, 1), later(ffn_sum, 0), later(ffn_sum, 1),
-        later(input_step, 2), later(ffn_sum, 2), later(ffn_sum, 3), later(input_step, 3),
-        later(ffn_sum, 4), later(ffn_sum, 5), later(sums_step, 0), later(ffn_total, 0),
-        later(sums_step, 1), later(sums_step, 2), later(ffn_total, 1), later(input_step, 4),
-        later(sums_step, 3), later(ffn_total, 2), later(sums_step, 4),
+        later(input_step, 0), later(input_step, 1), later(layer_step, 0), later(ffn_sum, 0),
+        later(ffn_sum, 1), later(sums_step, 0), later(input_step, 2), later(sums_step, 1),
+        later(layer_step, 1), later(sums_step, 2), later(input_step, 3), later(sums_step, 3),
+        later(ffn_total, 0), later(sums_step, 4), later(layer_step, 2), later(input_step, 4),
+        later(ffn_total, 1),
     ]
     extra += [later(sums_step, index) for index in range(5, rounds + 1)]
-    extra += [later(ffn_total, index) for index in range(3, FFN_CHUNKS)]
     for index in range(FFN_CHUNKS):
         ffn_near_copy(index).start()
         ffn_load(index).start()
@@ -967,7 +1063,7 @@
         ffn_drain(index)
 
 
-def finish(parts, part, hidden, scales, gain, middle, sums, ffn, outer, sp_n, tp_n):
+def finish(parts, part, hidden, scales, gain, middle, sums, ffn_last, layer, outer, sp_n, tp_n):
     streams = len(parts)
     sides = tp_n // 2
     quarter, model = hidden.shape
@@ -984,9 +1080,12 @@
             jax.ShapeDtypeStruct((sides, 2, quarter, model), BF16),
             jax.ShapeDtypeStruct(sums.shape, F32),
         ]
-        + [jax.ShapeDtypeStruct(f.shape, BF16) for f in ffn],
-        in_specs=[vmem] * (streams + 6) + [anywhere] * 2,
-        out_specs=[vmem] * (streams + 2) + [anywhere] * 2,
+        + [
+            jax.ShapeDtypeStruct(ffn_last.shape, BF16),
+            jax.ShapeDtypeStruct((sides, 2, quarter, model), BF16),
+        ],
+        in_specs=[vmem] * (streams + 6) + [anywhere, vmem],
+        out_specs=[vmem] * (streams + 2) + [anywhere, vmem],
         scratch_shapes=[pltpu.VMEM(c, BF16) for c in chunk]
         + [pltpu.VMEM(c, BF16) for c in chunk]
         + [
@@ -997,8 +1096,8 @@
             pltpu.VMEM((rounds,) + sums.shape, F32),
             pltpu.VMEM((rounds,) + sums.shape, F32),
         ]
-        + [pltpu.VMEM((2, ffn[0].shape[1] // 2, ffn[0].shape[2]), BF16)] * 3
-        + [pltpu.VMEM((ffn[1].shape[0] // 2, ffn[1].shape[1]), BF16)] * 3
+        + [pltpu.VMEM((ffn_last.shape[0] // 2, ffn_last.shape[1]), BF16)] * 3
+        + [dma((4,))] * 2
         + [dma((FFN_CHUNKS,))] * 8
         + [dma((streams, 2, last))] * 4
         + [dma((streams, 1 + 2 * last))] * 2
@@ -1009,7 +1108,7 @@
         ),
         cost_estimate=pl.CostEstimate(flops=10**9, bytes_accessed=10**8, transcendentals=0),
         name="finish",
-    )(*parts, part, hidden, scales, gain, middle, sums, *ffn)
+    )(*parts, part, hidden, scales, gain, middle, sums, ffn_last, layer)
 
 
 def body(
@@ -1192,7 +1291,7 @@
 
     fused = outer * quarter <= 512 and outer > 1 and tp_n == 4
     if fused:
-        middle, grad_middle_quarter, ffn_gain_sum, branch, inner_rows, *ffn_parts = middle_layer(
+        layer_quarter, grad_middle_quarter, ffn_gain_sum, branch, *ffn_parts = middle_layer(
             gated,
             output_proj,
             lax.dynamic_slice_in_dim(hidden, quarter_first, quarter),
@@ -1206,9 +1305,6 @@
         )
         grad_branch = branch.reshape(rows_dev, model)
         ffn_gain_sum = ffn_gain_sum[0]
-        inner_list = [
-            inner_rows[k * 2 * quarter : (k + 1) * 2 * quarter] for k in range(outer)
-        ]
     else:
         attn_quarter = scatter_tp(matmul(gated, output_proj))
         hidden_quarter = lax.dynamic_slice_in_dim(hidden, quarter_first, quarter).astype(F32)
@@ -1240,10 +1336,16 @@
         grad_middle_quarter = grad_quarter.astype(F32) + norm_grad_two
         grad_branch = gather_tp(grad_middle_quarter.astype(BF16))
         ffn_gain_sum = jnp.sum(ffn_gain_terms, axis=0)
-
-    mlp_parts = [matmul(inner_list[k], ffn_down).reshape(2, quarter, model) for k in range(outer)]
-    mlp_quarter = scatter_sp(mlp_parts)
-    layer_out = gather_tp((middle + mlp_quarter).astype(BF16))
+        mlp_parts = [
+            matmul(inner_list[k], ffn_down).reshape(2, quarter, model) for k in range(outer)
+        ]
+        layer_quarter = (middle + scatter_sp(mlp_parts)).astype(BF16)
+
+    def sum_tp(part):
+        total = part.astype(BF16).astype(F32)
+        total = total + core(total.astype(BF16)).astype(F32)
+        low = total.astype(BF16)
+        return (low.astype(F32) + side(low).astype(F32)).astype(BF16)
 
     if not fused:
         rows_all = jnp.concatenate(rows_list)
@@ -1255,7 +1357,8 @@
             jnp.stack([outer_sum(rows_all, gate_all), outer_sum(rows_all, grad_up_all)]),
             outer_sum(inner_all, up_all),
         ]
-    ffn_parts = [part.astype(BF16) for part in ffn_parts]
+        ffn_parts = [sum_tp(ffn_parts[0]), ffn_parts[1].astype(BF16)]
+    ffn_both, ffn_last = ffn_parts
 
     branch_other = swap_half(grad_branch)
     branch_own = lax.dynamic_slice_in_dim(grad_branch, pair_i * (model // 2), model // 2, 1)
@@ -1333,12 +1436,13 @@
         attn_norm[None, :],
         grad_middle_quarter,
         gains,
-        ffn_parts,
+        ffn_last,
+        layer_quarter,
         outer,
         sp_n,
         tp_n,
     )
-    output_all, gate_all_w, query_all, kv_all, input_all, gains, ffn_both, ffn_last = finished
+    output_all, gate_all_w, query_all, kv_all, input_all, gains, ffn_last, layer_all = finished
     output_grad = jnp.concatenate([output_all[0], output_all[1]], axis=1).astype(F32)
     gate_grad = gate_all_w.reshape(model, heads * head_width).astype(F32)
     query_grad = query_all.reshape(model, heads * head_width).astype(F32)
@@ -1348,7 +1452,7 @@
     hidden_grad = input_all.reshape(rows_dev, model).astype(F32)
     gains = gains.reshape(-1)
     return (
-        layer_out,
+        layer_all.reshape(rows_dev, model),
         hidden_grad,
         gains[:model],
         query_grad,

time: 694 us -> 642 us (0.925)
  waiting for transfers between devices: 109 us -> 73.6 us
  starting transfers between devices: 65.1 us -> 43.8 us
  Pallas kernels: 349 us -> 366 us
    pallas_call x1, Pallas kernels: 133 us -> 186 us  [middle_layer(): pl.pallas_call(functools.partial(middle_kernel, outer), out_shape=[jax.Sh...]
    ppermute x20 -> x16, waiting for transfers between devices: 104 us -> 62.1 us  [pair(): return lax.ppermute(value, 'sp', pair_pairs)]
    pallas_call x1, Pallas kernels: 189 us -> 153 us  [finish(): pl.pallas_call(functools.partial(finish_kernel, outer, sides, sp_n, tp_n,...]
    ppermute x6 -> x3, starting transfers between devices: 28.2 us -> 13 us  [ring(): return lax.ppermute(value, 'sp', ring_pairs)]
    ppermute x2, waiting for transfers between devices: 0.01 us -> 9.55 us  [body(): travelling = lax.ppermute(total.astype(BF16), 'sp', down_pairs(k))]
    dot_general x8 -> x4, matrix products: 18.9 us -> 9.79 us  [matmul(): return jnp.dot(left, right, preferred_element_type=F32)]
    ppermute x20 -> x16, starting transfers between devices: 26.3 us -> 22.1 us  [pair(): return lax.ppermute(value, 'sp', pair_pairs)]
  transfers between devices with their start and end apart: 34 -> 25, of which waited for: 12 -> 10; matrix products, arithmetic and copies ran while one was open for 17% -> 13% of each run, Pallas kernels for 31% -> 4%
where the time goes in v6:
time: 642 us; the launch traced here: 633 us
  Pallas kernels  366 us (57%)
  waiting for transfers between devices  73.6 us (11%)
  other arithmetic  58.7 us (9%)
  local copies, waits for them, and re-layouts  44.2 us (7%)
  starting transfers between devices  43.8 us (7%)
  matrix products  37.6 us (6%)
  between operations  9.5 us (1%)
    pallas_call x1, Pallas kernels, middle_layer(): pl.pallas_call(functools.partial(middle_kernel, outer), out_shape=[jax.Sh...  186 us
    pallas_call x1, Pallas kernels, finish(): pl.pallas_call(functools.partial(finish_kernel, outer, sides, sp_n, tp_n,...  153 us
    ppermute x16, waiting for transfers between devices, pair(): return lax.ppermute(value, 'sp', pair_pairs)  62.1 us
    ppermute x16, starting transfers between devices, pair(): return lax.ppermute(value, 'sp', pair_pairs)  22.1 us
    dot_general x5, matrix products, times_transpose(): lax.dot_general(left, right, (((1,), (1,)), ((), ())), preferred_element_...  17.6 us
    pallas_call x3, Pallas kernels, attn_backward(): pl.pallas_call(functools.partial(attn_backward_kernel, first, diagonal, s...  14.4 us
    ppermute x3, starting transfers between devices, ring(): return lax.ppermute(value, 'sp', ring_pairs)  13 us
  transfers between devices with their start and end apart: 25, of which 10 were waited for; matrix products, arithmetic and copies ran while one was open for 13% of the time, Pallas kernels for 4%

profile of v6, /device:TPU:0, one launch (start us, length us, event | category | flops | bytes accessed | tf_op | source)
XLA Modules:
  0.0 633.1 jit_solution(16103038685048540515)
XLA Ops:
  0.7 2.2 fusion
  11.7 1.8 pad_maximum_fusion.6.kv_a
  13.5 5.8 collective-permute-start
  19.3 1.5 collective-permute-start.4
  20.8 1.9 constant_dynamic-slice_fusion.4.refs_7_
  23.5 1.9 constant_dynamic-slice_fusion
  26.9 4.7 fusion.14
  32.2 2.9 multiply_reduce_fusion.1
  35.1 1.6 copy.89
  38.9 1.7 multiply_multiply_fusion
  46.2 2.0 copy.107
  57.6 2.3 constant_dynamic-slice_fusion.1
  63.4 3.0 collective-permute-start.9
  67.6 1.5 collective-permute-start.3
  70.2 1.5 collective-permute-start.2
  71.7 4.6 attn_forward.3
  76.3 1.9 collective-permute-done.9.refs_11_
  78.2 1.5 collective-permute-start.8
  79.8 9.2 %collective-permute-start.11 = (bf16[128,2048]{1,0:T(8,128)(2,1)}, bf16[128,2048]{1,0:T(8,128)(2,1)}, u32[]{:S(2)}, u32[]{:S(2)}) collective-permute-start(bf16[128,2048]{1,0:T(8,128)(2,1)} %collective-permute-done.9.refs_11_), channel_id=1, source_target_pairs={{0,2},{1,3},{2,4},{3,5},{4,6},{5,7},{6,0},{7,1},{8,10},{9,11},{10,... | collective-permute-start | bytes 1572872 | tf_op jit(solution)/shard_map/ppermute | solution.py:1158
  89.0 2.5 maximum_select_fusion.1
  92.3 3.8 attn_forward.4
  96.1 9.0 %collective-permute-done.2.kv_b = bf16[2,512,256]{2,1,0:T(8,128)(2,1)S(1)} collective-permute-done((bf16[2,512,256]{2,1,0:T(8,128)(2,1)S(1)}, bf16[2,512,256]{2,1,0:T(8,128)(2,1)S(1)}, u32[]{:S(2)}, u32[]{:S(2)}) %collective-permute-start.2) | collective-permute-done | bytes 524320 | tf_op jit(solution)/shard_map/ppermute | solution.py:1161
  105.9 3.8 attn_forward.5
  109.7 1.7 reshape.258
  111.8 1.6 collective-permute-start.12
  114.0 2.7 multiply_convert_fusion.1
  116.7 10.9 %collective-permute-done.10.refs_12_ = bf16[128,2048]{1,0:T(8,128)(2,1)} collective-permute-done((bf16[128,2048]{1,0:T(8,128)(2,1)}, bf16[128,2048]{1,0:T(8,128)(2,1)}, u32[]{:S(2)}, u32[]{:S(2)}) %collective-permute-start.10) | collective-permute-done | bytes 524320 | tf_op jit(solution)/shard_map/ppermute | solution.py:1161
  127.6 10.8 %collective-permute-done.12.refs_14_ = bf16[128,2048]{1,0:T(8,128)(2,1)} collective-permute-done((bf16[128,2048]{1,0:T(8,128)(2,1)}, bf16[128,2048]{1,0:T(8,128)(2,1)}, u32[]{:S(2)}, u32[]{:S(2)}) %collective-permute-start.12) | collective-permute-done | bytes 524320 | tf_op jit(solution)/shard_map/ppermute | solution.py:1161
  138.4 185.9 %middle.1 = (bf16[128,2048]{1,0:T(8,128)(2,1)}, f32[128,2048]{1,0:T(8,128)}, f32[1,2048]{1,0:T(1,128)}, bf16[2,2,128,2048]{3,2,1,0:T(8,128)(2,1)}, bf16[2,2048,7...) custom-call(bf16[512,512]{1,0:T(8,128)(2,1)} %get-tuple-element.76.refs_0_, bf16[512,2048]{1,0:T(8,128)(2,1)} %refs_1_.1, ...), custom_call_target="tpu_custom_call" | custom-call | flops 30000001024 | bytes 40000000 | tf_op jit(solution)/shard_map/middle/pallas_call | solution.py:657
  324.3 1.9 constant_dynamic-slice_fusion.2
  326.8 5.2 convert_multiply_fusion.3
  331.9 1.5 collective-permute-start.17
  335.1 3.3 attn_backward.3
  338.4 3.9 attn_backward.4
  342.3 7.2 %attn_backward.5 = (f32[512,512]{1,0:T(8,128)}, bf16[2,512,256]{2,1,0:T(8,128)(2,1)}, bf16[2,512,256]{2,1,0:T(8,128)(2,1)}) custom-call(s32[7]{0:T(128)} %stack.145.info, s32[1,512]{1,0:T(1,128)} %compare_select_fusion.starts, f32[2,2,512]{2,1,0:T(2,128)} %reshape.259.lse, f32[2,2,512]{2,1,0:T(2,128)} %reshape.261.deltas, bf16[512,512]{1,0:T(8,128)(2,1)} %bitcast.171, ...), custom_call_target="tpu_custom_call" | custom-call | flops 2684354560 | bytes 2097152 | tf_op jit(solution)/shard_map/attn_backward/pallas_call | solution.py:229
  356.3 3.8 collective-permute-start.18
  360.1 1.9 collective-permute-start.20
  362.1 8.8 %bitcast_convert_fusion = (f32[2048,768]{1,0:T(8,128)}, f32[2048,768]{1,0:T(8,128)}) fusion(bf16[2,2048,768]{2,1,0:T(8,128)(2,1)} %get-tuple-element.70), kind=kLoop, calls=%fused_computation.9 | loop fusion | flops 3145728 | bytes 18874368 | tf_op jit(solution)/shard_map/convert_element_type | solution.py:1467
  370.8 13.2 %collective-permute-done.21 = bf16[2,512,256]{2,1,0:T(8,128)(2,1)S(1)} collective-permute-done((bf16[2,512,256]{2,1,0:T(8,128)(2,1)S(1)}, bf16[2,512,256]{2,1,0:T(8,128)(2,1)S(1)}, u32[]{:S(2)}, u32[]{:S(2)}) %collective-permute-start.21) | collective-permute-done | bytes 524320 | tf_op jit(solution)/shard_map/ppermute | solution.py:1161
  385.0 3.3 fusion.51
  388.5 2.1 collective-permute-start.5
  390.6 3.5 convolution_convert_fusion.2.refs_1_
  395.3 2.0 collective-permute-start.19
  399.0 2.3 convolution_convert_fusion.1.refs_2_
  401.3 1.5 maximum_select_fusion
  402.8 3.7 collective-permute-done.5
  406.5 2.2 fusion.9.refs_0_
  408.7 8.1 %collective-permute-done.19 = bf16[2,512,256]{2,1,0:T(8,128)(2,1)S(1)} collective-permute-done((bf16[2,512,256]{2,1,0:T(8,128)(2,1)S(1)}, bf16[2,512,256]{2,1,0:T(8,128)(2,1)S(1)}, u32[]{:S(2)}, u32[]{:S(2)}) %collective-permute-start.19) | collective-permute-done | bytes 524320 | tf_op jit(solution)/shard_map/ppermute | solution.py:1161
  416.9 9.5 %collective-permute-done.23 = bf16[2,512,256]{2,1,0:T(8,128)(2,1)S(1)} collective-permute-done((bf16[2,512,256]{2,1,0:T(8,128)(2,1)S(1)}, bf16[2,512,256]{2,1,0:T(8,128)(2,1)S(1)}, u32[]{:S(2)}, u32[]{:S(2)}) %collective-permute-start.23) | collective-permute-done | bytes 524320 | tf_op jit(solution)/shard_map/ppermute | solution.py:1391
  427.8 2.8 fusion.49
  432.4 2.2 copy.115
  435.4 1.7 mul.521
  439.1 2.1 fusion.52
  443.3 4.2 fusion.4
  448.1 5.2 collective-permute-done.24
  453.4 2.3 convolution_convert_fusion.refs_3_
  455.6 153.1 %finish.1 = (bf16[2,512,1024]{2,1,0:T(8,128)(2,1)}, bf16[2,1024,512]{2,1,0:T(8,128)(2,1)}, bf16[2,1024,512]{2,1,0:T(8,128)(2,1)}, bf16[2,1024,512]{2,1,0:T(8,128...) custom-call(bf16[512,1024]{1,0:T(8,128)(2,1)} %fusion.9.refs_0_, ...), custom_call_target="tpu_custom_call" | custom-call | flops 1000000000 | bytes 100000000 | tf_op jit(solution)/shard_map/finish/pallas_call | solution.py:1076
  611.3 4.3 bitcast_convert_fusion.4
  615.6 2.7 bitcast_convert_fusion.3
  618.4 2.3 slice_convert_fusion
  620.8 2.7 bitcast_convert_fusion.2
  623.7 1.7 copy-done.12
  625.4 3.6 convert_element_type.200
  629.0 2.5 maximum_convert_fusion
  (218 shorter events, 55.1 us)
Async XLA Ops:
  0.6 4.8 copy-start.1
  0.7 3.5 copy-start.47
  0.7 4.8 copy-start.42
  2.9 39.2 %copy-start.44 = (f32[512]{0:T(512)}, f32[512]{0:T(512)S(1)}, u32[]{:S(2)}) copy-start(f32[512]{0:T(512)S(1)} %add_rsqrt_fusion.2) | copy-start | bytes 6148
  9.4 22.2 %copy-start.8 = (f32[512,256]{0,1:T(8,128)}, f32[512,256]{0,1:T(8,128)S(1)}, u32[]{:S(2)}) copy-start(f32[512,256]{0,1:T(8,128)S(1)} %get-tuple-element.116) | copy-start | bytes 1572868
  11.3 14.6 %copy-start.23 = (f32[512,64]{0,1:T(8,128)}, f32[512,64]{0,1:T(8,128)S(1)}, u32[]{:S(2)}) copy-start(f32[512,64]{0,1:T(8,128)S(1)} %get-tuple-element.110) | copy-start | bytes 393220
  13.5 48.6 %collective-permute-start = (bf16[2,512,256]{2,1,0:T(8,128)(2,1)}, bf16[2,512,256]{2,1,0:T(8,128)(2,1)}, u32[]{:S(2)}, u32[]{:S(2)}) collective-permute-start(bf16[2,512,256]{2,1,0:T(8,128)(2,1)} %pad_maximum_fusion.6.kv_a), channel_id=1, source_target_pairs={{0,2},{1,3},{2,4},{3,5},{4,6},{5,7},{8,10},{9,11},{10,12},{11,13},... | collective-permute-start | bytes 1572872 | tf_op jit(solution)/shard_map/ppermute | solution.py:1221
  19.3 50.4 %collective-permute-start.4 = (bf16[2,512,256]{2,1,0:T(8,128)(2,1)}, bf16[2,512,256]{2,1,0:T(8,128)(2,1)}, u32[]{:S(2)}, u32[]{:S(2)}) collective-permute-start(bf16[2,512,256]{2,1,0:T(8,128)(2,1)} %pad_maximum_fusion.6.kv_a), channel_id=1, source_target_pairs={{0,1},{1,0},{2,3},{3,2},{4,5},{5,4},{6,7},{7,6},{8,9},{9,8},{10,11... | collective-permute-start | bytes 1572872 | tf_op jit(solution)/shard_map/ppermute | solution.py:1161
  22.7 40.7 %collective-permute-start.7 = (bf16[128,2048]{1,0:T(8,128)(2,1)}, bf16[128,2048]{1,0:T(8,128)(2,1)}, u32[]{:S(2)}, u32[]{:S(2)}) collective-permute-start(bf16[128,2048]{1,0:T(8,128)(2,1)} %constant_dynamic-slice_fusion.4.refs_7_), channel_id=1, source_target_pairs={{0,2},{1,3},{2,4},{3,5},{4,6},{5,7},{6,0},{7,1},{8,10},{9,11},{10,... | collective-permute-start | bytes 1572872 | tf_op jit(solution)/shard_map/ppermute | solution.py:1158
  25.4 41.0 %collective-permute-start.15 = (bf16[512,512]{1,0:T(8,128)(2,1)}, bf16[512,512]{1,0:T(8,128)(2,1)}, u32[]{:S(2)}, u32[]{:S(2)}) collective-permute-start(bf16[512,512]{1,0:T(8,128)(2,1)} %constant_dynamic-slice_fusion), channel_id=1, source_target_pairs={{0,1},{1,0},{2,3},{3,2},{4,5},{5,4},{6,7},{7,6},{8,9},{9,8},{10,11... | collective-permute-start | bytes 1572872 | tf_op jit(solution)/shard_map/ppermute | solution.py:1161
  26.9 5.3 copy-start.7
  26.9 5.3 copy-start.25
  36.7 4.7 copy-start.4
  42.2 12.0 %copy-start.46 = (f32[512,2]{0,1:T(2,128)S(1)}, f32[512,2]{0,1:T(2,128)}, u32[]{:S(2)}) copy-start(f32[512,2]{0,1:T(2,128)} %get-tuple-element.107) | copy-start | bytes 12292
  54.2 8.6 %copy-start.49 = (f32[128]{0:T(128)S(1)}, f32[128]{0:T(128)}, u32[]{:S(2)}) copy-start(f32[128]{0:T(128)} %param.23) | copy-start | bytes 1540
  54.2 14.9 %copy-start.52 = (f32[128]{0:T(128)S(1)}, f32[128]{0:T(128)}, u32[]{:S(2)}) copy-start(f32[128]{0:T(128)} %param.24) | copy-start | bytes 1540
  62.1 8.1 %collective-permute-start.1 = (bf16[2,512,256]{2,1,0:T(8,128)(2,1)}, bf16[2,512,256]{2,1,0:T(8,128)(2,1)S(1)}, u32[]{:S(2)}, u32[]{:S(2)}) collective-permute-start(bf16[2,512,256]{2,1,0:T(8,128)(2,1)} %collective-permute-done.kv_a), channel_id=1, source_target_pairs={{2,4},{3,5},{4,6},{5,7},{10,12},{11,13},{12,14},{13,15},{18,20},{1... | collective-permute-start | bytes 1572872 | tf_op jit(solution)/shard_map/ppermute | solution.py:1221
  63.4 14.9 %collective-permute-start.9 = (bf16[128,2048]{1,0:T(8,128)(2,1)}, bf16[128,2048]{1,0:T(8,128)(2,1)}, u32[]{:S(2)}, u32[]{:S(2)}) collective-permute-start(bf16[128,2048]{1,0:T(8,128)(2,1)} %collective-permute-done.7.refs_9_), channel_id=1, source_target_pairs={{0,2},{1,3},{2,4},{3,5},{4,6},{5,7},{6,0},{7,1},{8,10},{9,11},{10,... | collective-permute-start | bytes 1572872 | tf_op jit(solution)/shard_map/ppermute | solution.py:1158
  66.3 13.4 %collective-permute-start.16 = (bf16[512,512]{1,0:T(8,128)(2,1)}, bf16[512,512]{1,0:T(8,128)(2,1)S(1)}, u32[]{:S(2)}, u32[]{:S(2)}) collective-permute-start(bf16[512,512]{1,0:T(8,128)(2,1)} %collective-permute-done.15), channel_id=1, source_target_pairs={{0,8},{8,0},{16,24},{24,16},{1,9},{9,1},{17,25},{25,17},{2,10},{10... | collective-permute-start | bytes 1572872 | tf_op jit(solution)/shard_map/ppermute | solution.py:1167
  67.6 23.9 %collective-permute-start.3 = (bf16[2,512,256]{2,1,0:T(8,128)(2,1)}, bf16[2,512,256]{2,1,0:T(8,128)(2,1)S(1)}, u32[]{:S(2)}, u32[]{:S(2)}) collective-permute-start(bf16[2,512,256]{2,1,0:T(8,128)(2,1)} %collective-permute-done.kv_a), channel_id=1, source_target_pairs={{0,1},{1,0},{2,3},{3,2},{4,5},{5,4},{6,7},{7,6},{8,9},{9,8},{10,11... | collective-permute-start | bytes 1572872 | tf_op jit(solution)/shard_map/ppermute | solution.py:1161
  69.7 47.0 %collective-permute-start.6 = (bf16[128,2048]{1,0:T(8,128)(2,1)}, bf16[128,2048]{1,0:T(8,128)(2,1)}, u32[]{:S(2)}, u32[]{:S(2)}) collective-permute-start(bf16[128,2048]{1,0:T(8,128)(2,1)} %constant_dynamic-slice_fusion.4.refs_7_), channel_id=1, source_target_pairs={{0,1},{1,0},{2,3},{3,2},{4,5},{5,4},{6,7},{7,6},{8,9},{9,8},{10,11... | collective-permute-start | bytes 1572872 | tf_op jit(solution)/shard_map/ppermute | solution.py:1161
  70.2 6.1 copy-start.55
  70.2 34.8 %collective-permute-start.2 = (bf16[2,512,256]{2,1,0:T(8,128)(2,1)S(1)}, bf16[2,512,256]{2,1,0:T(8,128)(2,1)S(1)}, u32[]{:S(2)}, u32[]{:S(2)}) collective-permute-start(bf16[2,512,256]{2,1,0:T(8,128)(2,1)S(1)} %collective-permute-done.1.kv_a), channel_id=1, source_target_pairs={{0,1},{1,0},{2,3},{3,2},{4,5},{5,4},{6,7},{7,6},{8,9},{9,8},{10,11... | collective-permute-start | bytes 1572872 | tf_op jit(solution)/shard_map/ppermute | solution.py:1161
  78.2 38.5 %collective-permute-start.8 = (bf16[128,2048]{1,0:T(8,128)(2,1)}, bf16[128,2048]{1,0:T(8,128)(2,1)}, u32[]{:S(2)}, u32[]{:S(2)}) collective-permute-start(bf16[128,2048]{1,0:T(8,128)(2,1)} %collective-permute-done.7.refs_9_), channel_id=1, source_target_pairs={{0,1},{1,0},{2,3},{3,2},{4,5},{5,4},{6,7},{7,6},{8,9},{9,8},{10,11... | collective-permute-start | bytes 1572872 | tf_op jit(solution)/shard_map/ppermute | solution.py:1161
  79.8 32.0 %collective-permute-start.11 = (bf16[128,2048]{1,0:T(8,128)(2,1)}, bf16[128,2048]{1,0:T(8,128)(2,1)}, u32[]{:S(2)}, u32[]{:S(2)}) collective-permute-start(bf16[128,2048]{1,0:T(8,128)(2,1)} %collective-permute-done.9.refs_11_), channel_id=1, source_target_pairs={{0,2},{1,3},{2,4},{3,5},{4,6},{5,7},{6,0},{7,1},{8,10},{9,11},{10,... | collective-permute-start | bytes 1572872 | tf_op jit(solution)/shard_map/ppermute | solution.py:1158
  91.5 36.2 %collective-permute-start.10 = (bf16[128,2048]{1,0:T(8,128)(2,1)}, bf16[128,2048]{1,0:T(8,128)(2,1)}, u32[]{:S(2)}, u32[]{:S(2)}) collective-permute-start(bf16[128,2048]{1,0:T(8,128)(2,1)} %collective-permute-done.9.refs_11_), channel_id=1, source_target_pairs={{0,1},{1,0},{2,3},{3,2},{4,5},{5,4},{6,7},{7,6},{8,9},{9,8},{10,11... | collective-permute-start | bytes 1572872 | tf_op jit(solution)/shard_map/ppermute | solution.py:1161
  109.7 4.3 copy-start.11
  109.7 4.3 copy-start.37
  111.8 26.6 %collective-permute-start.12 = (bf16[128,2048]{1,0:T(8,128)(2,1)}, bf16[128,2048]{1,0:T(8,128)(2,1)}, u32[]{:S(2)}, u32[]{:S(2)}) collective-permute-start(bf16[128,2048]{1,0:T(8,128)(2,1)} %collective-permute-done.11.refs_13_), channel_id=1, source_target_pairs={{0,1},{1,0},{2,3},{3,2},{4,5},{5,4},{6,7},{7,6},{8,9},{9,8},{10,11... | collective-permute-start | bytes 1572872 | tf_op jit(solution)/shard_map/ppermute | solution.py:1161
  326.2 62.3 %collective-permute-start.13 = (bf16[512,512]{1,0:T(8,128)(2,1)}, bf16[512,512]{1,0:T(8,128)(2,1)}, u32[]{:S(2)}, u32[]{:S(2)}) collective-permute-start(bf16[512,512]{1,0:T(8,128)(2,1)} %constant_dynamic-slice_fusion.2), channel_id=1, source_target_pairs={{0,1},{1,0},{2,3},{3,2},{4,5},{5,4},{6,7},{7,6},{8,9},{9,8},{10,11... | collective-permute-start | bytes 1572872 | tf_op jit(solution)/shard_map/ppermute | solution.py:1161
  331.9 58.7 %collective-permute-start.17 = (bf16[512,512]{1,0:T(8,128)(2,1)}, bf16[512,512]{1,0:T(8,128)(2,1)}, u32[]{:S(2)}, u32[]{:S(2)}) collective-permute-start(bf16[512,512]{1,0:T(8,128)(2,1)} %get-tuple-element.82), channel_id=1, source_target_pairs={{0,1},{1,0},{2,3},{3,2},{4,5},{5,4},{6,7},{7,6},{8,9},{9,8},{10,11... | collective-permute-start | bytes 1572872 | tf_op jit(solution)/shard_map/ppermute | solution.py:1161
  354.3 5.8 copy-start.59
  354.4 5.6 copy-start.60
  356.3 42.7 %collective-permute-start.18 = (bf16[512,512]{0,1:T(8,128)(2,1)S(1)}, bf16[512,512]{0,1:T(8,128)(2,1)S(1)}, u32[]{:S(2)}, u32[]{:S(2)}) collective-permute-start(bf16[512,512]{0,1:T(8,128)(2,1)S(1)} %get-tuple-element.84), channel_id=1, source_target_pairs={{0,1},{1,0},{2,3},{3,2},{4,5},{5,4},{6,7},{7,6},{8,9},{9,8},{10,11... | collective-permute-start | bytes 1572872 | tf_op jit(solution)/shard_map/ppermute | solution.py:1161
  360.0 24.0 %collective-permute-start.21 = (bf16[2,512,256]{2,1,0:T(8,128)(2,1)S(1)}, bf16[2,512,256]{2,1,0:T(8,128)(2,1)S(1)}, u32[]{:S(2)}, u32[]{:S(2)}) collective-permute-start(bf16[2,512,256]{2,1,0:T(8,128)(2,1)S(1)} %copy-done.60), channel_id=1, source_target_pairs={{0,1},{1,0},{2,3},{3,2},{4,5},{5,4},{6,7},{7,6},{8,9},{9,8},{10,11... | collective-permute-start | bytes 1572872 | tf_op jit(solution)/shard_map/ppermute | solution.py:1161
  360.1 35.2 %collective-permute-start.20 = (bf16[2,512,256]{2,1,0:T(8,128)(2,1)S(1)}, bf16[2,512,256]{2,1,0:T(8,128)(2,1)S(1)}, u32[]{:S(2)}, u32[]{:S(2)}) collective-permute-start(bf16[2,512,256]{2,1,0:T(8,128)(2,1)S(1)} %copy-done.59), channel_id=1, source_target_pairs={{0,1},{1,0},{2,3},{3,2},{4,5},{5,4},{6,7},{7,6},{8,9},{9,8},{10,11... | collective-permute-start | bytes 1572872 | tf_op jit(solution)/shard_map/ppermute | solution.py:1161
  362.1 22.0 %copy-start.40 = (bf16[2,512,256]{2,1,0:T(8,128)(2,1)S(1)}, bf16[2,512,256]{2,1,0:T(8,128)(2,1)}, u32[]{:S(2)}) copy-start(bf16[2,512,256]{2,1,0:T(8,128)(2,1)} %get-tuple-element.57) | copy-start | bytes 1572868
  362.1 23.0 %copy-start.26 = (bf16[2048,512]{1,0:T(8,128)(2,1)S(1)}, bf16[2048,512]{1,0:T(8,128)(2,1)}, u32[]{:S(2)}) copy-start(bf16[2048,512]{1,0:T(8,128)(2,1)} %param.18) | copy-start | bytes 6291460
  384.2 4.2 copy-start.27
  384.2 13.1 %collective-permute-start.22 = (bf16[2,512,256]{2,1,0:T(8,128)(2,1)S(1)}, bf16[2,512,256]{2,1,0:T(8,128)(2,1)S(1)}, u32[]{:S(2)}, u32[]{:S(2)}) collective-permute-start(bf16[2,512,256]{2,1,0:T(8,128)(2,1)S(1)} %add_convert_fusion.1), channel_id=1, source_target_pairs={{4,2},{5,3},{6,4},{7,5},{12,10},{13,11},{14,12},{15,13},{20,18},{2... | collective-permute-start | bytes 1572872 | tf_op jit(solution)/shard_map/ppermute | solution.py:1391
  385.0 3.5 copy-start.38
  388.5 6.8 %copy-start.57 = (bf16[2,512,256]{2,1,0:T(8,128)(2,1)S(1)}, bf16[2,512,256]{2,1,0:T(8,128)(2,1)}, u32[]{:S(2)}) copy-start(bf16[2,512,256]{2,1,0:T(8,128)(2,1)} %get-tuple-element.54) | copy-start | bytes 1572868
  388.5 8.8 %copy-start.41 = (bf16[2,512,256]{2,1,0:T(8,128)(2,1)S(1)}, bf16[2,512,256]{2,1,0:T(8,128)(2,1)}, u32[]{:S(2)}) copy-start(bf16[2,512,256]{2,1,0:T(8,128)(2,1)} %get-tuple-element.55) | copy-start | bytes 1572868
  388.5 18.0 %collective-permute-start.5 = (bf16[512,512]{1,0:T(8,128)(2,1)S(1)}, bf16[512,512]{1,0:T(8,128)(2,1)S(1)}, u32[]{:S(2)}, u32[]{:S(2)}) collective-permute-start(bf16[512,512]{1,0:T(8,128)(2,1)S(1)} %copy-done.38), channel_id=1, source_target_pairs={{0,1},{1,0},{2,3},{3,2},{4,5},{5,4},{6,7},{7,6},{8,9},{9,8},{10,11... | collective-permute-start | bytes 1572872 | tf_op jit(solution)/shard_map/ppermute | solution.py:1161
  390.6 10.7 %collective-permute-start.14 = (bf16[512,512]{1,0:T(8,128)(2,1)}, bf16[512,512]{1,0:T(8,128)(2,1)S(1)}, u32[]{:S(2)}, u32[]{:S(2)}) collective-permute-start(bf16[512,512]{1,0:T(8,128)(2,1)} %collective-permute-done.13), channel_id=1, source_target_pairs={{0,8},{8,0},{16,24},{24,16},{1,9},{9,1},{17,25},{25,17},{2,10},{10... | collective-permute-start | bytes 1572872 | tf_op jit(solution)/shard_map/ppermute | solution.py:1167
  395.3 21.6 %collective-permute-start.19 = (bf16[2,512,256]{2,1,0:T(8,128)(2,1)S(1)}, bf16[2,512,256]{2,1,0:T(8,128)(2,1)S(1)}, u32[]{:S(2)}, u32[]{:S(2)}) collective-permute-start(bf16[2,512,256]{2,1,0:T(8,128)(2,1)S(1)} %copy-done.57), channel_id=1, source_target_pairs={{0,1},{1,0},{2,3},{3,2},{4,5},{5,4},{6,7},{7,6},{8,9},{9,8},{10,11... | collective-permute-start | bytes 1572872 | tf_op jit(solution)/shard_map/ppermute | solution.py:1161
  397.5 28.9 %collective-permute-start.23 = (bf16[2,512,256]{2,1,0:T(8,128)(2,1)S(1)}, bf16[2,512,256]{2,1,0:T(8,128)(2,1)S(1)}, u32[]{:S(2)}, u32[]{:S(2)}) collective-permute-start(bf16[2,512,256]{2,1,0:T(8,128)(2,1)S(1)} %add_convert_fusion), channel_id=1, source_target_pairs={{2,0},{3,1},{4,2},{5,3},{6,4},{7,5},{10,8},{11,9},{12,10},{13,11},... | collective-permute-start | bytes 1572872 | tf_op jit(solution)/shard_map/ppermute | solution.py:1391
  402.8 23.6 %copy-start.39 = (bf16[2,512,256]{2,1,0:T(8,128)(2,1)S(1)}, bf16[2,512,256]{2,1,0:T(8,128)(2,1)}, u32[]{:S(2)}) copy-start(bf16[2,512,256]{2,1,0:T(8,128)(2,1)} %get-tuple-element.53) | copy-start | bytes 1572868
  427.7 3.0 copy-start.24
  430.8 6.3 %copy-start.32 = (f32[512,2]{1,0:T(8,128)S(1)}, f32[512,2]{1,0:T(8,128)}, u32[]{:S(2)}) copy-start(f32[512,2]{1,0:T(8,128)} %copy.106) | copy-start | bytes 12292
  431.6 6.2 copy-start.19
  431.6 6.2 copy-start.54
  431.6 11.7 %copy-start.15 = (bf16[2048,512]{1,0:T(8,128)(2,1)S(1)}, bf16[2048,512]{1,0:T(8,128)(2,1)}, u32[]{:S(2)}) copy-start(bf16[2048,512]{1,0:T(8,128)(2,1)} %param.21) | copy-start | bytes 6291460
  432.4 5.4 copy-start.20
  435.4 7.8 %copy-start.3 = (f32[512,2048]{1,0:T(8,128)S(1)}, f32[512,2048]{1,0:T(8,128)}, u32[]{:S(2)}) copy-start(f32[512,2048]{1,0:T(8,128)} %fusion.49) | copy-start | bytes 12582916
  439.1 4.2 copy-start
  439.1 4.2 copy-start.2
  439.1 4.2 copy-start.45
  442.2 5.3 copy-start.48
  442.2 11.1 %copy-start.29 = (bf16[512,1024]{1,0:T(8,128)(2,1)S(1)}, bf16[512,1024]{1,0:T(8,128)(2,1)}, u32[]{:S(2)}) copy-start(bf16[512,1024]{1,0:T(8,128)(2,1)} %constant_dynamic-slice_fusion.1) | copy-start | bytes 3145732
  442.2 11.1 %copy-start.31 = (bf16[512,1024]{1,0:T(8,128)(2,1)S(1)}, bf16[512,1024]{1,0:T(8,128)(2,1)}, u32[]{:S(2)}) copy-start(bf16[512,1024]{1,0:T(8,128)(2,1)} %maximum_select_fusion.1) | copy-start | bytes 3145732
  442.3 11.1 %copy-start.33 = (bf16[512,256]{1,0:T(8,128)(2,1)S(1)}, bf16[512,256]{1,0:T(8,128)(2,1)}, u32[]{:S(2)}) copy-start(bf16[512,256]{1,0:T(8,128)(2,1)} %fusion.39) | copy-start | bytes 786436
  442.3 11.1 %collective-permute-start.24 = (bf16[512,512]{1,0:T(8,128)(2,1)S(1)}, bf16[512,512]{1,0:T(8,128)(2,1)S(1)}, u32[]{:S(2)}, u32[]{:S(2)}) collective-permute-start(bf16[512,512]{1,0:T(8,128)(2,1)S(1)} %pad_maximum_fusion.8), channel_id=1, source_target_pairs={{0,1},{1,0},{2,3},{3,2},{4,5},{5,4},{6,7},{7,6},{8,9},{9,8},{10,11... | collective-permute-start | bytes 1572872 | tf_op jit(solution)/shard_map/ppermute | solution.py:1161
  611.3 4.3 copy-start.18
  (22 other events, 37.5 us)

commit v7 on v6

--- a/solution.py
+++ b/solution.py
@@ -249,9 +249,12 @@
     )(info, *operands)
 
 
+LATE_BLOCKS = 2
+
+
 def middle_kernel(outer, *refs):
     MESH = pl.DeviceIdType.MESH
-    blocks = 2 * outer
+    blocks = 2 * outer - LATE_BLOCKS
     (gated, out_proj, hidden_ref, gain_ref, gate_in, up_in, down_in) = refs[:7]
     ups_in = refs[7 : 7 + blocks]
     (layer_out, grad_out, gain_out, branch, dw_both, dw_down) = refs[7 + blocks : 13 + blocks]
@@ -260,7 +263,7 @@
         near_buf, far_stage, far_got, middle_buf,
         keep, y_stage, y_got, z_stage, z_got, part_got, part_far,
         load_sem, store_sem, tp_send, tp_recv, zs, zr, ys, yr, rys, ryr, rzs, rzr,
-        p_near_send, p_near_recv, p_far_send, p_far_recv, p_out_send, p_out_recv,
+        p_near_send, p_near_recv, p_far_send, p_far_recv, p_out_send, p_out_recv, us, ur,
     ) = refs[13 + blocks :]
     stage_gate, stage_up, stage_down = w_gate, w_up, rows
     far_keep, own_keep = grad_out, middle_buf
@@ -285,11 +288,13 @@
     side_dev = ((1 - side) * 2 + core, sp_i)
     nexts = (sp_at(jnp.minimum(line + 1, last), half), sp_at(jnp.maximum(line - 1, 0), half))
 
+    late = list(range(outer - LATE_BLOCKS, outer))
+    ups_at = [at for at in range(2 * outer) if at % 2 == 0 or at // 2 not in late]
     loads = [
         pltpu.make_async_copy(src, dst, load_sem.at[index])
         for index, (src, dst) in enumerate(
             [(down_in, w_down)]
-            + [(ups_in[b], ups.at[pl.ds(b * quarter, quarter), :]) for b in range(blocks)]
+            + [(src, ups.at[pl.ds(at * quarter, quarter), :]) for at, src in zip(ups_at, ups_in)]
             + [(gate_in, w_gate), (up_in, w_up)]
         )
     ]
@@ -314,6 +319,13 @@
     def aligned(index, count):
         return pl.ds(pl.multiple_of(index * count, count), count)
 
+    def late_copy(index):
+        at = late[index] * 2
+        return remote(
+            ups.at[pl.ds(at * quarter, quarter), :], ups.at[pl.ds((at + 1) * quarter, quarter), :],
+            us.at[index], ur.at[index], pair_dev,
+        )
+
     def near_copy(j):
         return remote(near_buf.at[j], near_buf.at[2 + j], tp_send.at[j], tp_recv.at[j], core_dev)
 
@@ -327,6 +339,9 @@
     near_copy(0).start()
     near_buf[1] = projected(side, 1 - core).astype(BF16)
     near_copy(1).start()
+    for index in range(LATE_BLOCKS):
+        loads[1 + ups_at.index(late[index] * 2)].wait()
+        late_copy(index).start()
     far_keep[...] = projected(1 - side, core)
     near_copy(0).wait_recv()
     far_stage[...] = (far_keep[...] + near_buf[2].astype(F32)).astype(BF16)
@@ -388,8 +403,12 @@
             pl.when(exists)(z_copy(way, k).start)
         y_copy(k).start()
 
-    for load in loads:
-        load.wait()
+    waited = [1 + ups_at.index(k * 2) for k in late]
+    for index, load in enumerate(loads):
+        if index not in waited:
+            load.wait()
+    for index in range(LATE_BLOCKS):
+        late_copy(index).wait_recv()
     forward(1)
 
     def turn_forward(i, carry):
@@ -438,6 +457,10 @@
         k = slot_of(delta_of(last - step))
         near_buf[k] = matmul(inner[half_rows(k, 1), :], w_down[...]).astype(BF16)
         y_sum(1, k).start()
+        return carry
+
+    def turn_keep(step, carry):
+        k = slot_of(delta_of(last - step))
         part = times_transpose(grad_gate[half_rows(k, 0), :], w_gate[...]) + times_transpose(
             grad_up[half_rows(k, 0), :], w_up[...]
         )
@@ -445,7 +468,7 @@
         return carry
 
     lax.fori_loop(0, outer, turn_parts, 0)
-    lax.fori_loop(0, outer, turn_outputs, 0)
+    lax.fori_loop(0, outer, turn_keep, 0)
 
     def z_got_rows(which, way, k):
         return aligned((which * 2 + way) * outer + k, quarter)
@@ -564,18 +587,16 @@
             piece_store(a, r).start()
             piece_out(a, r).start()
 
-    work = [
-        functools.partial(pieces, False, 0), functools.partial(pieces, True, 0),
-        functools.partial(pieces_sum, 0), functools.partial(pieces, False, 1),
-        functools.partial(pieces, True, 1), functools.partial(pieces_sum, 1),
-    ]
-    for step in range(last):
-        for _ in range(2):
-            if work:
-                work.pop(0)()
+    pieces(False, 0)
+    pieces(True, 0)
+    pieces_sum(0)
+    lax.fori_loop(0, outer, turn_outputs, 0)
+    chain(0, 0)
+    pieces(False, 1)
+    pieces(True, 1)
+    pieces_sum(1)
+    for step in range(1, last):
         chain(0, step)
-    for some_work in work:
-        some_work()
     grad_two = chain_end(0)
 
     values = middle_buf[...]
@@ -625,6 +646,8 @@
 
     down_store.wait()
     far_copy().wait_send()
+    for index in range(LATE_BLOCKS):
+        late_copy(index).wait_send()
 
     def turn_drain(i, carry):
         k = slot_of(delta_of(i))
@@ -699,7 +722,8 @@
             dma((2, outer)),
             dma((2, 2, outer)),
         ]
-        + [dma((2, 2))] * 6,
+        + [dma((2, 2))] * 6
+        + [dma((LATE_BLOCKS,))] * 2,
         compiler_params=pltpu.CompilerParams(
             collective_id=2, has_side_effects=True, vmem_limit_bytes=63 * 1024 * 1024
         ),
@@ -1166,10 +1190,10 @@
     def core(value):
         return lax.ppermute(value, "tp", core_pairs)
 
-    def gather_sp(block):
+    def gather_sp(block, paired):
         blocks = []
         for k in range(outer):
-            blocks.append((block, pair(block)))
+            blocks.append((block, pair(block)) if k < paired else (block,))
             if k < outer - 1:
                 block = ring(block)
         return blocks
@@ -1237,7 +1261,8 @@
     both_normed = jnp.concatenate([normed_own, swap_half(normed)])
 
     grad_quarter = lax.dynamic_slice_in_dim(upstream, quarter_first, quarter)
-    up_blocks = gather_sp(grad_quarter)
+    fused = 2 < outer and outer * quarter <= 512 and tp_n == 4
+    up_blocks = gather_sp(grad_quarter, outer - LATE_BLOCKS if fused else outer)
 
     row_start_low = own_starts[0]
     row_start_high = own_starts[-1]
@@ -1289,7 +1314,6 @@
         )
         return full.reshape((rows_dev,) + block.shape[1:])
 
-    fused = outer * quarter <= 512 and outer > 1 and tp_n == 4
     if fused:
         layer_quarter, grad_middle_quarter, ffn_gain_sum, branch, *ffn_parts = middle_layer(
             gated,
@@ -1312,7 +1336,7 @@
         normed_two_full, ffn_scales = norm_rows(middle, ffn_norm)
         normed_two = normed_two_full.astype(BF16)
 
-        two_blocks = gather_sp(normed_two)
+        two_blocks = gather_sp(normed_two, outer)
         rows_list, up_list, inner_list, gate_list, grad_up_list = [None] * outer, [None] * outer, [None] * outer, [None] * outer, [None] * outer
         grad_parts = [None] * outer
         for k in list(range(1, outer)) + [0]:

time: 642 us -> 624 us (0.972)
  waiting for transfers between devices: 73.6 us -> 47.6 us
    ppermute x16 -> x14, waiting for transfers between devices: 62.1 us -> 45.2 us  [pair(): return lax.ppermute(value, 'sp', pair_pairs)]
    ppermute x2, waiting for transfers between devices: 9.55 us -> 0.54 us  [body(): travelling = lax.ppermute(total.astype(BF16), 'sp', down_pairs(k))]
    ppermute x16 -> x14, starting transfers between devices: 22.1 us -> 20.3 us  [pair(): return lax.ppermute(value, 'sp', pair_pairs)]
  transfers between devices with their start and end apart: 25 -> 23, of which waited for: 10 -> 9; matrix products, arithmetic and copies ran while one was open for 13% -> 13% of each run, Pallas kernels for 4% -> 4%
where the time goes in v7:
time: 624 us; the launch traced here: 615 us
  Pallas kernels  372 us (60%)
  other arithmetic  61.7 us (10%)
  waiting for transfers between devices  47.6 us (8%)
  local copies, waits for them, and re-layouts  45.7 us (7%)
  starting transfers between devices  42.1 us (7%)
  matrix products  37 us (6%)
  between operations  9.49 us (2%)
    pallas_call x1, Pallas kernels, middle_layer(): pl.pallas_call(functools.partial(middle_kernel, outer), out_shape=[jax.Sh...  188 us
    pallas_call x1, Pallas kernels, finish(): pl.pallas_call(functools.partial(finish_kernel, outer, sides, sp_n, tp_n,...  157 us
    ppermute x14, waiting for transfers between devices, pair(): return lax.ppermute(value, 'sp', pair_pairs)  45.2 us
    ppermute x14, starting transfers between devices, pair(): return lax.ppermute(value, 'sp', pair_pairs)  20.3 us
    dot_general x5, matrix products, times_transpose(): lax.dot_general(left, right, (((1,), (1,)), ((), ())), preferred_element_...  17 us
    pallas_call x3, Pallas kernels, attn_backward(): pl.pallas_call(functools.partial(attn_backward_kernel, first, diagonal, s...  14.4 us
    ppermute x3, starting transfers between devices, ring(): return lax.ppermute(value, 'sp', ring_pairs)  13.1 us
  transfers between devices with their start and end apart: 23, of which 9 were waited for; matrix products, arithmetic and copies ran while one was open for 13% of the time, Pallas kernels for 4%

profile of v7, /device:TPU:0, one launch (start us, length us, event | category | flops | bytes accessed | tf_op | source)
XLA Modules:
  0.0 615.4 jit_solution(3899530651725685370)
XLA Ops:
  0.7 2.2 fusion
  6.7 1.4 fusion.15
  11.7 1.8 pad_maximum_fusion.6.kv_a
  13.5 5.8 collective-permute-start
  19.3 1.5 collective-permute-start.4
  20.8 1.9 constant_dynamic-slice_fusion.4.refs_7_
  23.5 1.9 constant_dynamic-slice_fusion
  26.9 4.7 fusion.14
  32.2 2.9 multiply_reduce_fusion.1
  35.1 1.6 copy.89
  38.9 1.7 multiply_multiply_fusion
  46.2 2.1 copy.107
  57.6 2.3 constant_dynamic-slice_fusion.1
  63.4 3.0 collective-permute-start.9
  67.6 1.5 collective-permute-start.3
  70.2 1.5 collective-permute-start.2
  71.7 4.6 attn_forward.3
  76.3 1.8 collective-permute-done.9.refs_11_
  78.1 1.5 collective-permute-start.8
  79.7 9.3 %collective-permute-start.10 = (bf16[128,2048]{1,0:T(8,128)(2,1)S(1)}, bf16[128,2048]{1,0:T(8,128)(2,1)}, u32[]{:S(2)}, u32[]{:S(2)}) collective-permute-start(bf16[128,2048]{1,0:T(8,128)(2,1)S(1)} %collective-permute-done.9.refs_11_), channel_id=1, source_target_pairs={{0,2},{1,3},{2,4},{3,5},{4,6},{5,7},{6,0},{7,1},{8,10},{9,11},{10,... | collective-permute-start | bytes 1572872 | tf_op jit(solution)/shard_map/ppermute | solution.py:1182
  89.0 2.5 maximum_select_fusion.1
  92.3 3.8 attn_forward.4
  96.1 8.9 %collective-permute-done.2.kv_b = bf16[2,512,256]{2,1,0:T(8,128)(2,1)S(1)} collective-permute-done((bf16[2,512,256]{2,1,0:T(8,128)(2,1)S(1)}, bf16[2,512,256]{2,1,0:T(8,128)(2,1)S(1)}, u32[]{:S(2)}, u32[]{:S(2)}) %collective-permute-start.2) | collective-permute-done | bytes 524320 | tf_op jit(solution)/shard_map/ppermute | solution.py:1185
  105.9 4.0 attn_forward.5
  109.8 3.0 multiply_convert_fusion.1
  112.9 3.1 collective-permute-done.8.refs_10_
  116.0 188.2 %middle.1 = (bf16[128,2048]{1,0:T(8,128)(2,1)}, f32[128,2048]{1,0:T(8,128)}, f32[1,2048]{1,0:T(1,128)}, bf16[2,2,128,2048]{3,2,1,0:T(8,128)(2,1)}, bf16[2,2048,7...) custom-call(bf16[512,512]{1,0:T(8,128)(2,1)} %get-tuple-element.76.refs_0_, bf16[512,2048]{1,0:T(8,128)(2,1)} %refs_1_.1, ...), custom_call_target="tpu_custom_call" | custom-call | flops 30000001024 | bytes 40000000 | tf_op jit(solution)/shard_map/middle/pallas_call | solution.py:680
  304.2 1.9 constant_dynamic-slice_fusion.2
  306.1 4.6 fusion.51
  312.6 2.6 convert_multiply_fusion.3
  315.2 1.4 collective-permute-start.15
  316.7 1.5 copy.117
  320.6 3.3 attn_backward.3
  323.9 3.9 attn_backward.4
  327.8 7.2 %attn_backward.5 = (f32[512,512]{1,0:T(8,128)}, bf16[2,512,256]{2,1,0:T(8,128)(2,1)}, bf16[2,512,256]{2,1,0:T(8,128)(2,1)}) custom-call(s32[7]{0:T(128)} %stack.145.info, s32[1,512]{1,0:T(1,128)} %compare_select_fusion.starts, f32[2,2,512]{2,1,0:T(2,128)} %reshape.259.lse, f32[2,2,512]{2,1,0:T(2,128)} %reshape.261.deltas, bf16[512,512]{1,0:T(8,128)(2,1)} %bitcast.171, ...), custom_call_target="tpu_custom_call" | custom-call | flops 2684354560 | bytes 2097152 | tf_op jit(solution)/shard_map/attn_backward/pallas_call | solution.py:229
  341.7 3.8 collective-permute-start.16
  345.6 1.9 collective-permute-start.18
  347.6 8.8 %bitcast_convert_fusion = (f32[2048,768]{1,0:T(8,128)}, f32[2048,768]{1,0:T(8,128)}) fusion(bf16[2,2048,768]{2,1,0:T(8,128)(2,1)} %get-tuple-element.70), kind=kLoop, calls=%fused_computation.9 | loop fusion | flops 3145728 | bytes 18874368 | tf_op jit(solution)/shard_map/convert_element_type | solution.py:1491
  356.3 13.2 %collective-permute-done.19 = bf16[2,512,256]{2,1,0:T(8,128)(2,1)S(1)} collective-permute-done((bf16[2,512,256]{2,1,0:T(8,128)(2,1)S(1)}, bf16[2,512,256]{2,1,0:T(8,128)(2,1)S(1)}, u32[]{:S(2)}, u32[]{:S(2)}) %collective-permute-start.19) | collective-permute-done | bytes 524320 | tf_op jit(solution)/shard_map/ppermute | solution.py:1185
  370.6 3.3 fusion.52
  374.0 2.1 collective-permute-start.5
  376.2 3.5 convolution_convert_fusion.2.refs_1_
  380.8 2.0 collective-permute-start.17
  383.0 1.5 collective-permute-start.21
  384.5 2.3 convolution_convert_fusion.1.refs_2_
  386.8 1.5 maximum_select_fusion
  388.3 3.7 collective-permute-done.5
  392.0 2.2 fusion.9.refs_0_
  394.3 8.4 %collective-permute-done.17 = bf16[2,512,256]{2,1,0:T(8,128)(2,1)S(1)} collective-permute-done((bf16[2,512,256]{2,1,0:T(8,128)(2,1)S(1)}, bf16[2,512,256]{2,1,0:T(8,128)(2,1)S(1)}, u32[]{:S(2)}, u32[]{:S(2)}) %collective-permute-start.17) | collective-permute-done | bytes 524320 | tf_op jit(solution)/shard_map/ppermute | solution.py:1185
  404.5 2.8 fusion.49
  409.2 2.2 copy.115
  412.2 1.7 mul.521
  415.9 2.1 fusion.53
  420.4 4.2 fusion.4
  425.2 6.7 %collective-permute-done.22 = bf16[512,512]{1,0:T(8,128)(2,1)S(1)} collective-permute-done((bf16[512,512]{1,0:T(8,128)(2,1)S(1)}, bf16[512,512]{1,0:T(8,128)(2,1)S(1)}, u32[]{:S(2)}, u32[]{:S(2)}) %collective-permute-start.22) | collective-permute-done | bytes 524320 | tf_op jit(solution)/shard_map/ppermute | solution.py:1185
  431.9 2.3 convolution_convert_fusion.refs_3_
  434.2 156.8 %finish.1 = (bf16[2,512,1024]{2,1,0:T(8,128)(2,1)}, bf16[2,1024,512]{2,1,0:T(8,128)(2,1)}, bf16[2,1024,512]{2,1,0:T(8,128)(2,1)}, bf16[2,1024,512]{2,1,0:T(8,128...) custom-call(bf16[512,1024]{1,0:T(8,128)(2,1)} %fusion.9.refs_0_, ...), custom_call_target="tpu_custom_call" | custom-call | flops 1000000000 | bytes 100000000 | tf_op jit(solution)/shard_map/finish/pallas_call | solution.py:1100
  593.6 4.3 bitcast_convert_fusion.4
  597.9 2.7 bitcast_convert_fusion.3
  600.7 2.3 slice_convert_fusion
  603.1 2.7 bitcast_convert_fusion.2
  606.0 1.7 copy-done.15
  607.8 3.6 convert_element_type.200
  611.3 2.5 maximum_convert_fusion
  (221 shorter events, 54.1 us)
Async XLA Ops:
  0.6 4.8 copy-start.1
  0.7 3.5 copy-start.49
  0.7 4.8 copy-start.44
  2.9 39.2 %copy-start.46 = (f32[512]{0:T(512)}, f32[512]{0:T(512)S(1)}, u32[]{:S(2)}) copy-start(f32[512]{0:T(512)S(1)} %add_rsqrt_fusion.2) | copy-start | bytes 6148
  9.4 22.2 %copy-start.8 = (f32[512,256]{0,1:T(8,128)}, f32[512,256]{0,1:T(8,128)S(1)}, u32[]{:S(2)}) copy-start(f32[512,256]{0,1:T(8,128)S(1)} %get-tuple-element.116) | copy-start | bytes 1572868
  11.3 14.6 %copy-start.26 = (f32[512,64]{0,1:T(8,128)}, f32[512,64]{0,1:T(8,128)S(1)}, u32[]{:S(2)}) copy-start(f32[512,64]{0,1:T(8,128)S(1)} %get-tuple-element.110) | copy-start | bytes 393220
  13.5 48.6 %collective-permute-start = (bf16[2,512,256]{2,1,0:T(8,128)(2,1)}, bf16[2,512,256]{2,1,0:T(8,128)(2,1)}, u32[]{:S(2)}, u32[]{:S(2)}) collective-permute-start(bf16[2,512,256]{2,1,0:T(8,128)(2,1)} %pad_maximum_fusion.6.kv_a), channel_id=1, source_target_pairs={{0,2},{1,3},{2,4},{3,5},{4,6},{5,7},{8,10},{9,11},{10,12},{11,13},... | collective-permute-start | bytes 1572872 | tf_op jit(solution)/shard_map/ppermute | solution.py:1245
  19.3 50.4 %collective-permute-start.4 = (bf16[2,512,256]{2,1,0:T(8,128)(2,1)}, bf16[2,512,256]{2,1,0:T(8,128)(2,1)}, u32[]{:S(2)}, u32[]{:S(2)}) collective-permute-start(bf16[2,512,256]{2,1,0:T(8,128)(2,1)} %pad_maximum_fusion.6.kv_a), channel_id=1, source_target_pairs={{0,1},{1,0},{2,3},{3,2},{4,5},{5,4},{6,7},{7,6},{8,9},{9,8},{10,11... | collective-permute-start | bytes 1572872 | tf_op jit(solution)/shard_map/ppermute | solution.py:1185
  22.7 40.7 %collective-permute-start.7 = (bf16[128,2048]{1,0:T(8,128)(2,1)}, bf16[128,2048]{1,0:T(8,128)(2,1)}, u32[]{:S(2)}, u32[]{:S(2)}) collective-permute-start(bf16[128,2048]{1,0:T(8,128)(2,1)} %constant_dynamic-slice_fusion.4.refs_7_), channel_id=1, source_target_pairs={{0,2},{1,3},{2,4},{3,5},{4,6},{5,7},{6,0},{7,1},{8,10},{9,11},{10,... | collective-permute-start | bytes 1572872 | tf_op jit(solution)/shard_map/ppermute | solution.py:1182
  25.4 41.0 %collective-permute-start.13 = (bf16[512,512]{1,0:T(8,128)(2,1)}, bf16[512,512]{1,0:T(8,128)(2,1)}, u32[]{:S(2)}, u32[]{:S(2)}) collective-permute-start(bf16[512,512]{1,0:T(8,128)(2,1)} %constant_dynamic-slice_fusion), channel_id=1, source_target_pairs={{0,1},{1,0},{2,3},{3,2},{4,5},{5,4},{6,7},{7,6},{8,9},{9,8},{10,11... | collective-permute-start | bytes 1572872 | tf_op jit(solution)/shard_map/ppermute | solution.py:1185
  26.9 5.3 copy-start.7
  26.9 5.3 copy-start.28
  36.7 4.7 copy-start.4
  42.2 12.0 %copy-start.48 = (f32[512,2]{0,1:T(2,128)S(1)}, f32[512,2]{0,1:T(2,128)}, u32[]{:S(2)}) copy-start(f32[512,2]{0,1:T(2,128)} %get-tuple-element.107) | copy-start | bytes 12292
  54.2 8.6 %copy-start.51 = (f32[128]{0:T(128)S(1)}, f32[128]{0:T(128)}, u32[]{:S(2)}) copy-start(f32[128]{0:T(128)} %param.23) | copy-start | bytes 1540
  54.2 15.0 %copy-start.53 = (f32[128]{0:T(128)S(1)}, f32[128]{0:T(128)}, u32[]{:S(2)}) copy-start(f32[128]{0:T(128)} %param.24) | copy-start | bytes 1540
  62.1 8.1 %collective-permute-start.1 = (bf16[2,512,256]{2,1,0:T(8,128)(2,1)}, bf16[2,512,256]{2,1,0:T(8,128)(2,1)S(1)}, u32[]{:S(2)}, u32[]{:S(2)}) collective-permute-start(bf16[2,512,256]{2,1,0:T(8,128)(2,1)} %collective-permute-done.kv_a), channel_id=1, source_target_pairs={{2,4},{3,5},{4,6},{5,7},{10,12},{11,13},{12,14},{13,15},{18,20},{1... | collective-permute-start | bytes 1572872 | tf_op jit(solution)/shard_map/ppermute | solution.py:1245
  63.4 14.8 %collective-permute-start.9 = (bf16[128,2048]{1,0:T(8,128)(2,1)}, bf16[128,2048]{1,0:T(8,128)(2,1)S(1)}, u32[]{:S(2)}, u32[]{:S(2)}) collective-permute-start(bf16[128,2048]{1,0:T(8,128)(2,1)} %collective-permute-done.7.refs_9_), channel_id=1, source_target_pairs={{0,2},{1,3},{2,4},{3,5},{4,6},{5,7},{6,0},{7,1},{8,10},{9,11},{10,... | collective-permute-start | bytes 1572872 | tf_op jit(solution)/shard_map/ppermute | solution.py:1182
  66.4 13.3 %collective-permute-start.14 = (bf16[512,512]{1,0:T(8,128)(2,1)}, bf16[512,512]{1,0:T(8,128)(2,1)S(1)}, u32[]{:S(2)}, u32[]{:S(2)}) collective-permute-start(bf16[512,512]{1,0:T(8,128)(2,1)} %collective-permute-done.13), channel_id=1, source_target_pairs={{0,8},{8,0},{16,24},{24,16},{1,9},{9,1},{17,25},{25,17},{2,10},{10... | collective-permute-start | bytes 1572872 | tf_op jit(solution)/shard_map/ppermute | solution.py:1191
  67.6 23.9 %collective-permute-start.3 = (bf16[2,512,256]{2,1,0:T(8,128)(2,1)}, bf16[2,512,256]{2,1,0:T(8,128)(2,1)S(1)}, u32[]{:S(2)}, u32[]{:S(2)}) collective-permute-start(bf16[2,512,256]{2,1,0:T(8,128)(2,1)} %collective-permute-done.kv_a), channel_id=1, source_target_pairs={{0,1},{1,0},{2,3},{3,2},{4,5},{5,4},{6,7},{7,6},{8,9},{9,8},{10,11... | collective-permute-start | bytes 1572872 | tf_op jit(solution)/shard_map/ppermute | solution.py:1185
  69.7 43.2 %collective-permute-start.6 = (bf16[128,2048]{1,0:T(8,128)(2,1)}, bf16[128,2048]{1,0:T(8,128)(2,1)S(1)}, u32[]{:S(2)}, u32[]{:S(2)}) collective-permute-start(bf16[128,2048]{1,0:T(8,128)(2,1)} %constant_dynamic-slice_fusion.4.refs_7_), channel_id=1, source_target_pairs={{0,1},{1,0},{2,3},{3,2},{4,5},{5,4},{6,7},{7,6},{8,9},{9,8},{10,11... | collective-permute-start | bytes 1572872 | tf_op jit(solution)/shard_map/ppermute | solution.py:1185
  70.2 6.1 copy-start.56
  70.2 34.8 %collective-permute-start.2 = (bf16[2,512,256]{2,1,0:T(8,128)(2,1)S(1)}, bf16[2,512,256]{2,1,0:T(8,128)(2,1)S(1)}, u32[]{:S(2)}, u32[]{:S(2)}) collective-permute-start(bf16[2,512,256]{2,1,0:T(8,128)(2,1)S(1)} %collective-permute-done.1.kv_a), channel_id=1, source_target_pairs={{0,1},{1,0},{2,3},{3,2},{4,5},{5,4},{6,7},{7,6},{8,9},{9,8},{10,11... | collective-permute-start | bytes 1572872 | tf_op jit(solution)/shard_map/ppermute | solution.py:1185
  78.1 18.0 %copy-start.61 = (bf16[128,2048]{1,0:T(8,128)(2,1)}, bf16[128,2048]{1,0:T(8,128)(2,1)S(1)}, u32[]{:S(2)}) copy-start(bf16[128,2048]{1,0:T(8,128)(2,1)S(1)} %collective-permute-done.9.refs_11_) | copy-start | bytes 1572868
  78.1 37.8 %collective-permute-start.8 = (bf16[128,2048]{1,0:T(8,128)(2,1)}, bf16[128,2048]{1,0:T(8,128)(2,1)}, u32[]{:S(2)}, u32[]{:S(2)}) collective-permute-start(bf16[128,2048]{1,0:T(8,128)(2,1)} %collective-permute-done.7.refs_9_), channel_id=1, source_target_pairs={{0,1},{1,0},{2,3},{3,2},{4,5},{5,4},{6,7},{7,6},{8,9},{9,8},{10,11... | collective-permute-start | bytes 1572872 | tf_op jit(solution)/shard_map/ppermute | solution.py:1185
  79.7 36.3 %collective-permute-start.10 = (bf16[128,2048]{1,0:T(8,128)(2,1)S(1)}, bf16[128,2048]{1,0:T(8,128)(2,1)}, u32[]{:S(2)}, u32[]{:S(2)}) collective-permute-start(bf16[128,2048]{1,0:T(8,128)(2,1)S(1)} %collective-permute-done.9.refs_11_), channel_id=1, source_target_pairs={{0,2},{1,3},{2,4},{3,5},{4,6},{5,7},{6,0},{7,1},{8,10},{9,11},{10,... | collective-permute-start | bytes 1572872 | tf_op jit(solution)/shard_map/ppermute | solution.py:1182
  105.9 4.0 copy-start.11
  112.9 3.1 copy-start.63
  306.1 4.6 copy-start.14
  312.0 62.1 %collective-permute-start.11 = (bf16[512,512]{1,0:T(8,128)(2,1)}, bf16[512,512]{1,0:T(8,128)(2,1)}, u32[]{:S(2)}, u32[]{:S(2)}) collective-permute-start(bf16[512,512]{1,0:T(8,128)(2,1)} %constant_dynamic-slice_fusion.2), channel_id=1, source_target_pairs={{0,1},{1,0},{2,3},{3,2},{4,5},{5,4},{6,7},{7,6},{8,9},{9,8},{10,11... | collective-permute-start | bytes 1572872 | tf_op jit(solution)/shard_map/ppermute | solution.py:1185
  315.2 60.9 %collective-permute-start.15 = (bf16[512,512]{1,0:T(8,128)(2,1)}, bf16[512,512]{1,0:T(8,128)(2,1)}, u32[]{:S(2)}, u32[]{:S(2)}) collective-permute-start(bf16[512,512]{1,0:T(8,128)(2,1)} %get-tuple-element.82), channel_id=1, source_target_pairs={{0,1},{1,0},{2,3},{3,2},{4,5},{5,4},{6,7},{7,6},{8,9},{9,8},{10,11... | collective-permute-start | bytes 1572872 | tf_op jit(solution)/shard_map/ppermute | solution.py:1185
  339.7 5.9 copy-start.60
  339.8 5.7 copy-start.62
  341.7 42.8 %collective-permute-start.16 = (bf16[512,512]{0,1:T(8,128)(2,1)S(1)}, bf16[512,512]{0,1:T(8,128)(2,1)S(1)}, u32[]{:S(2)}, u32[]{:S(2)}) collective-permute-start(bf16[512,512]{0,1:T(8,128)(2,1)S(1)} %get-tuple-element.84), channel_id=1, source_target_pairs={{0,1},{1,0},{2,3},{3,2},{4,5},{5,4},{6,7},{7,6},{8,9},{9,8},{10,11... | collective-permute-start | bytes 1572872 | tf_op jit(solution)/shard_map/ppermute | solution.py:1185
  345.5 24.0 %collective-permute-start.19 = (bf16[2,512,256]{2,1,0:T(8,128)(2,1)S(1)}, bf16[2,512,256]{2,1,0:T(8,128)(2,1)S(1)}, u32[]{:S(2)}, u32[]{:S(2)}) collective-permute-start(bf16[2,512,256]{2,1,0:T(8,128)(2,1)S(1)} %copy-done.62), channel_id=1, source_target_pairs={{0,1},{1,0},{2,3},{3,2},{4,5},{5,4},{6,7},{7,6},{8,9},{9,8},{10,11... | collective-permute-start | bytes 1572872 | tf_op jit(solution)/shard_map/ppermute | solution.py:1185
  345.6 35.2 %collective-permute-start.18 = (bf16[2,512,256]{2,1,0:T(8,128)(2,1)S(1)}, bf16[2,512,256]{2,1,0:T(8,128)(2,1)S(1)}, u32[]{:S(2)}, u32[]{:S(2)}) collective-permute-start(bf16[2,512,256]{2,1,0:T(8,128)(2,1)S(1)} %copy-done.60), channel_id=1, source_target_pairs={{0,1},{1,0},{2,3},{3,2},{4,5},{5,4},{6,7},{7,6},{8,9},{9,8},{10,11... | collective-permute-start | bytes 1572872 | tf_op jit(solution)/shard_map/ppermute | solution.py:1185
  347.6 22.0 %copy-start.42 = (bf16[2,512,256]{2,1,0:T(8,128)(2,1)S(1)}, bf16[2,512,256]{2,1,0:T(8,128)(2,1)}, u32[]{:S(2)}) copy-start(bf16[2,512,256]{2,1,0:T(8,128)(2,1)} %get-tuple-element.57) | copy-start | bytes 1572868
  347.6 23.0 %copy-start.29 = (bf16[2048,512]{1,0:T(8,128)(2,1)S(1)}, bf16[2048,512]{1,0:T(8,128)(2,1)}, u32[]{:S(2)}) copy-start(bf16[2048,512]{1,0:T(8,128)(2,1)} %param.18) | copy-start | bytes 6291460
  369.7 4.2 copy-start.30
  369.7 13.1 %collective-permute-start.20 = (bf16[2,512,256]{2,1,0:T(8,128)(2,1)S(1)}, bf16[2,512,256]{2,1,0:T(8,128)(2,1)S(1)}, u32[]{:S(2)}, u32[]{:S(2)}) collective-permute-start(bf16[2,512,256]{2,1,0:T(8,128)(2,1)S(1)} %add_convert_fusion.1), channel_id=1, source_target_pairs={{4,2},{5,3},{6,4},{7,5},{12,10},{13,11},{14,12},{15,13},{20,18},{2... | collective-permute-start | bytes 1572872 | tf_op jit(solution)/shard_map/ppermute | solution.py:1415
  370.6 3.5 copy-start.40
  374.0 6.8 %copy-start.57 = (bf16[2,512,256]{2,1,0:T(8,128)(2,1)S(1)}, bf16[2,512,256]{2,1,0:T(8,128)(2,1)}, u32[]{:S(2)}) copy-start(bf16[2,512,256]{2,1,0:T(8,128)(2,1)} %get-tuple-element.54) | copy-start | bytes 1572868
  374.0 8.8 %copy-start.43 = (bf16[2,512,256]{2,1,0:T(8,128)(2,1)S(1)}, bf16[2,512,256]{2,1,0:T(8,128)(2,1)}, u32[]{:S(2)}) copy-start(bf16[2,512,256]{2,1,0:T(8,128)(2,1)} %get-tuple-element.55) | copy-start | bytes 1572868
  374.0 18.0 %collective-permute-start.5 = (bf16[512,512]{1,0:T(8,128)(2,1)S(1)}, bf16[512,512]{1,0:T(8,128)(2,1)S(1)}, u32[]{:S(2)}, u32[]{:S(2)}) collective-permute-start(bf16[512,512]{1,0:T(8,128)(2,1)S(1)} %copy-done.40), channel_id=1, source_target_pairs={{0,1},{1,0},{2,3},{3,2},{4,5},{5,4},{6,7},{7,6},{8,9},{9,8},{10,11... | collective-permute-start | bytes 1572872 | tf_op jit(solution)/shard_map/ppermute | solution.py:1185
  376.1 10.7 %collective-permute-start.12 = (bf16[512,512]{1,0:T(8,128)(2,1)}, bf16[512,512]{1,0:T(8,128)(2,1)S(1)}, u32[]{:S(2)}, u32[]{:S(2)}) collective-permute-start(bf16[512,512]{1,0:T(8,128)(2,1)} %collective-permute-done.11), channel_id=1, source_target_pairs={{0,8},{8,0},{16,24},{24,16},{1,9},{9,1},{17,25},{25,17},{2,10},{10... | collective-permute-start | bytes 1572872 | tf_op jit(solution)/shard_map/ppermute | solution.py:1191
  380.8 21.9 %collective-permute-start.17 = (bf16[2,512,256]{2,1,0:T(8,128)(2,1)S(1)}, bf16[2,512,256]{2,1,0:T(8,128)(2,1)S(1)}, u32[]{:S(2)}, u32[]{:S(2)}) collective-permute-start(bf16[2,512,256]{2,1,0:T(8,128)(2,1)S(1)} %copy-done.57), channel_id=1, source_target_pairs={{0,1},{1,0},{2,3},{3,2},{4,5},{5,4},{6,7},{7,6},{8,9},{9,8},{10,11... | collective-permute-start | bytes 1572872 | tf_op jit(solution)/shard_map/ppermute | solution.py:1185
  383.0 20.2 %collective-permute-start.21 = (bf16[2,512,256]{2,1,0:T(8,128)(2,1)S(1)}, bf16[2,512,256]{2,1,0:T(8,128)(2,1)S(1)}, u32[]{:S(2)}, u32[]{:S(2)}) collective-permute-start(bf16[2,512,256]{2,1,0:T(8,128)(2,1)S(1)} %add_convert_fusion), channel_id=1, source_target_pairs={{2,0},{3,1},{4,2},{5,3},{6,4},{7,5},{10,8},{11,9},{12,10},{13,11},... | collective-permute-start | bytes 1572872 | tf_op jit(solution)/shard_map/ppermute | solution.py:1415
  388.3 14.9 %copy-start.41 = (bf16[2,512,256]{2,1,0:T(8,128)(2,1)S(1)}, bf16[2,512,256]{2,1,0:T(8,128)(2,1)}, u32[]{:S(2)}) copy-start(bf16[2,512,256]{2,1,0:T(8,128)(2,1)} %get-tuple-element.53) | copy-start | bytes 1572868
  404.5 3.0 copy-start.27
  407.6 6.3 %copy-start.35 = (f32[512,2]{1,0:T(8,128)S(1)}, f32[512,2]{1,0:T(8,128)}, u32[]{:S(2)}) copy-start(f32[512,2]{1,0:T(8,128)} %copy.106) | copy-start | bytes 12292
  408.3 6.2 %copy-start.22 = (f32[512,256]{1,0:T(8,128)S(1)}, f32[512,256]{1,0:T(8,128)}, u32[]{:S(2)}) copy-start(f32[512,256]{1,0:T(8,128)} %copy.107) | copy-start | bytes 1572868
  408.3 6.2 %copy-start.55 = (f32[256]{0:T(256)S(1)}, f32[256]{0:T(256)}, u32[]{:S(2)}) copy-start(f32[256]{0:T(256)} %broadcast_bitcast_fusion.1) | copy-start | bytes 3076
  408.3 12.0 %copy-start.18 = (bf16[2048,512]{1,0:T(8,128)(2,1)S(1)}, bf16[2048,512]{1,0:T(8,128)(2,1)}, u32[]{:S(2)}) copy-start(bf16[2048,512]{1,0:T(8,128)(2,1)} %param.21) | copy-start | bytes 6291460
  409.2 5.4 copy-start.23
  412.2 8.1 %copy-start.3 = (f32[512,2048]{1,0:T(8,128)S(1)}, f32[512,2048]{1,0:T(8,128)}, u32[]{:S(2)}) copy-start(f32[512,2048]{1,0:T(8,128)} %fusion.49) | copy-start | bytes 12582916
  415.8 4.5 copy-start
  415.9 4.5 copy-start.2
  415.9 4.5 copy-start.47
  419.0 5.6 copy-start.50
  419.0 12.9 %copy-start.32 = (bf16[512,1024]{1,0:T(8,128)(2,1)S(1)}, bf16[512,1024]{1,0:T(8,128)(2,1)}, u32[]{:S(2)}) copy-start(bf16[512,1024]{1,0:T(8,128)(2,1)} %constant_dynamic-slice_fusion.1) | copy-start | bytes 3145732
  419.0 12.9 %copy-start.34 = (bf16[512,1024]{1,0:T(8,128)(2,1)S(1)}, bf16[512,1024]{1,0:T(8,128)(2,1)}, u32[]{:S(2)}) copy-start(bf16[512,1024]{1,0:T(8,128)(2,1)} %maximum_select_fusion.1) | copy-start | bytes 3145732
  419.0 12.9 %copy-start.36 = (bf16[512,256]{1,0:T(8,128)(2,1)S(1)}, bf16[512,256]{1,0:T(8,128)(2,1)}, u32[]{:S(2)}) copy-start(bf16[512,256]{1,0:T(8,128)(2,1)} %fusion.39) | copy-start | bytes 786436
  419.1 12.9 %collective-permute-start.22 = (bf16[512,512]{1,0:T(8,128)(2,1)S(1)}, bf16[512,512]{1,0:T(8,128)(2,1)S(1)}, u32[]{:S(2)}, u32[]{:S(2)}) collective-permute-start(bf16[512,512]{1,0:T(8,128)(2,1)S(1)} %pad_maximum_fusion.8), channel_id=1, source_target_pairs={{0,1},{1,0},{2,3},{3,2},{4,5},{5,4},{6,7},{7,6},{8,9},{9,8},{10,11... | collective-permute-start | bytes 1572872 | tf_op jit(solution)/shard_map/ppermute | solution.py:1185
  593.6 4.3 copy-start.21
  (23 other events, 40.0 us)

commit v8 on v7

--- a/solution.py
+++ b/solution.py
@@ -1181,6 +1181,10 @@
     def ring(value):
         return lax.ppermute(value, "sp", ring_pairs)
 
+    def far(value, step):
+        pairs = [(z * 2 + y, ((z + step) % outer) * 2 + y) for z in range(outer) for y in range(2)]
+        return lax.ppermute(value, "sp", pairs)
+
     def pair(value):
         return lax.ppermute(value, "sp", pair_pairs)
 
@@ -1192,10 +1196,11 @@
 
     def gather_sp(block, paired):
         blocks = []
+        first = block
         for k in range(outer):
             blocks.append((block, pair(block)) if k < paired else (block,))
             if k < outer - 1:
-                block = ring(block)
+                block = ring(block) if paired == outer else far(first, k + 1)
         return blocks
 
     def scatter_sp(parts):
@@ -1237,12 +1242,22 @@
             if z + 1 - step >= 0 and (z + 1 - step >= low or z + 1 < high)
         ]
 
+    def far_pairs(step):
+        return [
+            (z * 2 + y, (z + step) * 2 + y)
+            for z in range(outer - step)
+            for y in range(2)
+            if z >= low or z + step < high
+        ]
+
     kv_blocks = []
     travelling = kv_own
     for k in range(reach + 1):
+        if k > 0 and reach <= 2:
+            travelling = lax.ppermute(kv_own, "sp", far_pairs(k))
+        elif k > 0:
+            travelling = lax.ppermute(travelling, "sp", up_pairs(k))
         kv_blocks.append((travelling, pair(travelling)))
-        if k < reach:
-            travelling = lax.ppermute(travelling, "sp", up_pairs(k + 1))
 
     query_raw = matmul(normed, query_proj).reshape(rows_dev, heads, head_width)
     gate_raw = matmul(normed, gate_proj)
@@ -1283,6 +1298,8 @@
     starts_row = own_starts[None, :]
     carried = None
     for k in range(reach + 1):
+        if fused and k == reach:
+            carried, up_blocks = lax.optimization_barrier((carried, up_blocks))
         carried = attn_forward(
             infos[k], starts_column, queries, kv_blocks[k][0], kv_blocks[k][1], carried, scale
         )

time: 624 us -> 618 us (level)
  waiting for transfers between devices: 47.6 us -> 40.5 us
    ppermute x14, waiting for transfers between devices: 45.2 us -> 37.1 us  [pair(): return lax.ppermute(value, 'sp', pair_pairs)]
    pallas_call x1, Pallas kernels: 188 us -> 195 us  [middle_layer(): pl.pallas_call(functools.partial(middle_kernel, outer), out_shape=[jax.Sh...]
  transfers between devices with their start and end apart: 23 -> 23, of which waited for: 9 -> 8; matrix products, arithmetic and copies ran while one was open for 13% -> 15% of each run, Pallas kernels for 4% -> 36%
where the time goes in v8:
time: 618 us; the launch traced here: 611 us
  Pallas kernels  376 us (61%)
  other arithmetic  64.8 us (10%)
  local copies, waits for them, and re-layouts  42.6 us (7%)
  waiting for transfers between devices  40.5 us (7%)
  starting transfers between devices  38.9 us (6%)
  matrix products  38.7 us (6%)
  between operations  9.99 us (2%)
    pallas_call x1, Pallas kernels, middle_layer(): pl.pallas_call(functools.partial(middle_kernel, outer), out_shape=[jax.Sh...  195 us
    pallas_call x1, Pallas kernels, finish(): pl.pallas_call(functools.partial(finish_kernel, outer, sides, sp_n, tp_n,...  154 us
    ppermute x14, waiting for transfers between devices, pair(): return lax.ppermute(value, 'sp', pair_pairs)  37.1 us
    ppermute x14, starting transfers between devices, pair(): return lax.ppermute(value, 'sp', pair_pairs)  18.1 us
    dot_general x5, matrix products, times_transpose(): lax.dot_general(left, right, (((1,), (1,)), ((), ())), preferred_element_...  17 us
    pallas_call x3, Pallas kernels, attn_backward(): pl.pallas_call(functools.partial(attn_backward_kernel, first, diagonal, s...  14.2 us
    pallas_call x3, Pallas kernels, attn_forward(): pl.pallas_call(functools.partial(attn_forward_kernel, first, first, scale...  12.5 us
  transfers between devices with their start and end apart: 23, of which 8 were waited for; matrix products, arithmetic and copies ran while one was open for 15% of the time, Pallas kernels for 36%

profile of v8, /device:TPU:0, one launch (start us, length us, event | category | flops | bytes accessed | tf_op | source)
XLA Modules:
  0.0 611.0 jit_solution(5387865140364467925)
XLA Ops:
  0.7 2.2 fusion
  6.7 1.4 fusion.15
  11.8 1.8 pad_maximum_fusion.6.kv_a
  13.6 6.8 %collective-permute-start = (bf16[2,512,256]{2,1,0:T(8,128)(2,1)}, bf16[2,512,256]{2,1,0:T(8,128)(2,1)}, u32[]{:S(2)}, u32[]{:S(2)}) collective-permute-start(bf16[2,512,256]{2,1,0:T(8,128)(2,1)} %pad_maximum_fusion.6.kv_a), channel_id=1, source_target_pairs={{0,4},{1,5},{2,6},{3,7},{8,12},{9,13},{10,14},{11,15},{16,20},{17,... | collective-permute-start | bytes 1572872 | tf_op jit(solution)/shard_map/ppermute | solution.py:1257
  20.4 4.3 collective-permute-start.2
  24.7 1.5 collective-permute-start.4
  26.2 1.9 constant_dynamic-slice_fusion.5.refs_7_
  30.7 5.1 multiply_reduce_fusion.1
  35.8 1.6 copy.89
  39.6 1.9 constant_dynamic-slice_fusion
  41.5 2.3 constant_dynamic-slice_fusion.1
  46.0 1.5 pad_maximum_fusion.5
  50.3 1.5 collective-permute-start.3
  58.2 3.7 fusion.14
  62.0 6.8 %collective-permute-start.8 = (bf16[128,2048]{1,0:T(8,128)(2,1)}, bf16[128,2048]{1,0:T(8,128)(2,1)}, u32[]{:S(2)}, u32[]{:S(2)}) collective-permute-start(bf16[128,2048]{1,0:T(8,128)(2,1)} %constant_dynamic-slice_fusion.5.refs_7_), channel_id=1, source_target_pairs={{0,4},{1,5},{2,6},{3,7},{4,0},{5,1},{6,2},{7,3},{8,12},{9,13},{10,... | collective-permute-start | bytes 1572872 | tf_op jit(solution)/shard_map/ppermute | solution.py:1186
  69.8 1.5 collective-permute-start.7
  80.0 1.4 fusion.40.starts
  81.4 4.9 attn_forward.3
  86.3 3.8 attn_forward.4
  90.2 2.2 collective-permute-done.8.refs_11_
  93.5 1.4 collective-permute-done.7.refs_10_
  95.0 9.6 %collective-permute-done.1.kv_b = bf16[2,512,256]{2,1,0:T(8,128)(2,1)} collective-permute-done((bf16[2,512,256]{2,1,0:T(8,128)(2,1)}, bf16[2,512,256]{2,1,0:T(8,128)(2,1)}, u32[]{:S(2)}, u32[]{:S(2)}) %collective-permute-start.1) | collective-permute-done | bytes 524320 | tf_op jit(solution)/shard_map/ppermute | solution.py:1189
  104.6 3.8 attn_forward.5
  108.4 3.1 multiply_convert_fusion.1
  111.5 195.2 %middle.1 = (bf16[128,2048]{1,0:T(8,128)(2,1)}, f32[128,2048]{1,0:T(8,128)}, f32[1,2048]{1,0:T(1,128)}, bf16[2,2,128,2048]{3,2,1,0:T(8,128)(2,1)}, bf16[2,2048,7...) custom-call(bf16[512,512]{1,0:T(8,128)(2,1)} %get-tuple-element.92.refs_0_, bf16[512,2048]{1,0:T(8,128)(2,1)} %refs_1_.1, ...), custom_call_target="tpu_custom_call" | custom-call | flops 30000001024 | bytes 40000000 | tf_op jit(solution)/shard_map/middle/pallas_call | solution.py:680
  306.7 1.9 constant_dynamic-slice_fusion.2
  308.6 4.6 fusion.51
  315.6 2.9 convert_multiply_fusion.3
  319.4 1.5 copy.117
  323.3 3.3 attn_backward.3
  326.6 3.8 attn_backward.4
  330.5 7.1 %attn_backward.5 = (f32[512,512]{1,0:T(8,128)}, bf16[2,512,256]{2,1,0:T(8,128)(2,1)}, bf16[2,512,256]{2,1,0:T(8,128)(2,1)}) custom-call(s32[7]{0:T(128)} %stack.145.info, s32[1,512]{1,0:T(1,128)} %compare_select_fusion.starts, f32[2,2,512]{2,1,0:T(2,128)} %reshape.259.lse, f32[2,2,512]{2,1,0:T(2,128)} %reshape.261.deltas, bf16[512,512]{1,0:T(8,128)(2,1)} %bitcast.171, ...), custom_call_target="tpu_custom_call" | custom-call | flops 2684354560 | bytes 2097152 | tf_op jit(solution)/shard_map/attn_backward/pallas_call | solution.py:229
  337.6 1.4 broadcast_multiply_fusion
  340.4 4.4 collective-permute-start.19
  344.9 8.7 %bitcast_convert_fusion = (f32[2048,768]{1,0:T(8,128)}, f32[2048,768]{1,0:T(8,128)}) fusion(bf16[2,2048,768]{2,1,0:T(8,128)(2,1)} %get-tuple-element.86), kind=kLoop, calls=%fused_computation.9 | loop fusion | flops 3145728 | bytes 18874368 | tf_op jit(solution)/shard_map/convert_element_type | solution.py:1508
  356.4 1.8 fusion.20
  358.3 3.3 fusion.52
  363.8 2.0 collective-permute-start.16
  365.9 1.9 maximum_select_fusion.1
  368.0 3.9 convolution_convert_fusion.2.refs_1_
  371.9 1.5 collective-permute-start.17
  374.6 1.5 collective-permute-start.21
  376.2 4.1 collective-permute-done.16
  380.3 2.3 convolution_convert_fusion.1.refs_2_
  382.5 1.5 maximum_select_fusion
  384.1 7.4 %collective-permute-done.10 = bf16[512,512]{1,0:T(8,128)(2,1)S(1)} collective-permute-done((bf16[512,512]{1,0:T(8,128)(2,1)S(1)}, bf16[512,512]{1,0:T(8,128)(2,1)S(1)}, u32[]{:S(2)}, u32[]{:S(2)}) %collective-permute-start.10) | collective-permute-done | bytes 524320 | tf_op jit(solution)/shard_map/ppermute | solution.py:1189
  391.5 2.2 fusion.9.refs_0_
  393.7 8.1 %collective-permute-done.17 = bf16[2,512,256]{2,1,0:T(8,128)(2,1)S(1)} collective-permute-done((bf16[2,512,256]{2,1,0:T(8,128)(2,1)S(1)}, bf16[2,512,256]{2,1,0:T(8,128)(2,1)S(1)}, u32[]{:S(2)}, u32[]{:S(2)}) %collective-permute-start.17) | collective-permute-done | bytes 524320 | tf_op jit(solution)/shard_map/ppermute | solution.py:1189
  403.2 2.8 fusion.49
  407.5 2.1 copy.115
  410.5 1.7 mul.521
  414.1 2.1 fusion.53
  417.3 1.8 collective-permute-start.22
  419.1 4.2 fusion.4
  423.9 6.5 %collective-permute-done.22 = bf16[512,512]{1,0:T(8,128)(2,1)S(1)} collective-permute-done((bf16[512,512]{1,0:T(8,128)(2,1)S(1)}, bf16[512,512]{1,0:T(8,128)(2,1)S(1)}, u32[]{:S(2)}, u32[]{:S(2)}) %collective-permute-start.22) | collective-permute-done | bytes 524320 | tf_op jit(solution)/shard_map/ppermute | solution.py:1189
  430.4 2.3 convolution_convert_fusion.refs_3_
  432.7 153.7 %finish.1 = (bf16[2,512,1024]{2,1,0:T(8,128)(2,1)}, bf16[2,1024,512]{2,1,0:T(8,128)(2,1)}, bf16[2,1024,512]{2,1,0:T(8,128)(2,1)}, bf16[2,1024,512]{2,1,0:T(8,128...) custom-call(bf16[512,1024]{1,0:T(8,128)(2,1)} %fusion.9.refs_0_, ...), custom_call_target="tpu_custom_call" | custom-call | flops 1000000000 | bytes 100000000 | tf_op jit(solution)/shard_map/finish/pallas_call | solution.py:1100
  589.0 4.3 bitcast_convert_fusion.4
  593.3 2.7 bitcast_convert_fusion.3
  596.0 2.3 slice_convert_fusion
  598.5 2.7 bitcast_convert_fusion.2
  601.4 1.7 copy-done.13
  603.1 3.6 convert_element_type.200
  606.7 2.5 maximum_convert_fusion
  (207 shorter events, 51.5 us)
Async XLA Ops:
  0.6 4.8 copy-start.1
  0.7 3.5 copy-start.47
  0.7 4.8 copy-start.44
  6.7 2.8 copy-start.6
  9.5 4.1 copy-start.7
  11.4 17.2 %copy-start.25 = (f32[512,64]{0,1:T(8,128)}, f32[512,64]{0,1:T(8,128)S(1)}, u32[]{:S(2)}) copy-start(f32[512,64]{0,1:T(8,128)S(1)} %get-tuple-element.126) | copy-start | bytes 393220
  11.6 17.9 %copy-start.53 = (f32[128]{0:T(128)S(1)}, f32[128]{0:T(128)}, u32[]{:S(2)}) copy-start(f32[128]{0:T(128)} %param.24) | copy-start | bytes 1540
  13.6 48.4 %collective-permute-start = (bf16[2,512,256]{2,1,0:T(8,128)(2,1)}, bf16[2,512,256]{2,1,0:T(8,128)(2,1)}, u32[]{:S(2)}, u32[]{:S(2)}) collective-permute-start(bf16[2,512,256]{2,1,0:T(8,128)(2,1)} %pad_maximum_fusion.6.kv_a), channel_id=1, source_target_pairs={{0,4},{1,5},{2,6},{3,7},{8,12},{9,13},{10,14},{11,15},{16,20},{17,... | collective-permute-start | bytes 1572872 | tf_op jit(solution)/shard_map/ppermute | solution.py:1257
  20.4 29.9 %collective-permute-start.2 = (bf16[2,512,256]{2,1,0:T(8,128)(2,1)}, bf16[2,512,256]{2,1,0:T(8,128)(2,1)}, u32[]{:S(2)}, u32[]{:S(2)}) collective-permute-start(bf16[2,512,256]{2,1,0:T(8,128)(2,1)} %pad_maximum_fusion.6.kv_a), channel_id=1, source_target_pairs={{0,2},{1,3},{2,4},{3,5},{4,6},{5,7},{8,10},{9,11},{10,12},{11,13},... | collective-permute-start | bytes 1572872 | tf_op jit(solution)/shard_map/ppermute | solution.py:1257
  24.7 44.2 %collective-permute-start.4 = (bf16[2,512,256]{2,1,0:T(8,128)(2,1)}, bf16[2,512,256]{2,1,0:T(8,128)(2,1)}, u32[]{:S(2)}, u32[]{:S(2)}) collective-permute-start(bf16[2,512,256]{2,1,0:T(8,128)(2,1)} %pad_maximum_fusion.6.kv_a), channel_id=1, source_target_pairs={{0,1},{1,0},{2,3},{3,2},{4,5},{5,4},{6,7},{7,6},{8,9},{9,8},{10,11... | collective-permute-start | bytes 1572872 | tf_op jit(solution)/shard_map/ppermute | solution.py:1189
  28.1 41.3 %collective-permute-start.5 = (bf16[128,2048]{1,0:T(8,128)(2,1)}, bf16[128,2048]{1,0:T(8,128)(2,1)}, u32[]{:S(2)}, u32[]{:S(2)}) collective-permute-start(bf16[128,2048]{1,0:T(8,128)(2,1)} %constant_dynamic-slice_fusion.5.refs_7_), channel_id=1, source_target_pairs={{0,1},{1,0},{2,3},{3,2},{4,5},{5,4},{6,7},{7,6},{8,9},{9,8},{10,11... | collective-permute-start | bytes 1572872 | tf_op jit(solution)/shard_map/ppermute | solution.py:1189
  28.6 41.2 %collective-permute-start.6 = (bf16[128,2048]{1,0:T(8,128)(2,1)}, bf16[128,2048]{1,0:T(8,128)(2,1)}, u32[]{:S(2)}, u32[]{:S(2)}) collective-permute-start(bf16[128,2048]{1,0:T(8,128)(2,1)} %constant_dynamic-slice_fusion.5.refs_7_), channel_id=1, source_target_pairs={{0,2},{1,3},{2,4},{3,5},{4,6},{5,7},{6,0},{7,1},{8,10},{9,11},{10,... | collective-permute-start | bytes 1572872 | tf_op jit(solution)/shard_map/ppermute | solution.py:1186
  37.4 7.8 %copy-start.4 = (f32[512,4,128]{2,1,0:T(4,128)}, f32[512,4,128]{2,1,0:T(4,128)S(1)}, u32[]{:S(2)}) copy-start(f32[512,4,128]{2,1,0:T(4,128)S(1)} %copy.89) | copy-start | bytes 3145732
  41.5 3.7 copy-start.14
  45.2 3.7 copy-start.50
  46.0 9.8 %copy-start.8 = (f32[512,256]{0,1:T(8,128)S(1)}, f32[512,256]{0,1:T(8,128)}, u32[]{:S(2)}) copy-start(f32[512,256]{0,1:T(8,128)} %copy-done.7) | copy-start | bytes 1572868
  50.3 22.6 %collective-permute-start.3 = (bf16[2,512,256]{2,1,0:T(8,128)(2,1)}, bf16[2,512,256]{2,1,0:T(8,128)(2,1)}, u32[]{:S(2)}, u32[]{:S(2)}) collective-permute-start(bf16[2,512,256]{2,1,0:T(8,128)(2,1)} %collective-permute-done.2.kv_a), channel_id=1, source_target_pairs={{0,1},{1,0},{2,3},{3,2},{4,5},{5,4},{6,7},{7,6},{8,9},{9,8},{10,11... | collective-permute-start | bytes 1572872 | tf_op jit(solution)/shard_map/ppermute | solution.py:1189
  58.2 10.6 %copy-start.42 = (bf16[512,512]{1,0:T(8,128)(2,1)S(1)}, bf16[512,512]{1,0:T(8,128)(2,1)}, u32[]{:S(2)}) copy-start(bf16[512,512]{1,0:T(8,128)(2,1)} %constant_dynamic-slice_fusion) | copy-start | bytes 1572868
  58.2 13.1 %copy-start.22 = (bf16[512,4,128]{2,1,0:T(4,128)(2,1)S(1)}, bf16[512,4,128]{2,1,0:T(4,128)(2,1)}, u32[]{:S(2)}) copy-start(bf16[512,4,128]{2,1,0:T(4,128)(2,1)} %pad_maximum_fusion.5) | copy-start | bytes 1572868
  61.9 46.5 %copy-start.10 = (f32[512,512]{1,0:T(8,128)}, f32[512,512]{1,0:T(8,128)S(1)}, u32[]{:S(2)}) copy-start(f32[512,512]{1,0:T(8,128)S(1)} %fusion.14) | copy-start | bytes 3145732
  62.0 14.6 %copy-start.46 = (f32[512,2]{0,1:T(2,128)S(1)}, f32[512,2]{0,1:T(2,128)}, u32[]{:S(2)}) copy-start(f32[512,2]{0,1:T(2,128)} %get-tuple-element.123) | copy-start | bytes 12292
  62.0 30.4 %collective-permute-start.8 = (bf16[128,2048]{1,0:T(8,128)(2,1)}, bf16[128,2048]{1,0:T(8,128)(2,1)}, u32[]{:S(2)}, u32[]{:S(2)}) collective-permute-start(bf16[128,2048]{1,0:T(8,128)(2,1)} %constant_dynamic-slice_fusion.5.refs_7_), channel_id=1, source_target_pairs={{0,4},{1,5},{2,6},{3,7},{4,0},{5,1},{6,2},{7,3},{8,12},{9,13},{10,... | collective-permute-start | bytes 1572872 | tf_op jit(solution)/shard_map/ppermute | solution.py:1186
  68.8 21.3 %collective-permute-start.13 = (bf16[512,512]{1,0:T(8,128)(2,1)S(1)}, bf16[512,512]{1,0:T(8,128)(2,1)}, u32[]{:S(2)}, u32[]{:S(2)}) collective-permute-start(bf16[512,512]{1,0:T(8,128)(2,1)S(1)} %copy-done.42), channel_id=1, source_target_pairs={{0,1},{1,0},{2,3},{3,2},{4,5},{5,4},{6,7},{7,6},{8,9},{9,8},{10,11... | collective-permute-start | bytes 1572872 | tf_op jit(solution)/shard_map/ppermute | solution.py:1189
  69.3 24.2 %collective-permute-start.9 = (bf16[128,2048]{1,0:T(8,128)(2,1)}, bf16[128,2048]{1,0:T(8,128)(2,1)}, u32[]{:S(2)}, u32[]{:S(2)}) collective-permute-start(bf16[128,2048]{1,0:T(8,128)(2,1)} %constant_dynamic-slice_fusion.5.refs_7_), channel_id=1, source_target_pairs={{0,6},{1,7},{2,0},{3,1},{4,2},{5,3},{6,4},{7,5},{8,14},{9,15},{10,... | collective-permute-start | bytes 1572872 | tf_op jit(solution)/shard_map/ppermute | solution.py:1186
  69.8 25.2 %collective-permute-start.7 = (bf16[128,2048]{1,0:T(8,128)(2,1)}, bf16[128,2048]{1,0:T(8,128)(2,1)}, u32[]{:S(2)}, u32[]{:S(2)}) collective-permute-start(bf16[128,2048]{1,0:T(8,128)(2,1)} %collective-permute-done.6.refs_9_), channel_id=1, source_target_pairs={{0,1},{1,0},{2,3},{3,2},{4,5},{5,4},{6,7},{7,6},{8,9},{9,8},{10,11... | collective-permute-start | bytes 1572872 | tf_op jit(solution)/shard_map/ppermute | solution.py:1189
  72.9 31.7 %collective-permute-start.1 = (bf16[2,512,256]{2,1,0:T(8,128)(2,1)}, bf16[2,512,256]{2,1,0:T(8,128)(2,1)}, u32[]{:S(2)}, u32[]{:S(2)}) collective-permute-start(bf16[2,512,256]{2,1,0:T(8,128)(2,1)} %collective-permute-done.kv_a), channel_id=1, source_target_pairs={{0,1},{1,0},{2,3},{3,2},{4,5},{5,4},{6,7},{7,6},{8,9},{9,8},{10,11... | collective-permute-start | bytes 1572872 | tf_op jit(solution)/shard_map/ppermute | solution.py:1189
  90.1 273.7 %collective-permute-start.14 = (bf16[512,512]{1,0:T(8,128)(2,1)}, bf16[512,512]{1,0:T(8,128)(2,1)}, u32[]{:S(2)}, u32[]{:S(2)}) collective-permute-start(bf16[512,512]{1,0:T(8,128)(2,1)} %collective-permute-done.13), channel_id=1, source_target_pairs={{0,8},{8,0},{16,24},{24,16},{1,9},{9,1},{17,25},{25,17},{2,10},{10... | collective-permute-start | bytes 1572872 | tf_op jit(solution)/shard_map/ppermute | solution.py:1195
  308.6 4.6 copy-start.12
  314.4 53.3 %collective-permute-start.11 = (bf16[512,512]{1,0:T(8,128)(2,1)}, bf16[512,512]{1,0:T(8,128)(2,1)}, u32[]{:S(2)}, u32[]{:S(2)}) collective-permute-start(bf16[512,512]{1,0:T(8,128)(2,1)} %constant_dynamic-slice_fusion.2), channel_id=1, source_target_pairs={{0,1},{1,0},{2,3},{3,2},{4,5},{5,4},{6,7},{7,6},{8,9},{9,8},{10,11... | collective-permute-start | bytes 1572872 | tf_op jit(solution)/shard_map/ppermute | solution.py:1189
  318.5 49.4 %collective-permute-start.15 = (bf16[512,512]{1,0:T(8,128)(2,1)}, bf16[512,512]{1,0:T(8,128)(2,1)}, u32[]{:S(2)}, u32[]{:S(2)}) collective-permute-start(bf16[512,512]{1,0:T(8,128)(2,1)} %get-tuple-element.98), channel_id=1, source_target_pairs={{0,1},{1,0},{2,3},{3,2},{4,5},{5,4},{6,7},{7,6},{8,9},{9,8},{10,11... | collective-permute-start | bytes 1572872 | tf_op jit(solution)/shard_map/ppermute | solution.py:1189
  340.4 21.3 %collective-permute-start.19 = (bf16[2,512,256]{2,1,0:T(8,128)(2,1)}, bf16[2,512,256]{2,1,0:T(8,128)(2,1)}, u32[]{:S(2)}, u32[]{:S(2)}) collective-permute-start(bf16[2,512,256]{2,1,0:T(8,128)(2,1)} %get-tuple-element.74), channel_id=1, source_target_pairs={{0,1},{1,0},{2,3},{3,2},{4,5},{5,4},{6,7},{7,6},{8,9},{9,8},{10,11... | collective-permute-start | bytes 1572872 | tf_op jit(solution)/shard_map/ppermute | solution.py:1189
  344.8 27.1 %collective-permute-start.18 = (bf16[2,512,256]{2,1,0:T(8,128)(2,1)}, bf16[2,512,256]{2,1,0:T(8,128)(2,1)}, u32[]{:S(2)}, u32[]{:S(2)}) collective-permute-start(bf16[2,512,256]{2,1,0:T(8,128)(2,1)} %get-tuple-element.72), channel_id=1, source_target_pairs={{0,1},{1,0},{2,3},{3,2},{4,5},{5,4},{6,7},{7,6},{8,9},{9,8},{10,11... | collective-permute-start | bytes 1572872 | tf_op jit(solution)/shard_map/ppermute | solution.py:1189
  344.9 8.7 %copy-start.5 = (f32[512,4,128]{2,1,0:T(4,128)S(1)}, f32[512,4,128]{2,1,0:T(4,128)}, u32[]{:S(2)}) copy-start(f32[512,4,128]{2,1,0:T(4,128)} %copy-done.4) | copy-start | bytes 3145732
  344.9 8.7 %copy-start.51 = (f32[128]{0:T(128)S(1)}, f32[128]{0:T(128)}, u32[]{:S(2)}) copy-start(f32[128]{0:T(128)} %param.23) | copy-start | bytes 1540
  358.3 3.3 copy-start.41
  358.3 5.4 copy-start.28
  362.9 4.9 copy-start.39
  362.9 5.1 copy-start.29
  362.9 10.5 %collective-permute-start.20 = (bf16[2,512,256]{2,1,0:T(8,128)(2,1)S(1)}, bf16[2,512,256]{2,1,0:T(8,128)(2,1)S(1)}, u32[]{:S(2)}, u32[]{:S(2)}) collective-permute-start(bf16[2,512,256]{2,1,0:T(8,128)(2,1)S(1)} %add_convert_fusion.1), channel_id=1, source_target_pairs={{4,2},{5,3},{6,4},{7,5},{12,10},{13,11},{14,12},{15,13},{20,18},{2... | collective-permute-start | bytes 1572872 | tf_op jit(solution)/shard_map/ppermute | solution.py:1432
  363.8 16.4 %collective-permute-start.16 = (bf16[512,512]{0,1:T(8,128)(2,1)S(1)}, bf16[512,512]{0,1:T(8,128)(2,1)S(1)}, u32[]{:S(2)}, u32[]{:S(2)}) collective-permute-start(bf16[512,512]{0,1:T(8,128)(2,1)S(1)} %get-tuple-element.100), channel_id=1, source_target_pairs={{0,1},{1,0},{2,3},{3,2},{4,5},{5,4},{6,7},{7,6},{8,9},{9,8},{10,11... | collective-permute-start | bytes 1572872 | tf_op jit(solution)/shard_map/ppermute | solution.py:1189
  367.7 12.5 %copy-start.31 = (bf16[512,1024]{1,0:T(8,128)(2,1)}, bf16[512,1024]{1,0:T(8,128)(2,1)S(1)}, u32[]{:S(2)}) copy-start(bf16[512,1024]{1,0:T(8,128)(2,1)S(1)} %maximum_select_fusion.1) | copy-start | bytes 3145732
  367.8 4.1 copy-start.56
  367.8 5.6 copy-start.43
  367.8 23.7 %collective-permute-start.10 = (bf16[512,512]{1,0:T(8,128)(2,1)S(1)}, bf16[512,512]{1,0:T(8,128)(2,1)S(1)}, u32[]{:S(2)}, u32[]{:S(2)}) collective-permute-start(bf16[512,512]{1,0:T(8,128)(2,1)S(1)} %copy-done.39), channel_id=1, source_target_pairs={{0,1},{1,0},{2,3},{3,2},{4,5},{5,4},{6,7},{7,6},{8,9},{9,8},{10,11... | collective-permute-start | bytes 1572872 | tf_op jit(solution)/shard_map/ppermute | solution.py:1189
  367.9 14.6 %collective-permute-start.12 = (bf16[512,512]{1,0:T(8,128)(2,1)}, bf16[512,512]{1,0:T(8,128)(2,1)S(1)}, u32[]{:S(2)}, u32[]{:S(2)}) collective-permute-start(bf16[512,512]{1,0:T(8,128)(2,1)} %collective-permute-done.11), channel_id=1, source_target_pairs={{0,8},{8,0},{16,24},{24,16},{1,9},{9,1},{17,25},{25,17},{2,10},{10... | collective-permute-start | bytes 1572872 | tf_op jit(solution)/shard_map/ppermute | solution.py:1195
  371.9 29.9 %collective-permute-start.17 = (bf16[2,512,256]{2,1,0:T(8,128)(2,1)S(1)}, bf16[2,512,256]{2,1,0:T(8,128)(2,1)S(1)}, u32[]{:S(2)}, u32[]{:S(2)}) collective-permute-start(bf16[2,512,256]{2,1,0:T(8,128)(2,1)S(1)} %copy-done.56), channel_id=1, source_target_pairs={{0,1},{1,0},{2,3},{3,2},{4,5},{5,4},{6,7},{7,6},{8,9},{9,8},{10,11... | collective-permute-start | bytes 1572872 | tf_op jit(solution)/shard_map/ppermute | solution.py:1189
  374.6 27.2 %collective-permute-start.21 = (bf16[2,512,256]{2,1,0:T(8,128)(2,1)S(1)}, bf16[2,512,256]{2,1,0:T(8,128)(2,1)S(1)}, u32[]{:S(2)}, u32[]{:S(2)}) collective-permute-start(bf16[2,512,256]{2,1,0:T(8,128)(2,1)S(1)} %add_convert_fusion), channel_id=1, source_target_pairs={{2,0},{3,1},{4,2},{5,3},{6,4},{7,5},{10,8},{11,9},{12,10},{13,11},... | collective-permute-start | bytes 1572872 | tf_op jit(solution)/shard_map/ppermute | solution.py:1432
  384.1 17.8 %copy-start.40 = (bf16[2,512,256]{2,1,0:T(8,128)(2,1)S(1)}, bf16[2,512,256]{2,1,0:T(8,128)(2,1)}, u32[]{:S(2)}) copy-start(bf16[2,512,256]{2,1,0:T(8,128)(2,1)} %get-tuple-element.69) | copy-start | bytes 1572868
  403.2 3.0 copy-start.26
  406.2 5.9 copy-start.33
  406.6 6.2 %copy-start.55 = (f32[256]{0:T(256)S(1)}, f32[256]{0:T(256)}, u32[]{:S(2)}) copy-start(f32[256]{0:T(256)} %broadcast_bitcast_fusion.1) | copy-start | bytes 3076
  406.6 12.5 %copy-start.16 = (bf16[2048,512]{1,0:T(8,128)(2,1)S(1)}, bf16[2048,512]{1,0:T(8,128)(2,1)}, u32[]{:S(2)}) copy-start(bf16[2048,512]{1,0:T(8,128)(2,1)} %param.21) | copy-start | bytes 6291460
  407.4 5.3 copy-start.20
  407.5 5.3 copy-start.21
  410.5 8.6 %copy-start.3 = (f32[512,2048]{1,0:T(8,128)S(1)}, f32[512,2048]{1,0:T(8,128)}, u32[]{:S(2)}) copy-start(f32[512,2048]{1,0:T(8,128)} %fusion.49) | copy-start | bytes 12582916
  414.1 5.0 copy-start
  414.1 5.0 copy-start.2
  417.2 6.1 copy-start.48
  417.2 13.2 %copy-start.30 = (bf16[512,1024]{1,0:T(8,128)(2,1)S(1)}, bf16[512,1024]{1,0:T(8,128)(2,1)}, u32[]{:S(2)}) copy-start(bf16[512,1024]{1,0:T(8,128)(2,1)} %constant_dynamic-slice_fusion.1) | copy-start | bytes 3145732
  417.3 13.2 %copy-start.32 = (bf16[512,1024]{1,0:T(8,128)(2,1)S(1)}, bf16[512,1024]{1,0:T(8,128)(2,1)}, u32[]{:S(2)}) copy-start(bf16[512,1024]{1,0:T(8,128)(2,1)} %copy-done.31) | copy-start | bytes 3145732
  417.3 13.1 %copy-start.35 = (bf16[512,256]{1,0:T(8,128)(2,1)S(1)}, bf16[512,256]{1,0:T(8,128)(2,1)}, u32[]{:S(2)}) copy-start(bf16[512,256]{1,0:T(8,128)(2,1)} %fusion.39) | copy-start | bytes 786436
  417.3 13.1 %collective-permute-start.22 = (bf16[512,512]{1,0:T(8,128)(2,1)S(1)}, bf16[512,512]{1,0:T(8,128)(2,1)S(1)}, u32[]{:S(2)}, u32[]{:S(2)}) collective-permute-start(bf16[512,512]{1,0:T(8,128)(2,1)S(1)} %pad_maximum_fusion.8), channel_id=1, source_target_pairs={{0,1},{1,0},{2,3},{3,2},{4,5},{5,4},{6,7},{7,6},{8,9},{9,8},{10,11... | collective-permute-start | bytes 1572872 | tf_op jit(solution)/shard_map/ppermute | solution.py:1189
  589.0 4.3 copy-start.19
  593.3 2.7 copy-start.18
  (16 other events, 30.5 us)

commit v9 on v8

--- a/solution.py
+++ b/solution.py
@@ -1058,13 +1058,14 @@
             layer_copy(2, 1 - side, core_dev).wait()
 
     extra = [
-        later(input_step, 0), later(input_step, 1), later(layer_step, 0), later(ffn_sum, 0),
-        later(ffn_sum, 1), later(sums_step, 0), later(input_step, 2), later(sums_step, 1),
-        later(layer_step, 1), later(sums_step, 2), later(input_step, 3), later(sums_step, 3),
-        later(ffn_total, 0), later(sums_step, 4), later(layer_step, 2), later(input_step, 4),
-        later(ffn_total, 1),
+        later(input_step, 0), later(sums_step, 0), later(input_step, 1), later(layer_step, 0),
+        later(ffn_sum, 0), later(ffn_sum, 1), later(lambda: None), later(lambda: None), later(input_step, 2),
+        later(sums_step, 1), later(lambda: None), later(sums_step, 2), later(lambda: None), later(sums_step, 3),
+        later(layer_step, 1), later(lambda: None), later(sums_step, 4), later(input_step, 3),
+        later(lambda: None), later(sums_step, 5), later(ffn_total, 0), later(ffn_total, 1),
+        later(layer_step, 2), later(input_step, 4),
     ]
-    extra += [later(sums_step, index) for index in range(5, rounds + 1)]
+    extra += [later(sums_step, index) for index in range(6, rounds + 1)]
     for index in range(FFN_CHUNKS):
         ffn_near_copy(index).start()
         ffn_load(index).start()
@@ -1403,13 +1404,10 @@
 
     branch_other = swap_half(grad_branch)
     branch_own = lax.dynamic_slice_in_dim(grad_branch, pair_i * (model // 2), model // 2, 1)
-    output_half = outer_sum(
-        jnp.concatenate([gated, gated_other]), jnp.concatenate([branch_own, branch_other])
-    )
     grad_gated = times_transpose(grad_branch, output_proj)
     grad_mixed = (grad_gated * gate_sig).astype(BF16)
     grad_gate_raw = (grad_gated * mixed * (gate_sig * (1.0 - gate_sig))).astype(BF16)
-    gate_half = outer_sum(both_normed, jnp.concatenate([grad_gate_raw, pair(grad_gate_raw)]))
+    gate_other = pair(grad_gate_raw)
     deltas = jnp.sum(
         (grad_mixed.astype(F32) * mixed).reshape(rows_dev, heads, head_width), axis=-1
     )
@@ -1420,16 +1418,28 @@
 
     query_acc = None
     travelling = None
+    paired = {}
     for k in list(range(reach, -1, -1)):
+        if k + 2 in paired:
+            query_acc, paired[k + 2] = lax.optimization_barrier((query_acc, paired[k + 2]))
         query_acc, grad_a, grad_b = attn_backward(
             infos[k], starts_row, lse_rows, delta_rows, queries, grad_mixed,
             kv_blocks[k][0], kv_blocks[k][1], query_acc, k == 0, scale,
         )
-        total = grad_a.astype(F32) + pair(grad_b).astype(F32)
+        if k == reach:
+            query_acc, grad_a, grad_b, gated_other, branch_other, gate_other = lax.optimization_barrier(
+                (query_acc, grad_a, grad_b, gated_other, branch_other, gate_other)
+            )
+        paired[k] = pair(grad_b)
+        total = grad_a.astype(F32) + paired[k].astype(F32)
         if travelling is not None:
             total = total + travelling.astype(F32)
         if k > 0:
             travelling = lax.ppermute(total.astype(BF16), "sp", down_pairs(k))
+    output_half = outer_sum(
+        jnp.concatenate([gated, gated_other]), jnp.concatenate([branch_own, branch_other])
+    )
+    gate_half = outer_sum(both_normed, jnp.concatenate([grad_gate_raw, gate_other]))
     grad_key_rot = total[0].reshape(rows_dev, groups, head_width)
     grad_value_low = total[1].astype(BF16)
     grad_query_rot = (query_acc * scale).reshape(rows_dev, heads, head_width)

time: 618 us -> 614 us (level)
  Pallas kernels: 376 us -> 357 us
  waiting for transfers between devices: 40.5 us -> 49 us
    pallas_call x1, Pallas kernels: 154 us -> 138 us  [finish(): pl.pallas_call(functools.partial(finish_kernel, outer, sides, sp_n, tp_n,...]
    ppermute x2, waiting for transfers between devices: 0.01 us -> 8.92 us  [body(): travelling = lax.ppermute(total.astype(BF16), 'sp', down_pairs(k))]
  transfers between devices with their start and end apart: 23 -> 23, of which waited for: 8 -> 10; matrix products, arithmetic and copies ran while one was open for 15% -> 16% of each run, Pallas kernels for 36% -> 36%
where the time goes in v9:
time: 614 us; the launch traced here: 605 us
  Pallas kernels  357 us (58%)
  other arithmetic  67.1 us (11%)
  waiting for transfers between devices  49 us (8%)
  local copies, waits for them, and re-layouts  43.3 us (7%)
  starting transfers between devices  40.4 us (7%)
  matrix products  38.5 us (6%)
  between operations  9.52 us (2%)
    pallas_call x1, Pallas kernels, middle_layer(): pl.pallas_call(functools.partial(middle_kernel, outer), out_shape=[jax.Sh...  193 us
    pallas_call x1, Pallas kernels, finish(): pl.pallas_call(functools.partial(finish_kernel, outer, sides, sp_n, tp_n,...  138 us
    ppermute x14, waiting for transfers between devices, pair(): return lax.ppermute(value, 'sp', pair_pairs)  36.4 us
    ppermute x14, starting transfers between devices, pair(): return lax.ppermute(value, 'sp', pair_pairs)  18.9 us
    dot_general x5, matrix products, times_transpose(): lax.dot_general(left, right, (((1,), (1,)), ((), ())), preferred_element_...  15.9 us
    pallas_call x3, Pallas kernels, attn_backward(): pl.pallas_call(functools.partial(attn_backward_kernel, first, diagonal, s...  14.2 us
    pallas_call x3, Pallas kernels, attn_forward(): pl.pallas_call(functools.partial(attn_forward_kernel, first, first, scale...  12.5 us
  transfers between devices with their start and end apart: 23, of which 10 were waited for; matrix products, arithmetic and copies ran while one was open for 16% of the time, Pallas kernels for 36%

profile of v9, /device:TPU:0, one launch (start us, length us, event | category | flops | bytes accessed | tf_op | source)
XLA Modules:
  0.0 605.3 jit_solution(12690304590315353953)
XLA Ops:
  2.0 2.0 convert_reduce_fusion
  4.0 2.1 fusion
  12.3 1.8 pad_maximum_fusion.6.kv_a
  14.1 6.8 %collective-permute-start = (bf16[2,512,256]{2,1,0:T(8,128)(2,1)}, bf16[2,512,256]{2,1,0:T(8,128)(2,1)}, u32[]{:S(2)}, u32[]{:S(2)}) collective-permute-start(bf16[2,512,256]{2,1,0:T(8,128)(2,1)} %pad_maximum_fusion.6.kv_a), channel_id=1, source_target_pairs={{0,4},{1,5},{2,6},{3,7},{8,12},{9,13},{10,14},{11,15},{16,20},{17,... | collective-permute-start | bytes 1572872 | tf_op jit(solution)/shard_map/ppermute | solution.py:1258
  20.9 4.3 collective-permute-start.2
  25.2 1.5 collective-permute-start.4
  26.7 1.9 constant_dynamic-slice_fusion.5.refs_7_
  31.2 5.1 multiply_reduce_fusion.1
  36.3 1.6 copy.89
  40.1 1.9 constant_dynamic-slice_fusion
  42.0 2.3 constant_dynamic-slice_fusion.1
  46.6 1.5 pad_maximum_fusion.5
  50.7 1.5 collective-permute-start.3
  58.5 3.7 fusion.14
  62.2 7.0 %collective-permute-start.8 = (bf16[128,2048]{1,0:T(8,128)(2,1)}, bf16[128,2048]{1,0:T(8,128)(2,1)}, u32[]{:S(2)}, u32[]{:S(2)}) collective-permute-start(bf16[128,2048]{1,0:T(8,128)(2,1)} %constant_dynamic-slice_fusion.5.refs_7_), channel_id=1, source_target_pairs={{0,4},{1,5},{2,6},{3,7},{4,0},{5,1},{6,2},{7,3},{8,12},{9,13},{10,... | collective-permute-start | bytes 1572872 | tf_op jit(solution)/shard_map/ppermute | solution.py:1187
  70.2 1.5 collective-permute-start.7
  81.5 4.9 attn_forward.3
  86.3 3.8 attn_forward.4
  90.2 2.6 collective-permute-done.8.refs_11_
  95.3 9.6 %collective-permute-done.1.kv_b = bf16[2,512,256]{2,1,0:T(8,128)(2,1)} collective-permute-done((bf16[2,512,256]{2,1,0:T(8,128)(2,1)}, bf16[2,512,256]{2,1,0:T(8,128)(2,1)}, u32[]{:S(2)}, u32[]{:S(2)}) %collective-permute-start.1) | collective-permute-done | bytes 524320 | tf_op jit(solution)/shard_map/ppermute | solution.py:1190
  105.0 3.8 attn_forward.5
  108.8 2.6 reshape.257
  111.4 2.7 multiply_convert_fusion.1
  114.7 193.0 %middle.1 = (bf16[128,2048]{1,0:T(8,128)(2,1)}, f32[128,2048]{1,0:T(8,128)}, f32[1,2048]{1,0:T(1,128)}, bf16[2,2,128,2048]{3,2,1,0:T(8,128)(2,1)}, bf16[2,2048,7...) custom-call(bf16[512,512]{1,0:T(8,128)(2,1)} %get-tuple-element.106.refs_0_, bf16[512,2048]{1,0:T(8,128)(2,1)} %refs_1_.1, ...), custom_call_target="tpu_custom_call" | custom-call | flops 30000001024 | bytes 40000000 | tf_op jit(solution)/shard_map/middle/pallas_call | solution.py:680
  307.7 4.6 fusion.51
  312.3 1.9 constant_dynamic-slice_fusion.3
  314.5 1.9 collective-permute-start.11
  316.4 8.7 %bitcast_convert_fusion = (f32[2048,768]{1,0:T(8,128)}, f32[2048,768]{1,0:T(8,128)}) fusion(bf16[2,2048,768]{2,1,0:T(8,128)(2,1)} %get-tuple-element.100), kind=kLoop, calls=%fused_computation.9 | loop fusion | flops 3145728 | bytes 18874368 | tf_op jit(solution)/shard_map/convert_element_type | solution.py:1518
  325.7 2.9 convert_multiply_fusion.3
  331.9 2.0 maximum_select_fusion.1
  333.9 3.3 attn_backward.3
  337.2 2.9 maximum_select_fusion
  340.1 4.5 collective-permute-done.13
  344.9 3.8 attn_backward.4
  348.8 1.8 collective-permute-start.19
  350.6 3.8 fusion.9.refs_0_
  354.4 3.3 convolution_convert_fusion.2.refs_1_
  357.7 2.1 collective-permute-done.16
  359.7 7.0 %attn_backward.5 = (f32[512,512]{1,0:T(8,128)}, bf16[2,512,256]{2,1,0:T(8,128)(2,1)}, bf16[2,512,256]{2,1,0:T(8,128)(2,1)}) custom-call(s32[7]{0:T(128)} %stack.145.info, s32[1,512]{1,0:T(1,128)} %compare_select_fusion.starts, f32[2,2,512]{2,1,0:T(2,128)} %reshape.258.lse, f32[2,2,512]{2,1,0:T(2,128)} %reshape.261.deltas, bf16[512,512]{1,0:T(8,128)(2,1)} %bitcast.171, ...), custom_call_target="tpu_custom_call" | custom-call | flops 2684354560 | bytes 2097152 | tf_op jit(solution)/shard_map/attn_backward/pallas_call | solution.py:229
  368.5 2.1 add_convert_fusion.1
  370.6 1.6 collective-permute-start.20
  376.2 1.8 fusion.20
  378.0 3.5 collective-permute-start.17
  383.1 1.4 collective-permute-start.21
  384.5 3.3 fusion.52
  387.9 6.5 %collective-permute-done.17 = bf16[512,512]{0,1:T(8,128)(2,1)S(1)} collective-permute-done((bf16[512,512]{0,1:T(8,128)(2,1)S(1)}, bf16[512,512]{0,1:T(8,128)(2,1)S(1)}, u32[]{:S(2)}, u32[]{:S(2)}) %collective-permute-start.17) | collective-permute-done | bytes 524320 | tf_op jit(solution)/shard_map/ppermute | solution.py:1190
  394.3 2.3 convolution_convert_fusion.1.refs_2_
  396.6 5.2 collective-permute-done.18
  401.8 8.9 %collective-permute-done.21 = bf16[2,512,256]{2,1,0:T(8,128)(2,1)S(1)} collective-permute-done((bf16[2,512,256]{2,1,0:T(8,128)(2,1)S(1)}, bf16[2,512,256]{2,1,0:T(8,128)(2,1)S(1)}, u32[]{:S(2)}, u32[]{:S(2)}) %collective-permute-start.21) | collective-permute-done | bytes 524320 | tf_op jit(solution)/shard_map/ppermute | solution.py:1438
  412.0 2.8 fusion.49
  418.5 1.7 mul.521
  422.1 2.1 fusion.53
  425.3 4.5 collective-permute-start.22
  429.8 3.1 fusion.4
  433.6 7.1 %collective-permute-done.22 = bf16[512,512]{1,0:T(8,128)(2,1)S(1)} collective-permute-done((bf16[512,512]{1,0:T(8,128)(2,1)S(1)}, bf16[512,512]{1,0:T(8,128)(2,1)S(1)}, u32[]{:S(2)}, u32[]{:S(2)}) %collective-permute-start.22) | collective-permute-done | bytes 524320 | tf_op jit(solution)/shard_map/ppermute | solution.py:1190
  440.7 2.3 convolution_convert_fusion.refs_3_
  442.9 137.8 %finish.1 = (bf16[2,512,1024]{2,1,0:T(8,128)(2,1)}, bf16[2,1024,512]{2,1,0:T(8,128)(2,1)}, bf16[2,1024,512]{2,1,0:T(8,128)(2,1)}, bf16[2,1024,512]{2,1,0:T(8,128...) custom-call(bf16[512,1024]{1,0:T(8,128)(2,1)} %fusion.9.refs_0_, ...), custom_call_target="tpu_custom_call" | custom-call | flops 1000000000 | bytes 100000000 | tf_op jit(solution)/shard_map/finish/pallas_call | solution.py:1101
  583.3 4.3 bitcast_convert_fusion.4
  587.6 2.7 bitcast_convert_fusion.3
  590.3 2.3 slice_convert_fusion
  592.8 2.7 bitcast_convert_fusion.2
  595.7 1.7 copy-done.14
  597.4 3.6 convert_element_type.200
  601.0 2.5 maximum_convert_fusion
  (205 shorter events, 54.0 us)
Async XLA Ops:
  0.6 5.4 copy-start.1
  0.7 5.4 copy-start.45
  7.3 2.8 copy-start.6
  10.1 4.0 copy-start.7
  11.9 17.2 %copy-start.27 = (f32[512,64]{0,1:T(8,128)}, f32[512,64]{0,1:T(8,128)S(1)}, u32[]{:S(2)}) copy-start(f32[512,64]{0,1:T(8,128)S(1)} %get-tuple-element.140) | copy-start | bytes 393220
  12.1 17.9 %copy-start.53 = (f32[128]{0:T(128)S(1)}, f32[128]{0:T(128)}, u32[]{:S(2)}) copy-start(f32[128]{0:T(128)} %param.24) | copy-start | bytes 1540
  14.1 48.1 %collective-permute-start = (bf16[2,512,256]{2,1,0:T(8,128)(2,1)}, bf16[2,512,256]{2,1,0:T(8,128)(2,1)}, u32[]{:S(2)}, u32[]{:S(2)}) collective-permute-start(bf16[2,512,256]{2,1,0:T(8,128)(2,1)} %pad_maximum_fusion.6.kv_a), channel_id=1, source_target_pairs={{0,4},{1,5},{2,6},{3,7},{8,12},{9,13},{10,14},{11,15},{16,20},{17,... | collective-permute-start | bytes 1572872 | tf_op jit(solution)/shard_map/ppermute | solution.py:1258
  20.9 29.8 %collective-permute-start.2 = (bf16[2,512,256]{2,1,0:T(8,128)(2,1)}, bf16[2,512,256]{2,1,0:T(8,128)(2,1)}, u32[]{:S(2)}, u32[]{:S(2)}) collective-permute-start(bf16[2,512,256]{2,1,0:T(8,128)(2,1)} %pad_maximum_fusion.6.kv_a), channel_id=1, source_target_pairs={{0,2},{1,3},{2,4},{3,5},{4,6},{5,7},{8,10},{9,11},{10,12},{11,13},... | collective-permute-start | bytes 1572872 | tf_op jit(solution)/shard_map/ppermute | solution.py:1258
  25.2 44.0 %collective-permute-start.4 = (bf16[2,512,256]{2,1,0:T(8,128)(2,1)}, bf16[2,512,256]{2,1,0:T(8,128)(2,1)}, u32[]{:S(2)}, u32[]{:S(2)}) collective-permute-start(bf16[2,512,256]{2,1,0:T(8,128)(2,1)} %pad_maximum_fusion.6.kv_a), channel_id=1, source_target_pairs={{0,1},{1,0},{2,3},{3,2},{4,5},{5,4},{6,7},{7,6},{8,9},{9,8},{10,11... | collective-permute-start | bytes 1572872 | tf_op jit(solution)/shard_map/ppermute | solution.py:1190
  28.6 41.1 %collective-permute-start.5 = (bf16[128,2048]{1,0:T(8,128)(2,1)}, bf16[128,2048]{1,0:T(8,128)(2,1)}, u32[]{:S(2)}, u32[]{:S(2)}) collective-permute-start(bf16[128,2048]{1,0:T(8,128)(2,1)} %constant_dynamic-slice_fusion.5.refs_7_), channel_id=1, source_target_pairs={{0,1},{1,0},{2,3},{3,2},{4,5},{5,4},{6,7},{7,6},{8,9},{9,8},{10,11... | collective-permute-start | bytes 1572872 | tf_op jit(solution)/shard_map/ppermute | solution.py:1190
  29.1 41.1 %collective-permute-start.6 = (bf16[128,2048]{1,0:T(8,128)(2,1)}, bf16[128,2048]{1,0:T(8,128)(2,1)}, u32[]{:S(2)}, u32[]{:S(2)}) collective-permute-start(bf16[128,2048]{1,0:T(8,128)(2,1)} %constant_dynamic-slice_fusion.5.refs_7_), channel_id=1, source_target_pairs={{0,2},{1,3},{2,4},{3,5},{4,6},{5,7},{6,0},{7,1},{8,10},{9,11},{10,... | collective-permute-start | bytes 1572872 | tf_op jit(solution)/shard_map/ppermute | solution.py:1187
  37.9 7.8 %copy-start.4 = (f32[512,4,128]{2,1,0:T(4,128)}, f32[512,4,128]{2,1,0:T(4,128)S(1)}, u32[]{:S(2)}) copy-start(f32[512,4,128]{2,1,0:T(4,128)S(1)} %copy.89) | copy-start | bytes 3145732
  42.0 3.7 copy-start.15
  45.7 3.5 copy-start.50
  46.6 9.6 %copy-start.8 = (f32[512,256]{0,1:T(8,128)S(1)}, f32[512,256]{0,1:T(8,128)}, u32[]{:S(2)}) copy-start(f32[512,256]{0,1:T(8,128)} %copy-done.7) | copy-start | bytes 1572868
  50.7 22.5 %collective-permute-start.3 = (bf16[2,512,256]{2,1,0:T(8,128)(2,1)}, bf16[2,512,256]{2,1,0:T(8,128)(2,1)}, u32[]{:S(2)}, u32[]{:S(2)}) collective-permute-start(bf16[2,512,256]{2,1,0:T(8,128)(2,1)} %collective-permute-done.2.kv_a), channel_id=1, source_target_pairs={{0,1},{1,0},{2,3},{3,2},{4,5},{5,4},{6,7},{7,6},{8,9},{9,8},{10,11... | collective-permute-start | bytes 1572872 | tf_op jit(solution)/shard_map/ppermute | solution.py:1190
  58.5 10.7 %copy-start.43 = (bf16[512,512]{1,0:T(8,128)(2,1)S(1)}, bf16[512,512]{1,0:T(8,128)(2,1)}, u32[]{:S(2)}) copy-start(bf16[512,512]{1,0:T(8,128)(2,1)} %constant_dynamic-slice_fusion) | copy-start | bytes 1572868
  58.5 13.2 %copy-start.24 = (bf16[512,4,128]{2,1,0:T(4,128)(2,1)S(1)}, bf16[512,4,128]{2,1,0:T(4,128)(2,1)}, u32[]{:S(2)}) copy-start(bf16[512,4,128]{2,1,0:T(4,128)(2,1)} %pad_maximum_fusion.5) | copy-start | bytes 1572868
  62.2 49.2 %copy-start.10 = (f32[512,512]{1,0:T(8,128)}, f32[512,512]{1,0:T(8,128)S(1)}, u32[]{:S(2)}) copy-start(f32[512,512]{1,0:T(8,128)S(1)} %fusion.14) | copy-start | bytes 3145732
  62.2 14.5 %copy-start.47 = (f32[512,2]{0,1:T(2,128)S(1)}, f32[512,2]{0,1:T(2,128)}, u32[]{:S(2)}) copy-start(f32[512,2]{0,1:T(2,128)} %get-tuple-element.137) | copy-start | bytes 12292
  62.2 30.6 %collective-permute-start.8 = (bf16[128,2048]{1,0:T(8,128)(2,1)}, bf16[128,2048]{1,0:T(8,128)(2,1)}, u32[]{:S(2)}, u32[]{:S(2)}) collective-permute-start(bf16[128,2048]{1,0:T(8,128)(2,1)} %constant_dynamic-slice_fusion.5.refs_7_), channel_id=1, source_target_pairs={{0,4},{1,5},{2,6},{3,7},{4,0},{5,1},{6,2},{7,3},{8,12},{9,13},{10,... | collective-permute-start | bytes 1572872 | tf_op jit(solution)/shard_map/ppermute | solution.py:1187
  69.2 20.9 %collective-permute-start.14 = (bf16[512,512]{1,0:T(8,128)(2,1)S(1)}, bf16[512,512]{1,0:T(8,128)(2,1)}, u32[]{:S(2)}, u32[]{:S(2)}) collective-permute-start(bf16[512,512]{1,0:T(8,128)(2,1)S(1)} %copy-done.43), channel_id=1, source_target_pairs={{0,1},{1,0},{2,3},{3,2},{4,5},{5,4},{6,7},{7,6},{8,9},{9,8},{10,11... | collective-permute-start | bytes 1572872 | tf_op jit(solution)/shard_map/ppermute | solution.py:1190
  69.7 24.2 %collective-permute-start.9 = (bf16[128,2048]{1,0:T(8,128)(2,1)}, bf16[128,2048]{1,0:T(8,128)(2,1)}, u32[]{:S(2)}, u32[]{:S(2)}) collective-permute-start(bf16[128,2048]{1,0:T(8,128)(2,1)} %constant_dynamic-slice_fusion.5.refs_7_), channel_id=1, source_target_pairs={{0,6},{1,7},{2,0},{3,1},{4,2},{5,3},{6,4},{7,5},{8,14},{9,15},{10,... | collective-permute-start | bytes 1572872 | tf_op jit(solution)/shard_map/ppermute | solution.py:1187
  70.2 25.2 %collective-permute-start.7 = (bf16[128,2048]{1,0:T(8,128)(2,1)}, bf16[128,2048]{1,0:T(8,128)(2,1)}, u32[]{:S(2)}, u32[]{:S(2)}) collective-permute-start(bf16[128,2048]{1,0:T(8,128)(2,1)} %collective-permute-done.6.refs_9_), channel_id=1, source_target_pairs={{0,1},{1,0},{2,3},{3,2},{4,5},{5,4},{6,7},{7,6},{8,9},{9,8},{10,11... | collective-permute-start | bytes 1572872 | tf_op jit(solution)/shard_map/ppermute | solution.py:1190
  73.2 31.8 %collective-permute-start.1 = (bf16[2,512,256]{2,1,0:T(8,128)(2,1)}, bf16[2,512,256]{2,1,0:T(8,128)(2,1)}, u32[]{:S(2)}, u32[]{:S(2)}) collective-permute-start(bf16[2,512,256]{2,1,0:T(8,128)(2,1)} %collective-permute-done.kv_a), channel_id=1, source_target_pairs={{0,1},{1,0},{2,3},{3,2},{4,5},{5,4},{6,7},{7,6},{8,9},{9,8},{10,11... | collective-permute-start | bytes 1572872 | tf_op jit(solution)/shard_map/ppermute | solution.py:1190
  90.1 241.7 %collective-permute-start.15 = (bf16[512,512]{1,0:T(8,128)(2,1)}, bf16[512,512]{1,0:T(8,128)(2,1)}, u32[]{:S(2)}, u32[]{:S(2)}) collective-permute-start(bf16[512,512]{1,0:T(8,128)(2,1)} %collective-permute-done.14), channel_id=1, source_target_pairs={{0,8},{8,0},{16,24},{24,16},{1,9},{9,1},{17,25},{25,17},{2,10},{10... | collective-permute-start | bytes 1572872 | tf_op jit(solution)/shard_map/ppermute | solution.py:1196
  114.2 226.0 %collective-permute-start.10 = (bf16[512,512]{1,0:T(8,128)(2,1)}, bf16[512,512]{1,0:T(8,128)(2,1)}, u32[]{:S(2)}, u32[]{:S(2)}) collective-permute-start(bf16[512,512]{1,0:T(8,128)(2,1)} %get-tuple-element.106.refs_0_), channel_id=1, source_target_pairs={{0,1},{1,0},{2,3},{3,2},{4,5},{5,4},{6,7},{7,6},{8,9},{9,8},{10,11... | collective-permute-start | bytes 1572872 | tf_op jit(solution)/shard_map/ppermute | solution.py:1190
  307.7 6.5 %copy-start.12 = (f32[512,4,128]{2,1,0:T(4,128)S(1)}, f32[512,4,128]{2,1,0:T(4,128)}, u32[]{:S(2)}) copy-start(f32[512,4,128]{2,1,0:T(4,128)} %reshape.257) | copy-start | bytes 3145732
  314.5 16.0 %collective-permute-start.11 = (bf16[512,512]{1,0:T(8,128)(2,1)}, bf16[512,512]{1,0:T(8,128)(2,1)}, u32[]{:S(2)}, u32[]{:S(2)}) collective-permute-start(bf16[512,512]{1,0:T(8,128)(2,1)} %constant_dynamic-slice_fusion.3), channel_id=1, source_target_pairs={{0,1},{1,0},{2,3},{3,2},{4,5},{5,4},{6,7},{7,6},{8,9},{9,8},{10,11... | collective-permute-start | bytes 1572872 | tf_op jit(solution)/shard_map/ppermute | solution.py:1190
  316.4 9.3 %copy-start.11 = (f32[512,512]{1,0:T(8,128)S(1)}, f32[512,512]{1,0:T(8,128)}, u32[]{:S(2)}) copy-start(f32[512,512]{1,0:T(8,128)} %copy-done.10) | copy-start | bytes 3145732
  330.4 14.2 %collective-permute-start.13 = (bf16[512,512]{1,0:T(8,128)(2,1)}, bf16[512,512]{1,0:T(8,128)(2,1)}, u32[]{:S(2)}, u32[]{:S(2)}) collective-permute-start(bf16[512,512]{1,0:T(8,128)(2,1)} %get-tuple-element.112), channel_id=1, source_target_pairs={{0,1},{1,0},{2,3},{3,2},{4,5},{5,4},{6,7},{7,6},{8,9},{9,8},{10,11... | collective-permute-start | bytes 1572872 | tf_op jit(solution)/shard_map/ppermute | solution.py:1190
  330.6 6.6 %collective-permute-start.12 = (bf16[512,512]{1,0:T(8,128)(2,1)}, bf16[512,512]{1,0:T(8,128)(2,1)}, u32[]{:S(2)}, u32[]{:S(2)}) collective-permute-start(bf16[512,512]{1,0:T(8,128)(2,1)} %collective-permute-done.11), channel_id=1, source_target_pairs={{0,8},{8,0},{16,24},{24,16},{1,9},{9,1},{17,25},{25,17},{2,10},{10... | collective-permute-start | bytes 1572872 | tf_op jit(solution)/shard_map/ppermute | solution.py:1196
  333.9 20.5 %copy-start.33 = (bf16[512,1024]{1,0:T(8,128)(2,1)}, bf16[512,1024]{1,0:T(8,128)(2,1)S(1)}, u32[]{:S(2)}) copy-start(bf16[512,1024]{1,0:T(8,128)(2,1)S(1)} %maximum_select_fusion.1) | copy-start | bytes 3145732
  344.6 15.1 %collective-permute-start.16 = (bf16[2,512,256]{2,1,0:T(8,128)(2,1)}, bf16[2,512,256]{2,1,0:T(8,128)(2,1)}, u32[]{:S(2)}, u32[]{:S(2)}) collective-permute-start(bf16[2,512,256]{2,1,0:T(8,128)(2,1)} %get-tuple-element.81), channel_id=1, source_target_pairs={{0,1},{1,0},{2,3},{3,2},{4,5},{5,4},{6,7},{7,6},{8,9},{9,8},{10,11... | collective-permute-start | bytes 1572872 | tf_op jit(solution)/shard_map/ppermute | solution.py:1190
  348.8 5.6 copy-start.21
  348.8 5.6 copy-start.30
  348.8 32.9 %collective-permute-start.19 = (bf16[2,512,256]{2,1,0:T(8,128)(2,1)}, bf16[2,512,256]{2,1,0:T(8,128)(2,1)}, u32[]{:S(2)}, u32[]{:S(2)}) collective-permute-start(bf16[2,512,256]{2,1,0:T(8,128)(2,1)} %get-tuple-element.87), channel_id=1, source_target_pairs={{0,1},{1,0},{2,3},{3,2},{4,5},{5,4},{6,7},{7,6},{8,9},{9,8},{10,11... | collective-permute-start | bytes 1572872 | tf_op jit(solution)/shard_map/ppermute | solution.py:1190
  368.1 4.1 copy-start.16
  370.6 11.0 %collective-permute-start.20 = (bf16[2,512,256]{2,1,0:T(8,128)(2,1)}, bf16[2,512,256]{2,1,0:T(8,128)(2,1)}, u32[]{:S(2)}, u32[]{:S(2)}) collective-permute-start(bf16[2,512,256]{2,1,0:T(8,128)(2,1)} %add_convert_fusion.1), channel_id=1, source_target_pairs={{4,2},{5,3},{6,4},{7,5},{12,10},{13,11},{14,12},{15,13},{20,18},{2... | collective-permute-start | bytes 1572872 | tf_op jit(solution)/shard_map/ppermute | solution.py:1438
  376.0 5.6 copy-start.44
  376.2 8.4 %copy-start.29 = (bf16[2048,512]{1,0:T(8,128)(2,1)S(1)}, bf16[2048,512]{1,0:T(8,128)(2,1)}, u32[]{:S(2)}) copy-start(bf16[2048,512]{1,0:T(8,128)(2,1)} %param.18) | copy-start | bytes 6291460
  378.0 16.3 %collective-permute-start.17 = (bf16[512,512]{0,1:T(8,128)(2,1)S(1)}, bf16[512,512]{0,1:T(8,128)(2,1)S(1)}, u32[]{:S(2)}, u32[]{:S(2)}) collective-permute-start(bf16[512,512]{0,1:T(8,128)(2,1)S(1)} %get-tuple-element.114), channel_id=1, source_target_pairs={{0,1},{1,0},{2,3},{3,2},{4,5},{5,4},{6,7},{7,6},{8,9},{9,8},{10,11... | collective-permute-start | bytes 1572872 | tf_op jit(solution)/shard_map/ppermute | solution.py:1190
  381.5 20.2 %collective-permute-start.18 = (bf16[2,512,256]{2,1,0:T(8,128)(2,1)}, bf16[2,512,256]{2,1,0:T(8,128)(2,1)S(1)}, u32[]{:S(2)}, u32[]{:S(2)}) collective-permute-start(bf16[2,512,256]{2,1,0:T(8,128)(2,1)} %get-tuple-element.85), channel_id=1, source_target_pairs={{0,1},{1,0},{2,3},{3,2},{4,5},{5,4},{6,7},{7,6},{8,9},{9,8},{10,11... | collective-permute-start | bytes 1572872 | tf_op jit(solution)/shard_map/ppermute | solution.py:1190
  383.1 11.3 %copy-start.31 = (bf16[512,1024]{1,0:T(8,128)(2,1)S(1)}, bf16[512,1024]{1,0:T(8,128)(2,1)}, u32[]{:S(2)}) copy-start(bf16[512,1024]{1,0:T(8,128)(2,1)} %constant_dynamic-slice_fusion.1) | copy-start | bytes 3145732
  383.1 11.3 %copy-start.34 = (bf16[512,1024]{1,0:T(8,128)(2,1)S(1)}, bf16[512,1024]{1,0:T(8,128)(2,1)}, u32[]{:S(2)}) copy-start(bf16[512,1024]{1,0:T(8,128)(2,1)} %copy-done.33) | copy-start | bytes 3145732
  383.1 27.6 %collective-permute-start.21 = (bf16[2,512,256]{2,1,0:T(8,128)(2,1)S(1)}, bf16[2,512,256]{2,1,0:T(8,128)(2,1)S(1)}, u32[]{:S(2)}, u32[]{:S(2)}) collective-permute-start(bf16[2,512,256]{2,1,0:T(8,128)(2,1)S(1)} %add_convert_fusion), channel_id=1, source_target_pairs={{2,0},{3,1},{4,2},{5,3},{6,4},{7,5},{10,8},{11,9},{12,10},{13,11},... | collective-permute-start | bytes 1572872 | tf_op jit(solution)/shard_map/ppermute | solution.py:1438
  387.8 22.8 %copy-start.42 = (bf16[2,512,256]{2,1,0:T(8,128)(2,1)S(1)}, bf16[2,512,256]{2,1,0:T(8,128)(2,1)}, u32[]{:S(2)}) copy-start(bf16[2,512,256]{2,1,0:T(8,128)(2,1)} %get-tuple-element.84) | copy-start | bytes 1572868
  412.0 3.0 copy-start.28
  415.1 5.1 copy-start.36
  415.4 5.3 copy-start.55
  415.4 14.4 %copy-start.17 = (bf16[2048,512]{1,0:T(8,128)(2,1)S(1)}, bf16[2048,512]{1,0:T(8,128)(2,1)}, u32[]{:S(2)}) copy-start(bf16[2048,512]{1,0:T(8,128)(2,1)} %param.21) | copy-start | bytes 6291460
  416.3 4.5 copy-start.23
  418.5 11.3 %copy-start.3 = (f32[512,2048]{1,0:T(8,128)S(1)}, f32[512,2048]{1,0:T(8,128)}, u32[]{:S(2)}) copy-start(f32[512,2048]{1,0:T(8,128)} %fusion.49) | copy-start | bytes 12582916
  420.8 9.0 %copy-start.22 = (bf16[512,512]{1,0:T(8,128)(2,1)S(1)}, bf16[512,512]{1,0:T(8,128)(2,1)}, u32[]{:S(2)}) copy-start(bf16[512,512]{1,0:T(8,128)(2,1)} %get-tuple-element.112) | copy-start | bytes 1572868
  422.1 7.7 %copy-start = (f32[512,2048]{1,0:T(8,128)S(1)}, f32[512,2048]{1,0:T(8,128)}, u32[]{:S(2)}) copy-start(f32[512,2048]{1,0:T(8,128)} %fusion.52) | copy-start | bytes 12582916
  422.1 7.7 %copy-start.2 = (bf16[512,2048]{1,0:T(8,128)(2,1)S(1)}, bf16[512,2048]{1,0:T(8,128)(2,1)}, u32[]{:S(2)}) copy-start(bf16[512,2048]{1,0:T(8,128)(2,1)} %param.15) | copy-start | bytes 6291460
  425.3 7.7 %copy-start.48 = (f32[1,2048]{1,0:T(1,128)S(1)}, f32[1,2048]{1,0:T(1,128)}, u32[]{:S(2)}) copy-start(f32[1,2048]{1,0:T(1,128)} %get-tuple-element.90) | copy-start | bytes 24580
  425.3 15.4 %copy-start.32 = (bf16[512,1024]{1,0:T(8,128)(2,1)S(1)}, bf16[512,1024]{1,0:T(8,128)(2,1)}, u32[]{:S(2)}) copy-start(bf16[512,1024]{1,0:T(8,128)(2,1)} %constant_dynamic-slice_fusion.1) | copy-start | bytes 3145732
  425.3 15.4 %copy-start.35 = (bf16[512,1024]{1,0:T(8,128)(2,1)S(1)}, bf16[512,1024]{1,0:T(8,128)(2,1)}, u32[]{:S(2)}) copy-start(bf16[512,1024]{1,0:T(8,128)(2,1)} %copy-done.33) | copy-start | bytes 3145732
  425.3 15.4 %copy-start.38 = (bf16[512,256]{1,0:T(8,128)(2,1)S(1)}, bf16[512,256]{1,0:T(8,128)(2,1)}, u32[]{:S(2)}) copy-start(bf16[512,256]{1,0:T(8,128)(2,1)} %fusion.39) | copy-start | bytes 786436
  425.3 15.3 %collective-permute-start.22 = (bf16[512,512]{1,0:T(8,128)(2,1)S(1)}, bf16[512,512]{1,0:T(8,128)(2,1)S(1)}, u32[]{:S(2)}, u32[]{:S(2)}) collective-permute-start(bf16[512,512]{1,0:T(8,128)(2,1)S(1)} %pad_maximum_fusion.8), channel_id=1, source_target_pairs={{0,1},{1,0},{2,3},{3,2},{4,5},{5,4},{6,7},{7,6},{8,9},{9,8},{10,11... | collective-permute-start | bytes 1572872 | tf_op jit(solution)/shard_map/ppermute | solution.py:1190
  583.3 4.3 copy-start.20
  587.6 2.7 copy-start.19
  592.8 2.7 copy-start.26
  (15 other events, 29.4 us)

commit v10 on v9

--- a/solution.py
+++ b/solution.py
@@ -1452,6 +1452,8 @@
     grad_query_low = grad_query_raw.reshape(rows_dev, heads * head_width).astype(BF16)
     grad_key_low = grad_key_raw.reshape(rows_dev, group_width).astype(BF16)
     grad_kv_low = jnp.concatenate([grad_key_low, grad_value_low], axis=1)
+    grad_kv_low, ffn_both = lax.optimization_barrier((grad_kv_low, ffn_both))
+    ffn_gate_grad, ffn_up_grad = ffn_both[0].astype(F32), ffn_both[1].astype(F32)
 
     both_queries = jnp.concatenate([grad_query_low, pair(grad_query_low)])
     both_kv = jnp.concatenate([grad_kv_low, pair(grad_kv_low)])
@@ -1476,6 +1478,7 @@
             jnp.sum(key_gain_terms, axis=(0, 1)),
         ]
     )
+    gains, ffn_gate_grad, ffn_up_grad = lax.optimization_barrier((gains, ffn_gate_grad, ffn_up_grad))
     gains_at = 2 * model + 2 * head_width
     gains = jnp.pad(gains, (0, -gains_at % 1024)).reshape(-1, 128)
     scales_quarter = lax.dynamic_slice_in_dim(attn_scales, quarter_first, quarter)
@@ -1514,8 +1517,8 @@
         gains[2 * model : 2 * model + head_width],
         gains[2 * model + head_width : gains_at],
         gains[model : 2 * model],
-        ffn_both[0].astype(F32),
-        ffn_both[1].astype(F32),
+        ffn_gate_grad,
+        ffn_up_grad,
         ffn_last.astype(F32),
     )
 

time: 614 us -> 623 us (1.015)
  Pallas kernels: 357 us -> 380 us
  waiting for transfers between devices: 49 us -> 36.2 us
    pallas_call x1, Pallas kernels: 193 us -> 210 us  [middle_layer(): pl.pallas_call(functools.partial(middle_kernel, outer), out_shape=[jax.Sh...]
    ppermute x2, waiting for transfers between devices: 8.92 us -> 0.01 us  [body(): travelling = lax.ppermute(total.astype(BF16), 'sp', down_pairs(k))]
  transfers between devices with their start and end apart: 23 -> 23, of which waited for: 10 -> 6; matrix products, arithmetic and copies ran while one was open for 16% -> 15% of each run, Pallas kernels for 36% -> 39%
where the time goes in v10:
time: 623 us; the launch traced here: 613 us
  Pallas kernels  380 us (61%)
  other arithmetic  65.1 us (10%)
  local copies, waits for them, and re-layouts  44.5 us (7%)
  matrix products  38.9 us (6%)
  starting transfers between devices  38.8 us (6%)
  waiting for transfers between devices  36.2 us (6%)
  between operations  9.3 us (1%)
    pallas_call x1, Pallas kernels, middle_layer(): pl.pallas_call(functools.partial(middle_kernel, outer), out_shape=[jax.Sh...  210 us
    pallas_call x1, Pallas kernels, finish(): pl.pallas_call(functools.partial(finish_kernel, outer, sides, sp_n, tp_n,...  143 us
    ppermute x14, waiting for transfers between devices, pair(): return lax.ppermute(value, 'sp', pair_pairs)  35.1 us
    ppermute x14, starting transfers between devices, pair(): return lax.ppermute(value, 'sp', pair_pairs)  21.9 us
    dot_general x5, matrix products, times_transpose(): lax.dot_general(left, right, (((1,), (1,)), ((), ())), preferred_element_...  15.9 us
    pallas_call x3, Pallas kernels, attn_backward(): pl.pallas_call(functools.partial(attn_backward_kernel, first, diagonal, s...  14.2 us
    pallas_call x3, Pallas kernels, attn_forward(): pl.pallas_call(functools.partial(attn_forward_kernel, first, first, scale...  12.5 us
  transfers between devices with their start and end apart: 23, of which 6 were waited for; matrix products, arithmetic and copies ran while one was open for 15% of the time, Pallas kernels for 39%

profile of v10, /device:TPU:0, one launch (start us, length us, event | category | flops | bytes accessed | tf_op | source)
XLA Modules:
  0.0 612.6 jit_solution(7439715088657335924)
XLA Ops:
  2.0 2.1 convert_reduce_fusion
  4.1 2.1 fusion
  11.1 2.6 fusion.15
  14.6 3.0 collective-permute-start.4
  17.6 4.3 collective-permute-start.2
  21.9 1.9 constant_dynamic-slice_fusion.5.refs_7_
  25.0 3.7 collective-permute-start
  30.9 5.1 multiply_reduce_fusion.1
  36.0 1.6 copy.89
  39.8 1.9 constant_dynamic-slice_fusion
  41.7 2.3 constant_dynamic-slice_fusion.1
  46.3 1.5 pad_maximum_fusion.5
  50.4 1.5 collective-permute-start.3
  58.1 3.7 fusion.14
  62.6 4.8 collective-permute-start.9
  67.4 1.5 collective-permute-start.7
  78.6 4.9 attn_forward.3
  83.4 3.8 attn_forward.4
  88.5 8.5 %collective-permute-done.1.kv_b = bf16[2,512,256]{2,1,0:T(8,128)(2,1)} collective-permute-done((bf16[2,512,256]{2,1,0:T(8,128)(2,1)}, bf16[2,512,256]{2,1,0:T(8,128)(2,1)}, u32[]{:S(2)}, u32[]{:S(2)}) %collective-permute-start.1) | collective-permute-done | bytes 524320 | tf_op jit(solution)/shard_map/ppermute | solution.py:1190
  97.0 3.8 attn_forward.5
  100.8 3.1 multiply_convert_fusion.1
  103.9 210.1 %middle.1 = (bf16[128,2048]{1,0:T(8,128)(2,1)}, f32[128,2048]{1,0:T(8,128)}, f32[1,2048]{1,0:T(1,128)}, bf16[2,2,128,2048]{3,2,1,0:T(8,128)(2,1)}, bf16[2,2048,7...) custom-call(bf16[512,512]{1,0:T(8,128)(2,1)} %get-tuple-element.116.refs_0_, bf16[512,2048]{1,0:T(8,128)(2,1)} %refs_1_.1, ...), custom_call_target="tpu_custom_call" | custom-call | flops 30000001024 | bytes 40000000 | tf_op jit(solution)/shard_map/middle/pallas_call | solution.py:680
  314.0 1.9 constant_dynamic-slice_fusion.3
  315.8 4.6 fusion.48
  321.7 2.7 collective-permute-start.10
  324.4 3.0 convert_multiply_fusion.3
  328.7 1.9 reduce_sum.108
  332.4 2.0 collective-permute-start.13
  334.4 14.4 %collective-permute-done.11 = bf16[512,512]{1,0:T(8,128)(2,1)} collective-permute-done((bf16[512,512]{1,0:T(8,128)(2,1)}, bf16[512,512]{1,0:T(8,128)(2,1)}, u32[]{:S(2)}, u32[]{:S(2)}) %collective-permute-start.11) | collective-permute-done | bytes 524320 | tf_op jit(solution)/shard_map/ppermute | solution.py:1190
  348.7 2.3 constant_dynamic-slice_fusion.2
  351.0 2.8 maximum_select_fusion.1
  353.8 3.3 attn_backward.3
  357.2 2.5 maximum_select_fusion
  359.7 2.1 collective-permute-start.16
  361.8 3.8 attn_backward.4
  365.9 4.1 fusion.9.refs_0_
  370.0 2.3 convolution_convert_fusion.2.refs_1_
  372.2 2.7 collective-permute-done.16
  374.9 2.0 add_convert_fusion.1
  376.8 1.5 collective-permute-start.20
  378.3 7.0 %attn_backward.5 = (f32[512,512]{1,0:T(8,128)}, bf16[2,512,256]{2,1,0:T(8,128)(2,1)}, bf16[2,512,256]{2,1,0:T(8,128)(2,1)}) custom-call(s32[7]{0:T(128)} %stack.145.info, s32[1,512]{1,0:T(1,128)} %compare_select_fusion.starts, f32[2,2,512]{2,1,0:T(2,128)} %reshape.258.lse, f32[2,2,512]{2,1,0:T(2,128)} %reshape.261.deltas, bf16[512,512]{1,0:T(8,128)(2,1)} %bitcast.173, ...), custom_call_target="tpu_custom_call" | custom-call | flops 2684354560 | bytes 2097152 | tf_op jit(solution)/shard_map/attn_backward/pallas_call | solution.py:229
  385.3 5.2 collective-permute-start.18
  396.5 1.8 fusion.20
  398.4 1.4 add_convert_fusion
  399.9 1.7 collective-permute-start.21
  401.6 3.3 fusion.49
  404.9 8.4 %collective-permute-done.17 = bf16[512,512]{0,1:T(8,128)(2,1)S(1)} collective-permute-done((bf16[512,512]{0,1:T(8,128)(2,1)S(1)}, bf16[512,512]{0,1:T(8,128)(2,1)S(1)}, u32[]{:S(2)}, u32[]{:S(2)}) %collective-permute-start.17) | collective-permute-done | bytes 524320 | tf_op jit(solution)/shard_map/ppermute | solution.py:1190
  413.3 2.3 convolution_convert_fusion.1.refs_2_
  417.0 2.8 fusion.46
  423.8 1.7 mul.521
  427.4 2.1 fusion.50
  429.6 1.8 pad_maximum_fusion.8
  431.3 1.8 collective-permute-start.22
  433.2 3.1 fusion.4
  436.3 5.8 bitcast_convert_fusion
  443.9 2.3 convolution_convert_fusion.refs_3_
  446.1 142.9 %finish.1 = (bf16[2,512,1024]{2,1,0:T(8,128)(2,1)}, bf16[2,1024,512]{2,1,0:T(8,128)(2,1)}, bf16[2,1024,512]{2,1,0:T(8,128)(2,1)}, bf16[2,1024,512]{2,1,0:T(8,128...) custom-call(bf16[512,1024]{1,0:T(8,128)(2,1)} %fusion.9.refs_0_, ...), custom_call_target="tpu_custom_call" | custom-call | flops 1000000000 | bytes 100000000 | tf_op jit(solution)/shard_map/finish/pallas_call | solution.py:1101
  591.6 1.9 slice_bitcast_fusion.1
  594.1 3.6 convert_element_type.200
  597.7 2.3 slice_convert_fusion
  600.0 2.7 bitcast_convert_fusion.2
  602.8 2.7 bitcast_convert_fusion.3
  605.5 2.7 bitcast_convert_fusion.4
  608.2 2.5 maximum_convert_fusion
  (215 shorter events, 52.0 us)
Async XLA Ops:
  0.6 5.5 copy-start.1
  0.7 5.5 copy-start.45
  8.8 4.8 copy-start.7
  10.7 18.2 %copy-start.27 = (f32[512,64]{0,1:T(8,128)}, f32[512,64]{0,1:T(8,128)S(1)}, u32[]{:S(2)}) copy-start(f32[512,64]{0,1:T(8,128)S(1)} %get-tuple-element.150) | copy-start | bytes 393220
  13.7 16.0 %copy-start.53 = (f32[128]{0:T(128)S(1)}, f32[128]{0:T(128)}, u32[]{:S(2)}) copy-start(f32[128]{0:T(128)} %param.24) | copy-start | bytes 1540
  14.6 47.3 %collective-permute-start.4 = (bf16[2,512,256]{2,1,0:T(8,128)(2,1)}, bf16[2,512,256]{2,1,0:T(8,128)(2,1)}, u32[]{:S(2)}, u32[]{:S(2)}) collective-permute-start(bf16[2,512,256]{2,1,0:T(8,128)(2,1)} %pad_maximum_fusion.6.kv_a), channel_id=1, source_target_pairs={{0,1},{1,0},{2,3},{3,2},{4,5},{5,4},{6,7},{7,6},{8,9},{9,8},{10,11... | collective-permute-start | bytes 1572872 | tf_op jit(solution)/shard_map/ppermute | solution.py:1190
  17.6 32.8 %collective-permute-start.2 = (bf16[2,512,256]{2,1,0:T(8,128)(2,1)}, bf16[2,512,256]{2,1,0:T(8,128)(2,1)}, u32[]{:S(2)}, u32[]{:S(2)}) collective-permute-start(bf16[2,512,256]{2,1,0:T(8,128)(2,1)} %pad_maximum_fusion.6.kv_a), channel_id=1, source_target_pairs={{0,2},{1,3},{2,4},{3,5},{4,6},{5,7},{8,10},{9,11},{10,12},{11,13},... | collective-permute-start | bytes 1572872 | tf_op jit(solution)/shard_map/ppermute | solution.py:1258
  23.7 38.2 %collective-permute-start.6 = (bf16[128,2048]{1,0:T(8,128)(2,1)}, bf16[128,2048]{1,0:T(8,128)(2,1)}, u32[]{:S(2)}, u32[]{:S(2)}) collective-permute-start(bf16[128,2048]{1,0:T(8,128)(2,1)} %constant_dynamic-slice_fusion.5.refs_7_), channel_id=1, source_target_pairs={{0,2},{1,3},{2,4},{3,5},{4,6},{5,7},{6,0},{7,1},{8,10},{9,11},{10,... | collective-permute-start | bytes 1572872 | tf_op jit(solution)/shard_map/ppermute | solution.py:1187
  24.5 38.0 %collective-permute-start.5 = (bf16[128,2048]{1,0:T(8,128)(2,1)}, bf16[128,2048]{1,0:T(8,128)(2,1)}, u32[]{:S(2)}, u32[]{:S(2)}) collective-permute-start(bf16[128,2048]{1,0:T(8,128)(2,1)} %constant_dynamic-slice_fusion.5.refs_7_), channel_id=1, source_target_pairs={{0,1},{1,0},{2,3},{3,2},{4,5},{5,4},{6,7},{7,6},{8,9},{9,8},{10,11... | collective-permute-start | bytes 1572872 | tf_op jit(solution)/shard_map/ppermute | solution.py:1190
  25.0 42.4 %collective-permute-start = (bf16[2,512,256]{2,1,0:T(8,128)(2,1)}, bf16[2,512,256]{2,1,0:T(8,128)(2,1)}, u32[]{:S(2)}, u32[]{:S(2)}) collective-permute-start(bf16[2,512,256]{2,1,0:T(8,128)(2,1)} %pad_maximum_fusion.6.kv_a), channel_id=1, source_target_pairs={{0,4},{1,5},{2,6},{3,7},{8,12},{9,13},{10,14},{11,15},{16,20},{17,... | collective-permute-start | bytes 1572872 | tf_op jit(solution)/shard_map/ppermute | solution.py:1258
  37.6 7.8 %copy-start.4 = (f32[512,4,128]{2,1,0:T(4,128)}, f32[512,4,128]{2,1,0:T(4,128)S(1)}, u32[]{:S(2)}) copy-start(f32[512,4,128]{2,1,0:T(4,128)S(1)} %copy.89) | copy-start | bytes 3145732
  41.7 3.7 copy-start.15
  45.4 3.6 copy-start.50
  46.3 9.7 %copy-start.8 = (f32[512,256]{0,1:T(8,128)S(1)}, f32[512,256]{0,1:T(8,128)}, u32[]{:S(2)}) copy-start(f32[512,256]{0,1:T(8,128)} %copy-done.7) | copy-start | bytes 1572868
  50.4 19.9 %collective-permute-start.3 = (bf16[2,512,256]{2,1,0:T(8,128)(2,1)}, bf16[2,512,256]{2,1,0:T(8,128)(2,1)}, u32[]{:S(2)}, u32[]{:S(2)}) collective-permute-start(bf16[2,512,256]{2,1,0:T(8,128)(2,1)} %collective-permute-done.2.kv_a), channel_id=1, source_target_pairs={{0,1},{1,0},{2,3},{3,2},{4,5},{5,4},{6,7},{7,6},{8,9},{9,8},{10,11... | collective-permute-start | bytes 1572872 | tf_op jit(solution)/shard_map/ppermute | solution.py:1190
  58.1 3.9 copy-start.43
  58.1 10.8 %copy-start.25 = (bf16[512,4,128]{2,1,0:T(4,128)(2,1)S(1)}, bf16[512,4,128]{2,1,0:T(4,128)(2,1)}, u32[]{:S(2)}) copy-start(bf16[512,4,128]{2,1,0:T(4,128)(2,1)} %pad_maximum_fusion.5) | copy-start | bytes 1572868
  61.8 39.0 %copy-start.10 = (f32[512,512]{1,0:T(8,128)}, f32[512,512]{1,0:T(8,128)S(1)}, u32[]{:S(2)}) copy-start(f32[512,512]{1,0:T(8,128)S(1)} %fusion.14) | copy-start | bytes 3145732
  61.9 11.8 %copy-start.47 = (f32[512,2]{0,1:T(2,128)S(1)}, f32[512,2]{0,1:T(2,128)}, u32[]{:S(2)}) copy-start(f32[512,2]{0,1:T(2,128)} %get-tuple-element.147) | copy-start | bytes 12292
  61.9 26.6 %collective-permute-start.8 = (bf16[128,2048]{1,0:T(8,128)(2,1)}, bf16[128,2048]{1,0:T(8,128)(2,1)}, u32[]{:S(2)}, u32[]{:S(2)}) collective-permute-start(bf16[128,2048]{1,0:T(8,128)(2,1)} %constant_dynamic-slice_fusion.5.refs_7_), channel_id=1, source_target_pairs={{0,4},{1,5},{2,6},{3,7},{4,0},{5,1},{6,2},{7,3},{8,12},{9,13},{10,... | collective-permute-start | bytes 1572872 | tf_op jit(solution)/shard_map/ppermute | solution.py:1187
  62.0 25.3 %collective-permute-start.14 = (bf16[512,512]{1,0:T(8,128)(2,1)S(1)}, bf16[512,512]{1,0:T(8,128)(2,1)}, u32[]{:S(2)}, u32[]{:S(2)}) collective-permute-start(bf16[512,512]{1,0:T(8,128)(2,1)S(1)} %copy-done.43), channel_id=1, source_target_pairs={{0,1},{1,0},{2,3},{3,2},{4,5},{5,4},{6,7},{7,6},{8,9},{9,8},{10,11... | collective-permute-start | bytes 1572872 | tf_op jit(solution)/shard_map/ppermute | solution.py:1190
  62.6 25.9 %collective-permute-start.9 = (bf16[128,2048]{1,0:T(8,128)(2,1)}, bf16[128,2048]{1,0:T(8,128)(2,1)}, u32[]{:S(2)}, u32[]{:S(2)}) collective-permute-start(bf16[128,2048]{1,0:T(8,128)(2,1)} %constant_dynamic-slice_fusion.5.refs_7_), channel_id=1, source_target_pairs={{0,6},{1,7},{2,0},{3,1},{4,2},{5,3},{6,4},{7,5},{8,14},{9,15},{10,... | collective-permute-start | bytes 1572872 | tf_op jit(solution)/shard_map/ppermute | solution.py:1187
  67.4 21.1 %collective-permute-start.7 = (bf16[128,2048]{1,0:T(8,128)(2,1)}, bf16[128,2048]{1,0:T(8,128)(2,1)}, u32[]{:S(2)}, u32[]{:S(2)}) collective-permute-start(bf16[128,2048]{1,0:T(8,128)(2,1)} %collective-permute-done.6.refs_9_), channel_id=1, source_target_pairs={{0,1},{1,0},{2,3},{3,2},{4,5},{5,4},{6,7},{7,6},{8,9},{9,8},{10,11... | collective-permute-start | bytes 1572872 | tf_op jit(solution)/shard_map/ppermute | solution.py:1190
  70.4 26.6 %collective-permute-start.1 = (bf16[2,512,256]{2,1,0:T(8,128)(2,1)}, bf16[2,512,256]{2,1,0:T(8,128)(2,1)}, u32[]{:S(2)}, u32[]{:S(2)}) collective-permute-start(bf16[2,512,256]{2,1,0:T(8,128)(2,1)} %collective-permute-done.kv_a), channel_id=1, source_target_pairs={{0,1},{1,0},{2,3},{3,2},{4,5},{5,4},{6,7},{7,6},{8,9},{9,8},{10,11... | collective-permute-start | bytes 1572872 | tf_op jit(solution)/shard_map/ppermute | solution.py:1190
  87.3 263.7 %collective-permute-start.15 = (bf16[512,512]{1,0:T(8,128)(2,1)}, bf16[512,512]{1,0:T(8,128)(2,1)}, u32[]{:S(2)}, u32[]{:S(2)}) collective-permute-start(bf16[512,512]{1,0:T(8,128)(2,1)} %collective-permute-done.14), channel_id=1, source_target_pairs={{0,8},{8,0},{16,24},{24,16},{1,9},{9,1},{17,25},{25,17},{2,10},{10... | collective-permute-start | bytes 1572872 | tf_op jit(solution)/shard_map/ppermute | solution.py:1196
  315.8 4.6 copy-start.13
  320.4 4.0 copy-start.11
  321.7 38.0 %collective-permute-start.10 = (bf16[512,512]{1,0:T(8,128)(2,1)}, bf16[512,512]{1,0:T(8,128)(2,1)}, u32[]{:S(2)}, u32[]{:S(2)}) collective-permute-start(bf16[512,512]{1,0:T(8,128)(2,1)} %get-tuple-element.116.refs_0_), channel_id=1, source_target_pairs={{0,1},{1,0},{2,3},{3,2},{4,5},{5,4},{6,7},{7,6},{8,9},{9,8},{10,11... | collective-permute-start | bytes 1572872 | tf_op jit(solution)/shard_map/ppermute | solution.py:1190
  324.4 24.3 %collective-permute-start.11 = (bf16[512,512]{1,0:T(8,128)(2,1)}, bf16[512,512]{1,0:T(8,128)(2,1)}, u32[]{:S(2)}, u32[]{:S(2)}) collective-permute-start(bf16[512,512]{1,0:T(8,128)(2,1)} %constant_dynamic-slice_fusion.3), channel_id=1, source_target_pairs={{0,1},{1,0},{2,3},{3,2},{4,5},{5,4},{6,7},{7,6},{8,9},{9,8},{10,11... | collective-permute-start | bytes 1572872 | tf_op jit(solution)/shard_map/ppermute | solution.py:1190
  327.4 4.0 copy-start.12
  328.7 3.7 copy-start.22
  332.4 27.3 %collective-permute-start.13 = (bf16[512,512]{1,0:T(8,128)(2,1)S(1)}, bf16[512,512]{1,0:T(8,128)(2,1)S(1)}, u32[]{:S(2)}, u32[]{:S(2)}) collective-permute-start(bf16[512,512]{1,0:T(8,128)(2,1)S(1)} %copy-done.22), channel_id=1, source_target_pairs={{0,1},{1,0},{2,3},{3,2},{4,5},{5,4},{6,7},{7,6},{8,9},{9,8},{10,11... | collective-permute-start | bytes 1572872 | tf_op jit(solution)/shard_map/ppermute | solution.py:1190
  348.7 8.4 %collective-permute-start.12 = (bf16[512,512]{1,0:T(8,128)(2,1)}, bf16[512,512]{1,0:T(8,128)(2,1)S(1)}, u32[]{:S(2)}, u32[]{:S(2)}) collective-permute-start(bf16[512,512]{1,0:T(8,128)(2,1)} %collective-permute-done.11), channel_id=1, source_target_pairs={{0,8},{8,0},{16,24},{24,16},{1,9},{9,1},{17,25},{25,17},{2,10},{10... | collective-permute-start | bytes 1572872 | tf_op jit(solution)/shard_map/ppermute | solution.py:1196
  359.7 5.9 copy-start.56
  359.7 6.2 %copy-start.40 = (bf16[512,512]{1,0:T(8,128)(2,1)S(1)}, bf16[512,512]{1,0:T(8,128)(2,1)}, u32[]{:S(2)}) copy-start(bf16[512,512]{1,0:T(8,128)(2,1)} %get-tuple-element.116.refs_0_) | copy-start | bytes 1572868
  359.7 15.2 %collective-permute-start.16 = (bf16[2,512,256]{2,1,0:T(8,128)(2,1)}, bf16[2,512,256]{2,1,0:T(8,128)(2,1)}, u32[]{:S(2)}, u32[]{:S(2)}) collective-permute-start(bf16[2,512,256]{2,1,0:T(8,128)(2,1)} %get-tuple-element.86), channel_id=1, source_target_pairs={{0,1},{1,0},{2,3},{3,2},{4,5},{5,4},{6,7},{7,6},{8,9},{9,8},{10,11... | collective-permute-start | bytes 1572872 | tf_op jit(solution)/shard_map/ppermute | solution.py:1190
  365.6 4.3 copy-start.30
  365.6 4.3 copy-start.33
  365.6 4.3 copy-start.57
  365.7 32.8 %collective-permute-start.19 = (bf16[2,512,256]{2,1,0:T(8,128)(2,1)}, bf16[2,512,256]{2,1,0:T(8,128)(2,1)}, u32[]{:S(2)}, u32[]{:S(2)}) collective-permute-start(bf16[2,512,256]{2,1,0:T(8,128)(2,1)} %get-tuple-element.92), channel_id=1, source_target_pairs={{0,1},{1,0},{2,3},{3,2},{4,5},{5,4},{6,7},{7,6},{8,9},{9,8},{10,11... | collective-permute-start | bytes 1572872 | tf_op jit(solution)/shard_map/ppermute | solution.py:1190
  370.0 4.9 copy-start.42
  376.8 21.6 %collective-permute-start.20 = (bf16[2,512,256]{2,1,0:T(8,128)(2,1)}, bf16[2,512,256]{2,1,0:T(8,128)(2,1)}, u32[]{:S(2)}, u32[]{:S(2)}) collective-permute-start(bf16[2,512,256]{2,1,0:T(8,128)(2,1)} %add_convert_fusion.1), channel_id=1, source_target_pairs={{4,2},{5,3},{6,4},{7,5},{12,10},{13,11},{14,12},{15,13},{20,18},{2... | collective-permute-start | bytes 1572872 | tf_op jit(solution)/shard_map/ppermute | solution.py:1438
  385.3 30.3 %collective-permute-start.18 = (bf16[2,512,256]{2,1,0:T(8,128)(2,1)}, bf16[2,512,256]{2,1,0:T(8,128)(2,1)}, u32[]{:S(2)}, u32[]{:S(2)}) collective-permute-start(bf16[2,512,256]{2,1,0:T(8,128)(2,1)} %get-tuple-element.90), channel_id=1, source_target_pairs={{0,1},{1,0},{2,3},{3,2},{4,5},{5,4},{6,7},{7,6},{8,9},{9,8},{10,11... | collective-permute-start | bytes 1572872 | tf_op jit(solution)/shard_map/ppermute | solution.py:1190
  396.4 5.1 copy-start.29
  398.3 15.0 %collective-permute-start.17 = (bf16[512,512]{0,1:T(8,128)(2,1)S(1)}, bf16[512,512]{0,1:T(8,128)(2,1)S(1)}, u32[]{:S(2)}, u32[]{:S(2)}) collective-permute-start(bf16[512,512]{0,1:T(8,128)(2,1)S(1)} %get-tuple-element.124), channel_id=1, source_target_pairs={{0,1},{1,0},{2,3},{3,2},{4,5},{5,4},{6,7},{7,6},{8,9},{9,8},{10,11... | collective-permute-start | bytes 1572872 | tf_op jit(solution)/shard_map/ppermute | solution.py:1190
  399.8 13.5 %copy-start.31 = (bf16[512,1024]{1,0:T(8,128)(2,1)S(1)}, bf16[512,1024]{1,0:T(8,128)(2,1)}, u32[]{:S(2)}) copy-start(bf16[512,1024]{1,0:T(8,128)(2,1)} %constant_dynamic-slice_fusion.1) | copy-start | bytes 3145732
  399.8 13.5 %copy-start.34 = (bf16[512,1024]{1,0:T(8,128)(2,1)S(1)}, bf16[512,1024]{1,0:T(8,128)(2,1)}, u32[]{:S(2)}) copy-start(bf16[512,1024]{1,0:T(8,128)(2,1)} %maximum_select_fusion.1) | copy-start | bytes 3145732
  399.9 15.7 %collective-permute-start.21 = (bf16[2,512,256]{2,1,0:T(8,128)(2,1)S(1)}, bf16[2,512,256]{2,1,0:T(8,128)(2,1)S(1)}, u32[]{:S(2)}, u32[]{:S(2)}) collective-permute-start(bf16[2,512,256]{2,1,0:T(8,128)(2,1)S(1)} %add_convert_fusion), channel_id=1, source_target_pairs={{2,0},{3,1},{4,2},{5,3},{6,4},{7,5},{10,8},{11,9},{12,10},{13,11},... | collective-permute-start | bytes 1572872 | tf_op jit(solution)/shard_map/ppermute | solution.py:1438
  404.9 10.7 %copy-start.41 = (bf16[2,512,256]{2,1,0:T(8,128)(2,1)S(1)}, bf16[2,512,256]{2,1,0:T(8,128)(2,1)}, u32[]{:S(2)}) copy-start(bf16[2,512,256]{2,1,0:T(8,128)(2,1)} %get-tuple-element.89) | copy-start | bytes 1572868
  417.0 3.7 copy-start.28
  420.8 4.7 copy-start.36
  420.8 5.3 copy-start.55
  420.8 12.3 %copy-start.17 = (bf16[2048,512]{1,0:T(8,128)(2,1)S(1)}, bf16[2048,512]{1,0:T(8,128)(2,1)}, u32[]{:S(2)}) copy-start(bf16[2048,512]{1,0:T(8,128)(2,1)} %param.21) | copy-start | bytes 6291460
  421.7 4.4 copy-start.24
  423.8 9.4 %copy-start.3 = (f32[512,2048]{1,0:T(8,128)S(1)}, f32[512,2048]{1,0:T(8,128)}, u32[]{:S(2)}) copy-start(f32[512,2048]{1,0:T(8,128)} %fusion.46) | copy-start | bytes 12582916
  426.1 7.0 %copy-start.23 = (bf16[512,512]{1,0:T(8,128)(2,1)S(1)}, bf16[512,512]{1,0:T(8,128)(2,1)}, u32[]{:S(2)}) copy-start(bf16[512,512]{1,0:T(8,128)(2,1)} %get-tuple-element.122) | copy-start | bytes 1572868
  427.4 5.7 copy-start
  427.4 5.7 copy-start.2
  427.4 8.9 %slice-start = ((s8[6291456]{0:T(1024)(128)(4,1)}), s8[4194304]{0:T(1024)(128)(4,1)S(1)}, s32[]{:S(2)}) async-start(s8[6291456]{0:T(1024)(128)(4,1)} %bitcast.151), calls=%async_computation | async-start | bytes 8388608
  431.3 5.0 slice-start.1
  431.3 12.5 %collective-permute-start.22 = (bf16[512,512]{1,0:T(8,128)(2,1)S(1)}, bf16[512,512]{1,0:T(8,128)(2,1)S(1)}, u32[]{:S(2)}, u32[]{:S(2)}) collective-permute-start(bf16[512,512]{1,0:T(8,128)(2,1)S(1)} %pad_maximum_fusion.8), channel_id=1, source_target_pairs={{0,1},{1,0},{2,3},{3,2},{4,5},{5,4},{6,7},{7,6},{8,9},{9,8},{10,11... | collective-permute-start | bytes 1572872 | tf_op jit(solution)/shard_map/ppermute | solution.py:1190
  436.3 5.8 copy-start.48
  436.3 7.5 %copy-start.32 = (bf16[512,1024]{1,0:T(8,128)(2,1)S(1)}, bf16[512,1024]{1,0:T(8,128)(2,1)}, u32[]{:S(2)}) copy-start(bf16[512,1024]{1,0:T(8,128)(2,1)} %constant_dynamic-slice_fusion.1) | copy-start | bytes 3145732
  436.3 7.5 %copy-start.35 = (bf16[512,1024]{1,0:T(8,128)(2,1)S(1)}, bf16[512,1024]{1,0:T(8,128)(2,1)}, u32[]{:S(2)}) copy-start(bf16[512,1024]{1,0:T(8,128)(2,1)} %maximum_select_fusion.1) | copy-start | bytes 3145732
  (19 other events, 37.8 us)

commit v11 on v10

--- a/solution.py
+++ b/solution.py
@@ -1427,8 +1427,8 @@
             kv_blocks[k][0], kv_blocks[k][1], query_acc, k == 0, scale,
         )
         if k == reach:
-            query_acc, grad_a, grad_b, gated_other, branch_other, gate_other = lax.optimization_barrier(
-                (query_acc, grad_a, grad_b, gated_other, branch_other, gate_other)
+            query_acc, grad_a, grad_b, gated_other, gate_other = lax.optimization_barrier(
+                (query_acc, grad_a, grad_b, gated_other, gate_other)
             )
         paired[k] = pair(grad_b)
         total = grad_a.astype(F32) + paired[k].astype(F32)

time: 623 us -> 610 us (0.979)
    ppermute x14, waiting for transfers between devices: 35.1 us -> 26.3 us  [pair(): return lax.ppermute(value, 'sp', pair_pairs)]
    pallas_call x1, Pallas kernels: 143 us -> 135 us  [finish(): pl.pallas_call(functools.partial(finish_kernel, outer, sides, sp_n, tp_n,...]
  transfers between devices with their start and end apart: 23 -> 23, of which waited for: 6 -> 7; matrix products, arithmetic and copies ran while one was open for 15% -> 15% of each run, Pallas kernels for 39% -> 40%
where the time goes in v11:
time: 610 us; the launch traced here: 600 us
  Pallas kernels  376 us (62%)
  other arithmetic  61.9 us (10%)
  local copies, waits for them, and re-layouts  44.6 us (7%)
  matrix products  40.8 us (7%)
  starting transfers between devices  36.3 us (6%)
  waiting for transfers between devices  31.5 us (5%)
  between operations  9.37 us (2%)
    pallas_call x1, Pallas kernels, middle_layer(): pl.pallas_call(functools.partial(middle_kernel, outer), out_shape=[jax.Sh...  214 us
    pallas_call x1, Pallas kernels, finish(): pl.pallas_call(functools.partial(finish_kernel, outer, sides, sp_n, tp_n,...  135 us
    ppermute x14, waiting for transfers between devices, pair(): return lax.ppermute(value, 'sp', pair_pairs)  26.3 us
    ppermute x14, starting transfers between devices, pair(): return lax.ppermute(value, 'sp', pair_pairs)  19.5 us
    dot_general x5, matrix products, times_transpose(): lax.dot_general(left, right, (((1,), (1,)), ((), ())), preferred_element_...  17 us
    pallas_call x3, Pallas kernels, attn_backward(): pl.pallas_call(functools.partial(attn_backward_kernel, first, diagonal, s...  14.6 us
    pallas_call x3, Pallas kernels, attn_forward(): pl.pallas_call(functools.partial(attn_forward_kernel, first, first, scale...  12.5 us
  transfers between devices with their start and end apart: 23, of which 7 were waited for; matrix products, arithmetic and copies ran while one was open for 15% of the time, Pallas kernels for 40%

profile of v11, /device:TPU:0, one launch (start us, length us, event | category | flops | bytes accessed | tf_op | source)
XLA Modules:
  0.0 600.1 jit_solution(13578711212484830171)
XLA Ops:
  2.0 2.0 convert_reduce_fusion
  4.1 2.1 fusion
  11.1 2.6 fusion.15
  14.5 3.0 collective-permute-start.4
  17.5 4.3 collective-permute-start.2
  21.8 1.9 constant_dynamic-slice_fusion.5.refs_7_
  25.0 3.7 collective-permute-start
  30.9 5.1 multiply_reduce_fusion.1
  36.0 1.6 copy.89
  39.8 1.9 constant_dynamic-slice_fusion
  41.7 2.3 constant_dynamic-slice_fusion.1
  46.2 1.5 pad_maximum_fusion.5
  50.4 1.5 collective-permute-start.3
  58.2 3.7 fusion.14
  62.6 4.9 collective-permute-start.9
  67.4 1.5 collective-permute-start.7
  78.8 4.9 attn_forward.3
  83.6 3.8 attn_forward.4
  88.5 8.5 %collective-permute-done.1.kv_b = bf16[2,512,256]{2,1,0:T(8,128)(2,1)} collective-permute-done((bf16[2,512,256]{2,1,0:T(8,128)(2,1)}, bf16[2,512,256]{2,1,0:T(8,128)(2,1)}, u32[]{:S(2)}, u32[]{:S(2)}) %collective-permute-start.1) | collective-permute-done | bytes 524320 | tf_op jit(solution)/shard_map/ppermute | solution.py:1190
  97.0 3.8 attn_forward.5
  100.8 2.6 reshape.257
  103.5 2.7 multiply_convert_fusion.1
  106.2 1.5 collective-permute-start.10
  107.7 213.5 %middle.1 = (bf16[128,2048]{1,0:T(8,128)(2,1)}, f32[128,2048]{1,0:T(8,128)}, f32[1,2048]{1,0:T(1,128)}, bf16[2,2,128,2048]{3,2,1,0:T(8,128)(2,1)}, bf16[2,2048,7...) custom-call(bf16[512,512]{1,0:T(8,128)(2,1)} %get-tuple-element.114.refs_0_, bf16[512,2048]{1,0:T(8,128)(2,1)} %refs_1_.1, ...), custom_call_target="tpu_custom_call" | custom-call | flops 30000001024 | bytes 40000000 | tf_op jit(solution)/shard_map/middle/pallas_call | solution.py:680
  321.3 4.6 fusion.48
  326.3 3.0 convert_multiply_fusion.3
  332.7 1.9 constant_dynamic-slice_fusion.2
  335.5 3.5 attn_backward.3
  340.0 4.3 collective-permute-done.11
  345.5 1.9 maximum_select_fusion.1
  347.4 4.2 attn_backward.4
  352.6 3.0 collective-permute-done.12
  355.6 3.5 convolution_convert_fusion.2.refs_1_
  359.1 7.8 %collective-permute-done.16 = bf16[2,512,256]{2,1,0:T(8,128)(2,1)} collective-permute-done((bf16[2,512,256]{2,1,0:T(8,128)(2,1)}, bf16[2,512,256]{2,1,0:T(8,128)(2,1)}, u32[]{:S(2)}, u32[]{:S(2)}) %collective-permute-start.16) | collective-permute-done | bytes 524320 | tf_op jit(solution)/shard_map/ppermute | solution.py:1190
  366.8 2.0 add_convert_fusion.1
  368.8 1.5 collective-permute-start.20
  370.3 7.0 %attn_backward.5 = (f32[512,512]{1,0:T(8,128)}, bf16[2,512,256]{2,1,0:T(8,128)(2,1)}, bf16[2,512,256]{2,1,0:T(8,128)(2,1)}) custom-call(s32[7]{0:T(128)} %stack.145.info, s32[1,512]{1,0:T(1,128)} %compare_select_fusion.starts, f32[2,2,512]{2,1,0:T(2,128)} %reshape.258.lse, f32[2,2,512]{2,1,0:T(2,128)} %reshape.261.deltas, bf16[512,512]{1,0:T(8,128)(2,1)} %bitcast.173, ...), custom_call_target="tpu_custom_call" | custom-call | flops 2684354560 | bytes 2097152 | tf_op jit(solution)/shard_map/attn_backward/pallas_call | solution.py:229
  377.2 4.4 collective-permute-start.18
  387.4 1.8 fusion.20
  389.4 1.9 maximum_select_fusion
  391.3 3.3 fusion.49
  394.6 1.5 add_convert_fusion
  396.1 1.5 collective-permute-start.21
  397.7 3.6 fusion.9.refs_0_
  401.3 2.7 collective-permute-done.17
  404.0 2.3 convolution_convert_fusion.1.refs_2_
  406.3 4.2 collective-permute-done.21
  411.8 2.8 fusion.46
  417.4 2.0 copy.115
  419.4 1.7 mul.521
  423.0 2.1 fusion.50
  425.1 1.8 pad_maximum_fusion.8
  426.9 1.8 collective-permute-start.22
  428.7 4.2 fusion.4
  432.9 5.8 bitcast_convert_fusion
  439.4 2.3 convolution_convert_fusion.refs_3_
  441.6 135.0 %finish.1 = (bf16[2,512,1024]{2,1,0:T(8,128)(2,1)}, bf16[2,1024,512]{2,1,0:T(8,128)(2,1)}, bf16[2,1024,512]{2,1,0:T(8,128)(2,1)}, bf16[2,1024,512]{2,1,0:T(8,128...) custom-call(bf16[512,1024]{1,0:T(8,128)(2,1)} %fusion.9.refs_0_, ...), custom_call_target="tpu_custom_call" | custom-call | flops 1000000000 | bytes 100000000 | tf_op jit(solution)/shard_map/finish/pallas_call | solution.py:1101
  579.2 1.9 slice_bitcast_fusion.1
  581.7 3.6 convert_element_type.200
  585.3 2.3 slice_convert_fusion
  587.6 2.7 bitcast_convert_fusion.2
  590.4 2.7 bitcast_convert_fusion.3
  593.1 2.7 bitcast_convert_fusion.4
  595.8 2.5 maximum_convert_fusion
  (211 shorter events, 52.7 us)
Async XLA Ops:
  0.6 5.5 copy-start.1
  0.7 5.5 copy-start.45
  8.8 4.9 copy-start.7
  10.7 18.2 %copy-start.26 = (f32[512,64]{0,1:T(8,128)}, f32[512,64]{0,1:T(8,128)S(1)}, u32[]{:S(2)}) copy-start(f32[512,64]{0,1:T(8,128)S(1)} %get-tuple-element.148) | copy-start | bytes 393220
  13.7 16.1 %copy-start.53 = (f32[128]{0:T(128)S(1)}, f32[128]{0:T(128)}, u32[]{:S(2)}) copy-start(f32[128]{0:T(128)} %param.24) | copy-start | bytes 1540
  14.5 47.4 %collective-permute-start.4 = (bf16[2,512,256]{2,1,0:T(8,128)(2,1)}, bf16[2,512,256]{2,1,0:T(8,128)(2,1)}, u32[]{:S(2)}, u32[]{:S(2)}) collective-permute-start(bf16[2,512,256]{2,1,0:T(8,128)(2,1)} %pad_maximum_fusion.6.kv_a), channel_id=1, source_target_pairs={{0,1},{1,0},{2,3},{3,2},{4,5},{5,4},{6,7},{7,6},{8,9},{9,8},{10,11... | collective-permute-start | bytes 1572872 | tf_op jit(solution)/shard_map/ppermute | solution.py:1190
  17.5 32.9 %collective-permute-start.2 = (bf16[2,512,256]{2,1,0:T(8,128)(2,1)}, bf16[2,512,256]{2,1,0:T(8,128)(2,1)}, u32[]{:S(2)}, u32[]{:S(2)}) collective-permute-start(bf16[2,512,256]{2,1,0:T(8,128)(2,1)} %pad_maximum_fusion.6.kv_a), channel_id=1, source_target_pairs={{0,2},{1,3},{2,4},{3,5},{4,6},{5,7},{8,10},{9,11},{10,12},{11,13},... | collective-permute-start | bytes 1572872 | tf_op jit(solution)/shard_map/ppermute | solution.py:1258
  23.7 38.3 %collective-permute-start.6 = (bf16[128,2048]{1,0:T(8,128)(2,1)}, bf16[128,2048]{1,0:T(8,128)(2,1)}, u32[]{:S(2)}, u32[]{:S(2)}) collective-permute-start(bf16[128,2048]{1,0:T(8,128)(2,1)} %constant_dynamic-slice_fusion.5.refs_7_), channel_id=1, source_target_pairs={{0,2},{1,3},{2,4},{3,5},{4,6},{5,7},{6,0},{7,1},{8,10},{9,11},{10,... | collective-permute-start | bytes 1572872 | tf_op jit(solution)/shard_map/ppermute | solution.py:1187
  24.5 38.0 %collective-permute-start.5 = (bf16[128,2048]{1,0:T(8,128)(2,1)}, bf16[128,2048]{1,0:T(8,128)(2,1)}, u32[]{:S(2)}, u32[]{:S(2)}) collective-permute-start(bf16[128,2048]{1,0:T(8,128)(2,1)} %constant_dynamic-slice_fusion.5.refs_7_), channel_id=1, source_target_pairs={{0,1},{1,0},{2,3},{3,2},{4,5},{5,4},{6,7},{7,6},{8,9},{9,8},{10,11... | collective-permute-start | bytes 1572872 | tf_op jit(solution)/shard_map/ppermute | solution.py:1190
  25.0 42.4 %collective-permute-start = (bf16[2,512,256]{2,1,0:T(8,128)(2,1)}, bf16[2,512,256]{2,1,0:T(8,128)(2,1)}, u32[]{:S(2)}, u32[]{:S(2)}) collective-permute-start(bf16[2,512,256]{2,1,0:T(8,128)(2,1)} %pad_maximum_fusion.6.kv_a), channel_id=1, source_target_pairs={{0,4},{1,5},{2,6},{3,7},{8,12},{9,13},{10,14},{11,15},{16,20},{17,... | collective-permute-start | bytes 1572872 | tf_op jit(solution)/shard_map/ppermute | solution.py:1258
  37.6 7.8 %copy-start.4 = (f32[512,4,128]{2,1,0:T(4,128)}, f32[512,4,128]{2,1,0:T(4,128)S(1)}, u32[]{:S(2)}) copy-start(f32[512,4,128]{2,1,0:T(4,128)S(1)} %copy.89) | copy-start | bytes 3145732
  41.7 3.7 copy-start.15
  45.4 3.6 copy-start.50
  46.2 9.7 %copy-start.8 = (f32[512,256]{0,1:T(8,128)S(1)}, f32[512,256]{0,1:T(8,128)}, u32[]{:S(2)}) copy-start(f32[512,256]{0,1:T(8,128)} %copy-done.7) | copy-start | bytes 1572868
  50.4 20.0 %collective-permute-start.3 = (bf16[2,512,256]{2,1,0:T(8,128)(2,1)}, bf16[2,512,256]{2,1,0:T(8,128)(2,1)}, u32[]{:S(2)}, u32[]{:S(2)}) collective-permute-start(bf16[2,512,256]{2,1,0:T(8,128)(2,1)} %collective-permute-done.2.kv_a), channel_id=1, source_target_pairs={{0,1},{1,0},{2,3},{3,2},{4,5},{5,4},{6,7},{7,6},{8,9},{9,8},{10,11... | collective-permute-start | bytes 1572872 | tf_op jit(solution)/shard_map/ppermute | solution.py:1190
  58.1 3.9 copy-start.43
  58.2 10.8 %copy-start.24 = (bf16[512,4,128]{2,1,0:T(4,128)(2,1)S(1)}, bf16[512,4,128]{2,1,0:T(4,128)(2,1)}, u32[]{:S(2)}) copy-start(bf16[512,4,128]{2,1,0:T(4,128)(2,1)} %pad_maximum_fusion.5) | copy-start | bytes 1572868
  61.9 41.6 %copy-start.10 = (f32[512,512]{1,0:T(8,128)}, f32[512,512]{1,0:T(8,128)S(1)}, u32[]{:S(2)}) copy-start(f32[512,512]{1,0:T(8,128)S(1)} %fusion.14) | copy-start | bytes 3145732
  61.9 11.9 %copy-start.47 = (f32[512,2]{0,1:T(2,128)S(1)}, f32[512,2]{0,1:T(2,128)}, u32[]{:S(2)}) copy-start(f32[512,2]{0,1:T(2,128)} %get-tuple-element.145) | copy-start | bytes 12292
  61.9 26.6 %collective-permute-start.8 = (bf16[128,2048]{1,0:T(8,128)(2,1)}, bf16[128,2048]{1,0:T(8,128)(2,1)}, u32[]{:S(2)}, u32[]{:S(2)}) collective-permute-start(bf16[128,2048]{1,0:T(8,128)(2,1)} %constant_dynamic-slice_fusion.5.refs_7_), channel_id=1, source_target_pairs={{0,4},{1,5},{2,6},{3,7},{4,0},{5,1},{6,2},{7,3},{8,12},{9,13},{10,... | collective-permute-start | bytes 1572872 | tf_op jit(solution)/shard_map/ppermute | solution.py:1187
  62.0 25.4 %collective-permute-start.14 = (bf16[512,512]{1,0:T(8,128)(2,1)S(1)}, bf16[512,512]{1,0:T(8,128)(2,1)}, u32[]{:S(2)}, u32[]{:S(2)}) collective-permute-start(bf16[512,512]{1,0:T(8,128)(2,1)S(1)} %copy-done.43), channel_id=1, source_target_pairs={{0,1},{1,0},{2,3},{3,2},{4,5},{5,4},{6,7},{7,6},{8,9},{9,8},{10,11... | collective-permute-start | bytes 1572872 | tf_op jit(solution)/shard_map/ppermute | solution.py:1190
  62.6 25.9 %collective-permute-start.9 = (bf16[128,2048]{1,0:T(8,128)(2,1)}, bf16[128,2048]{1,0:T(8,128)(2,1)}, u32[]{:S(2)}, u32[]{:S(2)}) collective-permute-start(bf16[128,2048]{1,0:T(8,128)(2,1)} %constant_dynamic-slice_fusion.5.refs_7_), channel_id=1, source_target_pairs={{0,6},{1,7},{2,0},{3,1},{4,2},{5,3},{6,4},{7,5},{8,14},{9,15},{10,... | collective-permute-start | bytes 1572872 | tf_op jit(solution)/shard_map/ppermute | solution.py:1187
  67.4 21.1 %collective-permute-start.7 = (bf16[128,2048]{1,0:T(8,128)(2,1)}, bf16[128,2048]{1,0:T(8,128)(2,1)}, u32[]{:S(2)}, u32[]{:S(2)}) collective-permute-start(bf16[128,2048]{1,0:T(8,128)(2,1)} %collective-permute-done.6.refs_9_), channel_id=1, source_target_pairs={{0,1},{1,0},{2,3},{3,2},{4,5},{5,4},{6,7},{7,6},{8,9},{9,8},{10,11... | collective-permute-start | bytes 1572872 | tf_op jit(solution)/shard_map/ppermute | solution.py:1190
  70.4 26.6 %collective-permute-start.1 = (bf16[2,512,256]{2,1,0:T(8,128)(2,1)}, bf16[2,512,256]{2,1,0:T(8,128)(2,1)}, u32[]{:S(2)}, u32[]{:S(2)}) collective-permute-start(bf16[2,512,256]{2,1,0:T(8,128)(2,1)} %collective-permute-done.kv_a), channel_id=1, source_target_pairs={{0,1},{1,0},{2,3},{3,2},{4,5},{5,4},{6,7},{7,6},{8,9},{9,8},{10,11... | collective-permute-start | bytes 1572872 | tf_op jit(solution)/shard_map/ppermute | solution.py:1190
  87.4 258.0 %collective-permute-start.15 = (bf16[512,512]{1,0:T(8,128)(2,1)}, bf16[512,512]{1,0:T(8,128)(2,1)}, u32[]{:S(2)}, u32[]{:S(2)}) collective-permute-start(bf16[512,512]{1,0:T(8,128)(2,1)} %collective-permute-done.14), channel_id=1, source_target_pairs={{0,8},{8,0},{16,24},{24,16},{1,9},{9,1},{17,25},{25,17},{2,10},{10... | collective-permute-start | bytes 1572872 | tf_op jit(solution)/shard_map/ppermute | solution.py:1196
  106.2 238.2 %collective-permute-start.10 = (bf16[512,512]{1,0:T(8,128)(2,1)}, bf16[512,512]{1,0:T(8,128)(2,1)}, u32[]{:S(2)}, u32[]{:S(2)}) collective-permute-start(bf16[512,512]{1,0:T(8,128)(2,1)} %get-tuple-element.114.refs_0_), channel_id=1, source_target_pairs={{0,1},{1,0},{2,3},{3,2},{4,5},{5,4},{6,7},{7,6},{8,9},{9,8},{10,11... | collective-permute-start | bytes 1572872 | tf_op jit(solution)/shard_map/ppermute | solution.py:1190
  321.3 4.6 copy-start.12
  321.3 5.0 copy-start.11
  329.2 15.1 %collective-permute-start.11 = (bf16[512,512]{1,0:T(8,128)(2,1)}, bf16[512,512]{1,0:T(8,128)(2,1)}, u32[]{:S(2)}, u32[]{:S(2)}) collective-permute-start(bf16[512,512]{1,0:T(8,128)(2,1)} %get-tuple-element.120), channel_id=1, source_target_pairs={{0,1},{1,0},{2,3},{3,2},{4,5},{5,4},{6,7},{7,6},{8,9},{9,8},{10,11... | collective-permute-start | bytes 1572872 | tf_op jit(solution)/shard_map/ppermute | solution.py:1190
  334.6 21.0 %collective-permute-start.12 = (bf16[512,512]{1,0:T(8,128)(2,1)}, bf16[512,512]{1,0:T(8,128)(2,1)}, u32[]{:S(2)}, u32[]{:S(2)}) collective-permute-start(bf16[512,512]{1,0:T(8,128)(2,1)} %constant_dynamic-slice_fusion.2), channel_id=1, source_target_pairs={{0,1},{1,0},{2,3},{3,2},{4,5},{5,4},{6,7},{7,6},{8,9},{9,8},{10,11... | collective-permute-start | bytes 1572872 | tf_op jit(solution)/shard_map/ppermute | solution.py:1190
  335.5 3.5 copy-start.29
  344.4 22.5 %collective-permute-start.16 = (bf16[2,512,256]{2,1,0:T(8,128)(2,1)}, bf16[2,512,256]{2,1,0:T(8,128)(2,1)}, u32[]{:S(2)}, u32[]{:S(2)}) collective-permute-start(bf16[2,512,256]{2,1,0:T(8,128)(2,1)} %get-tuple-element.84), channel_id=1, source_target_pairs={{0,1},{1,0},{2,3},{3,2},{4,5},{5,4},{6,7},{7,6},{8,9},{9,8},{10,11... | collective-permute-start | bytes 1572872 | tf_op jit(solution)/shard_map/ppermute | solution.py:1190
  347.4 8.2 %copy-start.33 = (bf16[512,1024]{1,0:T(8,128)(2,1)}, bf16[512,1024]{1,0:T(8,128)(2,1)S(1)}, u32[]{:S(2)}) copy-start(bf16[512,1024]{1,0:T(8,128)(2,1)S(1)} %maximum_select_fusion.1) | copy-start | bytes 3145732
  347.4 8.2 %copy-start.30 = (bf16[512,1024]{1,0:T(8,128)(2,1)S(1)}, bf16[512,1024]{1,0:T(8,128)(2,1)}, u32[]{:S(2)}) copy-start(bf16[512,1024]{1,0:T(8,128)(2,1)} %constant_dynamic-slice_fusion.1) | copy-start | bytes 3145732
  351.6 15.2 %copy-start.42 = (bf16[2,512,256]{2,1,0:T(8,128)(2,1)S(1)}, bf16[2,512,256]{2,1,0:T(8,128)(2,1)}, u32[]{:S(2)}) copy-start(bf16[2,512,256]{2,1,0:T(8,128)(2,1)} %get-tuple-element.91) | copy-start | bytes 1572868
  351.6 43.0 %collective-permute-start.19 = (bf16[2,512,256]{2,1,0:T(8,128)(2,1)}, bf16[2,512,256]{2,1,0:T(8,128)(2,1)}, u32[]{:S(2)}, u32[]{:S(2)}) collective-permute-start(bf16[2,512,256]{2,1,0:T(8,128)(2,1)} %get-tuple-element.90), channel_id=1, source_target_pairs={{0,1},{1,0},{2,3},{3,2},{4,5},{5,4},{6,7},{7,6},{8,9},{9,8},{10,11... | collective-permute-start | bytes 1572872 | tf_op jit(solution)/shard_map/ppermute | solution.py:1190
  355.6 33.8 %collective-permute-start.13 = (bf16[512,512]{1,0:T(8,128)(2,1)}, bf16[512,512]{1,0:T(8,128)(2,1)}, u32[]{:S(2)}, u32[]{:S(2)}) collective-permute-start(bf16[512,512]{1,0:T(8,128)(2,1)} %collective-permute-done.12), channel_id=1, source_target_pairs={{0,8},{8,0},{16,24},{24,16},{1,9},{9,1},{17,25},{25,17},{2,10},{10... | collective-permute-start | bytes 1572872 | tf_op jit(solution)/shard_map/ppermute | solution.py:1196
  368.8 25.8 %collective-permute-start.20 = (bf16[2,512,256]{2,1,0:T(8,128)(2,1)}, bf16[2,512,256]{2,1,0:T(8,128)(2,1)}, u32[]{:S(2)}, u32[]{:S(2)}) collective-permute-start(bf16[2,512,256]{2,1,0:T(8,128)(2,1)} %add_convert_fusion.1), channel_id=1, source_target_pairs={{4,2},{5,3},{6,4},{7,5},{12,10},{13,11},{14,12},{15,13},{20,18},{2... | collective-permute-start | bytes 1572872 | tf_op jit(solution)/shard_map/ppermute | solution.py:1438
  377.2 29.1 %collective-permute-start.18 = (bf16[2,512,256]{2,1,0:T(8,128)(2,1)}, bf16[2,512,256]{2,1,0:T(8,128)(2,1)}, u32[]{:S(2)}, u32[]{:S(2)}) collective-permute-start(bf16[2,512,256]{2,1,0:T(8,128)(2,1)} %get-tuple-element.88), channel_id=1, source_target_pairs={{0,1},{1,0},{2,3},{3,2},{4,5},{5,4},{6,7},{7,6},{8,9},{9,8},{10,11... | collective-permute-start | bytes 1572872 | tf_op jit(solution)/shard_map/ppermute | solution.py:1190
  387.4 3.8 copy-start.28
  389.3 14.7 %collective-permute-start.17 = (bf16[512,512]{0,1:T(8,128)(2,1)S(1)}, bf16[512,512]{0,1:T(8,128)(2,1)S(1)}, u32[]{:S(2)}, u32[]{:S(2)}) collective-permute-start(bf16[512,512]{0,1:T(8,128)(2,1)S(1)} %get-tuple-element.122), channel_id=1, source_target_pairs={{0,1},{1,0},{2,3},{3,2},{4,5},{5,4},{6,7},{7,6},{8,9},{9,8},{10,11... | collective-permute-start | bytes 1572872 | tf_op jit(solution)/shard_map/ppermute | solution.py:1190
  391.3 3.3 copy-start.44
  394.6 3.1 copy-start.36
  396.1 14.4 %collective-permute-start.21 = (bf16[2,512,256]{2,1,0:T(8,128)(2,1)S(1)}, bf16[2,512,256]{2,1,0:T(8,128)(2,1)S(1)}, u32[]{:S(2)}, u32[]{:S(2)}) collective-permute-start(bf16[2,512,256]{2,1,0:T(8,128)(2,1)S(1)} %add_convert_fusion), channel_id=1, source_target_pairs={{2,0},{3,1},{4,2},{5,3},{6,4},{7,5},{10,8},{11,9},{12,10},{13,11},... | collective-permute-start | bytes 1572872 | tf_op jit(solution)/shard_map/ppermute | solution.py:1438
  397.7 6.4 %copy-start.31 = (bf16[512,1024]{1,0:T(8,128)(2,1)S(1)}, bf16[512,1024]{1,0:T(8,128)(2,1)}, u32[]{:S(2)}) copy-start(bf16[512,1024]{1,0:T(8,128)(2,1)} %constant_dynamic-slice_fusion.1) | copy-start | bytes 3145732
  397.7 6.3 %copy-start.34 = (bf16[512,1024]{1,0:T(8,128)(2,1)S(1)}, bf16[512,1024]{1,0:T(8,128)(2,1)}, u32[]{:S(2)}) copy-start(bf16[512,1024]{1,0:T(8,128)(2,1)} %copy-done.33) | copy-start | bytes 3145732
  401.3 9.2 %copy-start.41 = (bf16[2,512,256]{2,1,0:T(8,128)(2,1)S(1)}, bf16[2,512,256]{2,1,0:T(8,128)(2,1)}, u32[]{:S(2)}) copy-start(bf16[2,512,256]{2,1,0:T(8,128)(2,1)} %get-tuple-element.87) | copy-start | bytes 1572868
  406.3 5.5 copy-start.39
  411.8 3.7 copy-start.27
  415.6 5.5 copy-start.37
  415.6 6.1 %copy-start.55 = (f32[256]{0:T(256)S(1)}, f32[256]{0:T(256)}, u32[]{:S(2)}) copy-start(f32[256]{0:T(256)} %broadcast_bitcast_fusion.1) | copy-start | bytes 3076
  415.6 13.1 %copy-start.17 = (bf16[2048,512]{1,0:T(8,128)(2,1)S(1)}, bf16[2048,512]{1,0:T(8,128)(2,1)}, u32[]{:S(2)}) copy-start(bf16[2048,512]{1,0:T(8,128)(2,1)} %param.21) | copy-start | bytes 6291460
  416.5 5.2 copy-start.22
  416.5 5.2 copy-start.23
  419.4 9.3 %copy-start.3 = (f32[512,2048]{1,0:T(8,128)S(1)}, f32[512,2048]{1,0:T(8,128)}, u32[]{:S(2)}) copy-start(f32[512,2048]{1,0:T(8,128)} %fusion.46) | copy-start | bytes 12582916
  423.0 5.7 copy-start
  423.0 5.7 copy-start.2
  423.0 9.9 %slice-start = ((s8[6291456]{0:T(1024)(128)(4,1)}), s8[4194304]{0:T(1024)(128)(4,1)S(1)}, s32[]{:S(2)}) async-start(s8[6291456]{0:T(1024)(128)(4,1)} %bitcast.151), calls=%async_computation | async-start | bytes 8388608
  426.9 6.0 %slice-start.1 = ((s8[6291456]{0:T(1024)(128)(4,1)}), s8[2097152]{0:T(1024)(128)(4,1)S(1)}, s32[]{:S(2)}) async-start(s8[6291456]{0:T(1024)(128)(4,1)} %bitcast.151), calls=%async_computation.1 | async-start | bytes 4194304
  426.9 12.5 %collective-permute-start.22 = (bf16[512,512]{1,0:T(8,128)(2,1)S(1)}, bf16[512,512]{1,0:T(8,128)(2,1)S(1)}, u32[]{:S(2)}, u32[]{:S(2)}) collective-permute-start(bf16[512,512]{1,0:T(8,128)(2,1)S(1)} %pad_maximum_fusion.8), channel_id=1, source_target_pairs={{0,1},{1,0},{2,3},{3,2},{4,5},{5,4},{6,7},{7,6},{8,9},{9,8},{10,11... | collective-permute-start | bytes 1572872 | tf_op jit(solution)/shard_map/ppermute | solution.py:1190
  432.9 5.8 copy-start.48
  432.9 6.4 %copy-start.32 = (bf16[512,1024]{1,0:T(8,128)(2,1)S(1)}, bf16[512,1024]{1,0:T(8,128)(2,1)}, u32[]{:S(2)}) copy-start(bf16[512,1024]{1,0:T(8,128)(2,1)} %constant_dynamic-slice_fusion.1) | copy-start | bytes 3145732
  432.9 6.4 %copy-start.35 = (bf16[512,1024]{1,0:T(8,128)(2,1)S(1)}, bf16[512,1024]{1,0:T(8,128)(2,1)}, u32[]{:S(2)}) copy-start(bf16[512,1024]{1,0:T(8,128)(2,1)} %copy-done.33) | copy-start | bytes 3145732
  581.7 3.6 copy-start.21
  (17 other events, 33.4 us)
